TPU v7x, 32 devices: a whole 2x2x4 slice. The times are simulated.
32 devices in a mesh: tensor: 4 (over y, core), seq: 8 (over z, x).
Axes of the slice: x: 2, y: 2, z: 4, core: 2. Of those that a mesh axis runs over, the one named last changes fastest.
Arguments:
- frames: bfloat16 [4096, 1536], P('seq', 'tensor'), may hold values from -8 to 8
- segment: int32 [4096], replicated, may hold values from 0 to 15, never falling along the last dimension, each value on 1 to 512 neighbouring positions
- time_token: bfloat16 [2, 1536], replicated, may hold values from -6 to 6
- context: bfloat16 [2, 128, 768], replicated, may hold values from -6 to 6
- gain_attn: float32 [1536], P('tensor'), may hold values from 0.5 to 1.5
- bias_attn: float32 [1536], P('tensor'), may hold values from -1.75 to 1.75
- gain_cross: float32 [1536], P('tensor'), may hold values from 0.5 to 1.5
- bias_cross: float32 [1536], P('tensor'), may hold values from -1.75 to 1.75
- gain_ffn: float32 [1536], P('tensor'), may hold values from 0.5 to 1.5
- bias_ffn: float32 [1536], P('tensor'), may hold values from -1.75 to 1.75
- w_query: bfloat16 [1536, 1536], P(None, 'tensor'), may hold values from -0.15625 to 0.15625
- w_key: bfloat16 [1536, 1536], P(None, 'tensor'), may hold values from -0.15625 to 0.15625
- w_value: bfloat16 [1536, 1536], P(None, 'tensor'), may hold values from -0.15625 to 0.15625
- w_out: bfloat16 [1536, 1536], P('tensor'), may hold values from -1.25 to 1.25
- c_query: bfloat16 [1536, 1536], P(None, 'tensor'), may hold values from -0.15625 to 0.15625
- c_key: bfloat16 [768, 1536], P(None, 'tensor'), may hold values from -0.21875 to 0.21875
- c_value: bfloat16 [768, 1536], P(None, 'tensor'), may hold values from -0.21875 to 0.21875
- c_out: bfloat16 [1536, 1536], P('tensor'), may hold values from -1.25 to 1.25
- w_gate: bfloat16 [1536, 6144], P(None, 'tensor'), may hold values from -1 to 1
- w_up: bfloat16 [1536, 6144], P(None, 'tensor'), may hold values from -1 to 1
- w_down: bfloat16 [6144, 1536], P('tensor'), may hold values from -0.078125 to 0.078125
- out_grad: bfloat16 [4096, 1536], P('seq', 'tensor'), may hold values from -8 to 8
Outputs:
- block_out: bfloat16 [4096, 1536], P('seq', 'tensor')
- d_frames: float32 [4096, 1536], P('seq', 'tensor')
- d_gain_attn: float32 [1536], P(('tensor', 'seq'))
- d_bias_attn: float32 [1536], P(('tensor', 'seq'))
- d_gain_cross: float32 [1536], P(('tensor', 'seq'))
- d_bias_cross: float32 [1536], P(('tensor', 'seq'))
- d_gain_ffn: float32 [1536], P(('tensor', 'seq'))
- d_bias_ffn: float32 [1536], P(('tensor', 'seq'))
- d_w_query: float32 [1536, 1536], P('seq', 'tensor')
- d_w_key: float32 [1536, 1536], P('seq', 'tensor')
- d_w_value: float32 [1536, 1536], P('seq', 'tensor')
- d_w_out: float32 [1536, 1536], P(('tensor', 'seq'))
- d_c_query: float32 [1536, 1536], P('seq', 'tensor')
- d_c_key: float32 [768, 1536], P('seq', 'tensor')
- d_c_value: float32 [768, 1536], P('seq', 'tensor')
- d_c_out: float32 [1536, 1536], P(('tensor', 'seq'))
- d_w_gate: float32 [1536, 6144], P('seq', 'tensor')
- d_w_up: float32 [1536, 6144], P('seq', 'tensor')
- d_w_down: float32 [6144, 1536], P(('tensor', 'seq'))
Inputs may be any that keep to these rules, and one draw needn't show every extreme that they name: `segment`: clip numbers never fall along the frames; each clip covers 1 to 512 frames and one covers exactly 512.
All inputs are finite; a program needn't handle non-finite values.
Results may differ from a plain program's by a relative error of at most 0.03.
Values may be sent and summed in bfloat16 or wider, within the bound.
No kernel may reach another device: no remote copies, remote signals or barrier semaphores. Data moves between devices by JAX's collectives and lax.ppermute only.
A program may use at most 192 MiB of HBM per device.

v0:
```python
import functools
import math

import jax
import jax.numpy as jnp
from jax import lax
from jax.experimental import pallas as pl
from jax.experimental.pallas import tpu as pltpu
from jax.sharding import PartitionSpec as P

HEAD_SIZE = 64
ROW_MIN = 2048
TILE = 256
BF16 = jnp.bfloat16
F32 = jnp.float32


def meeting(*values):
    return lax.optimization_barrier(values)


def after(value, token):
    return lax.optimization_barrier((value, token))[0]


def swap(value, axis, by):
    return lax.ppermute(value, axis, [(i, i ^ by) for i in range(lax.axis_size(axis))])


def shift(value, axis, by):
    peers = lax.axis_size(axis)
    pairs = [(i, i + by) for i in range(peers) if 0 <= i + by < peers]
    return lax.ppermute(value, axis, pairs)


def tensor_place():
    place = lax.axis_index("tensor")
    return place // 2, place % 2


def ordered(own, far, mate, far_mate, axis):
    side, core = tensor_place()
    near = (jnp.where(core == 0, own, mate), jnp.where(core == 0, mate, own))
    away = (jnp.where(core == 0, far, far_mate), jnp.where(core == 0, far_mate, far))
    low = [jnp.where(side == 0, n, a) for n, a in zip(near, away)]
    high = [jnp.where(side == 0, a, n) for n, a in zip(near, away)]
    return jnp.concatenate(low + high, axis)


def gather_near(own):
    far = swap(own, "tensor", 2)
    return own, swap(own, "tensor", 1), far, swap(far, "tensor", 1)


def gather_staged(own, first, second):
    far = swap(after(own, first), "tensor", 2)
    far, late = after((far, own), second)
    return own, swap(late, "tensor", 1), far, swap(far, "tensor", 1)


def gather(own, axis):
    own, mate, far, far_mate = gather_near(own)
    return ordered(own, far, mate, far_mate, axis)


def scatter_near(away, low):
    got = swap(away, "tensor", 1)
    total = (low.astype(F32) + got[low.shape[0] :].astype(F32)).astype(BF16)
    return got, total, swap(total, "tensor", 2)


def rows_to_cols(own, mate, far, far_mate, later):
    width = own.shape[1]
    got = after(swap(jnp.concatenate([far, far_mate], 1), "tensor", 2), later)
    other = swap(jnp.concatenate([mate, got[:, width:]], 0), "tensor", 1)
    size = own.shape[0]
    return jnp.concatenate([own, other[:size], got[:, :width], other[size:]], 0)


def quarters(value, axis):
    return jnp.split(value, 4, axis)


def own_blocks(near):
    return jnp.concatenate([quarters(value, 1)[r] for r, value in enumerate(near)], 0)


def trade(value, start, done):
    return after(swap(after(value, start), "seq", 1), done)


def halve(blocks, bit):
    count, rows, cols = blocks.shape
    side = (lax.axis_index("seq") >> bit) % 2
    parts = blocks.reshape(count // 2, 2, rows, cols)
    send = lax.dynamic_index_in_dim(parts, 1 - side, 1, False)
    keep = lax.dynamic_index_in_dim(parts, side, 1, False)
    return keep, swap(send, "seq", 1 << bit)


def added(keep, got):
    return keep.astype(F32) + got.astype(F32)


def halve_all(blocks, bit):
    while blocks.shape[0] > 1:
        blocks = added(*halve(blocks.astype(BF16), bit))
        bit += 1
    return blocks[0].astype(F32)


def halve_end(keep, got, bit):
    return halve_all(added(keep, got), bit)


def frame_clip_labels(segment, row_length):
    frame_index = jnp.arange(segment.shape[0], dtype=jnp.int32)
    border = (frame_index % row_length == 0) | (segment != jnp.roll(segment, 1))
    clip_starts = lax.cummax(jnp.where(border, frame_index, 0), axis=0)
    return (clip_starts, (frame_index - clip_starts + 1).astype(jnp.float32))


def tile_ranges(q_labels, key_labels):
    q = q_labels.reshape(-1, TILE)
    k = key_labels.reshape(-1, TILE)
    meets = (k[None, :, 0] <= q[:, None, -1]) & (k[None, :, -1] >= q[:, None, 0])
    index = jnp.arange(k.shape[0], dtype=jnp.int32)[None]
    low = jnp.min(jnp.where(meets, index, k.shape[0]), 1)
    high = jnp.max(jnp.where(meets, index + 1, 0), 1)
    return jnp.stack([low, high], 1).reshape(-1)

def head_rows(g):
    return slice(g * HEAD_SIZE, (g + 1) * HEAD_SIZE)

def fill_natural(dest, refs, which):
    size = refs[0].shape[2]
    for part, ref in enumerate(refs):
        dest[part * size : (part + 1) * size, :] = ref[which].T


def fill_tiles(dest, refs, which):
    pieces = refs[0].shape[2] // TILE
    for part, ref in enumerate(refs):
        for piece in range(pieces):
            dest[part * pieces + piece] = ref[which, :, piece * TILE : (piece + 1) * TILE]


def relative(place, r, size):
    return pl.ds(pl.multiple_of((place ^ r) * size, size), size)


def absorb(state, start, stop, base, q, cols, lab, klab, keys, vals):
    group = q.shape[0] // HEAD_SIZE

    def step(j, state):
        seen = klab[pl.ds(pl.multiple_of(j * TILE, TILE), TILE), :] == lab
        at = pl.ds(pl.multiple_of((j - base) * TILE, TILE), TILE)
        fresh = []
        for g in range(group):
            top, total, acc = state[3 * g : 3 * g + 3]
            s = dot_nn(keys[at, head_rows(g)], q[head_rows(g), cols])
            s = jnp.where(seen, s, -1e30)
            new = jnp.maximum(top, jnp.max(s, 0, keepdims=True))
            fade = jnp.exp(top - new)
            p = jnp.exp(s - new)
            total = total * fade + jnp.sum(p, 0, keepdims=True)
            acc = acc * fade + dot_nn(vals[j - base, head_rows(g), :], p.astype(BF16))
            fresh += [new, total, acc]
        return tuple(fresh)

    return lax.fori_loop(start, stop, step, tuple(state))


def near_body(span, q, kv, tk, tv, qlab, klab, tops, totals, mix, keys, vals):
    rows, size = q.shape
    pieces = size // TILE
    fill_natural(keys, (kv,), 0)
    fill_tiles(vals, (kv,), 1)
    for tile in range(pieces):
        cols = slice(tile * TILE, (tile + 1) * TILE)
        state = []
        for g in range(rows // HEAD_SIZE):
            part = q[head_rows(g), cols].astype(F32)
            top = jnp.sum(part * tk[head_rows(g), :], 0, keepdims=True)
            state += [
                top,
                jnp.ones_like(top),
                jnp.broadcast_to(tv[head_rows(g), :], (HEAD_SIZE, TILE)),
            ]
        start = jnp.maximum(span[2 * tile], pieces)
        stop = jnp.minimum(span[2 * tile + 1], 2 * pieces)
        state = absorb(state, start, stop, pieces, q, cols, qlab[:, cols], klab, keys, vals)
        for g in range(rows // HEAD_SIZE):
            tops[g : g + 1, cols], totals[g : g + 1, cols], mix[head_rows(g), cols] = state[
                3 * g : 3 * g + 3
            ]


def far_body(span, q, kv0, kv2, qlab, klab, w_out, tops, totals, mix,
             out, lse, away, own, low, keys0, keys2, vals0, vals2):
    rows, size = q.shape
    pieces = size // TILE
    for kv, keys, vals in ((kv0, keys0, vals0), (kv2, keys2, vals2)):
        fill_natural(keys, (kv,), 0)
        fill_tiles(vals, (kv,), 1)
    for tile in range(pieces):
        cols = slice(tile * TILE, (tile + 1) * TILE)
        lab = qlab[:, cols]
        state = []
        for g in range(rows // HEAD_SIZE):
            state += [tops[g : g + 1, cols], totals[g : g + 1, cols], mix[head_rows(g), cols]]
        stop = jnp.minimum(span[2 * tile + 1], pieces)
        state = absorb(state, span[2 * tile], stop, 0, q, cols, lab, klab, keys0, vals0)
        start = jnp.maximum(span[2 * tile], 2 * pieces)
        state = absorb(
            state, start, span[2 * tile + 1], 2 * pieces, q, cols, lab, klab, keys2, vals2
        )
        for g in range(rows // HEAD_SIZE):
            top, total, acc = state[3 * g : 3 * g + 3]
            out[head_rows(g), cols] = (acc / total).astype(BF16)
            lse[g : g + 1, cols] = top + jnp.log(total)
    place = span[2 * pieces]
    share = own.shape[0]

    def sent(r):
        return dot_tn(out[:, relative(place, r, share)], w_out[...])

    away[:share, :] = sent(1).astype(BF16)
    away[share:, :] = sent(3).astype(BF16)
    low[...] = sent(2).astype(BF16)
    own[...] = sent(0)


def backward_body(span, q, kv0, kv1, kv2, tk, tv, qlab, klab, w_out, out, lse,
                  g0, g1, g2, g3, dq, to_prev, kept, to_next, dtk, dtv,
                  og, keys, vals, tkeys, ak, av):
    rows, size = q.shape
    group = rows // HEAD_SIZE
    pieces = size // TILE
    share = g0.shape[0]
    for r, ref in enumerate((g0, g1, g2, g3)):
        og[:, relative(span[2 * pieces], r, share)] = dot_nt(w_out[...], ref[...]).astype(BF16)
    fill_natural(keys, (kv0, kv1, kv2), 0)
    fill_natural(vals, (kv0, kv1, kv2), 1)
    fill_tiles(tkeys, (kv0, kv1, kv2), 0)
    ak[...] = jnp.zeros_like(ak)
    av[...] = jnp.zeros_like(av)
    for tile in range(pieces):
        cols = slice(tile * TILE, (tile + 1) * TILE)
        lab = qlab[:, cols]
        state, norms, deltas = [], [], []
        for g in range(group):
            hr = head_rows(g)
            qf = q[hr, cols].astype(F32)
            gf = og[hr, cols].astype(F32)
            norm = lse[g : g + 1, cols]
            delta = jnp.sum(gf * out[hr, cols].astype(F32), 0, keepdims=True)
            pt = jnp.exp(jnp.sum(qf * tk[hr, :], 0, keepdims=True) - norm)
            st = pt * (jnp.sum(gf * tv[hr, :], 0, keepdims=True) - delta)
            gk = jnp.sum(qf * st, 1, keepdims=True)
            gv = jnp.sum(gf * pt, 1, keepdims=True)
            if tile == 0:
                dtk[hr, :] = gk
                dtv[hr, :] = gv
            else:
                dtk[hr, :] += gk
                dtv[hr, :] += gv
            state.append(tk[hr, :] * st)
            norms.append(norm)
            deltas.append(delta)

        def step(j, state):
            start = pl.multiple_of(j * TILE, TILE)
            seen = klab[pl.ds(start, TILE), :] == lab
            fresh = []
            for g in range(group):
                hr = head_rows(g)
                s = dot_nn(keys[pl.ds(start, TILE), hr], q[hr, cols])
                p = jnp.exp(jnp.where(seen, s, -1e30) - norms[g])
                m = dot_nn(vals[pl.ds(start, TILE), hr], og[hr, cols])
                ds = (p * (m - deltas[g])).astype(BF16)
                av[j, hr, :] += dot_nt(og[hr, cols], p.astype(BF16))
                ak[j, hr, :] += dot_nt(q[hr, cols], ds)
                fresh.append(state[g] + dot_nn(tkeys[j, hr, :], ds))
            return tuple(fresh)

        state = lax.fori_loop(span[2 * tile], span[2 * tile + 1], step, tuple(state))
        for g in range(group):
            dq[head_rows(g), cols] = state[g]
    for part, dest in enumerate((to_prev, kept, to_next)):
        for piece in range(pieces):
            at = slice(piece * TILE, (piece + 1) * TILE)
            dest[0, :, at] = ak[part * pieces + piece].astype(dest.dtype)
            dest[1, :, at] = av[part * pieces + piece].astype(dest.dtype)


def attend_near(span, q, kv, tk, tv, qlab, klab):
    cols, size = q.shape
    wide = lambda *dims: jax.ShapeDtypeStruct(dims, F32)
    vmem = pl.BlockSpec(memory_space=pltpu.VMEM)
    return pl.pallas_call(
        near_body,
        in_specs=[pl.BlockSpec(memory_space=pltpu.SMEM)] + [vmem] * 6,
        out_specs=[vmem] * 3,
        out_shape=[wide(cols // HEAD_SIZE, size), wide(cols // HEAD_SIZE, size), wide(cols, size)],
        scratch_shapes=[pltpu.VMEM((size, cols), BF16), pltpu.VMEM((size // TILE, cols, TILE), BF16)],
        name="attend_near", cost_estimate=FREE,
    )(span, q, kv, tk, tv, qlab, klab)


def attend_far(span, q, behind, ahead, qlab, klab, w_out, state):
    cols, size = q.shape
    share, width = size // 4, w_out.shape[1]
    low = lambda *dims: jax.ShapeDtypeStruct(dims, BF16)
    wide = lambda *dims: jax.ShapeDtypeStruct(dims, F32)
    vmem = pl.BlockSpec(memory_space=pltpu.VMEM)
    keys = pltpu.VMEM((size, cols), BF16)
    vals = pltpu.VMEM((size // TILE, cols, TILE), BF16)
    return pl.pallas_call(
        far_body,
        in_specs=[pl.BlockSpec(memory_space=pltpu.SMEM)] + [vmem] * 9,
        out_specs=[vmem] * 5,
        out_shape=[low(cols, size), wide(cols // HEAD_SIZE, size), low(2 * share, width),
                   wide(share, width), low(share, width)],
        scratch_shapes=[keys, keys, vals, vals],
        name="attend_far", cost_estimate=FREE,
    )(span, q, behind, ahead, qlab, klab, w_out, *state)


def attend_back(span, q, kvs, tk, tv, qlab, klab, w_out, out, lse, grads):
    cols, size = q.shape
    tiles = 3 * size // TILE
    low = lambda *dims: jax.ShapeDtypeStruct(dims, BF16)
    wide = lambda *dims: jax.ShapeDtypeStruct(dims, F32)
    vmem = pl.BlockSpec(memory_space=pltpu.VMEM)
    return pl.pallas_call(
        backward_body,
        in_specs=[pl.BlockSpec(memory_space=pltpu.SMEM)] + [vmem] * 15,
        out_specs=[vmem] * 6,
        out_shape=[wide(cols, size), low(2, cols, size), wide(2, cols, size), low(2, cols, size),
                   wide(cols, 1), wide(cols, 1)],
        scratch_shapes=[pltpu.VMEM((cols, size), BF16), pltpu.VMEM((3 * size, cols), BF16),
                        pltpu.VMEM((3 * size, cols), BF16), pltpu.VMEM((tiles, cols, TILE), BF16),
                        pltpu.VMEM((tiles, cols, TILE), F32), pltpu.VMEM((tiles, cols, TILE), F32)],
        name="attend_back", cost_estimate=FREE,
    )(span, q, *kvs, tk, tv, qlab, klab, w_out, out, lse, *grads)


def tail_body(place, dq, kept, ahead, behind, cosine, sine, wq, wk, wv, raw, away, own, low, flipped):
    part, size = dq.shape
    half = HEAD_SIZE // 2

    def returned(block, base, scale):
        for h in range(part // HEAD_SIZE):
            a = block[h * HEAD_SIZE : h * HEAD_SIZE + half, :]
            b = block[h * HEAD_SIZE + half : (h + 1) * HEAD_SIZE, :]
            at = base + h * HEAD_SIZE
            raw[at : at + half, :] = ((a * cosine[...] + b * sine[...]) * scale).astype(BF16)
            raw[at + half : at + HEAD_SIZE, :] = (
                (b * cosine[...] - a * sine[...]) * scale
            ).astype(BF16)

    def whole(index):
        return kept[index] + ahead[index].astype(F32) + behind[index].astype(F32)

    returned(dq[...], 0, 1.0 / math.sqrt(HEAD_SIZE))
    returned(whole(0), part, 1.0)
    raw[2 * part :, :] = whole(1).astype(BF16)
    flipped[...] = raw[...].T

    def sent(r):
        at = relative(place[0], r, part)
        return sum(
            dot_nt(flipped[:, i * part : (i + 1) * part], weight[at, :])
            for i, weight in enumerate((wq, wk, wv))
        )

    away[:size, :] = sent(1).astype(BF16)
    away[size:, :] = sent(3).astype(BF16)
    low[...] = sent(2).astype(BF16)
    own[...] = sent(0)


def tail(place, dq, kept, ahead, behind, tables, wq, wk, wv):
    part, size = dq.shape
    low = lambda *dims: jax.ShapeDtypeStruct(dims, BF16)
    vmem = pl.BlockSpec(memory_space=pltpu.VMEM)
    return pl.pallas_call(
        tail_body,
        in_specs=[pl.BlockSpec(memory_space=pltpu.SMEM)] + [vmem] * 9,
        out_specs=[vmem] * 4,
        out_shape=[low(3 * part, size), low(2 * size, part), jax.ShapeDtypeStruct((size, part), F32),
                   low(size, part)],
        scratch_shapes=[pltpu.VMEM((size, 3 * part), BF16)],
        name="tail", cost_estimate=FREE,
    )(place, dq, kept, ahead, behind, *tables, wq, wk, wv)


def rotary_tables(frame_positions):
    half_dim = HEAD_SIZE // 2
    frequency = jnp.exp(jnp.arange(half_dim, dtype=jnp.float32) * (-math.log(10000.0) / half_dim))
    angles = frequency[:, None] * frame_positions[None, :]
    return (jnp.cos(angles), jnp.sin(angles))


def rotate(rows, tables, sign=1.0):
    count, size = rows.shape
    halves = rows.reshape(count // HEAD_SIZE, 2, HEAD_SIZE // 2, size)
    cosine, sine = tables[0][None], tables[1][None] * sign
    first = halves[:, 0] * cosine - halves[:, 1] * sine
    second = halves[:, 1] * cosine + halves[:, 0] * sine
    return jnp.stack([first, second], 1).reshape(count, size)


def product(left, right):
    return jnp.dot(left, right, preferred_element_type=jnp.float32)


def inner_rows(left, right):
    return jnp.einsum("nd,nf->df", left, right, preferred_element_type=jnp.float32)


def back_project(gradient, weight):
    return jnp.einsum("nf,df->nd", gradient, weight, preferred_element_type=jnp.float32)


def by_feature(left, right):
    return jnp.einsum("nd,df->fn", left, right, preferred_element_type=jnp.float32)


def columns(weight, start, size):
    return lax.dynamic_slice_in_dim(weight, start, size, 1)


def rows_of(weight, start, size):
    return lax.dynamic_slice_in_dim(weight, start, size, 0)


def normalize(value_rows):
    means = jnp.mean(value_rows, -1, keepdims=True)
    centred = value_rows - means
    inverse = lax.rsqrt(jnp.mean(centred * centred, -1, keepdims=True) + 1e-05)
    return centred * inverse, inverse


def norm_backward(gradient, scaled, inverse, norm_gain):
    scaled_grad = gradient * norm_gain
    plain = jnp.mean(scaled_grad, -1, keepdims=True)
    cross = jnp.mean(scaled_grad * scaled, -1, keepdims=True)
    return inverse * (scaled_grad - plain - scaled * cross)


FREE = pl.CostEstimate(flops=1, transcendentals=0, bytes_accessed=1)


def dot_nn(left, right):
    return lax.dot_general(left, right, (((1,), (0,)), ((), ())), preferred_element_type=F32)


def dot_nt(left, right):
    return lax.dot_general(left, right, (((1,), (1,)), ((), ())), preferred_element_type=F32)


def dot_tn(left, right):
    return lax.dot_general(left, right, (((0,), (0,)), ((), ())), preferred_element_type=F32)


def head_weights(query, key, lanes, which):
    mine = jnp.where(lanes == which, query, jnp.zeros_like(query))
    scores = dot_nt(mine, key) * (1.0 / math.sqrt(HEAD_SIZE))
    weights = jnp.exp(scores - jnp.max(scores, -1, keepdims=True))
    return weights / jnp.sum(weights, -1, keepdims=True)


def pair_cols(refs, p, rows):
    ref = refs[p * 2 * HEAD_SIZE // refs[0].shape[1]]
    start = p * 2 * HEAD_SIZE % refs[0].shape[1]
    return ref[rows, start : start + 2 * HEAD_SIZE]


def cross_forward_body(width_block, place, rows, own, got, far, norms, q0, q1, q2, q3,
                       c0, c1, c2, c3, o0, o1, o2, o3,
                       front, queries, first, second, normed_three,
                       flip_own, flip_away):
    width = rows.shape[1]
    kv = (c0, c1, c2, c3)
    context_rows = c0.shape[0] // 2
    key_rows, value_rows = slice(0, context_rows), slice(context_rows, 2 * context_rows)
    lanes = lax.broadcasted_iota(jnp.int32, (rows.shape[0], 2 * HEAD_SIZE), 1) // HEAD_SIZE
    residual = (
        rows[...].astype(F32) + own[...] + got[...].astype(F32) + far[...].astype(F32)
    )
    first[...] = residual
    scaled, _ = normalize(residual)
    low = (scaled * norms[2:3, :] + norms[3:4, :]).astype(BF16)
    front[:, :width] = low
    part = width // 4
    for b, ref in enumerate((q0, q1, q2, q3)):
        queries[:, b * part : (b + 1) * part] = dot_nn(low, ref[...]).astype(BF16)
    for p in range(width // (2 * HEAD_SIZE)):
        cols = slice(p * 2 * HEAD_SIZE, (p + 1) * 2 * HEAD_SIZE)
        q, k, v = queries[:, cols], pair_cols(kv, p, key_rows), pair_cols(kv, p, value_rows)
        mixed = [dot_nn(head_weights(q, k, lanes, g).astype(BF16), v) for g in (0, 1)]
        front[:, width + cols.start : width + cols.stop] = jnp.where(lanes == 0, mixed[0], mixed[1]).astype(BF16)
    for b, ref in enumerate((o0, o1, o2, o3)):
        residual = residual + dot_nn(front[:, width + b * part : width + (b + 1) * part], ref[...])
    second[...] = residual
    scaled, _ = normalize(residual)
    low = (scaled * norms[4:5, :] + norms[5:6, :]).astype(BF16)
    normed_three[...] = low
    deal_rows(low.T, width_block, place[0], flip_own, flip_away)


def cross_forward(devices, place, rows, own, got, far, norms, query_parts, kv_parts, out_parts):
    size, width = rows.shape
    low = jax.ShapeDtypeStruct(rows.shape, BF16)
    both = jax.ShapeDtypeStruct((size, 2 * width), BF16)
    wide = jax.ShapeDtypeStruct(rows.shape, F32)
    flip = jax.ShapeDtypeStruct((width // 2, size), BF16)
    vmem = pl.BlockSpec(memory_space=pltpu.VMEM)
    block = pl.BlockSpec((size, width), lambda i: (0, 0))
    return pl.pallas_call(
        functools.partial(cross_forward_body, width // devices),
        grid=(1,),
        in_specs=[pl.BlockSpec(memory_space=pltpu.SMEM)] + [block] * 4 + [vmem] * 13,
        out_shape=[both, low, wide, wide, low, flip, flip],
        cost_estimate=FREE, name="cross",
    )(place, rows, own, got, far, norms, *query_parts, *kv_parts, *out_parts)


def deal_rows(rows, size, column, own, away):
    for b in range(rows.shape[0] // (2 * size)):
        at = slice(b * size, (b + 1) * size)
        even = rows[2 * b * size : (2 * b + 1) * size, :]
        odd = rows[(2 * b + 1) * size : (2 * b + 2) * size, :]

        @pl.when(column == 0)
        def _():
            own[at, :] = even
            away[at, :] = odd

        @pl.when(column != 0)
        def _():
            own[at, :] = odd
            away[at, :] = even


def ffn_part(normed, grad, gate_w, up_w, down_w, hidden, hid_own, hid_away, gate_grad, lifted_grad,
             unit_block, column):
    gate = dot_nn(normed, gate_w[...])
    lifted = dot_nn(normed, up_w[...])
    back = dot_nt(grad, down_w[...]).astype(BF16).astype(F32)
    sig = jax.nn.sigmoid(gate)
    swish = gate * sig
    made = (swish * lifted).astype(BF16)
    hidden[...] = made
    deal_rows(made.T, unit_block, column, hid_own, hid_away)
    gg = (back * lifted * sig * (1.0 + gate * (1.0 - sig))).astype(BF16)
    lg = (back * swish).astype(BF16)
    gate_grad[...] = gg
    lifted_grad[...] = lg
    return dot_nt(gg, gate_w[...]) + dot_nt(lg, up_w[...])


def ffn_first_body(unit_block, place, n0, n1, n2, n3, g0, g1, g2, g3, gate_w, up_w, down_w,
                   hidden, hid_own, hid_away, gate_grad, lifted_grad, normed, grad, grad_pair,
                   total):
    share, part = n0.shape[0], g0.shape[2]
    for b, ref in enumerate((n0, n1, n2, n3)):
        normed[b * share : (b + 1) * share, :] = ref[...]
    for c, ref in enumerate((g0, g1, g2, g3)):
        for b in range(4):
            rows, cols = relative(place[1], b, share), relative(place[1], c, part)
            grad[b * share : (b + 1) * share, cols] = ref[0, rows, :]
            grad_pair[b * share : (b + 1) * share, cols] = ref[1, rows, :]
    total[...] = ffn_part(
        normed[...], grad[...], gate_w, up_w, down_w, hidden, hid_own, hid_away, gate_grad,
        lifted_grad, unit_block, place[0],
    )


def ffn_second_body(unit_block, place, normed, grad, total, gate_w, up_w, down_w,
                    hidden, hid_own, hid_away, gate_grad, lifted_grad, away, own, low):
    share = own.shape[0]
    found = total[...] + ffn_part(
        normed[...], grad[...], gate_w, up_w, down_w, hidden, hid_own, hid_away, gate_grad,
        lifted_grad, unit_block, place[0],
    )
    own[...] = found[:share, :]
    low[...] = found[2 * share : 3 * share, :].astype(BF16)
    away[:share, :] = found[share : 2 * share, :].astype(BF16)
    away[share:, :] = found[3 * share :, :].astype(BF16)


def ffn(devices, place, half, inputs, gate_w, up_w, down_w):
    share = inputs[0].shape[0] if half == 0 else inputs[0].shape[0] // 4
    width = inputs[0].shape[1]
    size, units = 4 * share, gate_w.shape[1]
    tile = units // 2
    low = lambda *dims: jax.ShapeDtypeStruct(dims, BF16)
    wide = lambda *dims: jax.ShapeDtypeStruct(dims, F32)
    vmem = pl.BlockSpec(memory_space=pltpu.VMEM)
    cols = pl.BlockSpec((width, tile), lambda i: (0, half))
    rows = pl.BlockSpec((tile, width), lambda i: (half, 0))
    made = [low(size, tile), low(tile // 2, size), low(tile // 2, size), low(size, tile),
            low(size, tile)]
    if half == 0:
        made += [low(size, width), low(size, width), low(size, width), wide(size, width)]
    else:
        made += [low(2 * share, width), wide(share, width), low(share, width)]
    return pl.pallas_call(
        functools.partial(ffn_second_body if half else ffn_first_body, units // devices),
        grid=(1,),
        in_specs=[pl.BlockSpec(memory_space=pltpu.SMEM)] + [vmem] * len(inputs)
        + [cols, cols, rows],
        out_specs=[vmem] * len(made),
        out_shape=made,
        cost_estimate=FREE, name="ffn",
    )(place, *inputs, gate_w, up_w, down_w)


def cross_backward_body(own, got, far, grad, first, second, norms, q0, q1, q2, q3,
                        c0, c1, c2, c3, o0, o1, o2, o3, queries,
                        back_rows, kv_grad, vectors, grad_one, crossed_grad):
    width = grad.shape[1]
    kv = (c0, c1, c2, c3)
    context_rows = c0.shape[0] // 2
    key_rows, value_rows = slice(0, context_rows), slice(context_rows, 2 * context_rows)
    part = width // 4
    lanes = lax.broadcasted_iota(jnp.int32, (grad.shape[0], 2 * HEAD_SIZE), 1) // HEAD_SIZE
    lane_k = lax.broadcasted_iota(jnp.int32, (context_rows, 2 * HEAD_SIZE), 1) // HEAD_SIZE
    scale = 1.0 / math.sqrt(HEAD_SIZE)
    arrived = own[...] + got[...].astype(F32) + far[...].astype(F32)
    scaled, inverse = normalize(second[...])
    vectors[0:1, :] = jnp.sum(arrived * scaled, 0, keepdims=True)
    vectors[1:2, :] = jnp.sum(arrived, 0, keepdims=True)
    two = grad[...].astype(F32) + norm_backward(arrived, scaled, inverse, norms[4:5, :])
    low = two.astype(BF16)
    back_rows[:, :width] = low
    for b, ref in enumerate((o0, o1, o2, o3)):
        crossed_grad[:, b * part : (b + 1) * part] = dot_nt(low, ref[...]).astype(BF16)
    for p in range(width // (2 * HEAD_SIZE)):
        cols = slice(p * 2 * HEAD_SIZE, (p + 1) * 2 * HEAD_SIZE)
        q, k, v = queries[:, cols], pair_cols(kv, p, key_rows), pair_cols(kv, p, value_rows)
        g_rows = crossed_grad[:, cols]
        found = []
        for g in (0, 1):
            probs = head_weights(q, k, lanes, g)
            change = dot_nt(jnp.where(lanes == g, g_rows, jnp.zeros_like(g_rows)), v)
            delta = jnp.sum(change * probs, -1, keepdims=True)
            ds = (probs * (change - delta)).astype(BF16)
            found.append((dot_nn(ds, k), dot_tn(ds, q), dot_tn(probs.astype(BF16), g_rows)))
        back_rows[:, width + cols.start : width + cols.stop] = (
            jnp.where(lanes == 0, found[0][0], found[1][0]) * scale
        ).astype(BF16)
        kv_grad[:context_rows, cols] = (
            jnp.where(lane_k == 0, found[0][1], found[1][1]) * scale
        ).astype(BF16)
        kv_grad[context_rows:, cols] = jnp.where(lane_k == 0, found[0][2], found[1][2]).astype(
            BF16
        )
    back = jnp.zeros(grad.shape, F32)
    for b, ref in enumerate((q0, q1, q2, q3)):
        back = back + dot_nt(back_rows[:, width + b * part : width + (b + 1) * part], ref[...])
    scaled, inverse = normalize(first[...])
    vectors[2:3, :] = jnp.sum(back * scaled, 0, keepdims=True)
    vectors[3:4, :] = jnp.sum(back, 0, keepdims=True)
    grad_one[...] = (two + norm_backward(back, scaled, inverse, norms[2:3, :])).astype(BF16)


def cross_backward(own, got, far, grad, first, second, norms, query_parts, kv_parts, out_parts,
                   queries):
    rows, width = own.shape
    low = lambda r: jax.ShapeDtypeStruct((r, width), BF16)
    block = pl.BlockSpec((rows, width), lambda i: (0, 0))
    return pl.pallas_call(
        cross_backward_body,
        grid=(1,),
        out_shape=[jax.ShapeDtypeStruct((rows, 2 * width), BF16), low(kv_parts[0].shape[0]),
                   jax.ShapeDtypeStruct((4, width), F32), low(rows)],
        in_specs=[block] * 6 + [pl.BlockSpec(memory_space=pltpu.VMEM)] * 14,
        scratch_shapes=[pltpu.VMEM((rows, width), BF16)],
        cost_estimate=FREE, name="cross_back",
    )(own, got, far, grad, first, second, norms, *query_parts, *kv_parts, *out_parts, queries)


def meet_rows_body(own_a, pair_a, own_b, pair_b, right, right_pair, out):
    count = own_a.shape[0]
    for b, (own, pair) in enumerate(((own_a, pair_a), (own_b, pair_b))):
        out[b * count : (b + 1) * count, :] = (
            dot_nn(own[...], right[...]) + dot_nn(pair[...], right_pair[...])
        ).astype(BF16)


def meet_rows(lefts, rights):
    count, size = lefts[0].shape
    width = rights[0].shape[1]
    tile = width // 3
    left = pl.BlockSpec((count, size), lambda i: (0, 0))
    right = pl.BlockSpec((size, tile), lambda i: (0, i))
    return pl.pallas_call(
        meet_rows_body,
        grid=(3,),
        in_specs=[left] * 4 + [right] * 2,
        out_specs=pl.BlockSpec((2 * count, tile), lambda i: (0, i)),
        out_shape=jax.ShapeDtypeStruct((2 * count, width), BF16),
        name="meet_rows", cost_estimate=FREE,
    )(*lefts, *rights)


def meet_cols_body(p0, p1, p2, p3, a, a_pair, b, b_pair, out):
    own, pair = (jnp.concatenate([p[i] for p in (p0, p1, p2, p3)], 1) for i in (0, 1))
    width = a.shape[1]
    out[:, :width] = (dot_nn(own, a[...]) + dot_nn(pair, a_pair[...])).astype(BF16)
    out[:, width:] = (dot_nn(own, b[...]) + dot_nn(pair, b_pair[...])).astype(BF16)


def meet_cols(near, rights):
    return pl.pallas_call(
        meet_cols_body,
        out_shape=jax.ShapeDtypeStruct((near[0].shape[1], 2 * rights[0].shape[1]), BF16),
        name="meet_cols", cost_estimate=FREE,
    )(*near, *rights)


def down_body(first, second, down_w, away, own, low):
    share, units = own.shape[0], first.shape[1]

    def sent(r):
        at = slice(r * share, (r + 1) * share)
        return dot_nn(first[at, :], down_w[:units, :]) + dot_nn(second[at, :], down_w[units:, :])

    away[:share, :] = sent(1).astype(BF16)
    away[share:, :] = sent(3).astype(BF16)
    low[...] = sent(2).astype(BF16)
    own[...] = sent(0)


def down_parts(first, second, down_w):
    share, width = first.shape[0] // 4, down_w.shape[1]
    low = lambda *dims: jax.ShapeDtypeStruct(dims, BF16)
    return pl.pallas_call(
        down_body,
        out_shape=[low(2 * share, width), jax.ShapeDtypeStruct((share, width), F32),
                   low(share, width)],
        name="down", cost_estimate=FREE,
    )(first, second, down_w)


def bundle_body(devices, place, f02, f13, b02, b13, a0, a1, a2, a3, attended,
                context, kv, out_a, out_b):
    width = a0.shape[1]
    part, share = width // 4, a0.shape[0]

    def near(even, odd):
        return even[0], odd[0], even[1], odd[1]

    own = lambda rows: jnp.concatenate(
        [row[:, width + r * part : width + (r + 1) * part] for r, row in enumerate(rows)], 0
    )
    full = lambda rows: jnp.concatenate([row[:, :width] for row in rows], 0)
    fronts, backs = near(f02, f13), near(b02, b13)
    rows = width // devices
    small = part // devices
    half = width // 2

    def put(block, base, left, out):
        for d in range(devices):
            at = slice(base, base + block.shape[0] // devices)
            piece = block[d * block.shape[0] // devices : (d + 1) * block.shape[0] // devices, :]
            out[d, at, left : left + block.shape[1]] = piece.astype(BF16)

    put(dot_tn(full(fronts), own(backs)), 0, 0, out_a)
    count = context.shape[0]
    put(dot_tn(context[...], kv[:count, :]), 0, part, out_a)
    put(dot_tn(context[...], kv[count:, :]), rows // 2, part, out_a)
    grads = dot_tn(own(fronts), full(backs))
    put(grads[:, :half], 0, 0, out_b)
    put(grads[:, half:], small, 0, out_b)
    grads = sum(
        dot_nn(attended[:, relative(place[0], r, share)], ref[...])
        for r, ref in enumerate((a0, a1, a2, a3))
    )
    put(grads[:, :half], 2 * small, 0, out_b)
    put(grads[:, half:], 3 * small, 0, out_b)


def bundle_grads(devices, place, fronts, backs, ones, attended, context, kv):
    width = ones[0].shape[1]
    vmem = pl.BlockSpec(memory_space=pltpu.VMEM)
    return pl.pallas_call(
        functools.partial(bundle_body, devices),
        in_specs=[pl.BlockSpec(memory_space=pltpu.SMEM)] + [vmem] * 11,
        out_specs=[vmem] * 2,
        out_shape=[jax.ShapeDtypeStruct((devices, width // devices, width // 2), BF16)] * 2,
        name="bundle", cost_estimate=FREE,
    )(place, *fronts, *backs, *ones, attended, context, kv)


def front_body(width_block, place, x0, x1, x2, x3, g0, g1, g2, g3, cosine, sine, wq, wk, wv,
               queries, pair, rows, low, nrm_own, nrm_away, norms, means, inverses, wide):
    size, part = x0.shape
    for r, (x, g) in enumerate(((x0, g0), (x1, g1), (x2, g2), (x3, g3))):
        start = pl.multiple_of((place[0] ^ r) * part, 128)
        wide[:, pl.ds(start, part)] = x[...]
        norms[:, pl.ds(start, part)] = g[...]
    share = size // 4
    rows[...] = wide[pl.ds(pl.multiple_of(place[0] * share, share), share), :]
    values = wide[...].astype(F32)
    mean = jnp.mean(values, -1, keepdims=True)
    centred = values - mean
    inverse = lax.rsqrt(jnp.mean(centred * centred, -1, keepdims=True) + 1e-05)
    means[...] = mean
    inverses[...] = inverse
    normed = (centred * inverse * norms[0:1, :] + norms[1:2, :]).astype(BF16)
    low[...] = normed
    half = HEAD_SIZE // 2

    def turned(weight):
        return dot_nn(normed, weight[...]).T

    def rotated(block, dest, scale):
        for h in range(part // HEAD_SIZE):
            a = block[h * HEAD_SIZE : h * HEAD_SIZE + half, :]
            b = block[h * HEAD_SIZE + half : (h + 1) * HEAD_SIZE, :]
            dest[h * HEAD_SIZE : h * HEAD_SIZE + half, :] = (
                (a * cosine[...] - b * sine[...]) * scale
            ).astype(BF16)
            dest[h * HEAD_SIZE + half : (h + 1) * HEAD_SIZE, :] = (
                (b * cosine[...] + a * sine[...]) * scale
            ).astype(BF16)

    rotated(turned(wk), pair.at[0], 1.0)
    pair[1] = turned(wv).astype(BF16)
    rotated(turned(wq), queries, 1.0 / math.sqrt(HEAD_SIZE))
    deal_rows(normed.T, width_block, place[1], nrm_own, nrm_away)


def front(devices, place, parts, norm_parts, tables, wq, wk, wv):
    size, part = parts[0].shape
    width = 4 * part
    low = lambda *s: jax.ShapeDtypeStruct(s, BF16)
    wide = lambda *s: jax.ShapeDtypeStruct(s, F32)
    vmem = pl.BlockSpec(memory_space=pltpu.VMEM)
    return pl.pallas_call(
        functools.partial(front_body, width // devices),
        in_specs=[pl.BlockSpec(memory_space=pltpu.SMEM)] + [vmem] * 13,
        out_specs=[vmem] * 9,
        out_shape=[low(part, size), low(2, part, size), low(size // 4, width), low(size, width),
                   low(width // 2, size), low(width // 2, size), wide(6, width),
                   wide(size, 1), wide(size, 1)],
        scratch_shapes=[pltpu.VMEM((size, width), BF16)],
        cost_estimate=FREE, name="front",
    )(place, *parts, *norm_parts, *tables, wq, wk, wv)


def per_device(
    frames,
    segment,
    time_token,
    context,
    gain_attn,
    bias_attn,
    gain_cross,
    bias_cross,
    gain_ffn,
    bias_ffn,
    w_query,
    w_key,
    w_value,
    w_out,
    c_query,
    c_key,
    c_value,
    c_out,
    w_gate,
    w_up,
    w_down,
    out_grad,
):
    local_rows = frames.shape[0]
    local_width = frames.shape[1]
    model_width = w_query.shape[0]
    head_cols = w_query.shape[1]
    heads = head_cols // HEAD_SIZE
    number_of_frames = lax.axis_size("seq") * local_rows
    row_length = min(max(ROW_MIN, 64 * lax.axis_size("seq")), number_of_frames)
    first_frame = lax.axis_index("seq") * local_rows
    own_start = lax.axis_index("tensor") * local_width

    def own_cols(value):
        return lax.dynamic_slice_in_dim(value, own_start, local_width, value.ndim - 1)

    place = lax.axis_index("tensor")
    share = local_rows // 4

    def row_block(value, index):
        return rows_of(value, index * share, share)

    column = lax.axis_index("seq") % 2
    frame_parts_near = gather_near(frames)
    norm_parts = gather_near(
        jnp.stack([gain_attn, bias_attn, gain_cross, bias_cross, gain_ffn, bias_ffn])
    )
    clip_starts, frame_positions = frame_clip_labels(segment, row_length)
    own_labels = lax.dynamic_slice_in_dim(clip_starts, first_frame, local_rows)
    own_positions = lax.dynamic_slice_in_dim(frame_positions, first_frame, local_rows)
    blanks = jnp.full((local_rows,), -1, jnp.int32)
    key_labels = lax.dynamic_slice_in_dim(
        jnp.concatenate([blanks, clip_starts, blanks]), first_frame, 3 * local_rows
    )
    spans = jnp.concatenate(
        [tile_ranges(own_labels, key_labels), place.astype(jnp.int32).reshape(1)]
    )
    places = jnp.stack([column, place]).astype(jnp.int32)
    label_row, label_column = own_labels[None, :], key_labels[:, None]
    row_index = first_frame // row_length
    time_row = lax.dynamic_slice_in_dim(time_token, row_index, 1, 0).astype(F32)
    row_context = lax.dynamic_slice_in_dim(context, row_index, 1, 0)[0]
    context_rows = row_context.shape[0]
    tables = rotary_tables(own_positions)
    score_scale = 1.0 / math.sqrt(HEAD_SIZE)
    all_heads = model_width // HEAD_SIZE

    (
        queries, both, frame_rows, frame_normed, one_own_half, one_away_half, norms, means_one,
        inverse_one,
    ) = front(
        lax.axis_size("seq"), jnp.flip(places), frame_parts_near, norm_parts, tables, w_query,
        w_key, w_value,
    )
    both, out_pair = meeting(both, swap(after(out_grad, frame_parts_near[2]), "seq", 1))
    grad_both = jnp.stack([out_grad, out_pair])
    gain_one, bias_one = norms[0:1], norms[1:2]
    behind, ahead = shift(both, "seq", 1), shift(both, "seq", -1)
    query_far = swap(after(c_query, frame_parts_near[3]), "tensor", 2)
    out_far = swap(after(c_out, frame_parts_near[3]), "tensor", 2)
    time_late = after(time_row, both)
    scaled_time, _ = normalize(time_late)
    time_normed = (scaled_time * gain_one + bias_one).astype(BF16)
    time_keys = by_feature(time_normed, w_key).astype(BF16).astype(F32)
    time_values = by_feature(time_normed, w_value).astype(BF16).astype(F32)
    context_late = after(row_context, both)
    context_kv = jnp.concatenate(
        [product(context_late, c_key), product(context_late, c_value)], 0
    ).astype(BF16)
    state = attend_near(spans, queries, both, time_keys, time_values, label_row, label_column)
    behind, ahead, query_far, out_far, *state = meeting(
        behind, ahead, query_far, out_far, *state
    )
    query_own, out_own, context_late = after((c_query, c_out, context_kv), behind)
    weights_near = [
        swap(value, "tensor", 1) for value in (query_own, query_far, out_own, out_far)
    ]
    kv_far = swap(context_late, "tensor", 2)
    attended, log_totals, one_away, one_own, one_low = attend_far(
        spans, queries, behind, ahead, label_row, label_column, w_out, state
    )
    one_away, one_low, kv_far, *weights_near = meeting(one_away, one_low, kv_far, *weights_near)
    kv_both = jnp.concatenate([context_kv, kv_far], 0)
    kv_other = swap(kv_both, "tensor", 1)
    kv_rows = context_kv.shape[0]
    kv_parts = (context_kv, kv_other[:kv_rows], kv_far, kv_other[kv_rows:])
    query_parts = (c_query, weights_near[0], query_far, weights_near[1])
    out_parts = (c_out, weights_near[2], out_far, weights_near[3])
    one_got, _, one_far = scatter_near(one_away, one_low)
    (
        front_rows, cross_queries, residual_one, residual_two, normed_share, flip_own, flip_away,
    ) = cross_forward(
        lax.axis_size("seq"), places, frame_rows, one_own, one_got, one_far, norms,
        query_parts, kv_parts, out_parts,
    )
    grad_far = swap(after(grad_both, one_far), "tensor", 2)
    normed_share, normed_got, grad_far = meeting(
        normed_share, swap(after(one_away_half, one_low), "seq", 1), grad_far
    )
    grad_late, grad_far_late = after((grad_both, grad_far), normed_share)
    grad_mate, grad_far_mate = swap(grad_late, "tensor", 1), swap(grad_far_late, "tensor", 1)
    grad_parts = (grad_both, grad_mate, grad_far, grad_far_mate)
    three_parts = gather_near(normed_share)
    flip_got = swap(after(flip_away, normed_share), "seq", 1)
    front_far = swap(after(front_rows, three_parts[3]), "tensor", 2)
    devices = lax.axis_size("seq")
    (
        hidden_a, hidden_own_a, hidden_away_a, gate_a, lifted_a, normed_three, grad_near, grad_pair,
        ffn_total,
    ) = ffn(devices, places, 0, (*three_parts, *grad_parts), w_gate, w_up, w_down)
    ffn_total, flip_got = meeting(ffn_total, flip_got)
    flip_both = jnp.stack([flip_own, flip_got])
    flip_far = swap(flip_both, "tensor", 2)
    hidden_got_a, gate_got_a = swap(hidden_away_a, "seq", 1), swap(gate_a, "seq", 1)
    hidden_b, hidden_own_b, hidden_away_b, gate_b, lifted_b, three_away, three_own, three_low = ffn(
        devices, places, 1, (normed_three, grad_near, ffn_total), w_gate, w_up, w_down
    )
    three_away, three_low, flip_far, front_far, hidden_got_a = meeting(
        three_away, three_low, flip_far, front_far, hidden_got_a
    )
    three_got, _, three_far = scatter_near(three_away, three_low)
    hidden_late, lifted_late = after((hidden_away_b, lifted_a), three_low)
    hidden_got_b, lifted_got_a = swap(hidden_late, "seq", 1), swap(lifted_late, "seq", 1)
    flip_late, flip_far_late, gate_late = after((flip_both, flip_far, gate_b), three_far)
    flip_mate, flip_far_mate = swap(flip_late, "tensor", 1), swap(flip_far_late, "tensor", 1)
    gate_got_b = swap(gate_late, "seq", 1)
    front_both = jnp.stack([front_rows, front_far])
    back_rows, kv_grad, norm_vectors, grad_one = cross_backward(
        three_own, three_got, three_far, grad_near, residual_one, residual_two, norms,
        query_parts, kv_parts, out_parts, cross_queries,
    )
    grad_one, gate_got_a, hidden_got_b, lifted_got_a, flip_mate, flip_far_mate = meeting(
        grad_one, gate_got_a, hidden_got_b, lifted_got_a, flip_mate, flip_far_mate
    )
    count = lax.axis_size("seq")

    def by_level(blocks):
        return blocks.reshape(count // 2, 2 * blocks.shape[0] // count, blocks.shape[1])

    down_keep, down_got = halve(
        by_level(
            meet_rows(
                (hidden_own_a, hidden_got_a, hidden_own_b, hidden_got_b), (grad_near, grad_pair)
            )
        ),
        1,
    )
    context_parts = quarters(kv_grad, 1)
    context_got = swap(jnp.concatenate([context_parts[1], context_parts[3]], 0), "tensor", 1)
    *one_parts, front_other, context_got, gate_got_b = meeting(
        *gather_near(grad_one), swap(after(front_both, grad_one), "tensor", 1), context_got,
        gate_got_b,
    )
    context_low = (
        context_parts[2].astype(F32) + context_got[context_parts[2].shape[0] :].astype(F32)
    ).astype(BF16)
    context_far = swap(context_low, "tensor", 2)
    back_far = swap(after(back_rows, one_parts[3]), "tensor", 2)
    lifted_got_b = swap(after(lifted_b, grad_one), "seq", 1)
    query_grad, to_prev, kept, to_next, time_key_grad, time_value_grad = attend_back(
        spans, queries, (behind, both, ahead), time_keys, time_values, label_row, label_column,
        w_out, attended, log_totals, one_parts,
    )
    to_prev, to_next, back_far, lifted_got_b, down_got, context_far = meeting(
        to_prev, to_next, back_far, lifted_got_b, down_got, context_far
    )
    time_both = jnp.concatenate([time_key_grad, time_value_grad], 0)
    time_got = swap(after(time_both, to_prev), "seq", 1)
    from_next, from_prev = shift(to_prev, "seq", -1), shift(to_next, "seq", 1)
    down_keep, down_got = halve(added(down_keep, down_got).astype(BF16), 2)
    flip_near = (flip_both, flip_mate, flip_far, flip_far_mate)
    first_keep, first_got = halve(
        by_level(meet_cols(flip_near, after((gate_a, gate_got_a, lifted_a, lifted_got_a), to_prev))),
        1,
    )
    down_away, down_own, down_low = down_parts(after(hidden_a, to_prev), hidden_b, w_down)
    back_both = jnp.stack([back_rows, back_far])
    back_other = swap(back_both, "tensor", 1)
    context_own = (
        context_parts[0].astype(F32)
        + context_got[: context_far.shape[0]].astype(F32)
        + context_far.astype(F32)
    )
    bundle_a, bundle_b = bundle_grads(
        count, places[1:], (front_both, front_other), (back_both, back_other), one_parts, attended,
        row_context,
        context_own.astype(BF16),
    )
    from_next, from_prev, bundle_a, bundle_b, time_got = meeting(
        from_next, from_prev, bundle_a, bundle_b, time_got
    )
    keep_a, got_a = halve(bundle_a, 0)
    raw, last_away, last_own, last_low = tail(
        places[1:], query_grad, kept, from_next, from_prev, tables, w_query, w_key, w_value
    )
    last_got = swap(last_away, "tensor", 1)
    raw_got = swap(raw, "seq", 1)
    last_sum = (
        last_low.astype(F32) + last_got[local_rows:].astype(F32)
    ).astype(BF16)
    last_sum, first_got, down_got = meeting(last_sum, first_got, down_got)
    first_keep, first_got = halve(added(first_keep, first_got).astype(BF16), 2)
    second = by_level(
        meet_cols(flip_near, after((gate_b, gate_got_b, lifted_b, lifted_got_b), from_next))
    )
    second_keep, second_got = halve(second, 1)
    last_far = swap(last_sum, "tensor", 2)
    last_far, got_a = meeting(last_far, got_a)
    keep_b, got_b = halve(after(bundle_b, last_far), 0)
    frame_grad = last_own + last_got[:local_rows].astype(F32) + last_far.astype(F32)

    def to_frames(rows, weight):
        return jnp.einsum("fn,df->nd", rows, weight, preferred_element_type=F32)

    time_key_grad, time_value_grad = after((time_key_grad, time_value_grad), from_next)
    time_grad = to_frames(time_key_grad.astype(BF16), w_key) + to_frames(
        time_value_grad.astype(BF16), w_value
    )
    own_scaled = (frames.astype(F32) - means_one) * inverse_one
    scaled_grad = frame_grad * gain_attn[None]
    sums = jnp.concatenate(
        [
            jnp.sum(scaled_grad, -1),
            jnp.sum(scaled_grad * own_scaled, -1),
            time_grad[0],
            norm_vectors.reshape(-1),
        ]
    )[None]
    sums = sums + swap(sums, "tensor", 1)
    sums = sums + swap(sums, "tensor", 2)
    sums, second_got = meeting(sums, second_got)
    plain = sums[0, :local_rows, None] / model_width
    cross = sums[0, local_rows : 2 * local_rows, None] / model_width
    vectors = own_cols(sums[0, 2 * local_rows :].reshape(5, model_width))
    attend_full = ordered(*[after(one_parts, from_next)[i] for i in (0, 2, 1, 3)], 0)
    d_frames = own_cols(attend_full).astype(F32) + inverse_one * (
        scaled_grad - plain - own_scaled * cross
    )
    d_gain_attn = jnp.sum(frame_grad * own_scaled, 0) + vectors[0] * own_cols(scaled_time)[0]
    d_bias_attn = jnp.sum(frame_grad, 0) + vectors[0]
    small = jnp.stack(
        [d_gain_attn, d_bias_attn, vectors[3], vectors[4], vectors[1], vectors[2]]
    ).reshape(6, devices, -1).transpose(1, 0, 2)
    small = added(*halve(small, 0))
    small, first_got = meeting(small, first_got)
    small = added(*halve(small, 1))
    small, raw_got = meeting(small, raw_got)
    bit = 2
    while small.shape[0] > 1:
        small = added(*halve(small, bit))
        bit += 1
    small = small[0]

    down_away, down_low = after((down_away, down_low), last_far)
    branch_got, _, branch_far = scatter_near(down_away, down_low)
    block_rows = (
        residual_two + down_own + branch_got[:share].astype(F32) + branch_far.astype(F32)
    ).astype(BF16)
    block_cols = rows_to_cols(
        *[
            lax.dynamic_slice_in_dim(block_rows, (place ^ r) * local_width, local_width, 1)
            for r in range(4)
        ],
        from_next,
    )
    block_out = jnp.concatenate([row_block(block_cols, place ^ b) for b in range(4)], 0)

    time_column = time_normed.astype(F32).T

    normed_pair = (one_own_half, normed_got)
    grad_down = halve_end(down_keep, down_got, 3)
    first, second = halve_end(first_keep, first_got, 3), halve_end(second_keep, second_got, 2)
    units = first.shape[1] // 2
    grad_gate_w = jnp.concatenate([first[:, :units], second[:, :units]], 1)
    grad_up_w = jnp.concatenate([first[:, units:], second[:, units:]], 1)
    left, right = halve_end(keep_a, got_a, 1), halve_end(keep_b, got_b, 1)
    part, rows = head_cols // count, model_width // count
    grad_c_query = left[:, :head_cols]
    grad_c_key, grad_c_value = left[: rows // 2, head_cols:], left[rows // 2 :, head_cols:]
    grad_c_out = jnp.concatenate([right[:part], right[part : 2 * part]], 1)
    grad_w_out = jnp.concatenate([right[2 * part : 3 * part], right[3 * part :]], 1)

    raw_pair = (raw, raw_got)
    time_both = time_both + time_got
    own_time_rows = lax.dynamic_index_in_dim(
        time_column.reshape(count // 2, 2, -1), column, 1, False
    ).reshape(-1, 1)
    outer = own_time_rows * jnp.concatenate([jnp.zeros((head_cols, 1), F32), time_both], 0).T
    blocks = sum(
        jnp.einsum("dn,fn->df", r, c, preferred_element_type=F32)
        for r, c in zip(normed_pair, raw_pair)
    )
    blocks = by_level((blocks + outer).astype(BF16))
    heads_sum = halve_all(blocks, 1)
    grad_w_query, grad_w_key, grad_w_value = (
        heads_sum[:, i * head_cols : (i + 1) * head_cols] for i in range(3)
    )
    return (
        block_out,
        d_frames,
        small[0],
        small[1],
        small[2],
        small[3],
        small[4],
        small[5],
        grad_w_query,
        grad_w_key,
        grad_w_value,
        grad_w_out,
        grad_c_query,
        grad_c_key,
        grad_c_value,
        grad_c_out,
        grad_gate_w,
        grad_up_w,
        grad_down,
    )


def solution(mesh):
    return jax.shard_map(
        per_device,
        mesh=mesh,
        in_specs=(
            P("seq", "tensor"),
            P(),
            P(),
            P(),
            P("tensor"),
            P("tensor"),
            P("tensor"),
            P("tensor"),
            P("tensor"),
            P("tensor"),
            P(None, "tensor"),
            P(None, "tensor"),
            P(None, "tensor"),
            P("tensor", None),
            P(None, "tensor"),
            P(None, "tensor"),
            P(None, "tensor"),
            P("tensor", None),
            P(None, "tensor"),
            P(None, "tensor"),
            P("tensor", None),
            P("seq", "tensor"),
        ),
        out_specs=(
            P("seq", "tensor"),
            P("seq", "tensor"),
            P(("tensor", "seq")),
            P(("tensor", "seq")),
            P(("tensor", "seq")),
            P(("tensor", "seq")),
            P(("tensor", "seq")),
            P(("tensor", "seq")),
            P("seq", "tensor"),
            P("seq", "tensor"),
            P("seq", "tensor"),
            P(("tensor", "seq"), None),
            P("seq", "tensor"),
            P("seq", "tensor"),
            P("seq", "tensor"),
            P(("tensor", "seq"), None),
            P("seq", "tensor"),
            P("seq", "tensor"),
            P(("tensor", "seq"), None),
        ),
        check_vma=False,
    )
```

profile of v0, /device:TPU:0, one launch (start us, length us, event | category | flops | bytes accessed | tf_op | source)
XLA Modules:
  0.0 505.6 jit_solution(16097069273480129285)
XLA Ops:
  4.9 3.0 collective-permute-start.4
  14.3 5.4 %collective-permute-done.1.x2 = bf16[512,384]{1,0:T(8,128)(2,1)S(1)} collective-permute-done((bf16[512,384]{1,0:T(8,128)(2,1)}, bf16[512,384]{1,0:T(8,128)(2,1)S(1)}, u32[]{:S(2)}, u32[]{:S(2)}) %collective-permute-start.1) | collective-permute-done | bytes 393248 | tf_op jit(solution)/shard_map/ppermute | solution.py:27
  26.1 8.7 %front.1 = (bf16[384,512]{1,0:T(8,128)(2,1)}, bf16[2,384,512]{2,1,0:T(8,128)(2,1)}, bf16[128,1536]{1,0:T(8,128)(2,1)}, bf16[512,1536]{1,0:T(8,128)(2,1)}, bf16[7...) custom-call(s32[2]{0:T(128)} %rev.4.place, ...), custom_call_target="tpu_custom_call" | custom-call | flops 1 | bytes 1 | tf_op jit(solution)/shard_map/front/pallas_call | solution.py:845
  36.3 5.5 %collective-permute-start.7 = (bf16[2,384,512]{2,1,0:T(8,128)(2,1)}, bf16[2,384,512]{2,1,0:T(8,128)(2,1)}, u32[]{:S(2)}, u32[]{:S(2)}) collective-permute-start(bf16[2,384,512]{2,1,0:T(8,128)(2,1)} %get-tuple-element.185.kv.kv1), channel_id=1, source_target_pairs={{0,1},{1,2},{2,3},{3,4},{4,5},{5,6},{6,7},{8,9},{9,10},{10,11},{11... | collective-permute-start | bytes 2359304 | tf_op jit(solution)/shard_map/ppermute | solution.py:33
  50.1 10.2 %attend_near.1 = (f32[6,512]{1,0:T(8,128)}, f32[6,512]{1,0:T(8,128)}, f32[384,512]{1,0:T(8,128)}) custom-call(s32[5]{0:T(128)} %pad_add_fusion.2.span, bf16[384,512]{1,0:T(8,128)(2,1)} %get-tuple-element.182.q, bf16[2,384,512]{2,1,0:T(8,128)(2,1)} %get-tuple-element.185.kv.kv1, f32[384,1]{1,0:T(8,128)} %reshape.282.tk, f32[384,1]{1,0:T(8,128)} %reshape.283.tv, ...), custom_call_target="tpu_custom_call" | custom-call | flops 1 | bytes 1 | tf_op jit(solution)/shard_map/attend_near/pallas_call | solution.py:301
  62.1 10.5 %collective-permute-done.7.kv0 = bf16[2,384,512]{2,1,0:T(8,128)(2,1)} collective-permute-done((bf16[2,384,512]{2,1,0:T(8,128)(2,1)}, bf16[2,384,512]{2,1,0:T(8,128)(2,1)}, u32[]{:S(2)}, u32[]{:S(2)}) %collective-permute-start.7) | collective-permute-done | bytes 786464 | tf_op jit(solution)/shard_map/ppermute | solution.py:33
  72.5 22.2 %collective-permute-done.10.o2 = bf16[384,1536]{1,0:T(8,128)(2,1)} collective-permute-done((bf16[384,1536]{1,0:T(8,128)(2,1)}, bf16[384,1536]{1,0:T(8,128)(2,1)}, u32[]{:S(2)}, u32[]{:S(2)}) %collective-permute-start.10) | collective-permute-done | bytes 1179680 | tf_op jit(solution)/shard_map/ppermute | solution.py:27
  96.3 8.7 %attend_far.1 = (bf16[384,512]{1,0:T(8,128)(2,1)}, f32[6,512]{1,0:T(8,128)}, bf16[256,1536]{1,0:T(8,128)(2,1)}, f32[128,1536]{1,0:T(8,128)}, bf16[128,1536]{1,0:T(8,128)(2,1)}) custom-call(s32[5]{0:T(128)} %pad_add_fusion.2.span, bf16[384,512]{1,0:T(8,128)(2,1)} %get-tuple-element.182.q, bf16[2,384,512]{2,1,0:T(8,128)(2,1)} %collective-permute-done.7.kv0, ...), custom_call_target="tpu_custom_call" | custom-call | flops 1 | bytes 1 | tf_op jit(solution)/shard_map/attend_far/pallas_call | solution.py:319
  105.2 2.5 collective-permute-done.16.got
  110.7 4.1 collective-permute-start.19
  114.9 5.4 %collective-permute-done.17.far = bf16[128,1536]{1,0:T(8,128)(2,1)S(1)} collective-permute-done((bf16[128,1536]{1,0:T(8,128)(2,1)S(1)}, bf16[128,1536]{1,0:T(8,128)(2,1)S(1)}, u32[]{:S(2)}, u32[]{:S(2)}) %collective-permute-start.17) | collective-permute-done | bytes 393248 | tf_op jit(solution)/shard_map/ppermute | solution.py:27
  124.4 16.6 %cross.1 = (bf16[128,3072]{1,0:T(8,128)(2,1)}, bf16[128,1536]{1,0:T(8,128)(2,1)}, f32[128,1536]{1,0:T(8,128)}, f32[128,1536]{1,0:T(8,128)}, bf16[128,1536]{1,0:T...) custom-call(s32[2]{0:T(128)} %copy-done.66, bf16[128,1536]{1,0:T(8,128)(2,1)} %get-tuple-element.181.rows, ...), custom_call_target="tpu_custom_call" | custom-call | flops 1 | bytes 1 | tf_op jit(solution)/shard_map/cross/pallas_call | solution.py:522
  142.1 10.4 %collective-permute-done.22.n2 = bf16[128,1536]{1,0:T(8,128)(2,1)S(1)} collective-permute-done((bf16[128,1536]{1,0:T(8,128)(2,1)}, bf16[128,1536]{1,0:T(8,128)(2,1)S(1)}, u32[]{:S(2)}, u32[]{:S(2)}) %collective-permute-start.22) | collective-permute-done | bytes 393248 | tf_op jit(solution)/shard_map/ppermute | solution.py:27
  153.0 1.7 collective-permute-done.23.n3
  155.2 4.0 collective-permute-start.26
  160.8 14.7 %ffn.2 = (bf16[512,768]{1,0:T(8,128)(2,1)}, bf16[384,512]{1,0:T(8,128)(2,1)}, bf16[384,512]{1,0:T(8,128)(2,1)}, bf16[512,768]{1,0:T(8,128)(2,1)}, bf16[512,768]{...) custom-call(s32[2]{0:T(128)} %copy-done.66, ...), custom_call_target="tpu_custom_call" | custom-call | flops 1 | bytes 1 | tf_op jit(solution)/shard_map/ffn/pallas_call | solution.py:611
  175.6 1.7 collective-permute-start.27
  177.3 15.0 %ffn.3 = (bf16[512,768]{1,0:T(8,128)(2,1)}, bf16[384,512]{1,0:T(8,128)(2,1)}, bf16[384,512]{1,0:T(8,128)(2,1)}, bf16[512,768]{1,0:T(8,128)(2,1)}, bf16[512,768]{...) custom-call(s32[2]{0:T(128)} %copy-done.66, ...), custom_call_target="tpu_custom_call" | custom-call | flops 1 | bytes 1 | tf_op jit(solution)/shard_map/ffn/pallas_call | solution.py:611
  192.4 2.1 collective-permute-start.32
  196.7 2.0 collective-permute-start.34
  198.8 8.7 %collective-permute-done.31.far = bf16[128,1536]{1,0:T(8,128)(2,1)S(1)} collective-permute-done((bf16[128,1536]{1,0:T(8,128)(2,1)S(1)}, bf16[128,1536]{1,0:T(8,128)(2,1)S(1)}, u32[]{:S(2)}, u32[]{:S(2)}) %collective-permute-start.31) | collective-permute-done | bytes 393248 | tf_op jit(solution)/shard_map/ppermute | solution.py:27
  209.5 21.0 %cross_back.1 = (bf16[128,3072]{1,0:T(8,128)(2,1)}, bf16[256,1536]{1,0:T(8,128)(2,1)}, f32[4,1536]{1,0:T(4,128)}, bf16[128,1536]{1,0:T(8,128)(2,1)}) custom-call(f32[128,1536]{1,0:T(8,128)} %get-tuple-element.233.own, bf16[256,1536]{1,0:T(8,128)(2,1)} %copy-done.29, bf16[128,1536]{1,0:T(8,128)(2,1)} %copy-done.55, ...), custom_call_target="tpu_custom_call" | custom-call | flops 1 | bytes 1 | tf_op jit(solution)/shard_map/cross_back/pallas_call | solution.py:676
  230.5 7.7 %collective-permute-done.33.pair_b = bf16[384,512]{1,0:T(8,128)(2,1)} collective-permute-done((bf16[384,512]{1,0:T(8,128)(2,1)}, bf16[384,512]{1,0:T(8,128)(2,1)}, u32[]{:S(2)}, u32[]{:S(2)}) %collective-permute-start.33) | collective-permute-done | bytes 393248 | tf_op jit(solution)/shard_map/ppermute | solution.py:27
  238.4 1.8 collective-permute-start.42
  242.9 6.2 %meet_rows.1 = bf16[768,1536]{1,0:T(8,128)(2,1)} custom-call(bf16[384,512]{1,0:T(8,128)(2,1)} %get-tuple-element.270.own_a, bf16[384,512]{1,0:T(8,128)(2,1)} %copy-done.45, bf16[384,512]{1,0:T(8,128)(2,1)} %get-tuple-element.272.own_b, bf16[384,512]{1,0:T(8,128)(2,1)} %collective-permute-done.33.pair_b, bf16[512,1536]{1,0:T(8,128)(2,1)} %get-tuple-element.228.grad.right, ...), custom_call_target="tpu_custom_call" | custom-call | flops 1 | bytes 1 | tf_op jit(solution)/shard_map/meet_rows/pallas_call | solution.py:701
  249.2 2.5 collective-permute-done.38.g2.a2
  251.7 2.4 dynamic-slice_bitcast_fusion.4
  254.0 4.6 collective-permute-done.42.a_pair
  258.6 1.8 collective-permute-start.44
  262.6 1.7 collective-permute-start.46
  264.3 17.7 %attend_back.1 = (f32[384,512]{1,0:T(8,128)}, bf16[2,384,512]{2,1,0:T(8,128)(2,1)}, f32[2,384,512]{2,1,0:T(8,128)}, bf16[2,384,512]{2,1,0:T(8,128)(2,1)}, f32[384,1]{1,0:T(8,128)}, /*index=5*/f32[384,1]{1,0:T(8,128)}) custom-call(s32[5]{0:T(128)} %pad_add_fusion.2.span, bf16[384,512]{1,0:T(8,128)(2,1)} %get-tuple-element.182.q, ...), custom_call_target="tpu_custom_call" | custom-call | flops 1 | bytes 1 | tf_op jit(solution)/shard_map/attend_back/pallas_call | solution.py:336
  291.2 2.7 collective-permute-start.50
  293.9 3.0 collective-permute-start.48
  296.9 1.9 fusion.6
  300.6 6.3 %meet_cols.2 = bf16[768,1536]{1,0:T(8,128)(2,1)} custom-call(bf16[2,768,128]{2,1,0:T(8,128)(2,1)} %copy-done.16, bf16[2,768,128]{2,1,0:T(8,128)(2,1)} %collective-permute-done.35.p1, bf16[2,768,128]{2,1,0:T(8,128)(2,1)} %collective-permute-done.27.p2, bf16[2,768,128]{2,1,0:T(8,128)(2,1)} %collective-permute-done.36.p3, ...), custom_call_target="tpu_custom_call" | custom-call | flops 1 | bytes 1 | tf_op jit(solution)/shard_map/meet_cols/pallas_call | solution.py:719
  306.9 2.4 dynamic-slice_bitcast_fusion.3
  309.3 1.8 add_convert_fusion.5.kv
  311.0 6.5 %down.1 = (bf16[256,1536]{1,0:T(8,128)(2,1)}, f32[128,1536]{1,0:T(8,128)}, bf16[128,1536]{1,0:T(8,128)(2,1)}) custom-call(bf16[512,768]{1,0:T(8,128)(2,1)} %get-tuple-element.277.first, bf16[512,768]{1,0:T(8,128)(2,1)} %get-tuple-element.278.second, bf16[1536,1536]{1,0:T(8,128)(2,1)} %down_w.5), custom_call_target="tpu_custom_call" | custom-call | flops 1 | bytes 1 | tf_op jit(solution)/shard_map/down/pallas_call | solution.py:742
  319.1 8.0 %bundle.1 = (bf16[8,192,768]{2,1,0:T(8,128)(2,1)}, bf16[8,192,768]{2,1,0:T(8,128)(2,1)}) custom-call(s32[1]{0:T(128)} %bitcast.1.place, bf16[2,128,3072]{2,1,0:T(8,128)(2,1)} %copy-done.7, bf16[2,128,3072]{2,1,0:T(8,128)(2,1)} %collective-permute-done.40.f13, bf16[2,128,3072]{2,1,0:T(8,128)(2,1)} %copy-done.8, ...), custom_call_target="tpu_custom_call" | custom-call | flops 1 | bytes 1 | tf_op jit(solution)/shard_map/bundle/pallas_call | solution.py:791
  328.8 7.4 %tail.1 = (bf16[1152,512]{1,0:T(8,128)(2,1)}, bf16[1024,384]{1,0:T(8,128)(2,1)}, f32[512,384]{1,0:T(8,128)}, bf16[512,384]{1,0:T(8,128)(2,1)}) custom-call(s32[1]{0:T(128)} %bitcast.1.place, f32[384,512]{1,0:T(8,128)} %get-tuple-element.282.dq, f32[2,384,512]{2,1,0:T(8,128)} %get-tuple-element.283.kept, bf16[2,384,512]{2,1,0:T(8,128)(2,1)} %collective-permute-done.47.ahead, ...), custom_call_target="tpu_custom_call" | custom-call | flops 1 | bytes 1 | tf_op jit(solution)/shard_map/tail/pallas_call | solution.py:388
  336.3 6.6 %meet_cols.3 = bf16[768,1536]{1,0:T(8,128)(2,1)} custom-call(bf16[2,768,128]{2,1,0:T(8,128)(2,1)} %copy-done.16, bf16[2,768,128]{2,1,0:T(8,128)(2,1)} %collective-permute-done.35.p1, bf16[2,768,128]{2,1,0:T(8,128)(2,1)} %collective-permute-done.27.p2, bf16[2,768,128]{2,1,0:T(8,128)(2,1)} %collective-permute-done.36.p3, ...), custom_call_target="tpu_custom_call" | custom-call | flops 1 | bytes 1 | tf_op jit(solution)/shard_map/meet_cols/pallas_call | solution.py:719
  345.4 2.5 collective-permute-start.55
  348.0 2.6 broadcast_select_fusion.4
  352.6 6.0 %collective-permute-done.52 = bf16[2,192,1536]{2,1,0:T(8,128)(2,1)S(1)} collective-permute-done((bf16[2,192,1536]{2,1,0:T(8,128)(2,1)}, bf16[2,192,1536]{2,1,0:T(8,128)(2,1)S(1)}, u32[]{:S(2)}, u32[]{:S(2)}) %collective-permute-start.52) | collective-permute-done | bytes 1179680 | tf_op jit(solution)/shard_map/ppermute | solution.py:27
  363.1 2.2 add_bitcast_fusion
  365.3 2.0 collective-permute-done.54
  367.4 7.4 %collective-permute-done.55 = bf16[4,192,768]{2,1,0:T(8,128)(2,1)S(1)} collective-permute-done((bf16[4,192,768]{2,1,0:T(8,128)(2,1)S(1)}, bf16[4,192,768]{2,1,0:T(8,128)(2,1)S(1)}, u32[]{:S(2)}, u32[]{:S(2)}) %collective-permute-start.55) | collective-permute-done | bytes 1179680 | tf_op jit(solution)/shard_map/ppermute | solution.py:27
  374.8 2.3 multiply_reduce_fusion
  381.6 2.7 collective-permute-done.61
  384.4 12.1 %collective-permute-done.62 = bf16[2,192,1536]{2,1,0:T(8,128)(2,1)S(1)} collective-permute-done((bf16[2,192,1536]{2,1,0:T(8,128)(2,1)S(1)}, bf16[2,192,1536]{2,1,0:T(8,128)(2,1)S(1)}, u32[]{:S(2)}, u32[]{:S(2)}) %collective-permute-start.62) | collective-permute-done | bytes 1179680 | tf_op jit(solution)/shard_map/ppermute | solution.py:27
  398.2 2.4 multiply_add_fusion
  401.9 2.0 collective-permute-start.70
  405.3 2.3 collective-permute-done.65
  407.7 3.0 collective-permute-start.67
  410.6 2.7 fusion.42
  413.4 2.5 fusion.1
  416.0 17.7 %collective-permute-done.67 = f32[1,6,48]{2,0,1:T(1,128)S(1)} collective-permute-done((f32[1,6,48]{2,0,1:T(1,128)S(1)}, f32[1,6,48]{2,0,1:T(1,128)S(1)}, u32[]{:S(2)}, u32[]{:S(2)}) %collective-permute-start.67) | collective-permute-done | bytes 1184 | tf_op jit(solution)/shard_map/ppermute | solution.py:27
  435.6 1.8 collective-permute-start.74
  441.5 17.8 %collective-permute-done.74 = bf16[1,192,768]{2,1,0:T(8,128)(2,1)S(1)} collective-permute-done((bf16[1,192,768]{2,1,0:T(8,128)(2,1)S(1)}, bf16[1,192,768]{2,1,0:T(8,128)(2,1)S(1)}, u32[]{:S(2)}, u32[]{:S(2)}) %collective-permute-start.74) | collective-permute-done | bytes 294944 | tf_op jit(solution)/shard_map/ppermute | solution.py:27
  461.8 2.8 collective-permute-start.69
  467.1 5.0 collective-permute-done.58
  472.3 11.6 %collective-permute-done.69 = bf16[1,192,1152]{2,1,0:T(8,128)(2,1)S(1)} collective-permute-done((bf16[1,192,1152]{2,1,0:T(8,128)(2,1)S(1)}, bf16[1,192,1152]{2,1,0:T(8,128)(2,1)S(1)}, u32[]{:S(2)}, u32[]{:S(2)}) %collective-permute-start.69) | collective-permute-done | bytes 442400 | tf_op jit(solution)/shard_map/ppermute | solution.py:27
  485.0 5.7 %collective-permute-done.71 = bf16[2,192,768]{2,1,0:T(8,128)(2,1)S(1)} collective-permute-done((bf16[2,192,768]{2,1,0:T(8,128)(2,1)S(1)}, bf16[2,192,768]{2,1,0:T(8,128)(2,1)S(1)}, u32[]{:S(2)}, u32[]{:S(2)}) %collective-permute-start.71) | collective-permute-done | bytes 589856 | tf_op jit(solution)/shard_map/ppermute | solution.py:27
  491.9 12.2 %collective-permute-done.72 = bf16[1,192,768]{2,1,0:T(8,128)(2,1)S(1)} collective-permute-done((bf16[1,192,768]{2,1,0:T(8,128)(2,1)S(1)}, bf16[1,192,768]{2,1,0:T(8,128)(2,1)S(1)}, u32[]{:S(2)}, u32[]{:S(2)}) %collective-permute-start.72) | collective-permute-done | bytes 294944 | tf_op jit(solution)/shard_map/ppermute | solution.py:27
  (385 shorter events, 95.4 us)
Async XLA Ops:
  4.9 17.5 %collective-permute-start.4 = (f32[6,384]{1,0:T(8,128)S(1)}, f32[6,384]{1,0:T(8,128)S(1)}, u32[]{:S(2)}, u32[]{:S(2)}) collective-permute-start(f32[6,384]{1,0:T(8,128)S(1)} %stack.98.g0), channel_id=1, source_target_pairs={{0,16},{8,24},{16,0},{24,8},{1,17},{9,25},{17,1},{25,9},{2,18},{10... | collective-permute-start | bytes 27656 | tf_op jit(solution)/shard_map/ppermute | solution.py:27
  7.9 17.3 %collective-permute-start.3 = (f32[6,384]{1,0:T(8,128)S(1)}, f32[6,384]{1,0:T(8,128)S(1)}, u32[]{:S(2)}, u32[]{:S(2)}) collective-permute-start(f32[6,384]{1,0:T(8,128)S(1)} %stack.98.g0), channel_id=1, source_target_pairs={{0,8},{8,0},{16,24},{24,16},{1,9},{9,1},{17,25},{25,17},{2,10},{10... | collective-permute-start | bytes 27656 | tf_op jit(solution)/shard_map/ppermute | solution.py:27
  7.9 11.7 %collective-permute-start.1 = (bf16[512,384]{1,0:T(8,128)(2,1)}, bf16[512,384]{1,0:T(8,128)(2,1)S(1)}, u32[]{:S(2)}, u32[]{:S(2)}) collective-permute-start(bf16[512,384]{1,0:T(8,128)(2,1)} %x0.1), channel_id=1, source_target_pairs={{0,16},{8,24},{16,0},{24,8},{1,17},{9,25},{17,1},{25,9},{2,18},{10... | collective-permute-start | bytes 1179656 | tf_op jit(solution)/shard_map/ppermute | solution.py:27
  8.1 17.2 %collective-permute-start = (bf16[512,384]{1,0:T(8,128)(2,1)}, bf16[512,384]{1,0:T(8,128)(2,1)S(1)}, u32[]{:S(2)}, u32[]{:S(2)}) collective-permute-start(bf16[512,384]{1,0:T(8,128)(2,1)} %x0.1), channel_id=1, source_target_pairs={{0,8},{8,0},{16,24},{24,16},{1,9},{9,1},{17,25},{25,17},{2,10},{10... | collective-permute-start | bytes 1179656 | tf_op jit(solution)/shard_map/ppermute | solution.py:27
  19.6 15.2 %collective-permute-start.6 = (bf16[512,384]{1,0:T(8,128)(2,1)}, bf16[512,384]{1,0:T(8,128)(2,1)S(1)}, u32[]{:S(2)}, u32[]{:S(2)}) collective-permute-start(bf16[512,384]{1,0:T(8,128)(2,1)} %param.43), channel_id=1, source_target_pairs={{0,1},{1,0},{2,3},{3,2},{4,5},{5,4},{6,7},{7,6},{8,9},{9,8},{10,11... | collective-permute-start | bytes 1179656 | tf_op jit(solution)/shard_map/ppermute | solution.py:27
  34.9 27.2 %collective-permute-start.8 = (bf16[2,384,512]{2,1,0:T(8,128)(2,1)}, bf16[2,384,512]{2,1,0:T(8,128)(2,1)}, u32[]{:S(2)}, u32[]{:S(2)}) collective-permute-start(bf16[2,384,512]{2,1,0:T(8,128)(2,1)} %get-tuple-element.185.kv.kv1), channel_id=1, source_target_pairs={{1,0},{2,1},{3,2},{4,3},{5,4},{6,5},{7,6},{9,8},{10,9},{11,10},{12... | collective-permute-start | bytes 2359304 | tf_op jit(solution)/shard_map/ppermute | solution.py:33
  36.3 36.2 %collective-permute-start.7 = (bf16[2,384,512]{2,1,0:T(8,128)(2,1)}, bf16[2,384,512]{2,1,0:T(8,128)(2,1)}, u32[]{:S(2)}, u32[]{:S(2)}) collective-permute-start(bf16[2,384,512]{2,1,0:T(8,128)(2,1)} %get-tuple-element.185.kv.kv1), channel_id=1, source_target_pairs={{0,1},{1,2},{2,3},{3,4},{4,5},{5,6},{6,7},{8,9},{9,10},{10,11},{11... | collective-permute-start | bytes 2359304 | tf_op jit(solution)/shard_map/ppermute | solution.py:33
  41.8 30.7 %collective-permute-start.9 = (bf16[1536,384]{1,0:T(8,128)(2,1)}, bf16[1536,384]{1,0:T(8,128)(2,1)}, u32[]{:S(2)}, u32[]{:S(2)}) collective-permute-start(bf16[1536,384]{1,0:T(8,128)(2,1)} %q0.3), channel_id=1, source_target_pairs={{0,16},{8,24},{16,0},{24,8},{1,17},{9,25},{17,1},{25,9},{2,18},{10... | collective-permute-start | bytes 3538952 | tf_op jit(solution)/shard_map/ppermute | solution.py:27
  42.3 52.4 %collective-permute-start.10 = (bf16[384,1536]{1,0:T(8,128)(2,1)}, bf16[384,1536]{1,0:T(8,128)(2,1)}, u32[]{:S(2)}, u32[]{:S(2)}) collective-permute-start(bf16[384,1536]{1,0:T(8,128)(2,1)} %o0.3), channel_id=1, source_target_pairs={{0,16},{8,24},{16,0},{24,8},{1,17},{9,25},{17,1},{25,9},{2,18},{10... | collective-permute-start | bytes 3538952 | tf_op jit(solution)/shard_map/ppermute | solution.py:27
  94.7 10.3 %collective-permute-start.12 = (bf16[1536,384]{1,0:T(8,128)(2,1)S(1)}, bf16[1536,384]{1,0:T(8,128)(2,1)}, u32[]{:S(2)}, u32[]{:S(2)}) collective-permute-start(bf16[1536,384]{1,0:T(8,128)(2,1)S(1)} %copy-done.9), channel_id=1, source_target_pairs={{0,8},{8,0},{16,24},{24,16},{1,9},{9,1},{17,25},{25,17},{2,10},{10... | collective-permute-start | bytes 3538952 | tf_op jit(solution)/shard_map/ppermute | solution.py:27
  94.8 10.3 %collective-permute-start.14 = (bf16[384,1536]{1,0:T(8,128)(2,1)}, bf16[384,1536]{1,0:T(8,128)(2,1)}, u32[]{:S(2)}, u32[]{:S(2)}) collective-permute-start(bf16[384,1536]{1,0:T(8,128)(2,1)} %o0.3), channel_id=1, source_target_pairs={{0,8},{8,0},{16,24},{24,16},{1,9},{9,1},{17,25},{25,17},{2,10},{10... | collective-permute-start | bytes 3538952 | tf_op jit(solution)/shard_map/ppermute | solution.py:27
  95.3 9.8 %collective-permute-start.13 = (bf16[1536,384]{1,0:T(8,128)(2,1)}, bf16[1536,384]{1,0:T(8,128)(2,1)}, u32[]{:S(2)}, u32[]{:S(2)}) collective-permute-start(bf16[1536,384]{1,0:T(8,128)(2,1)} %collective-permute-done.9.q2), channel_id=1, source_target_pairs={{0,8},{8,0},{16,24},{24,16},{1,9},{9,1},{17,25},{25,17},{2,10},{10... | collective-permute-start | bytes 3538952 | tf_op jit(solution)/shard_map/ppermute | solution.py:27
  95.3 9.8 %collective-permute-start.15 = (bf16[384,1536]{1,0:T(8,128)(2,1)}, bf16[384,1536]{1,0:T(8,128)(2,1)}, u32[]{:S(2)}, u32[]{:S(2)}) collective-permute-start(bf16[384,1536]{1,0:T(8,128)(2,1)} %collective-permute-done.10.o2), channel_id=1, source_target_pairs={{0,8},{8,0},{16,24},{24,16},{1,9},{9,1},{17,25},{25,17},{2,10},{10... | collective-permute-start | bytes 3538952 | tf_op jit(solution)/shard_map/ppermute | solution.py:27
  95.8 9.3 %collective-permute-start.11 = (bf16[256,384]{1,0:T(8,128)(2,1)S(1)}, bf16[256,384]{1,0:T(8,128)(2,1)S(1)}, u32[]{:S(2)}, u32[]{:S(2)}) collective-permute-start(bf16[256,384]{1,0:T(8,128)(2,1)S(1)} %pad_maximum_fusion.12.c0), channel_id=1, source_target_pairs={{0,16},{8,24},{16,0},{24,8},{1,17},{9,25},{17,1},{25,9},{2,18},{10... | collective-permute-start | bytes 589832 | tf_op jit(solution)/shard_map/ppermute | solution.py:27
  109.0 11.2 %collective-permute-start.17 = (bf16[128,1536]{1,0:T(8,128)(2,1)S(1)}, bf16[128,1536]{1,0:T(8,128)(2,1)S(1)}, u32[]{:S(2)}, u32[]{:S(2)}) collective-permute-start(bf16[128,1536]{1,0:T(8,128)(2,1)S(1)} %add_convert_fusion.4), channel_id=1, source_target_pairs={{0,16},{8,24},{16,0},{24,8},{1,17},{9,25},{17,1},{25,9},{2,18},{10... | collective-permute-start | bytes 1179656 | tf_op jit(solution)/shard_map/ppermute | solution.py:27
  110.7 30.2 %collective-permute-start.19 = (bf16[768,512]{1,0:T(8,128)(2,1)}, bf16[768,512]{1,0:T(8,128)(2,1)}, u32[]{:S(2)}, u32[]{:S(2)}) collective-permute-start(bf16[768,512]{1,0:T(8,128)(2,1)} %get-tuple-element.217), channel_id=1, source_target_pairs={{0,1},{1,0},{2,3},{3,2},{4,5},{5,4},{6,7},{7,6},{8,9},{9,8},{10,11... | collective-permute-start | bytes 2359304 | tf_op jit(solution)/shard_map/ppermute | solution.py:27
  120.2 20.7 %collective-permute-start.20 = (bf16[2,512,384]{2,1,0:T(8,128)(2,1)S(1)}, bf16[2,512,384]{2,1,0:T(8,128)(2,1)S(1)}, u32[]{:S(2)}, u32[]{:S(2)}) collective-permute-start(bf16[2,512,384]{2,1,0:T(8,128)(2,1)S(1)} %pad_maximum_fusion.4.g0), channel_id=1, source_target_pairs={{0,16},{8,24},{16,0},{24,8},{1,17},{9,25},{17,1},{25,9},{2,18},{10... | collective-permute-start | bytes 2359304 | tf_op jit(solution)/shard_map/ppermute | solution.py:27
  141.0 11.4 %collective-permute-start.22 = (bf16[128,1536]{1,0:T(8,128)(2,1)}, bf16[128,1536]{1,0:T(8,128)(2,1)S(1)}, u32[]{:S(2)}, u32[]{:S(2)}) collective-permute-start(bf16[128,1536]{1,0:T(8,128)(2,1)} %get-tuple-element.220.n0), channel_id=1, source_target_pairs={{0,16},{8,24},{16,0},{24,8},{1,17},{9,25},{17,1},{25,9},{2,18},{10... | collective-permute-start | bytes 1179656 | tf_op jit(solution)/shard_map/ppermute | solution.py:27
  141.6 17.6 %collective-permute-start.24 = (bf16[2,512,384]{2,1,0:T(8,128)(2,1)S(1)}, bf16[2,512,384]{2,1,0:T(8,128)(2,1)S(1)}, u32[]{:S(2)}, u32[]{:S(2)}) collective-permute-start(bf16[2,512,384]{2,1,0:T(8,128)(2,1)S(1)} %pad_maximum_fusion.4.g0), channel_id=1, source_target_pairs={{0,8},{8,0},{16,24},{24,16},{1,9},{9,1},{17,25},{25,17},{2,10},{10... | collective-permute-start | bytes 2359304 | tf_op jit(solution)/shard_map/ppermute | solution.py:27
  141.6 19.2 %collective-permute-start.25 = (bf16[2,512,384]{2,1,0:T(8,128)(2,1)S(1)}, bf16[2,512,384]{2,1,0:T(8,128)(2,1)}, u32[]{:S(2)}, u32[]{:S(2)}) collective-permute-start(bf16[2,512,384]{2,1,0:T(8,128)(2,1)S(1)} %collective-permute-done.20.g2), channel_id=1, source_target_pairs={{0,8},{8,0},{16,24},{24,16},{1,9},{9,1},{17,25},{25,17},{2,10},{10... | collective-permute-start | bytes 2359304 | tf_op jit(solution)/shard_map/ppermute | solution.py:27
  154.7 37.6 %collective-permute-start.28 = (bf16[128,3072]{1,0:T(8,128)(2,1)}, bf16[128,3072]{1,0:T(8,128)(2,1)}, u32[]{:S(2)}, u32[]{:S(2)}) collective-permute-start(bf16[128,3072]{1,0:T(8,128)(2,1)} %get-tuple-element.239), channel_id=1, source_target_pairs={{0,16},{8,24},{16,0},{24,8},{1,17},{9,25},{17,1},{25,9},{2,18},{10... | collective-permute-start | bytes 2359304 | tf_op jit(solution)/shard_map/ppermute | solution.py:27
  155.2 20.3 %collective-permute-start.26 = (bf16[768,128]{1,0:T(8,128)(2,1)}, bf16[768,128]{1,0:T(8,128)(2,1)S(1)}, u32[]{:S(2)}, u32[]{:S(2)}) collective-permute-start(bf16[768,128]{1,0:T(8,128)(2,1)} %get-tuple-element.231), channel_id=1, source_target_pairs={{0,1},{1,0},{2,3},{3,2},{4,5},{5,4},{6,7},{7,6},{8,9},{9,8},{10,11... | collective-permute-start | bytes 589832 | tf_op jit(solution)/shard_map/ppermute | solution.py:27
  175.6 16.7 %collective-permute-start.27 = (bf16[2,768,128]{2,1,0:T(8,128)(2,1)S(1)}, bf16[2,768,128]{2,1,0:T(8,128)(2,1)}, u32[]{:S(2)}, u32[]{:S(2)}) collective-permute-start(bf16[2,768,128]{2,1,0:T(8,128)(2,1)S(1)} %pad_maximum_fusion.6.p0), channel_id=1, source_target_pairs={{0,16},{8,24},{16,0},{24,8},{1,17},{9,25},{17,1},{25,9},{2,18},{10... | collective-permute-start | bytes 1179656 | tf_op jit(solution)/shard_map/ppermute | solution.py:27
  177.3 15.0 %collective-permute-start.29 = (bf16[384,512]{1,0:T(8,128)(2,1)}, bf16[384,512]{1,0:T(8,128)(2,1)S(1)}, u32[]{:S(2)}, u32[]{:S(2)}) collective-permute-start(bf16[384,512]{1,0:T(8,128)(2,1)} %get-tuple-element.240), channel_id=1, source_target_pairs={{0,1},{1,0},{2,3},{3,2},{4,5},{5,4},{6,7},{7,6},{8,9},{9,8},{10,11... | collective-permute-start | bytes 1179656 | tf_op jit(solution)/shard_map/ppermute | solution.py:27
  192.4 38.1 %collective-permute-start.32 = (bf16[512,768]{1,0:T(8,128)(2,1)}, bf16[512,768]{1,0:T(8,128)(2,1)}, u32[]{:S(2)}, u32[]{:S(2)}) collective-permute-start(bf16[512,768]{1,0:T(8,128)(2,1)} %get-tuple-element.301.a), channel_id=1, source_target_pairs={{0,1},{1,0},{2,3},{3,2},{4,5},{5,4},{6,7},{7,6},{8,9},{9,8},{10,11... | collective-permute-start | bytes 2359304 | tf_op jit(solution)/shard_map/ppermute | solution.py:27
  196.3 11.2 %collective-permute-start.31 = (bf16[128,1536]{1,0:T(8,128)(2,1)S(1)}, bf16[128,1536]{1,0:T(8,128)(2,1)S(1)}, u32[]{:S(2)}, u32[]{:S(2)}) collective-permute-start(bf16[128,1536]{1,0:T(8,128)(2,1)S(1)} %add_convert_fusion.3), channel_id=1, source_target_pairs={{0,16},{8,24},{16,0},{24,8},{1,17},{9,25},{17,1},{25,9},{2,18},{10... | collective-permute-start | bytes 1179656 | tf_op jit(solution)/shard_map/ppermute | solution.py:27
  196.7 41.5 %collective-permute-start.34 = (bf16[512,768]{1,0:T(8,128)(2,1)}, bf16[512,768]{1,0:T(8,128)(2,1)}, u32[]{:S(2)}, u32[]{:S(2)}) collective-permute-start(bf16[512,768]{1,0:T(8,128)(2,1)} %get-tuple-element.303.b), channel_id=1, source_target_pairs={{0,1},{1,0},{2,3},{3,2},{4,5},{5,4},{6,7},{7,6},{8,9},{9,8},{10,11... | collective-permute-start | bytes 2359304 | tf_op jit(solution)/shard_map/ppermute | solution.py:27
  198.7 39.5 %collective-permute-start.33 = (bf16[384,512]{1,0:T(8,128)(2,1)}, bf16[384,512]{1,0:T(8,128)(2,1)}, u32[]{:S(2)}, u32[]{:S(2)}) collective-permute-start(bf16[384,512]{1,0:T(8,128)(2,1)} %get-tuple-element.249), channel_id=1, source_target_pairs={{0,1},{1,0},{2,3},{3,2},{4,5},{5,4},{6,7},{7,6},{8,9},{9,8},{10,11... | collective-permute-start | bytes 1179656 | tf_op jit(solution)/shard_map/ppermute | solution.py:27
  207.5 30.8 %collective-permute-start.35 = (bf16[2,768,128]{2,1,0:T(8,128)(2,1)S(1)}, bf16[2,768,128]{2,1,0:T(8,128)(2,1)}, u32[]{:S(2)}, u32[]{:S(2)}) collective-permute-start(bf16[2,768,128]{2,1,0:T(8,128)(2,1)S(1)} %pad_maximum_fusion.6.p0), channel_id=1, source_target_pairs={{0,8},{8,0},{16,24},{24,16},{1,9},{9,1},{17,25},{25,17},{2,10},{10... | collective-permute-start | bytes 1179656 | tf_op jit(solution)/shard_map/ppermute | solution.py:27
  207.5 30.8 %collective-permute-start.36 = (bf16[2,768,128]{2,1,0:T(8,128)(2,1)}, bf16[2,768,128]{2,1,0:T(8,128)(2,1)}, u32[]{:S(2)}, u32[]{:S(2)}) collective-permute-start(bf16[2,768,128]{2,1,0:T(8,128)(2,1)} %collective-permute-done.27.p2), channel_id=1, source_target_pairs={{0,8},{8,0},{16,24},{24,16},{1,9},{9,1},{17,25},{25,17},{2,10},{10... | collective-permute-start | bytes 1179656 | tf_op jit(solution)/shard_map/ppermute | solution.py:27
  238.3 22.1 %collective-permute-start.40 = (bf16[2,128,3072]{2,1,0:T(8,128)(2,1)S(1)}, bf16[2,128,3072]{2,1,0:T(8,128)(2,1)}, u32[]{:S(2)}, u32[]{:S(2)}) collective-permute-start(bf16[2,128,3072]{2,1,0:T(8,128)(2,1)S(1)} %pad_maximum_fusion.f02), channel_id=1, source_target_pairs={{0,8},{8,0},{16,24},{24,16},{1,9},{9,1},{17,25},{25,17},{2,10},{10... | collective-permute-start | bytes 4718600 | tf_op jit(solution)/shard_map/ppermute | solution.py:27
  238.4 20.3 %collective-permute-start.42 = (bf16[512,768]{1,0:T(8,128)(2,1)}, bf16[512,768]{1,0:T(8,128)(2,1)}, u32[]{:S(2)}, u32[]{:S(2)}) collective-permute-start(bf16[512,768]{1,0:T(8,128)(2,1)} %get-tuple-element.324.a), channel_id=1, source_target_pairs={{0,1},{1,0},{2,3},{3,2},{4,5},{5,4},{6,7},{7,6},{8,9},{9,8},{10,11... | collective-permute-start | bytes 2359304 | tf_op jit(solution)/shard_map/ppermute | solution.py:27
  240.2 11.5 %collective-permute-start.38 = (bf16[128,1536]{1,0:T(8,128)(2,1)}, bf16[128,1536]{1,0:T(8,128)(2,1)}, u32[]{:S(2)}, u32[]{:S(2)}) collective-permute-start(bf16[128,1536]{1,0:T(8,128)(2,1)} %get-tuple-element.312.g0.a0), channel_id=1, source_target_pairs={{0,16},{8,24},{16,0},{24,8},{1,17},{9,25},{17,1},{25,9},{2,18},{10... | collective-permute-start | bytes 1179656 | tf_op jit(solution)/shard_map/ppermute | solution.py:27
  242.4 11.6 %collective-permute-start.41 = (bf16[512,384]{1,0:T(8,128)(2,1)}, bf16[512,384]{1,0:T(8,128)(2,1)}, u32[]{:S(2)}, u32[]{:S(2)}) collective-permute-start(bf16[512,384]{1,0:T(8,128)(2,1)} %pad_maximum_fusion.7), channel_id=1, source_target_pairs={{0,8},{8,0},{16,24},{24,16},{1,9},{9,1},{17,25},{25,17},{2,10},{10... | collective-permute-start | bytes 1179656 | tf_op jit(solution)/shard_map/ppermute | solution.py:27
  242.4 18.0 %collective-permute-start.37 = (bf16[128,1536]{1,0:T(8,128)(2,1)S(1)}, bf16[128,1536]{1,0:T(8,128)(2,1)}, u32[]{:S(2)}, u32[]{:S(2)}) collective-permute-start(bf16[128,1536]{1,0:T(8,128)(2,1)S(1)} %copy-done.17), channel_id=1, source_target_pairs={{0,8},{8,0},{16,24},{24,16},{1,9},{9,1},{17,25},{25,17},{2,10},{10... | collective-permute-start | bytes 1179656 | tf_op jit(solution)/shard_map/ppermute | solution.py:27
  251.7 8.7 %collective-permute-start.39 = (bf16[128,1536]{1,0:T(8,128)(2,1)}, bf16[128,1536]{1,0:T(8,128)(2,1)S(1)}, u32[]{:S(2)}, u32[]{:S(2)}) collective-permute-start(bf16[128,1536]{1,0:T(8,128)(2,1)} %collective-permute-done.38.g2.a2), channel_id=1, source_target_pairs={{0,8},{8,0},{16,24},{24,16},{1,9},{9,1},{17,25},{25,17},{2,10},{10... | collective-permute-start | bytes 1179656 | tf_op jit(solution)/shard_map/ppermute | solution.py:27
  254.0 28.7 %collective-permute-start.45 = (bf16[2,192,1536]{2,1,0:T(8,128)(2,1)}, bf16[2,192,1536]{2,1,0:T(8,128)(2,1)}, u32[]{:S(2)}, u32[]{:S(2)}) collective-permute-start(bf16[2,192,1536]{2,1,0:T(8,128)(2,1)} %dynamic-slice_bitcast_fusion.4), channel_id=1, source_target_pairs={{0,2},{1,3},{2,0},{3,1},{4,6},{5,7},{6,4},{7,5},{8,10},{9,11},{10,... | collective-permute-start | bytes 3538952 | tf_op jit(solution)/shard_map/ppermute | solution.py:27
  258.6 23.4 %collective-permute-start.44 = (bf16[512,768]{1,0:T(8,128)(2,1)}, bf16[512,768]{1,0:T(8,128)(2,1)}, u32[]{:S(2)}, u32[]{:S(2)}) collective-permute-start(bf16[512,768]{1,0:T(8,128)(2,1)} %get-tuple-element.326.b), channel_id=1, source_target_pairs={{0,1},{1,0},{2,3},{3,2},{4,5},{5,4},{6,7},{7,6},{8,9},{9,8},{10,11... | collective-permute-start | bytes 2359304 | tf_op jit(solution)/shard_map/ppermute | solution.py:27
  261.2 23.3 %collective-permute-start.43 = (bf16[128,3072]{1,0:T(8,128)(2,1)}, bf16[128,3072]{1,0:T(8,128)(2,1)S(1)}, u32[]{:S(2)}, u32[]{:S(2)}) collective-permute-start(bf16[128,3072]{1,0:T(8,128)(2,1)} %get-tuple-element.267), channel_id=1, source_target_pairs={{0,16},{8,24},{16,0},{24,8},{1,17},{9,25},{17,1},{25,9},{2,18},{10... | collective-permute-start | bytes 2359304 | tf_op jit(solution)/shard_map/ppermute | solution.py:27
  262.6 21.8 %collective-permute-start.46 = (bf16[256,384]{1,0:T(8,128)(2,1)S(1)}, bf16[256,384]{1,0:T(8,128)(2,1)S(1)}, u32[]{:S(2)}, u32[]{:S(2)}) collective-permute-start(bf16[256,384]{1,0:T(8,128)(2,1)S(1)} %add_convert_fusion.6), channel_id=1, source_target_pairs={{0,16},{8,24},{16,0},{24,8},{1,17},{9,25},{17,1},{25,9},{2,18},{10... | collective-permute-start | bytes 589832 | tf_op jit(solution)/shard_map/ppermute | solution.py:27
  286.9 30.6 %collective-permute-start.49 = (bf16[2,128,3072]{2,1,0:T(8,128)(2,1)S(1)}, bf16[2,128,3072]{2,1,0:T(8,128)(2,1)}, u32[]{:S(2)}, u32[]{:S(2)}) collective-permute-start(bf16[2,128,3072]{2,1,0:T(8,128)(2,1)S(1)} %pad_maximum_fusion.1.b02), channel_id=1, source_target_pairs={{0,8},{8,0},{16,24},{24,16},{1,9},{9,1},{17,25},{25,17},{2,10},{10... | collective-permute-start | bytes 4718600 | tf_op jit(solution)/shard_map/ppermute | solution.py:27
  289.9 38.3 %collective-permute-start.47 = (bf16[2,384,512]{2,1,0:T(8,128)(2,1)}, bf16[2,384,512]{2,1,0:T(8,128)(2,1)}, u32[]{:S(2)}, u32[]{:S(2)}) collective-permute-start(bf16[2,384,512]{2,1,0:T(8,128)(2,1)} %get-tuple-element.276), channel_id=1, source_target_pairs={{1,0},{2,1},{3,2},{4,3},{5,4},{6,5},{7,6},{9,8},{10,9},{11,10},{12... | collective-permute-start | bytes 2359304 | tf_op jit(solution)/shard_map/ppermute | solution.py:33
  291.2 35.9 %collective-permute-start.50 = (f32[768,1]{0,1:T(1,128)S(1)}, f32[768,1]{0,1:T(1,128)S(1)}, u32[]{:S(2)}, u32[]{:S(2)}) collective-permute-start(f32[768,1]{0,1:T(1,128)S(1)} %pad_maximum_fusion.17), channel_id=1, source_target_pairs={{0,1},{1,0},{2,3},{3,2},{4,5},{5,4},{6,7},{7,6},{8,9},{9,8},{10,11... | collective-permute-start | bytes 9224 | tf_op jit(solution)/shard_map/ppermute | solution.py:27
  293.9 34.3 %collective-permute-start.48 = (bf16[2,384,512]{2,1,0:T(8,128)(2,1)}, bf16[2,384,512]{2,1,0:T(8,128)(2,1)}, u32[]{:S(2)}, u32[]{:S(2)}) collective-permute-start(bf16[2,384,512]{2,1,0:T(8,128)(2,1)} %get-tuple-element.284), channel_id=1, source_target_pairs={{0,1},{1,2},{2,3},{3,4},{4,5},{5,6},{6,7},{8,9},{9,10},{10,11},{11... | collective-permute-start | bytes 2359304 | tf_op jit(solution)/shard_map/ppermute | solution.py:33
  300.1 52.5 %collective-permute-start.53 = (bf16[1,192,1536]{2,1,0:T(8,128)(2,1)}, bf16[1,192,1536]{2,1,0:T(8,128)(2,1)}, u32[]{:S(2)}, u32[]{:S(2)}) collective-permute-start(bf16[1,192,1536]{2,1,0:T(8,128)(2,1)} %constant_dynamic-slice_fusion.22), channel_id=1, source_target_pairs={{0,4},{1,5},{2,6},{3,7},{4,0},{5,1},{6,2},{7,3},{8,12},{9,13},{10,... | collective-permute-start | bytes 1769480 | tf_op jit(solution)/shard_map/ppermute | solution.py:27
  317.5 41.1 %collective-permute-start.52 = (bf16[2,192,1536]{2,1,0:T(8,128)(2,1)}, bf16[2,192,1536]{2,1,0:T(8,128)(2,1)S(1)}, u32[]{:S(2)}, u32[]{:S(2)}) collective-permute-start(bf16[2,192,1536]{2,1,0:T(8,128)(2,1)} %dynamic-slice_bitcast_fusion.3), channel_id=1, source_target_pairs={{0,2},{1,3},{2,0},{3,1},{4,6},{5,7},{6,4},{7,5},{8,10},{9,11},{10,... | collective-permute-start | bytes 3538952 | tf_op jit(solution)/shard_map/ppermute | solution.py:27
  336.2 14.3 %collective-permute-start.51 = (bf16[1024,384]{1,0:T(8,128)(2,1)}, bf16[1024,384]{1,0:T(8,128)(2,1)}, u32[]{:S(2)}, u32[]{:S(2)}) collective-permute-start(bf16[1024,384]{1,0:T(8,128)(2,1)} %get-tuple-element.296), channel_id=1, source_target_pairs={{0,8},{8,0},{16,24},{24,16},{1,9},{9,1},{17,25},{25,17},{2,10},{10... | collective-permute-start | bytes 2359304 | tf_op jit(solution)/shard_map/ppermute | solution.py:27
  345.4 29.4 %collective-permute-start.55 = (bf16[4,192,768]{2,1,0:T(8,128)(2,1)S(1)}, bf16[4,192,768]{2,1,0:T(8,128)(2,1)S(1)}, u32[]{:S(2)}, u32[]{:S(2)}) collective-permute-start(bf16[4,192,768]{2,1,0:T(8,128)(2,1)S(1)} %dynamic-slice_bitcast_fusion.2), channel_id=1, source_target_pairs={{0,1},{1,0},{2,3},{3,2},{4,5},{5,4},{6,7},{7,6},{8,9},{9,8},{10,11... | collective-permute-start | bytes 3538952 | tf_op jit(solution)/shard_map/ppermute | solution.py:27
  347.9 48.5 %collective-permute-start.62 = (bf16[2,192,1536]{2,1,0:T(8,128)(2,1)S(1)}, bf16[2,192,1536]{2,1,0:T(8,128)(2,1)S(1)}, u32[]{:S(2)}, u32[]{:S(2)}) collective-permute-start(bf16[2,192,1536]{2,1,0:T(8,128)(2,1)S(1)} %dynamic-slice_bitcast_fusion.1), channel_id=1, source_target_pairs={{0,2},{1,3},{2,0},{3,1},{4,6},{5,7},{6,4},{7,5},{8,10},{9,11},{10,... | collective-permute-start | bytes 3538952 | tf_op jit(solution)/shard_map/ppermute | solution.py:27
  350.6 57.0 %collective-permute-start.66 = (bf16[1152,512]{1,0:T(8,128)(2,1)}, bf16[1152,512]{1,0:T(8,128)(2,1)}, u32[]{:S(2)}, u32[]{:S(2)}) collective-permute-start(bf16[1152,512]{1,0:T(8,128)(2,1)} %get-tuple-element.331), channel_id=1, source_target_pairs={{0,1},{1,0},{2,3},{3,2},{4,5},{5,4},{6,7},{7,6},{8,9},{9,8},{10,11... | collective-permute-start | bytes 3538952 | tf_op jit(solution)/shard_map/ppermute | solution.py:27
  359.6 7.8 %collective-permute-start.54 = (bf16[512,384]{1,0:T(8,128)(2,1)S(1)}, bf16[512,384]{1,0:T(8,128)(2,1)S(1)}, u32[]{:S(2)}, u32[]{:S(2)}) collective-permute-start(bf16[512,384]{1,0:T(8,128)(2,1)S(1)} %add_convert_fusion.2), channel_id=1, source_target_pairs={{0,16},{8,24},{16,0},{24,8},{1,17},{9,25},{17,1},{25,9},{2,18},{10... | collective-permute-start | bytes 1179656 | tf_op jit(solution)/shard_map/ppermute | solution.py:27
  362.5 41.4 %collective-permute-start.64 = (bf16[1,192,1536]{2,1,0:T(8,128)(2,1)}, bf16[1,192,1536]{2,1,0:T(8,128)(2,1)}, u32[]{:S(2)}, u32[]{:S(2)}) collective-permute-start(bf16[1,192,1536]{2,1,0:T(8,128)(2,1)} %constant_dynamic-slice_fusion.9), channel_id=1, source_target_pairs={{0,4},{1,5},{2,6},{3,7},{4,0},{5,1},{6,2},{7,3},{8,12},{9,13},{10,... | collective-permute-start | bytes 1769480 | tf_op jit(solution)/shard_map/ppermute | solution.py:27
  381.6 52.6 %collective-permute-start.73 = (bf16[2,192,768]{2,1,0:T(8,128)(2,1)}, bf16[2,192,768]{2,1,0:T(8,128)(2,1)}, u32[]{:S(2)}, u32[]{:S(2)}) collective-permute-start(bf16[2,192,768]{2,1,0:T(8,128)(2,1)} %dynamic-slice_bitcast_fusion.6), channel_id=1, source_target_pairs={{0,2},{1,3},{2,0},{3,1},{4,6},{5,7},{6,4},{7,5},{8,10},{9,11},{10,... | collective-permute-start | bytes 1769480 | tf_op jit(solution)/shard_map/ppermute | solution.py:27
  384.3 55.6 %collective-permute-start.56 = (bf16[256,1536]{1,0:T(8,128)(2,1)}, bf16[256,1536]{1,0:T(8,128)(2,1)}, u32[]{:S(2)}, u32[]{:S(2)}) collective-permute-start(bf16[256,1536]{1,0:T(8,128)(2,1)} %get-tuple-element.309), channel_id=1, source_target_pairs={{0,8},{8,0},{16,24},{24,16},{1,9},{9,1},{17,25},{25,17},{2,10},{10... | collective-permute-start | bytes 2359304 | tf_op jit(solution)/shard_map/ppermute | solution.py:27
  401.9 64.8 %collective-permute-start.70 = (bf16[4,192,768]{2,1,0:T(8,128)(2,1)S(1)}, bf16[4,192,768]{2,1,0:T(8,128)(2,1)S(1)}, u32[]{:S(2)}, u32[]{:S(2)}) collective-permute-start(bf16[4,192,768]{2,1,0:T(8,128)(2,1)S(1)} %copy-done.32), channel_id=1, source_target_pairs={{0,1},{1,0},{2,3},{3,2},{4,5},{5,4},{6,7},{7,6},{8,9},{9,8},{10,11... | collective-permute-start | bytes 3538952 | tf_op jit(solution)/shard_map/ppermute | solution.py:27
  407.6 29.8 %collective-permute-start.75 = (bf16[1,192,1536]{2,1,0:T(8,128)(2,1)S(1)}, bf16[1,192,1536]{2,1,0:T(8,128)(2,1)S(1)}, u32[]{:S(2)}, u32[]{:S(2)}) collective-permute-start(bf16[1,192,1536]{2,1,0:T(8,128)(2,1)S(1)} %constant_dynamic-slice_fusion), channel_id=1, source_target_pairs={{0,4},{1,5},{2,6},{3,7},{4,0},{5,1},{6,2},{7,3},{8,12},{9,13},{10,... | collective-permute-start | bytes 1769480 | tf_op jit(solution)/shard_map/ppermute | solution.py:27
  407.7 26.0 %collective-permute-start.67 = (f32[1,6,48]{2,0,1:T(1,128)S(1)}, f32[1,6,48]{2,0,1:T(1,128)S(1)}, u32[]{:S(2)}, u32[]{:S(2)}) collective-permute-start(f32[1,6,48]{2,0,1:T(1,128)S(1)} %constant_dynamic-slice_fusion.5), channel_id=1, source_target_pairs={{0,4},{1,5},{2,6},{3,7},{4,0},{5,1},{6,2},{7,3},{8,12},{9,13},{10,... | collective-permute-start | bytes 3464 | tf_op jit(solution)/shard_map/ppermute | solution.py:27
  433.7 27.9 %collective-permute-start.68 = (bf16[2,192,1152]{2,1,0:T(8,128)(2,1)S(1)}, bf16[2,192,1152]{2,1,0:T(8,128)(2,1)S(1)}, u32[]{:S(2)}, u32[]{:S(2)}) collective-permute-start(bf16[2,192,1152]{2,1,0:T(8,128)(2,1)S(1)} %dynamic-slice_bitcast_fusion.5), channel_id=1, source_target_pairs={{0,2},{1,3},{2,0},{3,1},{4,6},{5,7},{6,4},{7,5},{8,10},{9,11},{10,... | collective-permute-start | bytes 2654216 | tf_op jit(solution)/shard_map/ppermute | solution.py:27
  435.6 23.8 %collective-permute-start.74 = (bf16[1,192,768]{2,1,0:T(8,128)(2,1)S(1)}, bf16[1,192,768]{2,1,0:T(8,128)(2,1)S(1)}, u32[]{:S(2)}, u32[]{:S(2)}) collective-permute-start(bf16[1,192,768]{2,1,0:T(8,128)(2,1)S(1)} %constant_dynamic-slice_fusion.1), channel_id=1, source_target_pairs={{0,4},{1,5},{2,6},{3,7},{4,0},{5,1},{6,2},{7,3},{8,12},{9,13},{10,... | collective-permute-start | bytes 884744 | tf_op jit(solution)/shard_map/ppermute | solution.py:27
  441.0 23.6 %collective-permute-start.57 = (bf16[128,1536]{1,0:T(8,128)(2,1)S(1)}, bf16[128,1536]{1,0:T(8,128)(2,1)S(1)}, u32[]{:S(2)}, u32[]{:S(2)}) collective-permute-start(bf16[128,1536]{1,0:T(8,128)(2,1)S(1)} %add_convert_fusion.1), channel_id=1, source_target_pairs={{0,16},{8,24},{16,0},{24,8},{1,17},{9,25},{17,1},{25,9},{2,18},{10... | collective-permute-start | bytes 1179656 | tf_op jit(solution)/shard_map/ppermute | solution.py:27
  461.8 22.1 %collective-permute-start.69 = (bf16[1,192,1152]{2,1,0:T(8,128)(2,1)S(1)}, bf16[1,192,1152]{2,1,0:T(8,128)(2,1)S(1)}, u32[]{:S(2)}, u32[]{:S(2)}) collective-permute-start(bf16[1,192,1152]{2,1,0:T(8,128)(2,1)S(1)} %constant_dynamic-slice_fusion.3), channel_id=1, source_target_pairs={{0,4},{1,5},{2,6},{3,7},{4,0},{5,1},{6,2},{7,3},{8,12},{9,13},{10,... | collective-permute-start | bytes 1327112 | tf_op jit(solution)/shard_map/ppermute | solution.py:27
  467.1 23.6 %collective-permute-start.71 = (bf16[2,192,768]{2,1,0:T(8,128)(2,1)S(1)}, bf16[2,192,768]{2,1,0:T(8,128)(2,1)S(1)}, u32[]{:S(2)}, u32[]{:S(2)}) collective-permute-start(bf16[2,192,768]{2,1,0:T(8,128)(2,1)S(1)} %dynamic-slice_bitcast_fusion.7), channel_id=1, source_target_pairs={{0,2},{1,3},{2,0},{3,1},{4,6},{5,7},{6,4},{7,5},{8,10},{9,11},{10,... | collective-permute-start | bytes 1769480 | tf_op jit(solution)/shard_map/ppermute | solution.py:27
  472.2 12.8 %collective-permute-start.59 = (bf16[256,384]{1,0:T(8,128)(2,1)S(1)}, bf16[256,384]{1,0:T(8,128)(2,1)S(1)}, u32[]{:S(2)}, u32[]{:S(2)}) collective-permute-start(bf16[256,384]{1,0:T(8,128)(2,1)S(1)} %pad_maximum_fusion.14), channel_id=1, source_target_pairs={{0,8},{8,0},{16,24},{24,16},{1,9},{9,1},{17,25},{25,17},{2,10},{10... | collective-permute-start | bytes 589832 | tf_op jit(solution)/shard_map/ppermute | solution.py:27
  490.9 13.2 %collective-permute-start.72 = (bf16[1,192,768]{2,1,0:T(8,128)(2,1)S(1)}, bf16[1,192,768]{2,1,0:T(8,128)(2,1)S(1)}, u32[]{:S(2)}, u32[]{:S(2)}) collective-permute-start(bf16[1,192,768]{2,1,0:T(8,128)(2,1)S(1)} %constant_dynamic-slice_fusion.2), channel_id=1, source_target_pairs={{0,4},{1,5},{2,6},{3,7},{4,0},{5,1},{6,2},{7,3},{8,12},{9,13},{10,... | collective-permute-start | bytes 884744 | tf_op jit(solution)/shard_map/ppermute | solution.py:27
  (80 other events, 778.6 us)
where the time goes:
time: 515 us; the launch traced here: 506 us
  waiting for transfers between devices  192 us (37%)
  Pallas kernels  154 us (30%)
  starting transfers between devices  67.6 us (13%)
  other arithmetic  44.9 us (9%)
  local copies, waits for them, and re-layouts  35.6 us (7%)
  matrix products  8.39 us (2%)
    ppermute x72, waiting for transfers between devices, swap(): lax.ppermute(value, axis, [(i, i ^ by) for i in range(lax.axis_size(axis))])  180 us
    ppermute x72, starting transfers between devices, swap(): lax.ppermute(value, axis, [(i, i ^ by) for i in range(lax.axis_size(axis))])  56.5 us
    pallas_call x2, Pallas kernels, ffn(): pl.pallas_call(functools.partial(ffn_second_body if half else ffn_first_b...  29.7 us
    pallas_call x1, Pallas kernels, cross_backward(): pl.pallas_call(cross_backward_body, grid=(1,), out_shape=[jax.ShapeDtypeS...  21 us
    pallas_call x1, Pallas kernels, attend_back(): pl.pallas_call(backward_body, in_specs=[pl.BlockSpec(memory_space=pltpu.S...  17.7 us
    pallas_call x1, Pallas kernels, cross_forward(): pl.pallas_call(functools.partial(cross_forward_body, width // devices), g...  16.6 us
    pallas_call x2, Pallas kernels, meet_cols(): pl.pallas_call(meet_cols_body, out_shape=jax.ShapeDtypeStruct((near[0].sh...  13 us
    ppermute x4, waiting for transfers between devices, shift(): return lax.ppermute(value, axis, pairs)  11.5 us
  transfers between devices with their start and end apart: 76, of which 30 were waited for; matrix products, arithmetic and copies ran while one was open for 14% of the time, Pallas kernels for 30%

commit v1 on v0

--- a/solution.py
+++ b/solution.py
@@ -684,43 +684,47 @@
     )(own, got, far, grad, first, second, norms, *query_parts, *kv_parts, *out_parts, queries)
 
 
-def meet_rows_body(own_a, pair_a, own_b, pair_b, right, right_pair, out):
-    count = own_a.shape[0]
+def meet_rows_body(size, side, own_a, pair_a, own_b, pair_b, right, right_pair, keep, send):
+    half = keep.shape[0] // 2
     for b, (own, pair) in enumerate(((own_a, pair_a), (own_b, pair_b))):
-        out[b * count : (b + 1) * count, :] = (
-            dot_nn(own[...], right[...]) + dot_nn(pair[...], right_pair[...])
-        ).astype(BF16)
-
-
-def meet_rows(lefts, rights):
-    count, size = lefts[0].shape
+        made = (dot_nn(own[...], right[...]) + dot_nn(pair[...], right_pair[...])).astype(BF16)
+        at = pl.ds(b * half, half)
+        deal_rows(made, size, side[0], keep.at[at], send.at[at])
+
+
+def meet_rows(size, side, lefts, rights):
+    count, frames = lefts[0].shape
     width = rights[0].shape[1]
     tile = width // 3
-    left = pl.BlockSpec((count, size), lambda i: (0, 0))
-    right = pl.BlockSpec((size, tile), lambda i: (0, i))
+    left = pl.BlockSpec((count, frames), lambda i: (0, 0))
+    right = pl.BlockSpec((frames, tile), lambda i: (0, i))
     return pl.pallas_call(
-        meet_rows_body,
+        functools.partial(meet_rows_body, size),
         grid=(3,),
-        in_specs=[left] * 4 + [right] * 2,
-        out_specs=pl.BlockSpec((2 * count, tile), lambda i: (0, i)),
-        out_shape=jax.ShapeDtypeStruct((2 * count, width), BF16),
+        in_specs=[pl.BlockSpec(memory_space=pltpu.SMEM)] + [left] * 4 + [right] * 2,
+        out_specs=[pl.BlockSpec((count, tile), lambda i: (0, i))] * 2,
+        out_shape=[jax.ShapeDtypeStruct((count, width), BF16)] * 2,
         name="meet_rows", cost_estimate=FREE,
-    )(*lefts, *rights)
-
-
-def meet_cols_body(p0, p1, p2, p3, a, a_pair, b, b_pair, out):
+    )(side, *lefts, *rights)
+
+
+def meet_cols_body(size, side, p0, p1, p2, p3, a, a_pair, b, b_pair, keep, send):
     own, pair = (jnp.concatenate([p[i] for p in (p0, p1, p2, p3)], 1) for i in (0, 1))
     width = a.shape[1]
-    out[:, :width] = (dot_nn(own, a[...]) + dot_nn(pair, a_pair[...])).astype(BF16)
-    out[:, width:] = (dot_nn(own, b[...]) + dot_nn(pair, b_pair[...])).astype(BF16)
-
-
-def meet_cols(near, rights):
+    for left, (right, right_pair) in ((0, (a, a_pair)), (width, (b, b_pair))):
+        made = (dot_nn(own, right[...]) + dot_nn(pair, right_pair[...])).astype(BF16)
+        cols = pl.ds(left, width)
+        deal_rows(made, size, side[0], keep.at[:, cols], send.at[:, cols])
+
+
+def meet_cols(size, side, near, rights):
+    half = jax.ShapeDtypeStruct((near[0].shape[1] // 2, 2 * rights[0].shape[1]), BF16)
     return pl.pallas_call(
-        meet_cols_body,
-        out_shape=jax.ShapeDtypeStruct((near[0].shape[1], 2 * rights[0].shape[1]), BF16),
+        functools.partial(meet_cols_body, size),
+        in_specs=[pl.BlockSpec(memory_space=pltpu.SMEM)] + [pl.BlockSpec(memory_space=pltpu.VMEM)] * 8,
+        out_shape=[half] * 2,
         name="meet_cols", cost_estimate=FREE,
-    )(*near, *rights)
+    )(side, *near, *rights)
 
 
 def down_body(first, second, down_w, away, own, low):
@@ -748,7 +752,7 @@
 
 
 def bundle_body(devices, place, f02, f13, b02, b13, a0, a1, a2, a3, attended,
-                context, kv, out_a, out_b):
+                context, kv, keep_a, send_a, keep_b, send_b):
     width = a0.shape[1]
     part, share = width // 4, a0.shape[0]
 
@@ -765,24 +769,36 @@
     half = width // 2
 
     def put(block, base, left, out):
-        for d in range(devices):
-            at = slice(base, base + block.shape[0] // devices)
-            piece = block[d * block.shape[0] // devices : (d + 1) * block.shape[0] // devices, :]
-            out[d, at, left : left + block.shape[1]] = piece.astype(BF16)
-
-    put(dot_tn(full(fronts), own(backs)), 0, 0, out_a)
+        size = block.shape[0] // devices
+        cols = slice(left, left + block.shape[1])
+        low = block.astype(BF16)
+        for d in range(0, devices, 2):
+            at = slice(base, base + size)
+            even, odd = low[d * size : (d + 1) * size, :], low[(d + 1) * size : (d + 2) * size, :]
+
+            @pl.when(place[0] == 0)
+            def _():
+                out[0][d // 2, at, cols] = even
+                out[1][d // 2, at, cols] = odd
+
+            @pl.when(place[0] != 0)
+            def _():
+                out[0][d // 2, at, cols] = odd
+                out[1][d // 2, at, cols] = even
+
+    put(dot_tn(full(fronts), own(backs)), 0, 0, (keep_a, send_a))
     count = context.shape[0]
-    put(dot_tn(context[...], kv[:count, :]), 0, part, out_a)
-    put(dot_tn(context[...], kv[count:, :]), rows // 2, part, out_a)
+    put(dot_tn(context[...], kv[:count, :]), 0, part, (keep_a, send_a))
+    put(dot_tn(context[...], kv[count:, :]), rows // 2, part, (keep_a, send_a))
     grads = dot_tn(own(fronts), full(backs))
-    put(grads[:, :half], 0, 0, out_b)
-    put(grads[:, half:], small, 0, out_b)
+    put(grads[:, :half], 0, 0, (keep_b, send_b))
+    put(grads[:, half:], small, 0, (keep_b, send_b))
     grads = sum(
-        dot_nn(attended[:, relative(place[0], r, share)], ref[...])
+        dot_nn(attended[:, relative(place[1], r, share)], ref[...])
         for r, ref in enumerate((a0, a1, a2, a3))
     )
-    put(grads[:, :half], 2 * small, 0, out_b)
-    put(grads[:, half:], 3 * small, 0, out_b)
+    put(grads[:, :half], 2 * small, 0, (keep_b, send_b))
+    put(grads[:, half:], 3 * small, 0, (keep_b, send_b))
 
 
 def bundle_grads(devices, place, fronts, backs, ones, attended, context, kv):
@@ -791,14 +807,16 @@
     return pl.pallas_call(
         functools.partial(bundle_body, devices),
         in_specs=[pl.BlockSpec(memory_space=pltpu.SMEM)] + [vmem] * 11,
-        out_specs=[vmem] * 2,
-        out_shape=[jax.ShapeDtypeStruct((devices, width // devices, width // 2), BF16)] * 2,
+        out_specs=[vmem] * 4,
+        out_shape=[jax.ShapeDtypeStruct((devices // 2, width // devices, width // 2), BF16)] * 4,
         name="bundle", cost_estimate=FREE,
     )(place, *fronts, *backs, *ones, attended, context, kv)
 
 
 def front_body(width_block, place, x0, x1, x2, x3, g0, g1, g2, g3, cosine, sine, wq, wk, wv,
-               queries, pair, rows, low, nrm_own, nrm_away, norms, means, inverses, wide):
+               time_row, context, ck, cv,
+               queries, pair, rows, low, nrm_own, nrm_away, norms, means, inverses,
+               time_scaled, time_low, time_keys, time_values, kv, wide):
     size, part = x0.shape
     for r, (x, g) in enumerate(((x0, g0), (x1, g1), (x2, g2), (x3, g3))):
         start = pl.multiple_of((place[0] ^ r) * part, 128)
@@ -830,13 +848,22 @@
                 (b * cosine[...] + a * sine[...]) * scale
             ).astype(BF16)
 
+    scaled, _ = normalize(jnp.broadcast_to(time_row[...].astype(F32), (8, 4 * part)))
+    time_scaled[...] = scaled[:1, :]
+    made = (scaled * norms[0:1, :] + norms[1:2, :]).astype(BF16)
+    time_low[...] = made[:1, :].astype(F32)
+    time_keys[...] = dot_nn(made, wk[...]).astype(BF16).astype(F32).T[:, :1]
+    time_values[...] = dot_nn(made, wv[...]).astype(BF16).astype(F32).T[:, :1]
+    count = context.shape[0]
+    kv[:count, :] = dot_nn(context[...], ck[...]).astype(BF16)
+    kv[count:, :] = dot_nn(context[...], cv[...]).astype(BF16)
     rotated(turned(wk), pair.at[0], 1.0)
     pair[1] = turned(wv).astype(BF16)
     rotated(turned(wq), queries, 1.0 / math.sqrt(HEAD_SIZE))
     deal_rows(normed.T, width_block, place[1], nrm_own, nrm_away)
 
 
-def front(devices, place, parts, norm_parts, tables, wq, wk, wv):
+def front(devices, place, parts, norm_parts, tables, wq, wk, wv, time_row, context, ck, cv):
     size, part = parts[0].shape
     width = 4 * part
     low = lambda *s: jax.ShapeDtypeStruct(s, BF16)
@@ -844,14 +871,15 @@
     vmem = pl.BlockSpec(memory_space=pltpu.VMEM)
     return pl.pallas_call(
         functools.partial(front_body, width // devices),
-        in_specs=[pl.BlockSpec(memory_space=pltpu.SMEM)] + [vmem] * 13,
-        out_specs=[vmem] * 9,
+        in_specs=[pl.BlockSpec(memory_space=pltpu.SMEM)] + [vmem] * 17,
+        out_specs=[vmem] * 14,
         out_shape=[low(part, size), low(2, part, size), low(size // 4, width), low(size, width),
                    low(width // 2, size), low(width // 2, size), wide(6, width),
-                   wide(size, 1), wide(size, 1)],
+                   wide(size, 1), wide(size, 1), wide(1, width), wide(1, width), wide(part, 1),
+                   wide(part, 1), low(2 * context.shape[0], part)],
         scratch_shapes=[pltpu.VMEM((size, width), BF16)],
         cost_estimate=FREE, name="front",
-    )(place, *parts, *norm_parts, *tables, wq, wk, wv)
+    )(place, *parts, *norm_parts, *tables, wq, wk, wv, time_row, context, ck, cv)
 
 
 def per_device(
@@ -915,7 +943,7 @@
     places = jnp.stack([column, place]).astype(jnp.int32)
     label_row, label_column = own_labels[None, :], key_labels[:, None]
     row_index = first_frame // row_length
-    time_row = lax.dynamic_slice_in_dim(time_token, row_index, 1, 0).astype(F32)
+    time_row = lax.dynamic_slice_in_dim(time_token, row_index, 1, 0)
     row_context = lax.dynamic_slice_in_dim(context, row_index, 1, 0)[0]
     context_rows = row_context.shape[0]
     tables = rotary_tables(own_positions)
@@ -924,26 +952,16 @@
 
     (
         queries, both, frame_rows, frame_normed, one_own_half, one_away_half, norms, means_one,
-        inverse_one,
+        inverse_one, scaled_time, time_normed, time_keys, time_values, context_kv,
     ) = front(
         lax.axis_size("seq"), jnp.flip(places), frame_parts_near, norm_parts, tables, w_query,
-        w_key, w_value,
+        w_key, w_value, time_row, row_context, c_key, c_value,
     )
     both, out_pair = meeting(both, swap(after(out_grad, frame_parts_near[2]), "seq", 1))
     grad_both = jnp.stack([out_grad, out_pair])
-    gain_one, bias_one = norms[0:1], norms[1:2]
     behind, ahead = shift(both, "seq", 1), shift(both, "seq", -1)
     query_far = swap(after(c_query, frame_parts_near[3]), "tensor", 2)
     out_far = swap(after(c_out, frame_parts_near[3]), "tensor", 2)
-    time_late = after(time_row, both)
-    scaled_time, _ = normalize(time_late)
-    time_normed = (scaled_time * gain_one + bias_one).astype(BF16)
-    time_keys = by_feature(time_normed, w_key).astype(BF16).astype(F32)
-    time_values = by_feature(time_normed, w_value).astype(BF16).astype(F32)
-    context_late = after(row_context, both)
-    context_kv = jnp.concatenate(
-        [product(context_late, c_key), product(context_late, c_value)], 0
-    ).astype(BF16)
     state = attend_near(spans, queries, both, time_keys, time_values, label_row, label_column)
     behind, ahead, query_far, out_far, *state = meeting(
         behind, ahead, query_far, out_far, *state
@@ -1010,17 +1028,22 @@
         grad_one, gate_got_a, hidden_got_b, lifted_got_a, flip_mate, flip_far_mate
     )
     count = lax.axis_size("seq")
-
-    def by_level(blocks):
-        return blocks.reshape(count // 2, 2 * blocks.shape[0] // count, blocks.shape[1])
-
-    down_keep, down_got = halve(
-        by_level(
-            meet_rows(
-                (hidden_own_a, hidden_got_a, hidden_own_b, hidden_got_b), (grad_near, grad_pair)
-            )
-        ),
-        1,
+    level_side = ((lax.axis_index("seq") >> 1) % 2).astype(jnp.int32).reshape(1)
+    rows = model_width // count
+
+    def traded(dealt):
+        keep, send = [value.reshape(count // 4, rows, -1) for value in dealt]
+        return keep, swap(send, "seq", 2)
+
+    down_keep, down_got = traded(
+        meet_rows(
+            rows, level_side, (hidden_own_a, hidden_got_a, hidden_own_b, hidden_got_b),
+            (grad_near, grad_pair),
+        )
+    )
+    flip_near = (flip_both, flip_mate, flip_far, flip_far_mate)
+    first_keep, first_got = traded(
+        meet_cols(rows, level_side, flip_near, (gate_a, gate_got_a, lifted_a, lifted_got_a))
     )
     context_parts = quarters(kv_grad, 1)
     context_got = swap(jnp.concatenate([context_parts[1], context_parts[3]], 0), "tensor", 1)
@@ -1032,6 +1055,7 @@
         context_parts[2].astype(F32) + context_got[context_parts[2].shape[0] :].astype(F32)
     ).astype(BF16)
     context_far = swap(context_low, "tensor", 2)
+    *one_parts, first_keep = meeting(*one_parts, first_keep)
     back_far = swap(after(back_rows, one_parts[3]), "tensor", 2)
     lifted_got_b = swap(after(lifted_b, grad_one), "seq", 1)
     query_grad, to_prev, kept, to_next, time_key_grad, time_value_grad = attend_back(
@@ -1041,14 +1065,12 @@
     to_prev, to_next, back_far, lifted_got_b, down_got, context_far = meeting(
         to_prev, to_next, back_far, lifted_got_b, down_got, context_far
     )
-    time_both = jnp.concatenate([time_key_grad, time_value_grad], 0)
-    time_got = swap(after(time_both, to_prev), "seq", 1)
     from_next, from_prev = shift(to_prev, "seq", -1), shift(to_next, "seq", 1)
     down_keep, down_got = halve(added(down_keep, down_got).astype(BF16), 2)
-    flip_near = (flip_both, flip_mate, flip_far, flip_far_mate)
-    first_keep, first_got = halve(
-        by_level(meet_cols(flip_near, after((gate_a, gate_got_a, lifted_a, lifted_got_a), to_prev))),
-        1,
+    second_keep, second_got = traded(
+        meet_cols(
+            rows, level_side, flip_near, (gate_b, gate_got_b, lifted_b, lifted_got_b)
+        )
     )
     down_away, down_own, down_low = down_parts(after(hidden_a, to_prev), hidden_b, w_down)
     back_both = jnp.stack([back_rows, back_far])
@@ -1058,15 +1080,15 @@
         + context_got[: context_far.shape[0]].astype(F32)
         + context_far.astype(F32)
     )
-    bundle_a, bundle_b = bundle_grads(
-        count, places[1:], (front_both, front_other), (back_both, back_other), one_parts, attended,
+    keep_a, send_a, keep_b, send_b = bundle_grads(
+        count, places, (front_both, front_other), (back_both, back_other), one_parts, attended,
         row_context,
         context_own.astype(BF16),
     )
-    from_next, from_prev, bundle_a, bundle_b, time_got = meeting(
-        from_next, from_prev, bundle_a, bundle_b, time_got
-    )
-    keep_a, got_a = halve(bundle_a, 0)
+    from_next, from_prev, first_got, send_a, send_b = meeting(
+        from_next, from_prev, first_got, send_a, send_b
+    )
+    got_a = swap(send_a, "seq", 1)
     raw, last_away, last_own, last_low = tail(
         places[1:], query_grad, kept, from_next, from_prev, tables, w_query, w_key, w_value
     )
@@ -1075,15 +1097,13 @@
     last_sum = (
         last_low.astype(F32) + last_got[local_rows:].astype(F32)
     ).astype(BF16)
-    last_sum, first_got, down_got = meeting(last_sum, first_got, down_got)
+    last_sum, down_got, second_got, got_a = meeting(last_sum, down_got, second_got, got_a)
     first_keep, first_got = halve(added(first_keep, first_got).astype(BF16), 2)
-    second = by_level(
-        meet_cols(flip_near, after((gate_b, gate_got_b, lifted_b, lifted_got_b), from_next))
-    )
-    second_keep, second_got = halve(second, 1)
+    got_b = swap(after(send_b, got_a), "seq", 1)
+    left_keep, left_got = halve(added(keep_a, got_a).astype(BF16), 1)
     last_far = swap(last_sum, "tensor", 2)
-    last_far, got_a = meeting(last_far, got_a)
-    keep_b, got_b = halve(after(bundle_b, last_far), 0)
+    time_both = jnp.concatenate([time_key_grad, time_value_grad], 0)
+    last_far, time_got = meeting(last_far, swap(after(time_both, last_low), "seq", 1))
     frame_grad = last_own + last_got[:local_rows].astype(F32) + last_far.astype(F32)
 
     def to_frames(rows, weight):
@@ -1105,7 +1125,8 @@
     )[None]
     sums = sums + swap(sums, "tensor", 1)
     sums = sums + swap(sums, "tensor", 2)
-    sums, second_got = meeting(sums, second_got)
+    sums, first_got, left_got = meeting(sums, first_got, left_got)
+    left_keep, left_got = halve(added(left_keep, left_got).astype(BF16), 2)
     plain = sums[0, :local_rows, None] / model_width
     cross = sums[0, local_rows : 2 * local_rows, None] / model_width
     vectors = own_cols(sums[0, 2 * local_rows :].reshape(5, model_width))
@@ -1119,14 +1140,12 @@
         [d_gain_attn, d_bias_attn, vectors[3], vectors[4], vectors[1], vectors[2]]
     ).reshape(6, devices, -1).transpose(1, 0, 2)
     small = added(*halve(small, 0))
-    small, first_got = meeting(small, first_got)
     small = added(*halve(small, 1))
-    small, raw_got = meeting(small, raw_got)
     bit = 2
     while small.shape[0] > 1:
         small = added(*halve(small, bit))
         bit += 1
-    small = small[0]
+    small, raw_got = meeting(small[0], raw_got)
 
     down_away, down_low = after((down_away, down_low), last_far)
     branch_got, _, branch_far = scatter_near(down_away, down_low)
@@ -1142,21 +1161,14 @@
     )
     block_out = jnp.concatenate([row_block(block_cols, place ^ b) for b in range(4)], 0)
 
-    time_column = time_normed.astype(F32).T
+    time_column = time_normed.T
 
     normed_pair = (one_own_half, normed_got)
     grad_down = halve_end(down_keep, down_got, 3)
-    first, second = halve_end(first_keep, first_got, 3), halve_end(second_keep, second_got, 2)
+    first, second = halve_end(first_keep, first_got, 3), halve_all(after(added(second_keep, second_got), sums), 2)
     units = first.shape[1] // 2
     grad_gate_w = jnp.concatenate([first[:, :units], second[:, :units]], 1)
     grad_up_w = jnp.concatenate([first[:, units:], second[:, units:]], 1)
-    left, right = halve_end(keep_a, got_a, 1), halve_end(keep_b, got_b, 1)
-    part, rows = head_cols // count, model_width // count
-    grad_c_query = left[:, :head_cols]
-    grad_c_key, grad_c_value = left[: rows // 2, head_cols:], left[rows // 2 :, head_cols:]
-    grad_c_out = jnp.concatenate([right[:part], right[part : 2 * part]], 1)
-    grad_w_out = jnp.concatenate([right[2 * part : 3 * part], right[3 * part :]], 1)
-
     raw_pair = (raw, raw_got)
     time_both = time_both + time_got
     own_time_rows = lax.dynamic_index_in_dim(
@@ -1167,8 +1179,17 @@
         jnp.einsum("dn,fn->df", r, c, preferred_element_type=F32)
         for r, c in zip(normed_pair, raw_pair)
     )
-    blocks = by_level((blocks + outer).astype(BF16))
-    heads_sum = halve_all(blocks, 1)
+    heads_keep, heads_got = halve(
+        (blocks + outer).astype(BF16).reshape(count // 2, rows, 3 * head_cols), 1
+    )
+    heads_got, got_b = meeting(heads_got, got_b)
+    heads_sum = halve_end(heads_keep, heads_got, 2)
+    left, right = halve_end(left_keep, left_got, 3), halve_end(keep_b, got_b, 1)
+    part, rows = head_cols // count, model_width // count
+    grad_c_query = left[:, :head_cols]
+    grad_c_key, grad_c_value = left[: rows // 2, head_cols:], left[rows // 2 :, head_cols:]
+    grad_c_out = jnp.concatenate([right[:part], right[part : 2 * part]], 1)
+    grad_w_out = jnp.concatenate([right[2 * part : 3 * part], right[3 * part :]], 1)
     grad_w_query, grad_w_key, grad_w_value = (
         heads_sum[:, i * head_cols : (i + 1) * head_cols] for i in range(3)
     )

time: 515 us -> 534 us (1.037)
  starting transfers between devices: 67.6 us -> 94.7 us
  other arithmetic: 44.9 us -> 39.1 us
    ppermute x72, starting transfers between devices: 56.5 us -> 84.4 us  [swap(): lax.ppermute(value, axis, [(i, i ^ by) for i in range(lax.axis_size(axis))])]
    squeeze x15 -> x10, local copies, waits for them, and re-layouts: 10.4 us -> 1.24 us  [halve(): send = lax.dynamic_index_in_dim(parts, 1 - side, 1, False)]
    ppermute x4, waiting for transfers between devices: 11.5 us -> 18 us  [shift(): return lax.ppermute(value, axis, pairs)]
  transfers between devices with their start and end apart: 76 -> 76, of which waited for: 30 -> 28; matrix products, arithmetic and copies ran while one was open for 14% -> 12% of each run, Pallas kernels for 30% -> 30%
where the time goes in v1:
time: 534 us; the launch traced here: 524 us
  waiting for transfers between devices  194 us (36%)
  Pallas kernels  157 us (29%)
  starting transfers between devices  94.7 us (18%)
  other arithmetic  39.1 us (7%)
  local copies, waits for them, and re-layouts  31.1 us (6%)
  matrix products  5.94 us (1%)
    ppermute x72, waiting for transfers between devices, swap(): lax.ppermute(value, axis, [(i, i ^ by) for i in range(lax.axis_size(axis))])  176 us
    ppermute x72, starting transfers between devices, swap(): lax.ppermute(value, axis, [(i, i ^ by) for i in range(lax.axis_size(axis))])  84.4 us
    pallas_call x2, Pallas kernels, ffn(): pl.pallas_call(functools.partial(ffn_second_body if half else ffn_first_b...  29.7 us
    pallas_call x1, Pallas kernels, cross_backward(): pl.pallas_call(cross_backward_body, grid=(1,), out_shape=[jax.ShapeDtypeS...  21 us
    ppermute x4, waiting for transfers between devices, shift(): return lax.ppermute(value, axis, pairs)  18 us
    pallas_call x1, Pallas kernels, cross_forward(): pl.pallas_call(functools.partial(cross_forward_body, width // devices), g...  16.5 us
    pallas_call x1, Pallas kernels, attend_back(): pl.pallas_call(backward_body, in_specs=[pl.BlockSpec(memory_space=pltpu.S...  16.2 us
    pallas_call x2, Pallas kernels, meet_cols(): pl.pallas_call(functools.partial(meet_cols_body, size), in_specs=[pl.Bloc...  15.2 us
  transfers between devices with their start and end apart: 76, of which 28 were waited for; matrix products, arithmetic and copies ran while one was open for 12% of the time, Pallas kernels for 30%

profile of v1, /device:TPU:0, one launch (start us, length us, event | category | flops | bytes accessed | tf_op | source)
XLA Modules:
  0.0 524.4 jit_solution(1667271961857799030)
XLA Ops:
  0.7 3.0 collective-permute-start.1
  11.4 1.8 collective-permute-done.1.x2
  14.3 1.7 collective-permute-start.6
  22.4 9.6 %front.1 = (bf16[384,512]{1,0:T(8,128)(2,1)}, bf16[2,384,512]{2,1,0:T(8,128)(2,1)}, bf16[128,1536]{1,0:T(8,128)(2,1)}, bf16[512,1536]{1,0:T(8,128)(2,1)}, bf16[7...) custom-call(s32[2]{0:T(128)} %rev.4.place, ...), custom_call_target="tpu_custom_call" | custom-call | flops 1 | bytes 1 | tf_op jit(solution)/shard_map/front/pallas_call | solution.py:872
  33.3 5.4 %collective-permute-start.7 = (bf16[2,384,512]{2,1,0:T(8,128)(2,1)}, bf16[2,384,512]{2,1,0:T(8,128)(2,1)}, u32[]{:S(2)}, u32[]{:S(2)}) collective-permute-start(bf16[2,384,512]{2,1,0:T(8,128)(2,1)} %get-tuple-element.196.kv.kv1), channel_id=1, source_target_pairs={{0,1},{1,2},{2,3},{3,4},{4,5},{5,6},{6,7},{8,9},{9,10},{10,11},{11... | collective-permute-start | bytes 2359304 | tf_op jit(solution)/shard_map/ppermute | solution.py:33
  41.4 10.4 %attend_near.1 = (f32[6,512]{1,0:T(8,128)}, f32[6,512]{1,0:T(8,128)}, f32[384,512]{1,0:T(8,128)}) custom-call(s32[5]{0:T(128)} %pad_add_fusion.2.span, bf16[384,512]{1,0:T(8,128)(2,1)} %get-tuple-element.193.q, bf16[2,384,512]{2,1,0:T(8,128)(2,1)} %get-tuple-element.196.kv.kv1, f32[384,1]{1,0:T(8,128)} %get-tuple-element.199.tk, ...), custom_call_target="tpu_custom_call" | custom-call | flops 1 | bytes 1 | tf_op jit(solution)/shard_map/attend_near/pallas_call | solution.py:301
  51.8 2.0 collective-permute-done.8.kv2
  53.7 16.0 %collective-permute-done.7.kv0 = bf16[2,384,512]{2,1,0:T(8,128)(2,1)} collective-permute-done((bf16[2,384,512]{2,1,0:T(8,128)(2,1)}, bf16[2,384,512]{2,1,0:T(8,128)(2,1)}, u32[]{:S(2)}, u32[]{:S(2)}) %collective-permute-start.7) | collective-permute-done | bytes 786464 | tf_op jit(solution)/shard_map/ppermute | solution.py:33
  72.4 7.0 %attend_far.1 = (bf16[384,512]{1,0:T(8,128)(2,1)}, f32[6,512]{1,0:T(8,128)}, bf16[256,1536]{1,0:T(8,128)(2,1)}, f32[128,1536]{1,0:T(8,128)}, bf16[128,1536]{1,0:T(8,128)(2,1)}) custom-call(s32[5]{0:T(128)} %pad_add_fusion.2.span, bf16[384,512]{1,0:T(8,128)(2,1)} %get-tuple-element.193.q, bf16[2,384,512]{2,1,0:T(8,128)(2,1)} %collective-permute-done.7.kv0, ...), custom_call_target="tpu_custom_call" | custom-call | flops 1 | bytes 1 | tf_op jit(solution)/shard_map/attend_far/pallas_call | solution.py:319
  79.5 2.5 collective-permute-done.16.got
  84.1 4.3 collective-permute-start.19
  88.4 6.2 %collective-permute-done.17.far = bf16[128,1536]{1,0:T(8,128)(2,1)S(1)} collective-permute-done((bf16[128,1536]{1,0:T(8,128)(2,1)S(1)}, bf16[128,1536]{1,0:T(8,128)(2,1)S(1)}, u32[]{:S(2)}, u32[]{:S(2)}) %collective-permute-start.17) | collective-permute-done | bytes 393248 | tf_op jit(solution)/shard_map/ppermute | solution.py:27
  95.2 1.7 collective-permute-done.18
  97.7 16.5 %cross.1 = (bf16[128,3072]{1,0:T(8,128)(2,1)}, bf16[128,1536]{1,0:T(8,128)(2,1)}, f32[128,1536]{1,0:T(8,128)}, f32[128,1536]{1,0:T(8,128)}, bf16[128,1536]{1,0:T...) custom-call(s32[2]{0:T(128)} %copy-done.76, bf16[128,1536]{1,0:T(8,128)(2,1)} %get-tuple-element.192.rows, ...), custom_call_target="tpu_custom_call" | custom-call | flops 1 | bytes 1 | tf_op jit(solution)/shard_map/cross/pallas_call | solution.py:522
  116.4 9.3 %collective-permute-done.22.n2 = bf16[128,1536]{1,0:T(8,128)(2,1)S(1)} collective-permute-done((bf16[128,1536]{1,0:T(8,128)(2,1)}, bf16[128,1536]{1,0:T(8,128)(2,1)S(1)}, u32[]{:S(2)}, u32[]{:S(2)}) %collective-permute-start.22) | collective-permute-done | bytes 393248 | tf_op jit(solution)/shard_map/ppermute | solution.py:27
  126.3 1.7 collective-permute-done.23.n3
  129.5 4.2 collective-permute-start.26
  136.3 14.7 %ffn.2 = (bf16[512,768]{1,0:T(8,128)(2,1)}, bf16[384,512]{1,0:T(8,128)(2,1)}, bf16[384,512]{1,0:T(8,128)(2,1)}, bf16[512,768]{1,0:T(8,128)(2,1)}, bf16[512,768]{...) custom-call(s32[2]{0:T(128)} %copy-done.76, ...), custom_call_target="tpu_custom_call" | custom-call | flops 1 | bytes 1 | tf_op jit(solution)/shard_map/ffn/pallas_call | solution.py:611
  152.7 15.0 %ffn.3 = (bf16[512,768]{1,0:T(8,128)(2,1)}, bf16[384,512]{1,0:T(8,128)(2,1)}, bf16[384,512]{1,0:T(8,128)(2,1)}, bf16[512,768]{1,0:T(8,128)(2,1)}, bf16[512,768]{...) custom-call(s32[2]{0:T(128)} %copy-done.76, ...), custom_call_target="tpu_custom_call" | custom-call | flops 1 | bytes 1 | tf_op jit(solution)/shard_map/ffn/pallas_call | solution.py:611
  167.8 2.1 collective-permute-start.32
  173.2 2.0 collective-permute-start.34
  175.3 7.6 %collective-permute-done.31.far = bf16[128,1536]{1,0:T(8,128)(2,1)S(1)} collective-permute-done((bf16[128,1536]{1,0:T(8,128)(2,1)S(1)}, bf16[128,1536]{1,0:T(8,128)(2,1)S(1)}, u32[]{:S(2)}, u32[]{:S(2)}) %collective-permute-start.31) | collective-permute-done | bytes 393248 | tf_op jit(solution)/shard_map/ppermute | solution.py:27
  184.7 21.0 %cross_back.1 = (bf16[128,3072]{1,0:T(8,128)(2,1)}, bf16[256,1536]{1,0:T(8,128)(2,1)}, f32[4,1536]{1,0:T(4,128)}, bf16[128,1536]{1,0:T(8,128)(2,1)}) custom-call(f32[128,1536]{1,0:T(8,128)} %get-tuple-element.245.own, bf16[256,1536]{1,0:T(8,128)(2,1)} %copy-done.23, bf16[128,1536]{1,0:T(8,128)(2,1)} %copy-done.60, ...), custom_call_target="tpu_custom_call" | custom-call | flops 1 | bytes 1 | tf_op jit(solution)/shard_map/cross_back/pallas_call | solution.py:676
  205.7 7.9 %collective-permute-done.33.pair_b = bf16[384,512]{1,0:T(8,128)(2,1)} collective-permute-done((bf16[384,512]{1,0:T(8,128)(2,1)}, bf16[384,512]{1,0:T(8,128)(2,1)}, u32[]{:S(2)}, u32[]{:S(2)}) %collective-permute-start.33) | collective-permute-done | bytes 393248 | tf_op jit(solution)/shard_map/ppermute | solution.py:27
  213.7 1.8 collective-permute-start.42
  218.8 9.3 %collective-permute-done.38.g2.a2 = bf16[128,1536]{1,0:T(8,128)(2,1)S(1)} collective-permute-done((bf16[128,1536]{1,0:T(8,128)(2,1)}, bf16[128,1536]{1,0:T(8,128)(2,1)S(1)}, u32[]{:S(2)}, u32[]{:S(2)}) %collective-permute-start.38) | collective-permute-done | bytes 393248 | tf_op jit(solution)/shard_map/ppermute | solution.py:27
  228.1 6.7 %meet_rows.1 = (bf16[384,1536]{1,0:T(8,128)(2,1)}, bf16[384,1536]{1,0:T(8,128)(2,1)}) custom-call(s32[1]{0:T(128)} %bitcast.14.side, bf16[384,512]{1,0:T(8,128)(2,1)} %get-tuple-element.291.own_a, bf16[384,512]{1,0:T(8,128)(2,1)} %copy-done.52, bf16[384,512]{1,0:T(8,128)(2,1)} %get-tuple-element.293.own_b, bf16[384,512]{1,0:T(8,128)(2,1)} %collective-permute-done.33.pair_b, ...), custom_call_target="tpu_custom_call" | custom-call | flops 1 | bytes 1 | tf_op jit(solution)/shard_map/meet_rows/pallas_call | solution.py:701
  234.8 2.0 collective-permute-start.45
  236.8 7.5 %meet_cols.2 = (bf16[384,1536]{1,0:T(8,128)(2,1)}, bf16[384,1536]{1,0:T(8,128)(2,1)}) custom-call(s32[1]{0:T(128)} %bitcast.14.side, bf16[2,768,128]{2,1,0:T(8,128)(2,1)} %copy-done.11, bf16[2,768,128]{2,1,0:T(8,128)(2,1)} %collective-permute-done.35.p1, bf16[2,768,128]{2,1,0:T(8,128)(2,1)} %copy-done.27, bf16[2,768,128]{2,1,0:T(8,128)(2,1)} %collective-permute-done.36.p3, ...), custom_call_target="tpu_custom_call" | custom-call | flops 1 | bytes 1 | tf_op jit(solution)/shard_map/meet_cols/pallas_call | solution.py:722
  244.3 1.8 collective-permute-start.44
  249.3 16.2 %attend_back.1 = (f32[384,512]{1,0:T(8,128)}, bf16[2,384,512]{2,1,0:T(8,128)(2,1)}, f32[2,384,512]{2,1,0:T(8,128)}, bf16[2,384,512]{2,1,0:T(8,128)(2,1)}, f32[384,1]{1,0:T(8,128)}, /*index=5*/f32[384,1]{1,0:T(8,128)}) custom-call(s32[5]{0:T(128)} %pad_add_fusion.2.span, bf16[384,512]{1,0:T(8,128)(2,1)} %get-tuple-element.193.q, ...), custom_call_target="tpu_custom_call" | custom-call | flops 1 | bytes 1 | tf_op jit(solution)/shard_map/attend_back/pallas_call | solution.py:336
  265.5 4.4 collective-permute-done.46
  275.3 2.2 collective-permute-start.48
  278.9 1.9 fusion.2
  281.7 5.8 %collective-permute-start.52 = (bf16[1,192,1536]{2,1,0:T(8,128)(2,1)}, bf16[1,192,1536]{2,1,0:T(8,128)(2,1)}, u32[]{:S(2)}, u32[]{:S(2)}) collective-permute-start(bf16[1,192,1536]{2,1,0:T(8,128)(2,1)} %constant_dynamic-slice_fusion.22), channel_id=1, source_target_pairs={{0,4},{1,5},{2,6},{3,7},{4,0},{5,1},{6,2},{7,3},{8,12},{9,13},{10,... | collective-permute-start | bytes 1769480 | tf_op jit(solution)/shard_map/ppermute | solution.py:27
  287.5 7.7 %meet_cols.3 = (bf16[384,1536]{1,0:T(8,128)(2,1)}, bf16[384,1536]{1,0:T(8,128)(2,1)}) custom-call(s32[1]{0:T(128)} %bitcast.14.side, bf16[2,768,128]{2,1,0:T(8,128)(2,1)} %copy-done.11, bf16[2,768,128]{2,1,0:T(8,128)(2,1)} %collective-permute-done.35.p1, bf16[2,768,128]{2,1,0:T(8,128)(2,1)} %copy-done.27, bf16[2,768,128]{2,1,0:T(8,128)(2,1)} %collective-permute-done.36.p3, ...), custom_call_target="tpu_custom_call" | custom-call | flops 1 | bytes 1 | tf_op jit(solution)/shard_map/meet_cols/pallas_call | solution.py:722
  295.2 6.5 %down.1 = (bf16[256,1536]{1,0:T(8,128)(2,1)}, f32[128,1536]{1,0:T(8,128)}, bf16[128,1536]{1,0:T(8,128)(2,1)}) custom-call(bf16[512,768]{1,0:T(8,128)(2,1)} %get-tuple-element.299.first, bf16[512,768]{1,0:T(8,128)(2,1)} %get-tuple-element.300.second, bf16[1536,1536]{1,0:T(8,128)(2,1)} %down_w.5), custom_call_target="tpu_custom_call" | custom-call | flops 1 | bytes 1 | tf_op jit(solution)/shard_map/down/pallas_call | solution.py:746
  301.7 1.9 add_convert_fusion.8.kv
  303.8 10.9 %bundle.1 = (bf16[4,192,768]{2,1,0:T(8,128)(2,1)}, bf16[4,192,768]{2,1,0:T(8,128)(2,1)}, bf16[4,192,768]{2,1,0:T(8,128)(2,1)}, bf16[4,192,768]{2,1,0:T(8,128)(2,1)}) custom-call(s32[2]{0:T(128)} %copy-done.76, bf16[2,128,3072]{2,1,0:T(8,128)(2,1)} %copy-done.4, bf16[2,128,3072]{2,1,0:T(8,128)(2,1)} %collective-permute-done.40.f13, ...), custom_call_target="tpu_custom_call" | custom-call | flops 1 | bytes 1 | tf_op jit(solution)/shard_map/bundle/pallas_call | solution.py:807
  315.6 7.5 %tail.1 = (bf16[1152,512]{1,0:T(8,128)(2,1)}, bf16[1024,384]{1,0:T(8,128)(2,1)}, f32[512,384]{1,0:T(8,128)}, bf16[512,384]{1,0:T(8,128)(2,1)}) custom-call(s32[1]{0:T(128)} %bitcast.1.place, f32[384,512]{1,0:T(8,128)} %get-tuple-element.304.dq, f32[2,384,512]{2,1,0:T(8,128)} %get-tuple-element.305.kept, bf16[2,384,512]{2,1,0:T(8,128)(2,1)} %collective-permute-done.47.ahead, ...), custom_call_target="tpu_custom_call" | custom-call | flops 1 | bytes 1 | tf_op jit(solution)/shard_map/tail/pallas_call | solution.py:388
  323.8 17.0 %collective-permute-start.56 = (f32[768,1]{0,1:T(1,128)S(1)}, f32[768,1]{0,1:T(1,128)S(1)}, u32[]{:S(2)}, u32[]{:S(2)}) collective-permute-start(f32[768,1]{0,1:T(1,128)S(1)} %copy-done.82), channel_id=1, source_target_pairs={{0,1},{1,0},{2,3},{3,2},{4,5},{5,4},{6,7},{7,6},{8,9},{9,8},{10,11... | collective-permute-start | bytes 9224 | tf_op jit(solution)/shard_map/ppermute | solution.py:27
  340.9 1.7 add_convert_fusion.2
  344.6 1.6 collective-permute-start.63
  346.4 2.0 collective-permute-start.68
  348.3 15.5 %collective-permute-done.53 = bf16[2,192,1536]{2,1,0:T(8,128)(2,1)} collective-permute-done((bf16[2,192,1536]{2,1,0:T(8,128)(2,1)}, bf16[2,192,1536]{2,1,0:T(8,128)(2,1)}, u32[]{:S(2)}, u32[]{:S(2)}) %collective-permute-start.53) | collective-permute-done | bytes 1179680 | tf_op jit(solution)/shard_map/ppermute | solution.py:27
  363.8 6.1 %collective-permute-done.54 = bf16[4,192,768]{2,1,0:T(8,128)(2,1)S(1)} collective-permute-done((bf16[4,192,768]{2,1,0:T(8,128)(2,1)}, bf16[4,192,768]{2,1,0:T(8,128)(2,1)S(1)}, u32[]{:S(2)}, u32[]{:S(2)}) %collective-permute-start.54) | collective-permute-done | bytes 1179680 | tf_op jit(solution)/shard_map/ppermute | solution.py:27
  373.4 1.7 convert_add_fusion
  375.3 4.8 collective-permute-done.55
  381.3 2.2 add_bitcast_fusion
  385.9 1.8 collective-permute-done.62
  395.8 2.4 multiply_add_fusion
  398.9 21.3 %collective-permute-done.65 = f32[4,6,48]{2,0,1:T(4,128)S(1)} collective-permute-done((f32[4,6,48]{2,0,1:T(4,128)S(1)}, f32[4,6,48]{2,0,1:T(4,128)S(1)}, u32[]{:S(2)}, u32[]{:S(2)}) %collective-permute-start.65) | collective-permute-done | bytes 4640 | tf_op jit(solution)/shard_map/ppermute | solution.py:27
  420.4 3.7 collective-permute-start.74
  425.8 11.6 %collective-permute-done.67 = f32[1,6,48]{2,0,1:T(1,128)S(1)} collective-permute-done((f32[1,6,48]{2,0,1:T(1,128)S(1)}, f32[1,6,48]{2,0,1:T(1,128)S(1)}, u32[]{:S(2)}, u32[]{:S(2)}) %collective-permute-start.67) | collective-permute-done | bytes 1184 | tf_op jit(solution)/shard_map/ppermute | solution.py:27
  437.4 2.6 fusion.33
  440.0 2.5 fusion.1
  443.2 2.9 collective-permute-start.69
  447.6 17.4 %collective-permute-done.75 = bf16[1,192,1536]{2,1,0:T(8,128)(2,1)S(1)} collective-permute-done((bf16[1,192,1536]{2,1,0:T(8,128)(2,1)S(1)}, bf16[1,192,1536]{2,1,0:T(8,128)(2,1)S(1)}, u32[]{:S(2)}, u32[]{:S(2)}) %collective-permute-start.75) | collective-permute-done | bytes 589856 | tf_op jit(solution)/shard_map/ppermute | solution.py:27
  470.3 6.9 %collective-permute-done.69 = bf16[2,192,1152]{2,1,0:T(8,128)(2,1)S(1)} collective-permute-done((bf16[2,192,1152]{2,1,0:T(8,128)(2,1)S(1)}, bf16[2,192,1152]{2,1,0:T(8,128)(2,1)S(1)}, u32[]{:S(2)}, u32[]{:S(2)}) %collective-permute-start.69) | collective-permute-done | bytes 884768 | tf_op jit(solution)/shard_map/ppermute | solution.py:27
  477.8 2.0 collective-permute-done.58
  484.8 2.2 collective-permute-done.59
  487.2 11.1 %collective-permute-done.71 = bf16[1,192,1152]{2,1,0:T(8,128)(2,1)S(1)} collective-permute-done((bf16[1,192,1152]{2,1,0:T(8,128)(2,1)S(1)}, bf16[1,192,1152]{2,1,0:T(8,128)(2,1)S(1)}, u32[]{:S(2)}, u32[]{:S(2)}) %collective-permute-start.71) | collective-permute-done | bytes 442400 | tf_op jit(solution)/shard_map/ppermute | solution.py:27
  499.3 8.3 %collective-permute-done.72 = bf16[2,192,768]{2,1,0:T(8,128)(2,1)S(1)} collective-permute-done((bf16[2,192,768]{2,1,0:T(8,128)(2,1)S(1)}, bf16[2,192,768]{2,1,0:T(8,128)(2,1)S(1)}, u32[]{:S(2)}, u32[]{:S(2)}) %collective-permute-start.72) | collective-permute-done | bytes 589856 | tf_op jit(solution)/shard_map/ppermute | solution.py:27
  509.1 13.2 %collective-permute-done.73 = bf16[1,192,768]{2,1,0:T(8,128)(2,1)S(1)} collective-permute-done((bf16[1,192,768]{2,1,0:T(8,128)(2,1)S(1)}, bf16[1,192,768]{2,1,0:T(8,128)(2,1)S(1)}, u32[]{:S(2)}, u32[]{:S(2)}) %collective-permute-start.73) | collective-permute-done | bytes 294944 | tf_op jit(solution)/shard_map/ppermute | solution.py:27
  (405 shorter events, 91.8 us)
Async XLA Ops:
  0.7 12.5 %collective-permute-start.1 = (bf16[512,384]{1,0:T(8,128)(2,1)}, bf16[512,384]{1,0:T(8,128)(2,1)S(1)}, u32[]{:S(2)}, u32[]{:S(2)}) collective-permute-start(bf16[512,384]{1,0:T(8,128)(2,1)} %x0.1), channel_id=1, source_target_pairs={{0,16},{8,24},{16,0},{24,8},{1,17},{9,25},{17,1},{25,9},{2,18},{10... | collective-permute-start | bytes 1179656 | tf_op jit(solution)/shard_map/ppermute | solution.py:27
  3.7 18.0 %collective-permute-start = (bf16[512,384]{1,0:T(8,128)(2,1)}, bf16[512,384]{1,0:T(8,128)(2,1)S(1)}, u32[]{:S(2)}, u32[]{:S(2)}) collective-permute-start(bf16[512,384]{1,0:T(8,128)(2,1)} %x0.1), channel_id=1, source_target_pairs={{0,8},{8,0},{16,24},{24,16},{1,9},{9,1},{17,25},{25,17},{2,10},{10... | collective-permute-start | bytes 1179656 | tf_op jit(solution)/shard_map/ppermute | solution.py:27
  7.8 11.4 %collective-permute-start.4 = (f32[6,384]{1,0:T(8,128)S(1)}, f32[6,384]{1,0:T(8,128)S(1)}, u32[]{:S(2)}, u32[]{:S(2)}) collective-permute-start(f32[6,384]{1,0:T(8,128)S(1)} %stack.98.g0), channel_id=1, source_target_pairs={{0,16},{8,24},{16,0},{24,8},{1,17},{9,25},{17,1},{25,9},{2,18},{10... | collective-permute-start | bytes 27656 | tf_op jit(solution)/shard_map/ppermute | solution.py:27
  14.3 17.8 %collective-permute-start.6 = (bf16[512,384]{1,0:T(8,128)(2,1)}, bf16[512,384]{1,0:T(8,128)(2,1)S(1)}, u32[]{:S(2)}, u32[]{:S(2)}) collective-permute-start(bf16[512,384]{1,0:T(8,128)(2,1)} %param.43), channel_id=1, source_target_pairs={{0,1},{1,0},{2,3},{3,2},{4,5},{5,4},{6,7},{7,6},{8,9},{9,8},{10,11... | collective-permute-start | bytes 1179656 | tf_op jit(solution)/shard_map/ppermute | solution.py:27
  16.0 53.8 %collective-permute-start.9 = (bf16[1536,384]{1,0:T(8,128)(2,1)}, bf16[1536,384]{1,0:T(8,128)(2,1)}, u32[]{:S(2)}, u32[]{:S(2)}) collective-permute-start(bf16[1536,384]{1,0:T(8,128)(2,1)} %q0.3), channel_id=1, source_target_pairs={{0,16},{8,24},{16,0},{24,8},{1,17},{9,25},{17,1},{25,9},{2,18},{10... | collective-permute-start | bytes 3538952 | tf_op jit(solution)/shard_map/ppermute | solution.py:27
  17.5 52.3 %collective-permute-start.10 = (bf16[384,1536]{1,0:T(8,128)(2,1)}, bf16[384,1536]{1,0:T(8,128)(2,1)}, u32[]{:S(2)}, u32[]{:S(2)}) collective-permute-start(bf16[384,1536]{1,0:T(8,128)(2,1)} %o0.3), channel_id=1, source_target_pairs={{0,16},{8,24},{16,0},{24,8},{1,17},{9,25},{17,1},{25,9},{2,18},{10... | collective-permute-start | bytes 3538952 | tf_op jit(solution)/shard_map/ppermute | solution.py:27
  32.0 21.7 %collective-permute-start.8 = (bf16[2,384,512]{2,1,0:T(8,128)(2,1)}, bf16[2,384,512]{2,1,0:T(8,128)(2,1)S(1)}, u32[]{:S(2)}, u32[]{:S(2)}) collective-permute-start(bf16[2,384,512]{2,1,0:T(8,128)(2,1)} %get-tuple-element.196.kv.kv1), channel_id=1, source_target_pairs={{1,0},{2,1},{3,2},{4,3},{5,4},{6,5},{7,6},{9,8},{10,9},{11,10},{12... | collective-permute-start | bytes 2359304 | tf_op jit(solution)/shard_map/ppermute | solution.py:33
  33.3 36.4 %collective-permute-start.7 = (bf16[2,384,512]{2,1,0:T(8,128)(2,1)}, bf16[2,384,512]{2,1,0:T(8,128)(2,1)}, u32[]{:S(2)}, u32[]{:S(2)}) collective-permute-start(bf16[2,384,512]{2,1,0:T(8,128)(2,1)} %get-tuple-element.196.kv.kv1), channel_id=1, source_target_pairs={{0,1},{1,2},{2,3},{3,4},{4,5},{5,6},{6,7},{8,9},{9,10},{10,11},{11... | collective-permute-start | bytes 2359304 | tf_op jit(solution)/shard_map/ppermute | solution.py:33
  69.8 9.6 %collective-permute-start.12 = (bf16[1536,384]{1,0:T(8,128)(2,1)S(1)}, bf16[1536,384]{1,0:T(8,128)(2,1)}, u32[]{:S(2)}, u32[]{:S(2)}) collective-permute-start(bf16[1536,384]{1,0:T(8,128)(2,1)S(1)} %copy-done.6), channel_id=1, source_target_pairs={{0,8},{8,0},{16,24},{24,16},{1,9},{9,1},{17,25},{25,17},{2,10},{10... | collective-permute-start | bytes 3538952 | tf_op jit(solution)/shard_map/ppermute | solution.py:27
  69.9 9.6 %collective-permute-start.14 = (bf16[384,1536]{1,0:T(8,128)(2,1)S(1)}, bf16[384,1536]{1,0:T(8,128)(2,1)}, u32[]{:S(2)}, u32[]{:S(2)}) collective-permute-start(bf16[384,1536]{1,0:T(8,128)(2,1)S(1)} %copy-done.7), channel_id=1, source_target_pairs={{0,8},{8,0},{16,24},{24,16},{1,9},{9,1},{17,25},{25,17},{2,10},{10... | collective-permute-start | bytes 3538952 | tf_op jit(solution)/shard_map/ppermute | solution.py:27
  70.4 9.1 %collective-permute-start.13 = (bf16[1536,384]{1,0:T(8,128)(2,1)}, bf16[1536,384]{1,0:T(8,128)(2,1)}, u32[]{:S(2)}, u32[]{:S(2)}) collective-permute-start(bf16[1536,384]{1,0:T(8,128)(2,1)} %collective-permute-done.9.q2), channel_id=1, source_target_pairs={{0,8},{8,0},{16,24},{24,16},{1,9},{9,1},{17,25},{25,17},{2,10},{10... | collective-permute-start | bytes 3538952 | tf_op jit(solution)/shard_map/ppermute | solution.py:27
  70.4 9.0 %collective-permute-start.15 = (bf16[384,1536]{1,0:T(8,128)(2,1)}, bf16[384,1536]{1,0:T(8,128)(2,1)}, u32[]{:S(2)}, u32[]{:S(2)}) collective-permute-start(bf16[384,1536]{1,0:T(8,128)(2,1)} %collective-permute-done.10.o2), channel_id=1, source_target_pairs={{0,8},{8,0},{16,24},{24,16},{1,9},{9,1},{17,25},{25,17},{2,10},{10... | collective-permute-start | bytes 3538952 | tf_op jit(solution)/shard_map/ppermute | solution.py:27
  70.9 8.5 %collective-permute-start.11 = (bf16[256,384]{1,0:T(8,128)(2,1)S(1)}, bf16[256,384]{1,0:T(8,128)(2,1)S(1)}, u32[]{:S(2)}, u32[]{:S(2)}) collective-permute-start(bf16[256,384]{1,0:T(8,128)(2,1)S(1)} %copy-done.24), channel_id=1, source_target_pairs={{0,16},{8,24},{16,0},{24,8},{1,17},{9,25},{17,1},{25,9},{2,18},{10... | collective-permute-start | bytes 589832 | tf_op jit(solution)/shard_map/ppermute | solution.py:27
  83.4 11.2 %collective-permute-start.17 = (bf16[128,1536]{1,0:T(8,128)(2,1)S(1)}, bf16[128,1536]{1,0:T(8,128)(2,1)S(1)}, u32[]{:S(2)}, u32[]{:S(2)}) collective-permute-start(bf16[128,1536]{1,0:T(8,128)(2,1)S(1)} %add_convert_fusion.7), channel_id=1, source_target_pairs={{0,16},{8,24},{16,0},{24,8},{1,17},{9,25},{17,1},{25,9},{2,18},{10... | collective-permute-start | bytes 1179656 | tf_op jit(solution)/shard_map/ppermute | solution.py:27
  84.1 30.2 %collective-permute-start.19 = (bf16[768,512]{1,0:T(8,128)(2,1)}, bf16[768,512]{1,0:T(8,128)(2,1)S(1)}, u32[]{:S(2)}, u32[]{:S(2)}) collective-permute-start(bf16[768,512]{1,0:T(8,128)(2,1)} %get-tuple-element.229), channel_id=1, source_target_pairs={{0,1},{1,0},{2,3},{3,2},{4,5},{5,4},{6,7},{7,6},{8,9},{9,8},{10,11... | collective-permute-start | bytes 2359304 | tf_op jit(solution)/shard_map/ppermute | solution.py:27
  94.6 19.7 %collective-permute-start.20 = (bf16[2,512,384]{2,1,0:T(8,128)(2,1)S(1)}, bf16[2,512,384]{2,1,0:T(8,128)(2,1)S(1)}, u32[]{:S(2)}, u32[]{:S(2)}) collective-permute-start(bf16[2,512,384]{2,1,0:T(8,128)(2,1)S(1)} %pad_maximum_fusion.4.g0), channel_id=1, source_target_pairs={{0,16},{8,24},{16,0},{24,8},{1,17},{9,25},{17,1},{25,9},{2,18},{10... | collective-permute-start | bytes 2359304 | tf_op jit(solution)/shard_map/ppermute | solution.py:27
  114.3 11.4 %collective-permute-start.22 = (bf16[128,1536]{1,0:T(8,128)(2,1)}, bf16[128,1536]{1,0:T(8,128)(2,1)S(1)}, u32[]{:S(2)}, u32[]{:S(2)}) collective-permute-start(bf16[128,1536]{1,0:T(8,128)(2,1)} %get-tuple-element.232.n0), channel_id=1, source_target_pairs={{0,16},{8,24},{16,0},{24,8},{1,17},{9,25},{17,1},{25,9},{2,18},{10... | collective-permute-start | bytes 1179656 | tf_op jit(solution)/shard_map/ppermute | solution.py:27
  115.9 17.8 %collective-permute-start.24 = (bf16[2,512,384]{2,1,0:T(8,128)(2,1)S(1)}, bf16[2,512,384]{2,1,0:T(8,128)(2,1)S(1)}, u32[]{:S(2)}, u32[]{:S(2)}) collective-permute-start(bf16[2,512,384]{2,1,0:T(8,128)(2,1)S(1)} %pad_maximum_fusion.4.g0), channel_id=1, source_target_pairs={{0,8},{8,0},{16,24},{24,16},{1,9},{9,1},{17,25},{25,17},{2,10},{10... | collective-permute-start | bytes 2359304 | tf_op jit(solution)/shard_map/ppermute | solution.py:27
  115.9 18.6 %collective-permute-start.25 = (bf16[2,512,384]{2,1,0:T(8,128)(2,1)S(1)}, bf16[2,512,384]{2,1,0:T(8,128)(2,1)S(1)}, u32[]{:S(2)}, u32[]{:S(2)}) collective-permute-start(bf16[2,512,384]{2,1,0:T(8,128)(2,1)S(1)} %collective-permute-done.20.g2), channel_id=1, source_target_pairs={{0,8},{8,0},{16,24},{24,16},{1,9},{9,1},{17,25},{25,17},{2,10},{10... | collective-permute-start | bytes 2359304 | tf_op jit(solution)/shard_map/ppermute | solution.py:27
  125.8 8.0 %collective-permute-start.21 = (bf16[128,1536]{1,0:T(8,128)(2,1)}, bf16[128,1536]{1,0:T(8,128)(2,1)S(1)}, u32[]{:S(2)}, u32[]{:S(2)}) collective-permute-start(bf16[128,1536]{1,0:T(8,128)(2,1)} %get-tuple-element.232.n0), channel_id=1, source_target_pairs={{0,8},{8,0},{16,24},{24,16},{1,9},{9,1},{17,25},{25,17},{2,10},{10... | collective-permute-start | bytes 1179656 | tf_op jit(solution)/shard_map/ppermute | solution.py:27
  128.0 39.7 %collective-permute-start.28 = (bf16[128,3072]{1,0:T(8,128)(2,1)}, bf16[128,3072]{1,0:T(8,128)(2,1)}, u32[]{:S(2)}, u32[]{:S(2)}) collective-permute-start(bf16[128,3072]{1,0:T(8,128)(2,1)} %get-tuple-element.251), channel_id=1, source_target_pairs={{0,16},{8,24},{16,0},{24,8},{1,17},{9,25},{17,1},{25,9},{2,18},{10... | collective-permute-start | bytes 2359304 | tf_op jit(solution)/shard_map/ppermute | solution.py:27
  129.5 21.5 %collective-permute-start.26 = (bf16[768,128]{1,0:T(8,128)(2,1)}, bf16[768,128]{1,0:T(8,128)(2,1)}, u32[]{:S(2)}, u32[]{:S(2)}) collective-permute-start(bf16[768,128]{1,0:T(8,128)(2,1)} %get-tuple-element.243), channel_id=1, source_target_pairs={{0,1},{1,0},{2,3},{3,2},{4,5},{5,4},{6,7},{7,6},{8,9},{9,8},{10,11... | collective-permute-start | bytes 589832 | tf_op jit(solution)/shard_map/ppermute | solution.py:27
  152.1 15.6 %collective-permute-start.27 = (bf16[2,768,128]{2,1,0:T(8,128)(2,1)S(1)}, bf16[2,768,128]{2,1,0:T(8,128)(2,1)S(1)}, u32[]{:S(2)}, u32[]{:S(2)}) collective-permute-start(bf16[2,768,128]{2,1,0:T(8,128)(2,1)S(1)} %pad_maximum_fusion.6.p0), channel_id=1, source_target_pairs={{0,16},{8,24},{16,0},{24,8},{1,17},{9,25},{17,1},{25,9},{2,18},{10... | collective-permute-start | bytes 1179656 | tf_op jit(solution)/shard_map/ppermute | solution.py:27
  152.7 15.0 %collective-permute-start.29 = (bf16[384,512]{1,0:T(8,128)(2,1)}, bf16[384,512]{1,0:T(8,128)(2,1)S(1)}, u32[]{:S(2)}, u32[]{:S(2)}) collective-permute-start(bf16[384,512]{1,0:T(8,128)(2,1)} %get-tuple-element.252), channel_id=1, source_target_pairs={{0,1},{1,0},{2,3},{3,2},{4,5},{5,4},{6,7},{7,6},{8,9},{9,8},{10,11... | collective-permute-start | bytes 1179656 | tf_op jit(solution)/shard_map/ppermute | solution.py:27
  167.8 37.9 %collective-permute-start.32 = (bf16[512,768]{1,0:T(8,128)(2,1)}, bf16[512,768]{1,0:T(8,128)(2,1)}, u32[]{:S(2)}, u32[]{:S(2)}) collective-permute-start(bf16[512,768]{1,0:T(8,128)(2,1)} %get-tuple-element.258.a), channel_id=1, source_target_pairs={{0,1},{1,0},{2,3},{3,2},{4,5},{5,4},{6,7},{7,6},{8,9},{9,8},{10,11... | collective-permute-start | bytes 2359304 | tf_op jit(solution)/shard_map/ppermute | solution.py:27
  171.6 11.2 %collective-permute-start.31 = (bf16[128,1536]{1,0:T(8,128)(2,1)S(1)}, bf16[128,1536]{1,0:T(8,128)(2,1)S(1)}, u32[]{:S(2)}, u32[]{:S(2)}) collective-permute-start(bf16[128,1536]{1,0:T(8,128)(2,1)S(1)} %add_convert_fusion.6), channel_id=1, source_target_pairs={{0,16},{8,24},{16,0},{24,8},{1,17},{9,25},{17,1},{25,9},{2,18},{10... | collective-permute-start | bytes 1179656 | tf_op jit(solution)/shard_map/ppermute | solution.py:27
  173.2 40.4 %collective-permute-start.34 = (bf16[512,768]{1,0:T(8,128)(2,1)}, bf16[512,768]{1,0:T(8,128)(2,1)}, u32[]{:S(2)}, u32[]{:S(2)}) collective-permute-start(bf16[512,768]{1,0:T(8,128)(2,1)} %get-tuple-element.262.b), channel_id=1, source_target_pairs={{0,1},{1,0},{2,3},{3,2},{4,5},{5,4},{6,7},{7,6},{8,9},{9,8},{10,11... | collective-permute-start | bytes 2359304 | tf_op jit(solution)/shard_map/ppermute | solution.py:27
  175.3 38.4 %collective-permute-start.33 = (bf16[384,512]{1,0:T(8,128)(2,1)}, bf16[384,512]{1,0:T(8,128)(2,1)}, u32[]{:S(2)}, u32[]{:S(2)}) collective-permute-start(bf16[384,512]{1,0:T(8,128)(2,1)} %get-tuple-element.261), channel_id=1, source_target_pairs={{0,1},{1,0},{2,3},{3,2},{4,5},{5,4},{6,7},{7,6},{8,9},{9,8},{10,11... | collective-permute-start | bytes 1179656 | tf_op jit(solution)/shard_map/ppermute | solution.py:27
  182.9 30.8 %collective-permute-start.35 = (bf16[2,768,128]{2,1,0:T(8,128)(2,1)S(1)}, bf16[2,768,128]{2,1,0:T(8,128)(2,1)}, u32[]{:S(2)}, u32[]{:S(2)}) collective-permute-start(bf16[2,768,128]{2,1,0:T(8,128)(2,1)S(1)} %pad_maximum_fusion.6.p0), channel_id=1, source_target_pairs={{0,8},{8,0},{16,24},{24,16},{1,9},{9,1},{17,25},{25,17},{2,10},{10... | collective-permute-start | bytes 1179656 | tf_op jit(solution)/shard_map/ppermute | solution.py:27
  182.9 30.8 %collective-permute-start.36 = (bf16[2,768,128]{2,1,0:T(8,128)(2,1)S(1)}, bf16[2,768,128]{2,1,0:T(8,128)(2,1)}, u32[]{:S(2)}, u32[]{:S(2)}) collective-permute-start(bf16[2,768,128]{2,1,0:T(8,128)(2,1)S(1)} %collective-permute-done.27.p2), channel_id=1, source_target_pairs={{0,8},{8,0},{16,24},{24,16},{1,9},{9,1},{17,25},{25,17},{2,10},{10... | collective-permute-start | bytes 1179656 | tf_op jit(solution)/shard_map/ppermute | solution.py:27
  213.6 32.4 %collective-permute-start.40 = (bf16[2,128,3072]{2,1,0:T(8,128)(2,1)S(1)}, bf16[2,128,3072]{2,1,0:T(8,128)(2,1)}, u32[]{:S(2)}, u32[]{:S(2)}) collective-permute-start(bf16[2,128,3072]{2,1,0:T(8,128)(2,1)S(1)} %pad_maximum_fusion.f02), channel_id=1, source_target_pairs={{0,8},{8,0},{16,24},{24,16},{1,9},{9,1},{17,25},{25,17},{2,10},{10... | collective-permute-start | bytes 4718600 | tf_op jit(solution)/shard_map/ppermute | solution.py:27
  213.7 30.6 %collective-permute-start.42 = (bf16[512,768]{1,0:T(8,128)(2,1)}, bf16[512,768]{1,0:T(8,128)(2,1)}, u32[]{:S(2)}, u32[]{:S(2)}) collective-permute-start(bf16[512,768]{1,0:T(8,128)(2,1)} %get-tuple-element.271.a), channel_id=1, source_target_pairs={{0,1},{1,0},{2,3},{3,2},{4,5},{5,4},{6,7},{7,6},{8,9},{9,8},{10,11... | collective-permute-start | bytes 2359304 | tf_op jit(solution)/shard_map/ppermute | solution.py:27
  216.6 11.5 %collective-permute-start.38 = (bf16[128,1536]{1,0:T(8,128)(2,1)}, bf16[128,1536]{1,0:T(8,128)(2,1)S(1)}, u32[]{:S(2)}, u32[]{:S(2)}) collective-permute-start(bf16[128,1536]{1,0:T(8,128)(2,1)} %get-tuple-element.331.g0.a0), channel_id=1, source_target_pairs={{0,16},{8,24},{16,0},{24,8},{1,17},{9,25},{17,1},{25,9},{2,18},{10... | collective-permute-start | bytes 1179656 | tf_op jit(solution)/shard_map/ppermute | solution.py:27
  218.2 16.5 %collective-permute-start.41 = (bf16[512,384]{1,0:T(8,128)(2,1)S(1)}, bf16[512,384]{1,0:T(8,128)(2,1)}, u32[]{:S(2)}, u32[]{:S(2)}) collective-permute-start(bf16[512,384]{1,0:T(8,128)(2,1)S(1)} %pad_maximum_fusion.7), channel_id=1, source_target_pairs={{0,8},{8,0},{16,24},{24,16},{1,9},{9,1},{17,25},{25,17},{2,10},{10... | collective-permute-start | bytes 1179656 | tf_op jit(solution)/shard_map/ppermute | solution.py:27
  218.3 27.7 %collective-permute-start.37 = (bf16[128,1536]{1,0:T(8,128)(2,1)S(1)}, bf16[128,1536]{1,0:T(8,128)(2,1)S(1)}, u32[]{:S(2)}, u32[]{:S(2)}) collective-permute-start(bf16[128,1536]{1,0:T(8,128)(2,1)S(1)} %copy-done.12), channel_id=1, source_target_pairs={{0,8},{8,0},{16,24},{24,16},{1,9},{9,1},{17,25},{25,17},{2,10},{10... | collective-permute-start | bytes 1179656 | tf_op jit(solution)/shard_map/ppermute | solution.py:27
  228.1 18.0 %collective-permute-start.39 = (bf16[128,1536]{1,0:T(8,128)(2,1)S(1)}, bf16[128,1536]{1,0:T(8,128)(2,1)S(1)}, u32[]{:S(2)}, u32[]{:S(2)}) collective-permute-start(bf16[128,1536]{1,0:T(8,128)(2,1)S(1)} %collective-permute-done.38.g2.a2), channel_id=1, source_target_pairs={{0,8},{8,0},{16,24},{24,16},{1,9},{9,1},{17,25},{25,17},{2,10},{10... | collective-permute-start | bytes 1179656 | tf_op jit(solution)/shard_map/ppermute | solution.py:27
  234.8 30.7 %collective-permute-start.45 = (bf16[2,192,1536]{2,1,0:T(8,128)(2,1)}, bf16[2,192,1536]{2,1,0:T(8,128)(2,1)}, u32[]{:S(2)}, u32[]{:S(2)}) collective-permute-start(bf16[2,192,1536]{2,1,0:T(8,128)(2,1)} %bitcast.139), channel_id=1, source_target_pairs={{0,2},{1,3},{2,0},{3,1},{4,6},{5,7},{6,4},{7,5},{8,10},{9,11},{10,... | collective-permute-start | bytes 3538952 | tf_op jit(solution)/shard_map/ppermute | solution.py:27
  244.3 21.2 %collective-permute-start.44 = (bf16[512,768]{1,0:T(8,128)(2,1)}, bf16[512,768]{1,0:T(8,128)(2,1)}, u32[]{:S(2)}, u32[]{:S(2)}) collective-permute-start(bf16[512,768]{1,0:T(8,128)(2,1)} %get-tuple-element.290.b), channel_id=1, source_target_pairs={{0,1},{1,0},{2,3},{3,2},{4,5},{5,4},{6,7},{7,6},{8,9},{9,8},{10,11... | collective-permute-start | bytes 2359304 | tf_op jit(solution)/shard_map/ppermute | solution.py:27
  246.1 23.9 %collective-permute-start.43 = (bf16[128,3072]{1,0:T(8,128)(2,1)}, bf16[128,3072]{1,0:T(8,128)(2,1)S(1)}, u32[]{:S(2)}, u32[]{:S(2)}) collective-permute-start(bf16[128,3072]{1,0:T(8,128)(2,1)} %get-tuple-element.288), channel_id=1, source_target_pairs={{0,16},{8,24},{16,0},{24,8},{1,17},{9,25},{17,1},{25,9},{2,18},{10... | collective-permute-start | bytes 2359304 | tf_op jit(solution)/shard_map/ppermute | solution.py:27
  248.8 21.2 %collective-permute-start.46 = (bf16[256,384]{1,0:T(8,128)(2,1)S(1)}, bf16[256,384]{1,0:T(8,128)(2,1)S(1)}, u32[]{:S(2)}, u32[]{:S(2)}) collective-permute-start(bf16[256,384]{1,0:T(8,128)(2,1)S(1)} %add_convert_fusion.9), channel_id=1, source_target_pairs={{0,16},{8,24},{16,0},{24,8},{1,17},{9,25},{17,1},{25,9},{2,18},{10... | collective-permute-start | bytes 589832 | tf_op jit(solution)/shard_map/ppermute | solution.py:27
  272.3 31.3 %collective-permute-start.50 = (bf16[2,128,3072]{2,1,0:T(8,128)(2,1)S(1)}, bf16[2,128,3072]{2,1,0:T(8,128)(2,1)}, u32[]{:S(2)}, u32[]{:S(2)}) collective-permute-start(bf16[2,128,3072]{2,1,0:T(8,128)(2,1)S(1)} %pad_maximum_fusion.1.b02), channel_id=1, source_target_pairs={{0,8},{8,0},{16,24},{24,16},{1,9},{9,1},{17,25},{25,17},{2,10},{10... | collective-permute-start | bytes 4718600 | tf_op jit(solution)/shard_map/ppermute | solution.py:27
  272.4 42.3 %collective-permute-start.49 = (bf16[2,192,1536]{2,1,0:T(8,128)(2,1)}, bf16[2,192,1536]{2,1,0:T(8,128)(2,1)}, u32[]{:S(2)}, u32[]{:S(2)}) collective-permute-start(bf16[2,192,1536]{2,1,0:T(8,128)(2,1)} %bitcast.17), channel_id=1, source_target_pairs={{0,2},{1,3},{2,0},{3,1},{4,6},{5,7},{6,4},{7,5},{8,10},{9,11},{10,... | collective-permute-start | bytes 3538952 | tf_op jit(solution)/shard_map/ppermute | solution.py:27
  275.3 39.4 %collective-permute-start.48 = (bf16[2,384,512]{2,1,0:T(8,128)(2,1)}, bf16[2,384,512]{2,1,0:T(8,128)(2,1)S(1)}, u32[]{:S(2)}, u32[]{:S(2)}) collective-permute-start(bf16[2,384,512]{2,1,0:T(8,128)(2,1)} %get-tuple-element.306), channel_id=1, source_target_pairs={{0,1},{1,2},{2,3},{3,4},{4,5},{5,6},{6,7},{8,9},{9,10},{10,11},{11... | collective-permute-start | bytes 2359304 | tf_op jit(solution)/shard_map/ppermute | solution.py:33
  277.6 37.1 %collective-permute-start.47 = (bf16[2,384,512]{2,1,0:T(8,128)(2,1)}, bf16[2,384,512]{2,1,0:T(8,128)(2,1)}, u32[]{:S(2)}, u32[]{:S(2)}) collective-permute-start(bf16[2,384,512]{2,1,0:T(8,128)(2,1)} %get-tuple-element.298), channel_id=1, source_target_pairs={{1,0},{2,1},{3,2},{4,3},{5,4},{6,5},{7,6},{9,8},{10,9},{11,10},{12... | collective-permute-start | bytes 2359304 | tf_op jit(solution)/shard_map/ppermute | solution.py:33
  281.7 64.7 %collective-permute-start.52 = (bf16[1,192,1536]{2,1,0:T(8,128)(2,1)}, bf16[1,192,1536]{2,1,0:T(8,128)(2,1)}, u32[]{:S(2)}, u32[]{:S(2)}) collective-permute-start(bf16[1,192,1536]{2,1,0:T(8,128)(2,1)} %constant_dynamic-slice_fusion.22), channel_id=1, source_target_pairs={{0,4},{1,5},{2,6},{3,7},{4,0},{5,1},{6,2},{7,3},{8,12},{9,13},{10,... | collective-permute-start | bytes 1769480 | tf_op jit(solution)/shard_map/ppermute | solution.py:27
  303.5 60.3 %collective-permute-start.53 = (bf16[2,192,1536]{2,1,0:T(8,128)(2,1)}, bf16[2,192,1536]{2,1,0:T(8,128)(2,1)}, u32[]{:S(2)}, u32[]{:S(2)}) collective-permute-start(bf16[2,192,1536]{2,1,0:T(8,128)(2,1)} %bitcast.138), channel_id=1, source_target_pairs={{0,2},{1,3},{2,0},{3,1},{4,6},{5,7},{6,4},{7,5},{8,10},{9,11},{10,... | collective-permute-start | bytes 3538952 | tf_op jit(solution)/shard_map/ppermute | solution.py:27
  323.8 51.3 %collective-permute-start.56 = (f32[768,1]{0,1:T(1,128)S(1)}, f32[768,1]{0,1:T(1,128)S(1)}, u32[]{:S(2)}, u32[]{:S(2)}) collective-permute-start(f32[768,1]{0,1:T(1,128)S(1)} %copy-done.82), channel_id=1, source_target_pairs={{0,1},{1,0},{2,3},{3,2},{4,5},{5,4},{6,7},{7,6},{8,9},{9,8},{10,11... | collective-permute-start | bytes 9224 | tf_op jit(solution)/shard_map/ppermute | solution.py:27
  340.8 29.0 %collective-permute-start.54 = (bf16[4,192,768]{2,1,0:T(8,128)(2,1)}, bf16[4,192,768]{2,1,0:T(8,128)(2,1)S(1)}, u32[]{:S(2)}, u32[]{:S(2)}) collective-permute-start(bf16[4,192,768]{2,1,0:T(8,128)(2,1)} %get-tuple-element.322), channel_id=1, source_target_pairs={{0,1},{1,0},{2,3},{3,2},{4,5},{5,4},{6,7},{7,6},{8,9},{9,8},{10,11... | collective-permute-start | bytes 3538952 | tf_op jit(solution)/shard_map/ppermute | solution.py:27
  344.6 43.1 %collective-permute-start.63 = (bf16[1,192,1536]{2,1,0:T(8,128)(2,1)S(1)}, bf16[1,192,1536]{2,1,0:T(8,128)(2,1)S(1)}, u32[]{:S(2)}, u32[]{:S(2)}) collective-permute-start(bf16[1,192,1536]{2,1,0:T(8,128)(2,1)S(1)} %constant_dynamic-slice_fusion.12), channel_id=1, source_target_pairs={{0,4},{1,5},{2,6},{3,7},{4,0},{5,1},{6,2},{7,3},{8,12},{9,13},{10,... | collective-permute-start | bytes 1769480 | tf_op jit(solution)/shard_map/ppermute | solution.py:27
  346.4 91.0 %collective-permute-start.68 = (bf16[1152,512]{1,0:T(8,128)(2,1)}, bf16[1152,512]{1,0:T(8,128)(2,1)}, u32[]{:S(2)}, u32[]{:S(2)}) collective-permute-start(bf16[1152,512]{1,0:T(8,128)(2,1)} %get-tuple-element.347), channel_id=1, source_target_pairs={{0,1},{1,0},{2,3},{3,2},{4,5},{5,4},{6,7},{7,6},{8,9},{9,8},{10,11... | collective-permute-start | bytes 3538952 | tf_op jit(solution)/shard_map/ppermute | solution.py:27
  369.9 10.2 %collective-permute-start.55 = (bf16[512,384]{1,0:T(8,128)(2,1)S(1)}, bf16[512,384]{1,0:T(8,128)(2,1)S(1)}, u32[]{:S(2)}, u32[]{:S(2)}) collective-permute-start(bf16[512,384]{1,0:T(8,128)(2,1)S(1)} %add_convert_fusion.5), channel_id=1, source_target_pairs={{0,16},{8,24},{16,0},{24,8},{1,17},{9,25},{17,1},{25,9},{2,18},{10... | collective-permute-start | bytes 1179656 | tf_op jit(solution)/shard_map/ppermute | solution.py:27
  371.8 15.9 %collective-permute-start.64 = (bf16[2,192,768]{2,1,0:T(8,128)(2,1)S(1)}, bf16[2,192,768]{2,1,0:T(8,128)(2,1)S(1)}, u32[]{:S(2)}, u32[]{:S(2)}) collective-permute-start(bf16[2,192,768]{2,1,0:T(8,128)(2,1)S(1)} %dynamic-slice_bitcast_fusion.2), channel_id=1, source_target_pairs={{0,2},{1,3},{2,0},{3,1},{4,6},{5,7},{6,4},{7,5},{8,10},{9,11},{10,... | collective-permute-start | bytes 1769480 | tf_op jit(solution)/shard_map/ppermute | solution.py:27
  375.1 95.2 %collective-permute-start.70 = (bf16[4,192,768]{2,1,0:T(8,128)(2,1)}, bf16[4,192,768]{2,1,0:T(8,128)(2,1)}, u32[]{:S(2)}, u32[]{:S(2)}) collective-permute-start(bf16[4,192,768]{2,1,0:T(8,128)(2,1)} %get-tuple-element.355), channel_id=1, source_target_pairs={{0,1},{1,0},{2,3},{3,2},{4,5},{5,4},{6,7},{7,6},{8,9},{9,8},{10,11... | collective-permute-start | bytes 3538952 | tf_op jit(solution)/shard_map/ppermute | solution.py:27
  387.6 80.0 %collective-permute-start.57 = (bf16[256,1536]{1,0:T(8,128)(2,1)}, bf16[256,1536]{1,0:T(8,128)(2,1)}, u32[]{:S(2)}, u32[]{:S(2)}) collective-permute-start(bf16[256,1536]{1,0:T(8,128)(2,1)} %get-tuple-element.328), channel_id=1, source_target_pairs={{0,8},{8,0},{16,24},{24,16},{1,9},{9,1},{17,25},{25,17},{2,10},{10... | collective-permute-start | bytes 2359304 | tf_op jit(solution)/shard_map/ppermute | solution.py:27
  398.2 22.0 %collective-permute-start.65 = (f32[4,6,48]{2,0,1:T(4,128)S(1)}, f32[4,6,48]{2,0,1:T(4,128)S(1)}, u32[]{:S(2)}, u32[]{:S(2)}) collective-permute-start(f32[4,6,48]{2,0,1:T(4,128)S(1)} %bitcast.132), channel_id=1, source_target_pairs={{0,1},{1,0},{2,3},{3,2},{4,5},{5,4},{6,7},{7,6},{8,9},{9,8},{10,11... | collective-permute-start | bytes 13832 | tf_op jit(solution)/shard_map/ppermute | solution.py:27
  420.4 25.7 %collective-permute-start.74 = (bf16[1,192,768]{2,1,0:T(8,128)(2,1)S(1)}, bf16[1,192,768]{2,1,0:T(8,128)(2,1)S(1)}, u32[]{:S(2)}, u32[]{:S(2)}) collective-permute-start(bf16[1,192,768]{2,1,0:T(8,128)(2,1)S(1)} %constant_dynamic-slice_fusion.1), channel_id=1, source_target_pairs={{0,4},{1,5},{2,6},{3,7},{4,0},{5,1},{6,2},{7,3},{8,12},{9,13},{10,... | collective-permute-start | bytes 884744 | tf_op jit(solution)/shard_map/ppermute | solution.py:27
  424.1 13.2 %collective-permute-start.67 = (f32[1,6,48]{2,0,1:T(1,128)S(1)}, f32[1,6,48]{2,0,1:T(1,128)S(1)}, u32[]{:S(2)}, u32[]{:S(2)}) collective-permute-start(f32[1,6,48]{2,0,1:T(1,128)S(1)} %constant_dynamic-slice_fusion.5), channel_id=1, source_target_pairs={{0,4},{1,5},{2,6},{3,7},{4,0},{5,1},{6,2},{7,3},{8,12},{9,13},{10,... | collective-permute-start | bytes 3464 | tf_op jit(solution)/shard_map/ppermute | solution.py:27
  437.3 27.7 %collective-permute-start.75 = (bf16[1,192,1536]{2,1,0:T(8,128)(2,1)S(1)}, bf16[1,192,1536]{2,1,0:T(8,128)(2,1)S(1)}, u32[]{:S(2)}, u32[]{:S(2)}) collective-permute-start(bf16[1,192,1536]{2,1,0:T(8,128)(2,1)S(1)} %constant_dynamic-slice_fusion), channel_id=1, source_target_pairs={{0,4},{1,5},{2,6},{3,7},{4,0},{5,1},{6,2},{7,3},{8,12},{9,13},{10,... | collective-permute-start | bytes 1769480 | tf_op jit(solution)/shard_map/ppermute | solution.py:27
  443.2 34.1 %collective-permute-start.69 = (bf16[2,192,1152]{2,1,0:T(8,128)(2,1)S(1)}, bf16[2,192,1152]{2,1,0:T(8,128)(2,1)S(1)}, u32[]{:S(2)}, u32[]{:S(2)}) collective-permute-start(bf16[2,192,1152]{2,1,0:T(8,128)(2,1)S(1)} %dynamic-slice_bitcast_fusion), channel_id=1, source_target_pairs={{0,2},{1,3},{2,0},{3,1},{4,6},{5,7},{6,4},{7,5},{8,10},{9,11},{10,... | collective-permute-start | bytes 2654216 | tf_op jit(solution)/shard_map/ppermute | solution.py:27
  468.7 11.0 %collective-permute-start.58 = (bf16[128,1536]{1,0:T(8,128)(2,1)S(1)}, bf16[128,1536]{1,0:T(8,128)(2,1)S(1)}, u32[]{:S(2)}, u32[]{:S(2)}) collective-permute-start(bf16[128,1536]{1,0:T(8,128)(2,1)S(1)} %add_convert_fusion.4), channel_id=1, source_target_pairs={{0,16},{8,24},{16,0},{24,8},{1,17},{9,25},{17,1},{25,9},{2,18},{10... | collective-permute-start | bytes 1179656 | tf_op jit(solution)/shard_map/ppermute | solution.py:27
  477.5 20.8 %collective-permute-start.71 = (bf16[1,192,1152]{2,1,0:T(8,128)(2,1)S(1)}, bf16[1,192,1152]{2,1,0:T(8,128)(2,1)S(1)}, u32[]{:S(2)}, u32[]{:S(2)}) collective-permute-start(bf16[1,192,1152]{2,1,0:T(8,128)(2,1)S(1)} %constant_dynamic-slice_fusion.3), channel_id=1, source_target_pairs={{0,4},{1,5},{2,6},{3,7},{4,0},{5,1},{6,2},{7,3},{8,12},{9,13},{10,... | collective-permute-start | bytes 1327112 | tf_op jit(solution)/shard_map/ppermute | solution.py:27
  484.3 23.4 %collective-permute-start.72 = (bf16[2,192,768]{2,1,0:T(8,128)(2,1)S(1)}, bf16[2,192,768]{2,1,0:T(8,128)(2,1)S(1)}, u32[]{:S(2)}, u32[]{:S(2)}) collective-permute-start(bf16[2,192,768]{2,1,0:T(8,128)(2,1)S(1)} %dynamic-slice_bitcast_fusion.1), channel_id=1, source_target_pairs={{0,2},{1,3},{2,0},{3,1},{4,6},{5,7},{6,4},{7,5},{8,10},{9,11},{10,... | collective-permute-start | bytes 1769480 | tf_op jit(solution)/shard_map/ppermute | solution.py:27
  487.1 12.2 %collective-permute-start.60 = (bf16[256,384]{1,0:T(8,128)(2,1)S(1)}, bf16[256,384]{1,0:T(8,128)(2,1)S(1)}, u32[]{:S(2)}, u32[]{:S(2)}) collective-permute-start(bf16[256,384]{1,0:T(8,128)(2,1)S(1)} %pad_maximum_fusion.13), channel_id=1, source_target_pairs={{0,8},{8,0},{16,24},{24,16},{1,9},{9,1},{17,25},{25,17},{2,10},{10... | collective-permute-start | bytes 589832 | tf_op jit(solution)/shard_map/ppermute | solution.py:27
  507.9 14.5 %collective-permute-start.73 = (bf16[1,192,768]{2,1,0:T(8,128)(2,1)S(1)}, bf16[1,192,768]{2,1,0:T(8,128)(2,1)S(1)}, u32[]{:S(2)}, u32[]{:S(2)}) collective-permute-start(bf16[1,192,768]{2,1,0:T(8,128)(2,1)S(1)} %constant_dynamic-slice_fusion.2), channel_id=1, source_target_pairs={{0,4},{1,5},{2,6},{3,7},{4,0},{5,1},{6,2},{7,3},{8,12},{9,13},{10,... | collective-permute-start | bytes 884744 | tf_op jit(solution)/shard_map/ppermute | solution.py:27
  (96 other events, 942.3 us)

commit v2 on v1

--- a/solution.py
+++ b/solution.py
@@ -752,7 +752,7 @@
 
 
 def bundle_body(devices, place, f02, f13, b02, b13, a0, a1, a2, a3, attended,
-                context, kv, keep_a, send_a, keep_b, send_b):
+                context, kv, times, keep_a, send_a, keep_b, send_b):
     width = a0.shape[1]
     part, share = width // 4, a0.shape[0]
 
@@ -786,6 +786,9 @@
                 out[0][d // 2, at, cols] = odd
                 out[1][d // 2, at, cols] = even
 
+    send_a[:, rows:, :] = jnp.zeros((devices // 2, send_a.shape[1] - rows, half), BF16)
+    row = jnp.broadcast_to(times[...], (times.shape[0], 2 * HEAD_SIZE)).T[:1, :]
+    send_a[0, rows : rows + 1, :] = row.astype(BF16)
     put(dot_tn(full(fronts), own(backs)), 0, 0, (keep_a, send_a))
     count = context.shape[0]
     put(dot_tn(context[...], kv[:count, :]), 0, part, (keep_a, send_a))
@@ -801,16 +804,19 @@
     put(grads[:, half:], 3 * small, 0, (keep_b, send_b))
 
 
-def bundle_grads(devices, place, fronts, backs, ones, attended, context, kv):
+def bundle_grads(devices, place, fronts, backs, ones, attended, context, kv, times):
     width = ones[0].shape[1]
     vmem = pl.BlockSpec(memory_space=pltpu.VMEM)
     return pl.pallas_call(
         functools.partial(bundle_body, devices),
-        in_specs=[pl.BlockSpec(memory_space=pltpu.SMEM)] + [vmem] * 11,
+        in_specs=[pl.BlockSpec(memory_space=pltpu.SMEM)] + [vmem] * 12,
         out_specs=[vmem] * 4,
-        out_shape=[jax.ShapeDtypeStruct((devices // 2, width // devices, width // 2), BF16)] * 4,
+        out_shape=[
+            jax.ShapeDtypeStruct((devices // 2, width // devices + more, width // 2), BF16)
+            for more in (0, 16, 0, 0)
+        ],
         name="bundle", cost_estimate=FREE,
-    )(place, *fronts, *backs, *ones, attended, context, kv)
+    )(place, *fronts, *backs, *ones, attended, context, kv, times)
 
 
 def front_body(width_block, place, x0, x1, x2, x3, g0, g1, g2, g3, cosine, sine, wq, wk, wv,
@@ -1014,8 +1020,8 @@
         three_away, three_low, flip_far, front_far, hidden_got_a
     )
     three_got, _, three_far = scatter_near(three_away, three_low)
-    hidden_late, lifted_late = after((hidden_away_b, lifted_a), three_low)
-    hidden_got_b, lifted_got_a = swap(hidden_late, "seq", 1), swap(lifted_late, "seq", 1)
+    hidden_got_b = swap(after(hidden_away_b, three_low), "seq", 1)
+    lifted_got_a = swap(after(lifted_a, three_far), "seq", 1)
     flip_late, flip_far_late, gate_late = after((flip_both, flip_far, gate_b), three_far)
     flip_mate, flip_far_mate = swap(flip_late, "tensor", 1), swap(flip_far_late, "tensor", 1)
     gate_got_b = swap(gate_late, "seq", 1)
@@ -1024,8 +1030,8 @@
         three_own, three_got, three_far, grad_near, residual_one, residual_two, norms,
         query_parts, kv_parts, out_parts, cross_queries,
     )
-    grad_one, gate_got_a, hidden_got_b, lifted_got_a, flip_mate, flip_far_mate = meeting(
-        grad_one, gate_got_a, hidden_got_b, lifted_got_a, flip_mate, flip_far_mate
+    grad_one, gate_got_a, hidden_got_b, flip_mate, flip_far_mate = meeting(
+        grad_one, gate_got_a, hidden_got_b, flip_mate, flip_far_mate
     )
     count = lax.axis_size("seq")
     level_side = ((lax.axis_index("seq") >> 1) % 2).astype(jnp.int32).reshape(1)
@@ -1041,21 +1047,20 @@
             (grad_near, grad_pair),
         )
     )
-    flip_near = (flip_both, flip_mate, flip_far, flip_far_mate)
-    first_keep, first_got = traded(
-        meet_cols(rows, level_side, flip_near, (gate_a, gate_got_a, lifted_a, lifted_got_a))
-    )
     context_parts = quarters(kv_grad, 1)
     context_got = swap(jnp.concatenate([context_parts[1], context_parts[3]], 0), "tensor", 1)
-    *one_parts, front_other, context_got, gate_got_b = meeting(
-        *gather_near(grad_one), swap(after(front_both, grad_one), "tensor", 1), context_got,
-        gate_got_b,
+    one_far_rows, down_keep = meeting(swap(grad_one, "tensor", 2), down_keep)
+    one_parts = (
+        grad_one, swap(grad_one, "tensor", 1), one_far_rows, swap(one_far_rows, "tensor", 1)
+    )
+    *one_parts, front_other, context_got, gate_got_b, lifted_got_a = meeting(
+        *one_parts, swap(after(front_both, grad_one), "tensor", 1), context_got,
+        gate_got_b, lifted_got_a,
     )
     context_low = (
         context_parts[2].astype(F32) + context_got[context_parts[2].shape[0] :].astype(F32)
     ).astype(BF16)
     context_far = swap(context_low, "tensor", 2)
-    *one_parts, first_keep = meeting(*one_parts, first_keep)
     back_far = swap(after(back_rows, one_parts[3]), "tensor", 2)
     lifted_got_b = swap(after(lifted_b, grad_one), "seq", 1)
     query_grad, to_prev, kept, to_next, time_key_grad, time_value_grad = attend_back(
@@ -1067,6 +1072,10 @@
     )
     from_next, from_prev = shift(to_prev, "seq", -1), shift(to_next, "seq", 1)
     down_keep, down_got = halve(added(down_keep, down_got).astype(BF16), 2)
+    flip_near = (flip_both, flip_mate, flip_far, flip_far_mate)
+    first_keep, first_got = traded(
+        meet_cols(rows, level_side, flip_near, after((gate_a, gate_got_a, lifted_a, lifted_got_a), to_prev))
+    )
     second_keep, second_got = traded(
         meet_cols(
             rows, level_side, flip_near, (gate_b, gate_got_b, lifted_b, lifted_got_b)
@@ -1080,13 +1089,14 @@
         + context_got[: context_far.shape[0]].astype(F32)
         + context_far.astype(F32)
     )
+    time_both = jnp.concatenate([time_key_grad, time_value_grad], 0)
     keep_a, send_a, keep_b, send_b = bundle_grads(
         count, places, (front_both, front_other), (back_both, back_other), one_parts, attended,
         row_context,
-        context_own.astype(BF16),
-    )
-    from_next, from_prev, first_got, send_a, send_b = meeting(
-        from_next, from_prev, first_got, send_a, send_b
+        context_own.astype(BF16), time_both,
+    )
+    from_next, from_prev, down_got, send_a, send_b = meeting(
+        from_next, from_prev, down_got, send_a, send_b
     )
     got_a = swap(send_a, "seq", 1)
     raw, last_away, last_own, last_low = tail(
@@ -1097,13 +1107,10 @@
     last_sum = (
         last_low.astype(F32) + last_got[local_rows:].astype(F32)
     ).astype(BF16)
-    last_sum, down_got, second_got, got_a = meeting(last_sum, down_got, second_got, got_a)
+    last_sum, first_got, second_got = meeting(last_sum, first_got, second_got)
     first_keep, first_got = halve(added(first_keep, first_got).astype(BF16), 2)
-    got_b = swap(after(send_b, got_a), "seq", 1)
-    left_keep, left_got = halve(added(keep_a, got_a).astype(BF16), 1)
+    second_keep, second_got = halve(added(second_keep, second_got).astype(BF16), 2)
     last_far = swap(last_sum, "tensor", 2)
-    time_both = jnp.concatenate([time_key_grad, time_value_grad], 0)
-    last_far, time_got = meeting(last_far, swap(after(time_both, last_low), "seq", 1))
     frame_grad = last_own + last_got[:local_rows].astype(F32) + last_far.astype(F32)
 
     def to_frames(rows, weight):
@@ -1125,8 +1132,10 @@
     )[None]
     sums = sums + swap(sums, "tensor", 1)
     sums = sums + swap(sums, "tensor", 2)
-    sums, first_got, left_got = meeting(sums, first_got, left_got)
-    left_keep, left_got = halve(added(left_keep, left_got).astype(BF16), 2)
+    sums, got_a, raw_got = meeting(sums, got_a, raw_got)
+    got_b = swap(after(send_b, got_a), "seq", 1)
+    time_both = time_both + got_a[0, rows, :, None].astype(F32)
+    left_keep, left_got = halve(added(keep_a, got_a[:, :rows]).astype(BF16), 1)
     plain = sums[0, :local_rows, None] / model_width
     cross = sums[0, local_rows : 2 * local_rows, None] / model_width
     vectors = own_cols(sums[0, 2 * local_rows :].reshape(5, model_width))
@@ -1136,17 +1145,6 @@
     )
     d_gain_attn = jnp.sum(frame_grad * own_scaled, 0) + vectors[0] * own_cols(scaled_time)[0]
     d_bias_attn = jnp.sum(frame_grad, 0) + vectors[0]
-    small = jnp.stack(
-        [d_gain_attn, d_bias_attn, vectors[3], vectors[4], vectors[1], vectors[2]]
-    ).reshape(6, devices, -1).transpose(1, 0, 2)
-    small = added(*halve(small, 0))
-    small = added(*halve(small, 1))
-    bit = 2
-    while small.shape[0] > 1:
-        small = added(*halve(small, bit))
-        bit += 1
-    small, raw_got = meeting(small[0], raw_got)
-
     down_away, down_low = after((down_away, down_low), last_far)
     branch_got, _, branch_far = scatter_near(down_away, down_low)
     block_rows = (
@@ -1165,12 +1163,11 @@
 
     normed_pair = (one_own_half, normed_got)
     grad_down = halve_end(down_keep, down_got, 3)
-    first, second = halve_end(first_keep, first_got, 3), halve_all(after(added(second_keep, second_got), sums), 2)
+    first, second = halve_end(first_keep, first_got, 3), halve_end(second_keep, second_got, 3)
     units = first.shape[1] // 2
     grad_gate_w = jnp.concatenate([first[:, :units], second[:, :units]], 1)
     grad_up_w = jnp.concatenate([first[:, units:], second[:, units:]], 1)
     raw_pair = (raw, raw_got)
-    time_both = time_both + time_got
     own_time_rows = lax.dynamic_index_in_dim(
         time_column.reshape(count // 2, 2, -1), column, 1, False
     ).reshape(-1, 1)
@@ -1183,8 +1180,18 @@
         (blocks + outer).astype(BF16).reshape(count // 2, rows, 3 * head_cols), 1
     )
     heads_got, got_b = meeting(heads_got, got_b)
-    heads_sum = halve_end(heads_keep, heads_got, 2)
-    left, right = halve_end(left_keep, left_got, 3), halve_end(keep_b, got_b, 1)
+    heads_next = added(heads_keep, heads_got).astype(BF16)
+    heads_sum = halve_all(heads_next, 2)
+    small = jnp.stack(
+        [d_gain_attn, d_bias_attn, vectors[3], vectors[4], vectors[1], vectors[2]]
+    ).reshape(6, devices, -1).transpose(1, 0, 2)
+    small = after(small, heads_next)
+    bit = 0
+    while small.shape[0] > 1:
+        small = added(*halve(small, bit))
+        bit += 1
+    small = small[0]
+    left, right = halve_end(left_keep, left_got, 2), halve_end(keep_b, got_b, 1)
     part, rows = head_cols // count, model_width // count
     grad_c_query = left[:, :head_cols]
     grad_c_key, grad_c_value = left[: rows // 2, head_cols:], left[rows // 2 :, head_cols:]

time: 534 us -> 532 us (level)
  starting transfers between devices: 94.7 us -> 76.7 us
  local copies, waits for them, and re-layouts: 31.1 us -> 39 us
    ppermute x72 -> x71, starting transfers between devices: 84.4 us -> 65.6 us  [swap(): lax.ppermute(value, axis, [(i, i ^ by) for i in range(lax.axis_size(axis))])]
    ppermute x72 -> x71, waiting for transfers between devices: 176 us -> 180 us  [swap(): lax.ppermute(value, axis, [(i, i ^ by) for i in range(lax.axis_size(axis))])]
  transfers between devices with their start and end apart: 76 -> 75, of which waited for: 28 -> 31; matrix products, arithmetic and copies ran while one was open for 12% -> 13% of each run, Pallas kernels for 30% -> 31%
where the time goes in v2:
time: 532 us; the launch traced here: 521 us
  waiting for transfers between devices  198 us (37%)
  Pallas kernels  160 us (30%)
  starting transfers between devices  76.7 us (14%)
  other arithmetic  39.6 us (7%)
  local copies, waits for them, and re-layouts  39 us (7%)
    ppermute x71, waiting for transfers between devices, swap(): lax.ppermute(value, axis, [(i, i ^ by) for i in range(lax.axis_size(axis))])  180 us
    ppermute x71, starting transfers between devices, swap(): lax.ppermute(value, axis, [(i, i ^ by) for i in range(lax.axis_size(axis))])  65.6 us
    pallas_call x2, Pallas kernels, ffn(): pl.pallas_call(functools.partial(ffn_second_body if half else ffn_first_b...  29.7 us
    pallas_call x1, Pallas kernels, cross_backward(): pl.pallas_call(cross_backward_body, grid=(1,), out_shape=[jax.ShapeDtypeS...  21 us
    ppermute x4, waiting for transfers between devices, shift(): return lax.ppermute(value, axis, pairs)  17.9 us
    pallas_call x1, Pallas kernels, attend_back(): pl.pallas_call(backward_body, in_specs=[pl.BlockSpec(memory_space=pltpu.S...  17.7 us
    pallas_call x1, Pallas kernels, cross_forward(): pl.pallas_call(functools.partial(cross_forward_body, width // devices), g...  16.5 us
    pallas_call x2, Pallas kernels, meet_cols(): pl.pallas_call(functools.partial(meet_cols_body, size), in_specs=[pl.Bloc...  15.4 us
  transfers between devices with their start and end apart: 75, of which 31 were waited for; matrix products, arithmetic and copies ran while one was open for 13% of the time, Pallas kernels for 31%

profile of v2, /device:TPU:0, one launch (start us, length us, event | category | flops | bytes accessed | tf_op | source)
XLA Modules:
  0.0 521.2 jit_solution(4890862268686535268)
XLA Ops:
  0.7 3.0 collective-permute-start.1
  11.4 1.8 collective-permute-done.1.x2
  14.3 1.7 collective-permute-start.6
  22.4 9.6 %front.1 = (bf16[384,512]{1,0:T(8,128)(2,1)}, bf16[2,384,512]{2,1,0:T(8,128)(2,1)}, bf16[128,1536]{1,0:T(8,128)(2,1)}, bf16[512,1536]{1,0:T(8,128)(2,1)}, bf16[7...) custom-call(s32[2]{0:T(128)} %rev.4.place, ...), custom_call_target="tpu_custom_call" | custom-call | flops 1 | bytes 1 | tf_op jit(solution)/shard_map/front/pallas_call | solution.py:878
  33.3 5.5 %collective-permute-start.7 = (bf16[2,384,512]{2,1,0:T(8,128)(2,1)}, bf16[2,384,512]{2,1,0:T(8,128)(2,1)}, u32[]{:S(2)}, u32[]{:S(2)}) collective-permute-start(bf16[2,384,512]{2,1,0:T(8,128)(2,1)} %get-tuple-element.191.kv.kv1), channel_id=1, source_target_pairs={{0,1},{1,2},{2,3},{3,4},{4,5},{5,6},{6,7},{8,9},{9,10},{10,11},{11... | collective-permute-start | bytes 2359304 | tf_op jit(solution)/shard_map/ppermute | solution.py:33
  41.5 10.4 %attend_near.1 = (f32[6,512]{1,0:T(8,128)}, f32[6,512]{1,0:T(8,128)}, f32[384,512]{1,0:T(8,128)}) custom-call(s32[5]{0:T(128)} %pad_add_fusion.2.span, bf16[384,512]{1,0:T(8,128)(2,1)} %get-tuple-element.188.q, bf16[2,384,512]{2,1,0:T(8,128)(2,1)} %get-tuple-element.191.kv.kv1, f32[384,1]{1,0:T(8,128)} %get-tuple-element.194.tk, ...), custom_call_target="tpu_custom_call" | custom-call | flops 1 | bytes 1 | tf_op jit(solution)/shard_map/attend_near/pallas_call | solution.py:301
  51.8 1.9 collective-permute-done.8.kv2
  53.7 16.0 %collective-permute-done.7.kv0 = bf16[2,384,512]{2,1,0:T(8,128)(2,1)} collective-permute-done((bf16[2,384,512]{2,1,0:T(8,128)(2,1)}, bf16[2,384,512]{2,1,0:T(8,128)(2,1)}, u32[]{:S(2)}, u32[]{:S(2)}) %collective-permute-start.7) | collective-permute-done | bytes 786464 | tf_op jit(solution)/shard_map/ppermute | solution.py:33
  72.4 8.7 %attend_far.1 = (bf16[384,512]{1,0:T(8,128)(2,1)}, f32[6,512]{1,0:T(8,128)}, bf16[256,1536]{1,0:T(8,128)(2,1)}, f32[128,1536]{1,0:T(8,128)}, bf16[128,1536]{1,0:T(8,128)(2,1)}) custom-call(s32[5]{0:T(128)} %pad_add_fusion.2.span, bf16[384,512]{1,0:T(8,128)(2,1)} %get-tuple-element.188.q, bf16[2,384,512]{2,1,0:T(8,128)(2,1)} %collective-permute-done.7.kv0, ...), custom_call_target="tpu_custom_call" | custom-call | flops 1 | bytes 1 | tf_op jit(solution)/shard_map/attend_far/pallas_call | solution.py:319
  81.3 2.5 collective-permute-done.16.got
  85.8 6.0 %collective-permute-start.19 = (bf16[768,512]{1,0:T(8,128)(2,1)}, bf16[768,512]{1,0:T(8,128)(2,1)S(1)}, u32[]{:S(2)}, u32[]{:S(2)}) collective-permute-start(bf16[768,512]{1,0:T(8,128)(2,1)} %get-tuple-element.224), channel_id=1, source_target_pairs={{0,1},{1,0},{2,3},{3,2},{4,5},{5,4},{6,7},{7,6},{8,9},{9,8},{10,11... | collective-permute-start | bytes 2359304 | tf_op jit(solution)/shard_map/ppermute | solution.py:27
  91.8 4.5 collective-permute-done.17.far
  97.0 1.7 collective-permute-done.18
  99.5 16.5 %cross.1 = (bf16[128,3072]{1,0:T(8,128)(2,1)}, bf16[128,1536]{1,0:T(8,128)(2,1)}, f32[128,1536]{1,0:T(8,128)}, f32[128,1536]{1,0:T(8,128)}, bf16[128,1536]{1,0:T...) custom-call(s32[2]{0:T(128)} %copy-done.82, bf16[128,1536]{1,0:T(8,128)(2,1)} %get-tuple-element.187.rows, ...), custom_call_target="tpu_custom_call" | custom-call | flops 1 | bytes 1 | tf_op jit(solution)/shard_map/cross/pallas_call | solution.py:522
  118.2 9.3 %collective-permute-done.22.n2 = bf16[128,1536]{1,0:T(8,128)(2,1)S(1)} collective-permute-done((bf16[128,1536]{1,0:T(8,128)(2,1)}, bf16[128,1536]{1,0:T(8,128)(2,1)S(1)}, u32[]{:S(2)}, u32[]{:S(2)}) %collective-permute-start.22) | collective-permute-done | bytes 393248 | tf_op jit(solution)/shard_map/ppermute | solution.py:27
  128.0 1.7 collective-permute-done.23.n3
  131.3 5.9 %collective-permute-start.26 = (bf16[768,128]{1,0:T(8,128)(2,1)}, bf16[768,128]{1,0:T(8,128)(2,1)}, u32[]{:S(2)}, u32[]{:S(2)}) collective-permute-start(bf16[768,128]{1,0:T(8,128)(2,1)} %get-tuple-element.238), channel_id=1, source_target_pairs={{0,1},{1,0},{2,3},{3,2},{4,5},{5,4},{6,7},{7,6},{8,9},{9,8},{10,11... | collective-permute-start | bytes 589832 | tf_op jit(solution)/shard_map/ppermute | solution.py:27
  139.8 14.7 %ffn.2 = (bf16[512,768]{1,0:T(8,128)(2,1)}, bf16[384,512]{1,0:T(8,128)(2,1)}, bf16[384,512]{1,0:T(8,128)(2,1)}, bf16[512,768]{1,0:T(8,128)(2,1)}, bf16[512,768]{...) custom-call(s32[2]{0:T(128)} %copy-done.82, ...), custom_call_target="tpu_custom_call" | custom-call | flops 1 | bytes 1 | tf_op jit(solution)/shard_map/ffn/pallas_call | solution.py:611
  156.1 15.0 %ffn.3 = (bf16[512,768]{1,0:T(8,128)(2,1)}, bf16[384,512]{1,0:T(8,128)(2,1)}, bf16[384,512]{1,0:T(8,128)(2,1)}, bf16[512,768]{1,0:T(8,128)(2,1)}, bf16[512,768]{...) custom-call(s32[2]{0:T(128)} %copy-done.82, ...), custom_call_target="tpu_custom_call" | custom-call | flops 1 | bytes 1 | tf_op jit(solution)/shard_map/ffn/pallas_call | solution.py:611
  171.2 2.5 collective-permute-done.30.got
  176.7 2.0 collective-permute-start.32
  178.7 7.6 %collective-permute-done.31.far = bf16[128,1536]{1,0:T(8,128)(2,1)S(1)} collective-permute-done((bf16[128,1536]{1,0:T(8,128)(2,1)S(1)}, bf16[128,1536]{1,0:T(8,128)(2,1)S(1)}, u32[]{:S(2)}, u32[]{:S(2)}) %collective-permute-start.31) | collective-permute-done | bytes 393248 | tf_op jit(solution)/shard_map/ppermute | solution.py:27
  188.4 21.0 %cross_back.1 = (bf16[128,3072]{1,0:T(8,128)(2,1)}, bf16[256,1536]{1,0:T(8,128)(2,1)}, f32[4,1536]{1,0:T(4,128)}, bf16[128,1536]{1,0:T(8,128)(2,1)}) custom-call(f32[128,1536]{1,0:T(8,128)} %get-tuple-element.240.own, bf16[256,1536]{1,0:T(8,128)(2,1)} %copy-done.23, bf16[128,1536]{1,0:T(8,128)(2,1)} %copy-done.63, ...), custom_call_target="tpu_custom_call" | custom-call | flops 1 | bytes 1 | tf_op jit(solution)/shard_map/cross_back/pallas_call | solution.py:676
  209.6 2.1 collective-permute-start.41
  214.5 6.7 %meet_rows.1 = (bf16[384,1536]{1,0:T(8,128)(2,1)}, bf16[384,1536]{1,0:T(8,128)(2,1)}) custom-call(s32[1]{0:T(128)} %bitcast.12.side, bf16[384,512]{1,0:T(8,128)(2,1)} %get-tuple-element.261.own_a, bf16[384,512]{1,0:T(8,128)(2,1)} %copy-done.55, bf16[384,512]{1,0:T(8,128)(2,1)} %get-tuple-element.263.own_b, bf16[384,512]{1,0:T(8,128)(2,1)} %collective-permute-done.33.pair_b, ...), custom_call_target="tpu_custom_call" | custom-call | flops 1 | bytes 1 | tf_op jit(solution)/shard_map/meet_rows/pallas_call | solution.py:701
  221.2 3.0 collective-permute-done.37.g2.a2
  224.7 5.6 %collective-permute-done.41.a_pair = bf16[512,768]{1,0:T(8,128)(2,1)} collective-permute-done((bf16[512,768]{1,0:T(8,128)(2,1)}, bf16[512,768]{1,0:T(8,128)(2,1)}, u32[]{:S(2)}, u32[]{:S(2)}) %collective-permute-start.41) | collective-permute-done | bytes 786464 | tf_op jit(solution)/shard_map/ppermute | solution.py:27
  230.4 1.8 collective-permute-start.45
  232.2 14.7 %collective-permute-done.42.b_pair = bf16[512,768]{1,0:T(8,128)(2,1)} collective-permute-done((bf16[512,768]{1,0:T(8,128)(2,1)}, bf16[512,768]{1,0:T(8,128)(2,1)}, u32[]{:S(2)}, u32[]{:S(2)}) %collective-permute-start.42) | collective-permute-done | bytes 786464 | tf_op jit(solution)/shard_map/ppermute | solution.py:27
  246.9 1.8 collective-permute-start.44
  251.9 17.7 %attend_back.1 = (f32[384,512]{1,0:T(8,128)}, bf16[2,384,512]{2,1,0:T(8,128)(2,1)}, f32[2,384,512]{2,1,0:T(8,128)}, bf16[2,384,512]{2,1,0:T(8,128)(2,1)}, f32[384,1]{1,0:T(8,128)}, /*index=5*/f32[384,1]{1,0:T(8,128)}) custom-call(s32[5]{0:T(128)} %pad_add_fusion.2.span, bf16[384,512]{1,0:T(8,128)(2,1)} %get-tuple-element.188.q, ...), custom_call_target="tpu_custom_call" | custom-call | flops 1 | bytes 1 | tf_op jit(solution)/shard_map/attend_back/pallas_call | solution.py:336
  269.6 2.4 collective-permute-done.46
  274.4 3.0 collective-permute-start.48
  278.7 1.9 add_convert_fusion.2
  281.5 3.3 collective-permute-start.49
  293.7 1.6 copy.83.times
  295.4 7.8 %meet_cols.2 = (bf16[384,1536]{1,0:T(8,128)(2,1)}, bf16[384,1536]{1,0:T(8,128)(2,1)}) custom-call(s32[1]{0:T(128)} %bitcast.12.side, bf16[2,768,128]{2,1,0:T(8,128)(2,1)} %copy-done.10, bf16[2,768,128]{2,1,0:T(8,128)(2,1)} %copy-done.28, bf16[2,768,128]{2,1,0:T(8,128)(2,1)} %copy-done.27, bf16[2,768,128]{2,1,0:T(8,128)(2,1)} %collective-permute-done.35.p3, ...), custom_call_target="tpu_custom_call" | custom-call | flops 1 | bytes 1 | tf_op jit(solution)/shard_map/meet_cols/pallas_call | solution.py:722
  303.6 7.6 %meet_cols.3 = (bf16[384,1536]{1,0:T(8,128)(2,1)}, bf16[384,1536]{1,0:T(8,128)(2,1)}) custom-call(s32[1]{0:T(128)} %bitcast.12.side, bf16[2,768,128]{2,1,0:T(8,128)(2,1)} %copy-done.10, bf16[2,768,128]{2,1,0:T(8,128)(2,1)} %copy-done.28, bf16[2,768,128]{2,1,0:T(8,128)(2,1)} %copy-done.27, bf16[2,768,128]{2,1,0:T(8,128)(2,1)} %collective-permute-done.35.p3, ...), custom_call_target="tpu_custom_call" | custom-call | flops 1 | bytes 1 | tf_op jit(solution)/shard_map/meet_cols/pallas_call | solution.py:722
  311.2 6.5 %down.1 = (bf16[256,1536]{1,0:T(8,128)(2,1)}, f32[128,1536]{1,0:T(8,128)}, bf16[128,1536]{1,0:T(8,128)(2,1)}) custom-call(bf16[512,768]{1,0:T(8,128)(2,1)} %get-tuple-element.287.first, bf16[512,768]{1,0:T(8,128)(2,1)} %get-tuple-element.288.second, bf16[1536,1536]{1,0:T(8,128)(2,1)} %down_w.5), custom_call_target="tpu_custom_call" | custom-call | flops 1 | bytes 1 | tf_op jit(solution)/shard_map/down/pallas_call | solution.py:746
  317.8 1.9 add_convert_fusion.8.kv
  321.2 10.9 %bundle.1 = (bf16[4,192,768]{2,1,0:T(8,128)(2,1)}, bf16[4,208,768]{2,1,0:T(8,128)(2,1)}, bf16[4,192,768]{2,1,0:T(8,128)(2,1)}, bf16[4,192,768]{2,1,0:T(8,128)(2,1)}) custom-call(s32[2]{0:T(128)} %copy-done.82, bf16[2,128,3072]{2,1,0:T(8,128)(2,1)} %copy-done.4, bf16[2,128,3072]{2,1,0:T(8,128)(2,1)} %collective-permute-done.39.f13, ...), custom_call_target="tpu_custom_call" | custom-call | flops 1 | bytes 1 | tf_op jit(solution)/shard_map/bundle/pallas_call | solution.py:810
  332.9 7.4 %tail.1 = (bf16[1152,512]{1,0:T(8,128)(2,1)}, bf16[1024,384]{1,0:T(8,128)(2,1)}, f32[512,384]{1,0:T(8,128)}, bf16[512,384]{1,0:T(8,128)(2,1)}) custom-call(s32[1]{0:T(128)} %bitcast.1.place, f32[384,512]{1,0:T(8,128)} %get-tuple-element.292.dq, f32[2,384,512]{2,1,0:T(8,128)} %get-tuple-element.293.kept, bf16[2,384,512]{2,1,0:T(8,128)(2,1)} %collective-permute-done.47.ahead, ...), custom_call_target="tpu_custom_call" | custom-call | flops 1 | bytes 1 | tf_op jit(solution)/shard_map/tail/pallas_call | solution.py:388
  340.4 2.0 collective-permute-start.61
  342.4 2.2 add_bitcast_fusion
  348.0 20.4 %collective-permute-done.53 = bf16[2,192,1536]{2,1,0:T(8,128)(2,1)S(1)} collective-permute-done((bf16[2,192,1536]{2,1,0:T(8,128)(2,1)}, bf16[2,192,1536]{2,1,0:T(8,128)(2,1)S(1)}, u32[]{:S(2)}, u32[]{:S(2)}) %collective-permute-start.53) | collective-permute-done | bytes 1179680 | tf_op jit(solution)/shard_map/ppermute | solution.py:27
  371.3 1.7 fusion.3
  372.9 5.3 %collective-permute-done.54 = bf16[512,384]{1,0:T(8,128)(2,1)S(1)} collective-permute-done((bf16[512,384]{1,0:T(8,128)(2,1)S(1)}, bf16[512,384]{1,0:T(8,128)(2,1)S(1)}, u32[]{:S(2)}, u32[]{:S(2)}) %collective-permute-start.54) | collective-permute-done | bytes 393248 | tf_op jit(solution)/shard_map/ppermute | solution.py:27
  378.2 1.8 multiply_reduce_fusion
  381.4 1.6 collective-permute-start.60
  383.9 2.9 collective-permute-start.73
  386.9 9.4 %collective-permute-done.61 = bf16[4,208,768]{2,1,0:T(8,128)(2,1)S(1)} collective-permute-done((bf16[4,208,768]{2,1,0:T(8,128)(2,1)}, bf16[4,208,768]{2,1,0:T(8,128)(2,1)S(1)}, u32[]{:S(2)}, u32[]{:S(2)}) %collective-permute-start.61) | collective-permute-done | bytes 1277984 | tf_op jit(solution)/shard_map/ppermute | solution.py:27
  405.9 2.4 fusion.33
  412.3 12.6 %collective-permute-done.74 = bf16[1,192,1536]{2,1,0:T(8,128)(2,1)} collective-permute-done((bf16[1,192,1536]{2,1,0:T(8,128)(2,1)}, bf16[1,192,1536]{2,1,0:T(8,128)(2,1)}, u32[]{:S(2)}, u32[]{:S(2)}) %collective-permute-start.74) | collective-permute-done | bytes 589856 | tf_op jit(solution)/shard_map/ppermute | solution.py:27
  426.1 11.3 %collective-permute-done.73 = bf16[1,192,1536]{2,1,0:T(8,128)(2,1)} collective-permute-done((bf16[1,192,1536]{2,1,0:T(8,128)(2,1)}, bf16[1,192,1536]{2,1,0:T(8,128)(2,1)}, u32[]{:S(2)}, u32[]{:S(2)}) %collective-permute-start.73) | collective-permute-done | bytes 589856 | tf_op jit(solution)/shard_map/ppermute | solution.py:27
  438.8 1.7 pad_maximum_fusion.2
  440.5 4.8 collective-permute-done.71
  448.4 9.8 %collective-permute-done.72 = bf16[1,192,768]{2,1,0:T(8,128)(2,1)S(1)} collective-permute-done((bf16[1,192,768]{2,1,0:T(8,128)(2,1)S(1)}, bf16[1,192,768]{2,1,0:T(8,128)(2,1)S(1)}, u32[]{:S(2)}, u32[]{:S(2)}) %collective-permute-start.72) | collective-permute-done | bytes 294944 | tf_op jit(solution)/shard_map/ppermute | solution.py:27
  462.6 6.6 %collective-permute-done.63 = bf16[2,192,1152]{2,1,0:T(8,128)(2,1)S(1)} collective-permute-done((bf16[2,192,1152]{2,1,0:T(8,128)(2,1)S(1)}, bf16[2,192,1152]{2,1,0:T(8,128)(2,1)S(1)}, u32[]{:S(2)}, u32[]{:S(2)}) %collective-permute-start.63) | collective-permute-done | bytes 884768 | tf_op jit(solution)/shard_map/ppermute | solution.py:27
  470.7 2.6 collective-permute-done.65
  473.7 5.4 %collective-permute-done.66 = f32[2,6,48]{2,0,1:T(2,128)S(1)} collective-permute-done((f32[2,6,48]{2,0,1:T(2,128)S(1)}, f32[2,6,48]{2,0,1:T(2,128)S(1)}, u32[]{:S(2)}, u32[]{:S(2)}) %collective-permute-start.66) | collective-permute-done | bytes 2336 | tf_op jit(solution)/shard_map/ppermute | solution.py:27
  479.1 3.3 collective-permute-start.67
  482.5 8.6 %collective-permute-done.67 = f32[1,6,48]{2,0,1:T(1,128)S(1)} collective-permute-done((f32[1,6,48]{2,0,1:T(1,128)S(1)}, f32[1,6,48]{2,0,1:T(1,128)S(1)}, u32[]{:S(2)}, u32[]{:S(2)}) %collective-permute-start.67) | collective-permute-done | bytes 1184 | tf_op jit(solution)/shard_map/ppermute | solution.py:27
  493.7 10.0 %collective-permute-done.69 = bf16[2,192,768]{2,1,0:T(8,128)(2,1)S(1)} collective-permute-done((bf16[2,192,768]{2,1,0:T(8,128)(2,1)S(1)}, bf16[2,192,768]{2,1,0:T(8,128)(2,1)S(1)}, u32[]{:S(2)}, u32[]{:S(2)}) %collective-permute-start.69) | collective-permute-done | bytes 589856 | tf_op jit(solution)/shard_map/ppermute | solution.py:27
  505.0 14.2 %collective-permute-done.70 = bf16[1,192,768]{2,1,0:T(8,128)(2,1)S(1)} collective-permute-done((bf16[1,192,768]{2,1,0:T(8,128)(2,1)S(1)}, bf16[1,192,768]{2,1,0:T(8,128)(2,1)S(1)}, u32[]{:S(2)}, u32[]{:S(2)}) %collective-permute-start.70) | collective-permute-done | bytes 294944 | tf_op jit(solution)/shard_map/ppermute | solution.py:27
  (412 shorter events, 100.7 us)
Async XLA Ops:
  0.7 12.5 %collective-permute-start.1 = (bf16[512,384]{1,0:T(8,128)(2,1)}, bf16[512,384]{1,0:T(8,128)(2,1)S(1)}, u32[]{:S(2)}, u32[]{:S(2)}) collective-permute-start(bf16[512,384]{1,0:T(8,128)(2,1)} %x0.1), channel_id=1, source_target_pairs={{0,16},{8,24},{16,0},{24,8},{1,17},{9,25},{17,1},{25,9},{2,18},{10... | collective-permute-start | bytes 1179656 | tf_op jit(solution)/shard_map/ppermute | solution.py:27
  3.7 18.0 %collective-permute-start = (bf16[512,384]{1,0:T(8,128)(2,1)}, bf16[512,384]{1,0:T(8,128)(2,1)S(1)}, u32[]{:S(2)}, u32[]{:S(2)}) collective-permute-start(bf16[512,384]{1,0:T(8,128)(2,1)} %x0.1), channel_id=1, source_target_pairs={{0,8},{8,0},{16,24},{24,16},{1,9},{9,1},{17,25},{25,17},{2,10},{10... | collective-permute-start | bytes 1179656 | tf_op jit(solution)/shard_map/ppermute | solution.py:27
  7.8 11.4 %collective-permute-start.4 = (f32[6,384]{1,0:T(8,128)S(1)}, f32[6,384]{1,0:T(8,128)S(1)}, u32[]{:S(2)}, u32[]{:S(2)}) collective-permute-start(f32[6,384]{1,0:T(8,128)S(1)} %stack.98.g0), channel_id=1, source_target_pairs={{0,16},{8,24},{16,0},{24,8},{1,17},{9,25},{17,1},{25,9},{2,18},{10... | collective-permute-start | bytes 27656 | tf_op jit(solution)/shard_map/ppermute | solution.py:27
  14.3 17.8 %collective-permute-start.6 = (bf16[512,384]{1,0:T(8,128)(2,1)}, bf16[512,384]{1,0:T(8,128)(2,1)S(1)}, u32[]{:S(2)}, u32[]{:S(2)}) collective-permute-start(bf16[512,384]{1,0:T(8,128)(2,1)} %param.43), channel_id=1, source_target_pairs={{0,1},{1,0},{2,3},{3,2},{4,5},{5,4},{6,7},{7,6},{8,9},{9,8},{10,11... | collective-permute-start | bytes 1179656 | tf_op jit(solution)/shard_map/ppermute | solution.py:27
  16.0 53.8 %collective-permute-start.9 = (bf16[1536,384]{1,0:T(8,128)(2,1)}, bf16[1536,384]{1,0:T(8,128)(2,1)}, u32[]{:S(2)}, u32[]{:S(2)}) collective-permute-start(bf16[1536,384]{1,0:T(8,128)(2,1)} %q0.3), channel_id=1, source_target_pairs={{0,16},{8,24},{16,0},{24,8},{1,17},{9,25},{17,1},{25,9},{2,18},{10... | collective-permute-start | bytes 3538952 | tf_op jit(solution)/shard_map/ppermute | solution.py:27
  17.5 52.3 %collective-permute-start.10 = (bf16[384,1536]{1,0:T(8,128)(2,1)}, bf16[384,1536]{1,0:T(8,128)(2,1)}, u32[]{:S(2)}, u32[]{:S(2)}) collective-permute-start(bf16[384,1536]{1,0:T(8,128)(2,1)} %o0.3), channel_id=1, source_target_pairs={{0,16},{8,24},{16,0},{24,8},{1,17},{9,25},{17,1},{25,9},{2,18},{10... | collective-permute-start | bytes 3538952 | tf_op jit(solution)/shard_map/ppermute | solution.py:27
  32.0 21.7 %collective-permute-start.8 = (bf16[2,384,512]{2,1,0:T(8,128)(2,1)}, bf16[2,384,512]{2,1,0:T(8,128)(2,1)S(1)}, u32[]{:S(2)}, u32[]{:S(2)}) collective-permute-start(bf16[2,384,512]{2,1,0:T(8,128)(2,1)} %get-tuple-element.191.kv.kv1), channel_id=1, source_target_pairs={{1,0},{2,1},{3,2},{4,3},{5,4},{6,5},{7,6},{9,8},{10,9},{11,10},{12... | collective-permute-start | bytes 2359304 | tf_op jit(solution)/shard_map/ppermute | solution.py:33
  33.3 36.4 %collective-permute-start.7 = (bf16[2,384,512]{2,1,0:T(8,128)(2,1)}, bf16[2,384,512]{2,1,0:T(8,128)(2,1)}, u32[]{:S(2)}, u32[]{:S(2)}) collective-permute-start(bf16[2,384,512]{2,1,0:T(8,128)(2,1)} %get-tuple-element.191.kv.kv1), channel_id=1, source_target_pairs={{0,1},{1,2},{2,3},{3,4},{4,5},{5,6},{6,7},{8,9},{9,10},{10,11},{11... | collective-permute-start | bytes 2359304 | tf_op jit(solution)/shard_map/ppermute | solution.py:33
  69.8 11.4 %collective-permute-start.12 = (bf16[1536,384]{1,0:T(8,128)(2,1)S(1)}, bf16[1536,384]{1,0:T(8,128)(2,1)}, u32[]{:S(2)}, u32[]{:S(2)}) collective-permute-start(bf16[1536,384]{1,0:T(8,128)(2,1)S(1)} %copy-done.6), channel_id=1, source_target_pairs={{0,8},{8,0},{16,24},{24,16},{1,9},{9,1},{17,25},{25,17},{2,10},{10... | collective-permute-start | bytes 3538952 | tf_op jit(solution)/shard_map/ppermute | solution.py:27
  69.9 11.3 %collective-permute-start.14 = (bf16[384,1536]{1,0:T(8,128)(2,1)S(1)}, bf16[384,1536]{1,0:T(8,128)(2,1)}, u32[]{:S(2)}, u32[]{:S(2)}) collective-permute-start(bf16[384,1536]{1,0:T(8,128)(2,1)S(1)} %copy-done.7), channel_id=1, source_target_pairs={{0,8},{8,0},{16,24},{24,16},{1,9},{9,1},{17,25},{25,17},{2,10},{10... | collective-permute-start | bytes 3538952 | tf_op jit(solution)/shard_map/ppermute | solution.py:27
  70.4 10.8 %collective-permute-start.13 = (bf16[1536,384]{1,0:T(8,128)(2,1)}, bf16[1536,384]{1,0:T(8,128)(2,1)}, u32[]{:S(2)}, u32[]{:S(2)}) collective-permute-start(bf16[1536,384]{1,0:T(8,128)(2,1)} %collective-permute-done.9.q2), channel_id=1, source_target_pairs={{0,8},{8,0},{16,24},{24,16},{1,9},{9,1},{17,25},{25,17},{2,10},{10... | collective-permute-start | bytes 3538952 | tf_op jit(solution)/shard_map/ppermute | solution.py:27
  70.4 10.8 %collective-permute-start.15 = (bf16[384,1536]{1,0:T(8,128)(2,1)}, bf16[384,1536]{1,0:T(8,128)(2,1)}, u32[]{:S(2)}, u32[]{:S(2)}) collective-permute-start(bf16[384,1536]{1,0:T(8,128)(2,1)} %collective-permute-done.10.o2), channel_id=1, source_target_pairs={{0,8},{8,0},{16,24},{24,16},{1,9},{9,1},{17,25},{25,17},{2,10},{10... | collective-permute-start | bytes 3538952 | tf_op jit(solution)/shard_map/ppermute | solution.py:27
  70.9 10.3 %collective-permute-start.11 = (bf16[256,384]{1,0:T(8,128)(2,1)S(1)}, bf16[256,384]{1,0:T(8,128)(2,1)S(1)}, u32[]{:S(2)}, u32[]{:S(2)}) collective-permute-start(bf16[256,384]{1,0:T(8,128)(2,1)S(1)} %copy-done.24), channel_id=1, source_target_pairs={{0,16},{8,24},{16,0},{24,8},{1,17},{9,25},{17,1},{25,9},{2,18},{10... | collective-permute-start | bytes 589832 | tf_op jit(solution)/shard_map/ppermute | solution.py:27
  85.1 11.2 %collective-permute-start.17 = (bf16[128,1536]{1,0:T(8,128)(2,1)S(1)}, bf16[128,1536]{1,0:T(8,128)(2,1)S(1)}, u32[]{:S(2)}, u32[]{:S(2)}) collective-permute-start(bf16[128,1536]{1,0:T(8,128)(2,1)S(1)} %add_convert_fusion.7), channel_id=1, source_target_pairs={{0,16},{8,24},{16,0},{24,8},{1,17},{9,25},{17,1},{25,9},{2,18},{10... | collective-permute-start | bytes 1179656 | tf_op jit(solution)/shard_map/ppermute | solution.py:27
  85.8 30.2 %collective-permute-start.19 = (bf16[768,512]{1,0:T(8,128)(2,1)}, bf16[768,512]{1,0:T(8,128)(2,1)S(1)}, u32[]{:S(2)}, u32[]{:S(2)}) collective-permute-start(bf16[768,512]{1,0:T(8,128)(2,1)} %get-tuple-element.224), channel_id=1, source_target_pairs={{0,1},{1,0},{2,3},{3,2},{4,5},{5,4},{6,7},{7,6},{8,9},{9,8},{10,11... | collective-permute-start | bytes 2359304 | tf_op jit(solution)/shard_map/ppermute | solution.py:27
  96.4 19.7 %collective-permute-start.20 = (bf16[2,512,384]{2,1,0:T(8,128)(2,1)S(1)}, bf16[2,512,384]{2,1,0:T(8,128)(2,1)S(1)}, u32[]{:S(2)}, u32[]{:S(2)}) collective-permute-start(bf16[2,512,384]{2,1,0:T(8,128)(2,1)S(1)} %pad_maximum_fusion.4.g0), channel_id=1, source_target_pairs={{0,16},{8,24},{16,0},{24,8},{1,17},{9,25},{17,1},{25,9},{2,18},{10... | collective-permute-start | bytes 2359304 | tf_op jit(solution)/shard_map/ppermute | solution.py:27
  116.0 11.4 %collective-permute-start.22 = (bf16[128,1536]{1,0:T(8,128)(2,1)}, bf16[128,1536]{1,0:T(8,128)(2,1)S(1)}, u32[]{:S(2)}, u32[]{:S(2)}) collective-permute-start(bf16[128,1536]{1,0:T(8,128)(2,1)} %get-tuple-element.227.n0), channel_id=1, source_target_pairs={{0,16},{8,24},{16,0},{24,8},{1,17},{9,25},{17,1},{25,9},{2,18},{10... | collective-permute-start | bytes 1179656 | tf_op jit(solution)/shard_map/ppermute | solution.py:27
  117.7 19.6 %collective-permute-start.24 = (bf16[2,512,384]{2,1,0:T(8,128)(2,1)S(1)}, bf16[2,512,384]{2,1,0:T(8,128)(2,1)S(1)}, u32[]{:S(2)}, u32[]{:S(2)}) collective-permute-start(bf16[2,512,384]{2,1,0:T(8,128)(2,1)S(1)} %pad_maximum_fusion.4.g0), channel_id=1, source_target_pairs={{0,8},{8,0},{16,24},{24,16},{1,9},{9,1},{17,25},{25,17},{2,10},{10... | collective-permute-start | bytes 2359304 | tf_op jit(solution)/shard_map/ppermute | solution.py:27
  117.7 20.3 %collective-permute-start.25 = (bf16[2,512,384]{2,1,0:T(8,128)(2,1)S(1)}, bf16[2,512,384]{2,1,0:T(8,128)(2,1)S(1)}, u32[]{:S(2)}, u32[]{:S(2)}) collective-permute-start(bf16[2,512,384]{2,1,0:T(8,128)(2,1)S(1)} %collective-permute-done.20.g2), channel_id=1, source_target_pairs={{0,8},{8,0},{16,24},{24,16},{1,9},{9,1},{17,25},{25,17},{2,10},{10... | collective-permute-start | bytes 2359304 | tf_op jit(solution)/shard_map/ppermute | solution.py:27
  127.5 9.7 %collective-permute-start.21 = (bf16[128,1536]{1,0:T(8,128)(2,1)}, bf16[128,1536]{1,0:T(8,128)(2,1)S(1)}, u32[]{:S(2)}, u32[]{:S(2)}) collective-permute-start(bf16[128,1536]{1,0:T(8,128)(2,1)} %get-tuple-element.227.n0), channel_id=1, source_target_pairs={{0,8},{8,0},{16,24},{24,16},{1,9},{9,1},{17,25},{25,17},{2,10},{10... | collective-permute-start | bytes 1179656 | tf_op jit(solution)/shard_map/ppermute | solution.py:27
  129.7 41.4 %collective-permute-start.28 = (bf16[128,3072]{1,0:T(8,128)(2,1)}, bf16[128,3072]{1,0:T(8,128)(2,1)}, u32[]{:S(2)}, u32[]{:S(2)}) collective-permute-start(bf16[128,3072]{1,0:T(8,128)(2,1)} %get-tuple-element.246), channel_id=1, source_target_pairs={{0,16},{8,24},{16,0},{24,8},{1,17},{9,25},{17,1},{25,9},{2,18},{10... | collective-permute-start | bytes 2359304 | tf_op jit(solution)/shard_map/ppermute | solution.py:27
  131.3 23.2 %collective-permute-start.26 = (bf16[768,128]{1,0:T(8,128)(2,1)}, bf16[768,128]{1,0:T(8,128)(2,1)}, u32[]{:S(2)}, u32[]{:S(2)}) collective-permute-start(bf16[768,128]{1,0:T(8,128)(2,1)} %get-tuple-element.238), channel_id=1, source_target_pairs={{0,1},{1,0},{2,3},{3,2},{4,5},{5,4},{6,7},{7,6},{8,9},{9,8},{10,11... | collective-permute-start | bytes 589832 | tf_op jit(solution)/shard_map/ppermute | solution.py:27
  155.5 15.6 %collective-permute-start.27 = (bf16[2,768,128]{2,1,0:T(8,128)(2,1)S(1)}, bf16[2,768,128]{2,1,0:T(8,128)(2,1)S(1)}, u32[]{:S(2)}, u32[]{:S(2)}) collective-permute-start(bf16[2,768,128]{2,1,0:T(8,128)(2,1)S(1)} %pad_maximum_fusion.6.p0), channel_id=1, source_target_pairs={{0,16},{8,24},{16,0},{24,8},{1,17},{9,25},{17,1},{25,9},{2,18},{10... | collective-permute-start | bytes 1179656 | tf_op jit(solution)/shard_map/ppermute | solution.py:27
  156.1 15.0 %collective-permute-start.29 = (bf16[384,512]{1,0:T(8,128)(2,1)}, bf16[384,512]{1,0:T(8,128)(2,1)S(1)}, u32[]{:S(2)}, u32[]{:S(2)}) collective-permute-start(bf16[384,512]{1,0:T(8,128)(2,1)} %get-tuple-element.247), channel_id=1, source_target_pairs={{0,1},{1,0},{2,3},{3,2},{4,5},{5,4},{6,7},{7,6},{8,9},{9,8},{10,11... | collective-permute-start | bytes 1179656 | tf_op jit(solution)/shard_map/ppermute | solution.py:27
  175.1 11.2 %collective-permute-start.31 = (bf16[128,1536]{1,0:T(8,128)(2,1)S(1)}, bf16[128,1536]{1,0:T(8,128)(2,1)S(1)}, u32[]{:S(2)}, u32[]{:S(2)}) collective-permute-start(bf16[128,1536]{1,0:T(8,128)(2,1)S(1)} %add_convert_fusion.6), channel_id=1, source_target_pairs={{0,16},{8,24},{16,0},{24,8},{1,17},{9,25},{17,1},{25,9},{2,18},{10... | collective-permute-start | bytes 1179656 | tf_op jit(solution)/shard_map/ppermute | solution.py:27
  176.7 32.8 %collective-permute-start.32 = (bf16[512,768]{1,0:T(8,128)(2,1)}, bf16[512,768]{1,0:T(8,128)(2,1)}, u32[]{:S(2)}, u32[]{:S(2)}) collective-permute-start(bf16[512,768]{1,0:T(8,128)(2,1)} %get-tuple-element.312.a), channel_id=1, source_target_pairs={{0,1},{1,0},{2,3},{3,2},{4,5},{5,4},{6,7},{7,6},{8,9},{9,8},{10,11... | collective-permute-start | bytes 2359304 | tf_op jit(solution)/shard_map/ppermute | solution.py:27
  178.7 30.7 %collective-permute-start.33 = (bf16[384,512]{1,0:T(8,128)(2,1)}, bf16[384,512]{1,0:T(8,128)(2,1)}, u32[]{:S(2)}, u32[]{:S(2)}) collective-permute-start(bf16[384,512]{1,0:T(8,128)(2,1)} %get-tuple-element.255), channel_id=1, source_target_pairs={{0,1},{1,0},{2,3},{3,2},{4,5},{5,4},{6,7},{7,6},{8,9},{9,8},{10,11... | collective-permute-start | bytes 1179656 | tf_op jit(solution)/shard_map/ppermute | solution.py:27
  186.3 23.1 %collective-permute-start.34 = (bf16[2,768,128]{2,1,0:T(8,128)(2,1)S(1)}, bf16[2,768,128]{2,1,0:T(8,128)(2,1)S(1)}, u32[]{:S(2)}, u32[]{:S(2)}) collective-permute-start(bf16[2,768,128]{2,1,0:T(8,128)(2,1)S(1)} %pad_maximum_fusion.6.p0), channel_id=1, source_target_pairs={{0,8},{8,0},{16,24},{24,16},{1,9},{9,1},{17,25},{25,17},{2,10},{10... | collective-permute-start | bytes 1179656 | tf_op jit(solution)/shard_map/ppermute | solution.py:27
  186.3 23.2 %collective-permute-start.35 = (bf16[2,768,128]{2,1,0:T(8,128)(2,1)S(1)}, bf16[2,768,128]{2,1,0:T(8,128)(2,1)}, u32[]{:S(2)}, u32[]{:S(2)}) collective-permute-start(bf16[2,768,128]{2,1,0:T(8,128)(2,1)S(1)} %collective-permute-done.27.p2), channel_id=1, source_target_pairs={{0,8},{8,0},{16,24},{24,16},{1,9},{9,1},{17,25},{25,17},{2,10},{10... | collective-permute-start | bytes 1179656 | tf_op jit(solution)/shard_map/ppermute | solution.py:27
  209.5 39.2 %collective-permute-start.39 = (bf16[2,128,3072]{2,1,0:T(8,128)(2,1)S(1)}, bf16[2,128,3072]{2,1,0:T(8,128)(2,1)}, u32[]{:S(2)}, u32[]{:S(2)}) collective-permute-start(bf16[2,128,3072]{2,1,0:T(8,128)(2,1)S(1)} %pad_maximum_fusion.f02), channel_id=1, source_target_pairs={{0,8},{8,0},{16,24},{24,16},{1,9},{9,1},{17,25},{25,17},{2,10},{10... | collective-permute-start | bytes 4718600 | tf_op jit(solution)/shard_map/ppermute | solution.py:27
  209.6 20.8 %collective-permute-start.41 = (bf16[512,768]{1,0:T(8,128)(2,1)}, bf16[512,768]{1,0:T(8,128)(2,1)}, u32[]{:S(2)}, u32[]{:S(2)}) collective-permute-start(bf16[512,768]{1,0:T(8,128)(2,1)} %get-tuple-element.271.a), channel_id=1, source_target_pairs={{0,1},{1,0},{2,3},{3,2},{4,5},{5,4},{6,7},{7,6},{8,9},{9,8},{10,11... | collective-permute-start | bytes 2359304 | tf_op jit(solution)/shard_map/ppermute | solution.py:27
  211.6 35.3 %collective-permute-start.42 = (bf16[512,768]{1,0:T(8,128)(2,1)}, bf16[512,768]{1,0:T(8,128)(2,1)}, u32[]{:S(2)}, u32[]{:S(2)}) collective-permute-start(bf16[512,768]{1,0:T(8,128)(2,1)} %get-tuple-element.314.b), channel_id=1, source_target_pairs={{0,1},{1,0},{2,3},{3,2},{4,5},{5,4},{6,7},{7,6},{8,9},{9,8},{10,11... | collective-permute-start | bytes 2359304 | tf_op jit(solution)/shard_map/ppermute | solution.py:27
  212.8 11.4 %collective-permute-start.37 = (bf16[128,1536]{1,0:T(8,128)(2,1)}, bf16[128,1536]{1,0:T(8,128)(2,1)S(1)}, u32[]{:S(2)}, u32[]{:S(2)}) collective-permute-start(bf16[128,1536]{1,0:T(8,128)(2,1)} %get-tuple-element.324.g0.a0), channel_id=1, source_target_pairs={{0,16},{8,24},{16,0},{24,8},{1,17},{9,25},{17,1},{25,9},{2,18},{10... | collective-permute-start | bytes 1179656 | tf_op jit(solution)/shard_map/ppermute | solution.py:27
  214.4 9.8 %collective-permute-start.40 = (bf16[512,384]{1,0:T(8,128)(2,1)S(1)}, bf16[512,384]{1,0:T(8,128)(2,1)S(1)}, u32[]{:S(2)}, u32[]{:S(2)}) collective-permute-start(bf16[512,384]{1,0:T(8,128)(2,1)S(1)} %pad_maximum_fusion.7), channel_id=1, source_target_pairs={{0,8},{8,0},{16,24},{24,16},{1,9},{9,1},{17,25},{25,17},{2,10},{10... | collective-permute-start | bytes 1179656 | tf_op jit(solution)/shard_map/ppermute | solution.py:27
  224.2 24.5 %collective-permute-start.36 = (bf16[128,1536]{1,0:T(8,128)(2,1)S(1)}, bf16[128,1536]{1,0:T(8,128)(2,1)S(1)}, u32[]{:S(2)}, u32[]{:S(2)}) collective-permute-start(bf16[128,1536]{1,0:T(8,128)(2,1)S(1)} %copy-done.11), channel_id=1, source_target_pairs={{0,8},{8,0},{16,24},{24,16},{1,9},{9,1},{17,25},{25,17},{2,10},{10... | collective-permute-start | bytes 1179656 | tf_op jit(solution)/shard_map/ppermute | solution.py:27
  224.2 24.5 %collective-permute-start.38 = (bf16[128,1536]{1,0:T(8,128)(2,1)S(1)}, bf16[128,1536]{1,0:T(8,128)(2,1)S(1)}, u32[]{:S(2)}, u32[]{:S(2)}) collective-permute-start(bf16[128,1536]{1,0:T(8,128)(2,1)S(1)} %collective-permute-done.37.g2.a2), channel_id=1, source_target_pairs={{0,8},{8,0},{16,24},{24,16},{1,9},{9,1},{17,25},{25,17},{2,10},{10... | collective-permute-start | bytes 1179656 | tf_op jit(solution)/shard_map/ppermute | solution.py:27
  230.4 39.3 %collective-permute-start.45 = (bf16[2,192,1536]{2,1,0:T(8,128)(2,1)}, bf16[2,192,1536]{2,1,0:T(8,128)(2,1)}, u32[]{:S(2)}, u32[]{:S(2)}) collective-permute-start(bf16[2,192,1536]{2,1,0:T(8,128)(2,1)} %bitcast.139), channel_id=1, source_target_pairs={{0,2},{1,3},{2,0},{3,1},{4,6},{5,7},{6,4},{7,5},{8,10},{9,11},{10,... | collective-permute-start | bytes 3538952 | tf_op jit(solution)/shard_map/ppermute | solution.py:27
  246.9 22.7 %collective-permute-start.44 = (bf16[512,768]{1,0:T(8,128)(2,1)}, bf16[512,768]{1,0:T(8,128)(2,1)}, u32[]{:S(2)}, u32[]{:S(2)}) collective-permute-start(bf16[512,768]{1,0:T(8,128)(2,1)} %get-tuple-element.283.b), channel_id=1, source_target_pairs={{0,1},{1,0},{2,3},{3,2},{4,5},{5,4},{6,7},{7,6},{8,9},{9,8},{10,11... | collective-permute-start | bytes 2359304 | tf_op jit(solution)/shard_map/ppermute | solution.py:27
  248.7 23.3 %collective-permute-start.43 = (bf16[128,3072]{1,0:T(8,128)(2,1)}, bf16[128,3072]{1,0:T(8,128)(2,1)S(1)}, u32[]{:S(2)}, u32[]{:S(2)}) collective-permute-start(bf16[128,3072]{1,0:T(8,128)(2,1)} %get-tuple-element.281), channel_id=1, source_target_pairs={{0,16},{8,24},{16,0},{24,8},{1,17},{9,25},{17,1},{25,9},{2,18},{10... | collective-permute-start | bytes 2359304 | tf_op jit(solution)/shard_map/ppermute | solution.py:27
  251.3 20.7 %collective-permute-start.46 = (bf16[256,384]{1,0:T(8,128)(2,1)S(1)}, bf16[256,384]{1,0:T(8,128)(2,1)S(1)}, u32[]{:S(2)}, u32[]{:S(2)}) collective-permute-start(bf16[256,384]{1,0:T(8,128)(2,1)S(1)} %add_convert_fusion.9), channel_id=1, source_target_pairs={{0,16},{8,24},{16,0},{24,8},{1,17},{9,25},{17,1},{25,9},{2,18},{10... | collective-permute-start | bytes 589832 | tf_op jit(solution)/shard_map/ppermute | solution.py:27
  274.3 45.3 %collective-permute-start.50 = (bf16[2,128,3072]{2,1,0:T(8,128)(2,1)S(1)}, bf16[2,128,3072]{2,1,0:T(8,128)(2,1)}, u32[]{:S(2)}, u32[]{:S(2)}) collective-permute-start(bf16[2,128,3072]{2,1,0:T(8,128)(2,1)S(1)} %pad_maximum_fusion.1.b02), channel_id=1, source_target_pairs={{0,8},{8,0},{16,24},{24,16},{1,9},{9,1},{17,25},{25,17},{2,10},{10... | collective-permute-start | bytes 4718600 | tf_op jit(solution)/shard_map/ppermute | solution.py:27
  274.4 57.7 %collective-permute-start.48 = (bf16[2,384,512]{2,1,0:T(8,128)(2,1)}, bf16[2,384,512]{2,1,0:T(8,128)(2,1)S(1)}, u32[]{:S(2)}, u32[]{:S(2)}) collective-permute-start(bf16[2,384,512]{2,1,0:T(8,128)(2,1)} %get-tuple-element.294), channel_id=1, source_target_pairs={{0,1},{1,2},{2,3},{3,4},{4,5},{5,6},{6,7},{8,9},{9,10},{10,11},{11... | collective-permute-start | bytes 2359304 | tf_op jit(solution)/shard_map/ppermute | solution.py:33
  277.4 54.7 %collective-permute-start.47 = (bf16[2,384,512]{2,1,0:T(8,128)(2,1)}, bf16[2,384,512]{2,1,0:T(8,128)(2,1)}, u32[]{:S(2)}, u32[]{:S(2)}) collective-permute-start(bf16[2,384,512]{2,1,0:T(8,128)(2,1)} %get-tuple-element.286), channel_id=1, source_target_pairs={{1,0},{2,1},{3,2},{4,3},{5,4},{6,5},{7,6},{9,8},{10,9},{11,10},{12... | collective-permute-start | bytes 2359304 | tf_op jit(solution)/shard_map/ppermute | solution.py:33
  281.5 50.6 %collective-permute-start.49 = (bf16[1,192,1536]{2,1,0:T(8,128)(2,1)}, bf16[1,192,1536]{2,1,0:T(8,128)(2,1)}, u32[]{:S(2)}, u32[]{:S(2)}) collective-permute-start(bf16[1,192,1536]{2,1,0:T(8,128)(2,1)} %constant_dynamic-slice_fusion.22), channel_id=1, source_target_pairs={{0,4},{1,5},{2,6},{3,7},{4,0},{5,1},{6,2},{7,3},{8,12},{9,13},{10,... | collective-permute-start | bytes 1769480 | tf_op jit(solution)/shard_map/ppermute | solution.py:27
  303.2 44.8 %collective-permute-start.52 = (bf16[2,192,1536]{2,1,0:T(8,128)(2,1)}, bf16[2,192,1536]{2,1,0:T(8,128)(2,1)}, u32[]{:S(2)}, u32[]{:S(2)}) collective-permute-start(bf16[2,192,1536]{2,1,0:T(8,128)(2,1)} %bitcast.137), channel_id=1, source_target_pairs={{0,2},{1,3},{2,0},{3,1},{4,6},{5,7},{6,4},{7,5},{8,10},{9,11},{10,... | collective-permute-start | bytes 3538952 | tf_op jit(solution)/shard_map/ppermute | solution.py:27
  319.6 48.8 %collective-permute-start.53 = (bf16[2,192,1536]{2,1,0:T(8,128)(2,1)}, bf16[2,192,1536]{2,1,0:T(8,128)(2,1)S(1)}, u32[]{:S(2)}, u32[]{:S(2)}) collective-permute-start(bf16[2,192,1536]{2,1,0:T(8,128)(2,1)} %bitcast.138), channel_id=1, source_target_pairs={{0,2},{1,3},{2,0},{3,1},{4,6},{5,7},{6,4},{7,5},{8,10},{9,11},{10,... | collective-permute-start | bytes 3538952 | tf_op jit(solution)/shard_map/ppermute | solution.py:27
  340.3 7.6 %collective-permute-start.51 = (bf16[1024,384]{1,0:T(8,128)(2,1)}, bf16[1024,384]{1,0:T(8,128)(2,1)S(1)}, u32[]{:S(2)}, u32[]{:S(2)}) collective-permute-start(bf16[1024,384]{1,0:T(8,128)(2,1)} %get-tuple-element.307), channel_id=1, source_target_pairs={{0,8},{8,0},{16,24},{24,16},{1,9},{9,1},{17,25},{25,17},{2,10},{10... | collective-permute-start | bytes 2359304 | tf_op jit(solution)/shard_map/ppermute | solution.py:27
  340.4 46.6 %collective-permute-start.62 = (bf16[1152,512]{1,0:T(8,128)(2,1)}, bf16[1152,512]{1,0:T(8,128)(2,1)S(1)}, u32[]{:S(2)}, u32[]{:S(2)}) collective-permute-start(bf16[1152,512]{1,0:T(8,128)(2,1)} %get-tuple-element.335), channel_id=1, source_target_pairs={{0,1},{1,0},{2,3},{3,2},{4,5},{5,4},{6,7},{7,6},{8,9},{9,8},{10,11... | collective-permute-start | bytes 3538952 | tf_op jit(solution)/shard_map/ppermute | solution.py:27
  340.4 55.9 %collective-permute-start.61 = (bf16[4,208,768]{2,1,0:T(8,128)(2,1)}, bf16[4,208,768]{2,1,0:T(8,128)(2,1)S(1)}, u32[]{:S(2)}, u32[]{:S(2)}) collective-permute-start(bf16[4,208,768]{2,1,0:T(8,128)(2,1)} %get-tuple-element.334), channel_id=1, source_target_pairs={{0,1},{1,0},{2,3},{3,2},{4,5},{5,4},{6,7},{7,6},{8,9},{9,8},{10,11... | collective-permute-start | bytes 3833864 | tf_op jit(solution)/shard_map/ppermute | solution.py:27
  368.4 9.7 %collective-permute-start.54 = (bf16[512,384]{1,0:T(8,128)(2,1)S(1)}, bf16[512,384]{1,0:T(8,128)(2,1)S(1)}, u32[]{:S(2)}, u32[]{:S(2)}) collective-permute-start(bf16[512,384]{1,0:T(8,128)(2,1)S(1)} %add_convert_fusion.5), channel_id=1, source_target_pairs={{0,16},{8,24},{16,0},{24,8},{1,17},{9,25},{17,1},{25,9},{2,18},{10... | collective-permute-start | bytes 1179656 | tf_op jit(solution)/shard_map/ppermute | solution.py:27
  383.9 40.9 %collective-permute-start.74 = (bf16[1,192,1536]{2,1,0:T(8,128)(2,1)}, bf16[1,192,1536]{2,1,0:T(8,128)(2,1)}, u32[]{:S(2)}, u32[]{:S(2)}) collective-permute-start(bf16[1,192,1536]{2,1,0:T(8,128)(2,1)} %constant_dynamic-slice_fusion), channel_id=1, source_target_pairs={{0,4},{1,5},{2,6},{3,7},{4,0},{5,1},{6,2},{7,3},{8,12},{9,13},{10,... | collective-permute-start | bytes 1769480 | tf_op jit(solution)/shard_map/ppermute | solution.py:27
  383.9 53.5 %collective-permute-start.73 = (bf16[1,192,1536]{2,1,0:T(8,128)(2,1)}, bf16[1,192,1536]{2,1,0:T(8,128)(2,1)}, u32[]{:S(2)}, u32[]{:S(2)}) collective-permute-start(bf16[1,192,1536]{2,1,0:T(8,128)(2,1)} %constant_dynamic-slice_fusion.1), channel_id=1, source_target_pairs={{0,4},{1,5},{2,6},{3,7},{4,0},{5,1},{6,2},{7,3},{8,12},{9,13},{10,... | collective-permute-start | bytes 1769480 | tf_op jit(solution)/shard_map/ppermute | solution.py:27
  386.9 58.8 %collective-permute-start.55 = (bf16[256,1536]{1,0:T(8,128)(2,1)}, bf16[256,1536]{1,0:T(8,128)(2,1)}, u32[]{:S(2)}, u32[]{:S(2)}) collective-permute-start(bf16[256,1536]{1,0:T(8,128)(2,1)} %get-tuple-element.321), channel_id=1, source_target_pairs={{0,8},{8,0},{16,24},{24,16},{1,9},{9,1},{17,25},{25,17},{2,10},{10... | collective-permute-start | bytes 2359304 | tf_op jit(solution)/shard_map/ppermute | solution.py:27
  403.8 41.5 %collective-permute-start.71 = (bf16[2,192,768]{2,1,0:T(8,128)(2,1)S(1)}, bf16[2,192,768]{2,1,0:T(8,128)(2,1)S(1)}, u32[]{:S(2)}, u32[]{:S(2)}) collective-permute-start(bf16[2,192,768]{2,1,0:T(8,128)(2,1)S(1)} %dynamic-slice_bitcast_fusion.1), channel_id=1, source_target_pairs={{0,2},{1,3},{2,0},{3,1},{4,6},{5,7},{6,4},{7,5},{8,10},{9,11},{10,... | collective-permute-start | bytes 1769480 | tf_op jit(solution)/shard_map/ppermute | solution.py:27
  404.4 64.9 %collective-permute-start.64 = (bf16[4,192,768]{2,1,0:T(8,128)(2,1)}, bf16[4,192,768]{2,1,0:T(8,128)(2,1)S(1)}, u32[]{:S(2)}, u32[]{:S(2)}) collective-permute-start(bf16[4,192,768]{2,1,0:T(8,128)(2,1)} %get-tuple-element.344), channel_id=1, source_target_pairs={{0,1},{1,0},{2,3},{3,2},{4,5},{5,4},{6,7},{7,6},{8,9},{9,8},{10,11... | collective-permute-start | bytes 3538952 | tf_op jit(solution)/shard_map/ppermute | solution.py:27
  424.9 44.4 %collective-permute-start.63 = (bf16[2,192,1152]{2,1,0:T(8,128)(2,1)S(1)}, bf16[2,192,1152]{2,1,0:T(8,128)(2,1)S(1)}, u32[]{:S(2)}, u32[]{:S(2)}) collective-permute-start(bf16[2,192,1152]{2,1,0:T(8,128)(2,1)S(1)} %dynamic-slice_bitcast_fusion), channel_id=1, source_target_pairs={{0,2},{1,3},{2,0},{3,1},{4,6},{5,7},{6,4},{7,5},{8,10},{9,11},{10,... | collective-permute-start | bytes 2654216 | tf_op jit(solution)/shard_map/ppermute | solution.py:27
  445.5 12.7 %collective-permute-start.72 = (bf16[1,192,768]{2,1,0:T(8,128)(2,1)S(1)}, bf16[1,192,768]{2,1,0:T(8,128)(2,1)S(1)}, u32[]{:S(2)}, u32[]{:S(2)}) collective-permute-start(bf16[1,192,768]{2,1,0:T(8,128)(2,1)S(1)} %constant_dynamic-slice_fusion.2), channel_id=1, source_target_pairs={{0,4},{1,5},{2,6},{3,7},{4,0},{5,1},{6,2},{7,3},{8,12},{9,13},{10,... | collective-permute-start | bytes 884744 | tf_op jit(solution)/shard_map/ppermute | solution.py:27
  446.8 13.0 %collective-permute-start.56 = (bf16[128,1536]{1,0:T(8,128)(2,1)S(1)}, bf16[128,1536]{1,0:T(8,128)(2,1)S(1)}, u32[]{:S(2)}, u32[]{:S(2)}) collective-permute-start(bf16[128,1536]{1,0:T(8,128)(2,1)S(1)} %add_convert_fusion.4), channel_id=1, source_target_pairs={{0,16},{8,24},{16,0},{24,8},{1,17},{9,25},{17,1},{25,9},{2,18},{10... | collective-permute-start | bytes 1179656 | tf_op jit(solution)/shard_map/ppermute | solution.py:27
  461.0 30.1 %collective-permute-start.57 = (bf16[128,768]{1,0:T(8,128)(2,1)S(1)}, bf16[128,768]{1,0:T(8,128)(2,1)S(1)}, u32[]{:S(2)}, u32[]{:S(2)}) collective-permute-start(bf16[128,768]{1,0:T(8,128)(2,1)S(1)} %pad_maximum_fusion.12), channel_id=1, source_target_pairs={{0,16},{8,24},{16,0},{24,8},{1,17},{9,25},{17,1},{25,9},{2,18},{10... | collective-permute-start | bytes 589832 | tf_op jit(solution)/shard_map/ppermute | solution.py:27
  469.6 34.3 %collective-permute-start.68 = (bf16[1,192,1152]{2,1,0:T(8,128)(2,1)S(1)}, bf16[1,192,1152]{2,1,0:T(8,128)(2,1)S(1)}, u32[]{:S(2)}, u32[]{:S(2)}) collective-permute-start(bf16[1,192,1152]{2,1,0:T(8,128)(2,1)S(1)} %constant_dynamic-slice_fusion.4), channel_id=1, source_target_pairs={{0,4},{1,5},{2,6},{3,7},{4,0},{5,1},{6,2},{7,3},{8,12},{9,13},{10,... | collective-permute-start | bytes 1327112 | tf_op jit(solution)/shard_map/ppermute | solution.py:27
  473.3 5.8 %collective-permute-start.66 = (f32[2,6,48]{2,0,1:T(2,128)S(1)}, f32[2,6,48]{2,0,1:T(2,128)S(1)}, u32[]{:S(2)}, u32[]{:S(2)}) collective-permute-start(f32[2,6,48]{2,0,1:T(2,128)S(1)} %bitcast.134), channel_id=1, source_target_pairs={{0,2},{1,3},{2,0},{3,1},{4,6},{5,7},{6,4},{7,5},{8,10},{9,11},{10,... | collective-permute-start | bytes 6920 | tf_op jit(solution)/shard_map/ppermute | solution.py:27
  479.1 12.0 %collective-permute-start.67 = (f32[1,6,48]{2,0,1:T(1,128)S(1)}, f32[1,6,48]{2,0,1:T(1,128)S(1)}, u32[]{:S(2)}, u32[]{:S(2)}) collective-permute-start(f32[1,6,48]{2,0,1:T(1,128)S(1)} %constant_dynamic-slice_fusion.5), channel_id=1, source_target_pairs={{0,4},{1,5},{2,6},{3,7},{4,0},{5,1},{6,2},{7,3},{8,12},{9,13},{10,... | collective-permute-start | bytes 3464 | tf_op jit(solution)/shard_map/ppermute | solution.py:27
  482.4 21.2 %collective-permute-start.69 = (bf16[2,192,768]{2,1,0:T(8,128)(2,1)S(1)}, bf16[2,192,768]{2,1,0:T(8,128)(2,1)S(1)}, u32[]{:S(2)}, u32[]{:S(2)}) collective-permute-start(bf16[2,192,768]{2,1,0:T(8,128)(2,1)S(1)} %dynamic-slice_bitcast_fusion.2), channel_id=1, source_target_pairs={{0,2},{1,3},{2,0},{3,1},{4,6},{5,7},{6,4},{7,5},{8,10},{9,11},{10,... | collective-permute-start | bytes 1769480 | tf_op jit(solution)/shard_map/ppermute | solution.py:27
  503.8 15.3 %collective-permute-start.70 = (bf16[1,192,768]{2,1,0:T(8,128)(2,1)S(1)}, bf16[1,192,768]{2,1,0:T(8,128)(2,1)S(1)}, u32[]{:S(2)}, u32[]{:S(2)}) collective-permute-start(bf16[1,192,768]{2,1,0:T(8,128)(2,1)S(1)} %constant_dynamic-slice_fusion.3), channel_id=1, source_target_pairs={{0,4},{1,5},{2,6},{3,7},{4,0},{5,1},{6,2},{7,3},{8,12},{9,13},{10,... | collective-permute-start | bytes 884744 | tf_op jit(solution)/shard_map/ppermute | solution.py:27
  (100 other events, 934.1 us)

commit v3 on v2

--- a/solution.py
+++ b/solution.py
@@ -232,8 +232,8 @@
 
 
 def backward_body(span, q, kv0, kv1, kv2, tk, tv, qlab, klab, w_out, out, lse,
-                  g0, g1, g2, g3, dq, to_prev, kept, to_next, dtk, dtv,
-                  og, keys, vals, tkeys, ak, av):
+                  g0, g1, g2, g3, dq, to_prev, kept, to_next, times,
+                  og, keys, vals, tkeys, ak, av, dtk, dtv):
     rows, size = q.shape
     group = rows // HEAD_SIZE
     pieces = size // TILE
@@ -287,6 +287,9 @@
         state = lax.fori_loop(span[2 * tile], span[2 * tile + 1], step, tuple(state))
         for g in range(group):
             dq[head_rows(g), cols] = state[g]
+    for at, column in ((0, dtk), (1, dtv)):
+        spread = jnp.broadcast_to(column[...], (rows, 2 * HEAD_SIZE))
+        times[at : at + 1, :] = spread.T[:1, :]
     for part, dest in enumerate((to_prev, kept, to_next)):
         for piece in range(pieces):
             at = slice(piece * TILE, (piece + 1) * TILE)
@@ -336,12 +339,13 @@
     return pl.pallas_call(
         backward_body,
         in_specs=[pl.BlockSpec(memory_space=pltpu.SMEM)] + [vmem] * 15,
-        out_specs=[vmem] * 6,
+        out_specs=[vmem] * 5,
         out_shape=[wide(cols, size), low(2, cols, size), wide(2, cols, size), low(2, cols, size),
-                   wide(cols, 1), wide(cols, 1)],
+                   wide(2, cols)],
         scratch_shapes=[pltpu.VMEM((cols, size), BF16), pltpu.VMEM((3 * size, cols), BF16),
                         pltpu.VMEM((3 * size, cols), BF16), pltpu.VMEM((tiles, cols, TILE), BF16),
-                        pltpu.VMEM((tiles, cols, TILE), F32), pltpu.VMEM((tiles, cols, TILE), F32)],
+                        pltpu.VMEM((tiles, cols, TILE), F32), pltpu.VMEM((tiles, cols, TILE), F32),
+                        pltpu.VMEM((cols, 1), F32), pltpu.VMEM((cols, 1), F32)],
         name="attend_back", cost_estimate=FREE,
     )(span, q, *kvs, tk, tv, qlab, klab, w_out, out, lse, *grads)
 
@@ -708,20 +712,23 @@
     )(side, *lefts, *rights)
 
 
-def meet_cols_body(size, side, p0, p1, p2, p3, a, a_pair, b, b_pair, keep, send):
+def meet_cols_body(size, side, p0, p1, p2, p3, *refs):
     own, pair = (jnp.concatenate([p[i] for p in (p0, p1, p2, p3)], 1) for i in (0, 1))
-    width = a.shape[1]
-    for left, (right, right_pair) in ((0, (a, a_pair)), (width, (b, b_pair))):
-        made = (dot_nn(own, right[...]) + dot_nn(pair, right_pair[...])).astype(BF16)
-        cols = pl.ds(left, width)
-        deal_rows(made, size, side[0], keep.at[:, cols], send.at[:, cols])
+    *rights, keep, send = refs
+    width = rights[0].shape[1]
+    for at in range(len(rights) // 2):
+        made = dot_nn(own, rights[2 * at][...]) + dot_nn(pair, rights[2 * at + 1][...])
+        cols = pl.ds(at * width, width)
+        deal_rows(made.astype(BF16), size, side[0], keep.at[:, cols], send.at[:, cols])
 
 
 def meet_cols(size, side, near, rights):
-    half = jax.ShapeDtypeStruct((near[0].shape[1] // 2, 2 * rights[0].shape[1]), BF16)
+    width = rights[0].shape[1] * (len(rights) // 2)
+    half = jax.ShapeDtypeStruct((near[0].shape[1] // 2, width), BF16)
+    vmem = pl.BlockSpec(memory_space=pltpu.VMEM)
     return pl.pallas_call(
         functools.partial(meet_cols_body, size),
-        in_specs=[pl.BlockSpec(memory_space=pltpu.SMEM)] + [pl.BlockSpec(memory_space=pltpu.VMEM)] * 8,
+        in_specs=[pl.BlockSpec(memory_space=pltpu.SMEM)] + [vmem] * (4 + len(rights)),
         out_shape=[half] * 2,
         name="meet_cols", cost_estimate=FREE,
     )(side, *near, *rights)
@@ -787,8 +794,8 @@
                 out[1][d // 2, at, cols] = even
 
     send_a[:, rows:, :] = jnp.zeros((devices // 2, send_a.shape[1] - rows, half), BF16)
-    row = jnp.broadcast_to(times[...], (times.shape[0], 2 * HEAD_SIZE)).T[:1, :]
-    send_a[0, rows : rows + 1, :] = row.astype(BF16)
+    for at in (0, 1):
+        send_a[0, rows : rows + 1, at * part : (at + 1) * part] = times[at : at + 1, :].astype(BF16)
     put(dot_tn(full(fronts), own(backs)), 0, 0, (keep_a, send_a))
     count = context.shape[0]
     put(dot_tn(context[...], kv[:count, :]), 0, part, (keep_a, send_a))
@@ -1021,7 +1028,7 @@
     )
     three_got, _, three_far = scatter_near(three_away, three_low)
     hidden_got_b = swap(after(hidden_away_b, three_low), "seq", 1)
-    lifted_got_a = swap(after(lifted_a, three_far), "seq", 1)
+    lifted_got_a = swap(after(lifted_a, three_low), "seq", 1)
     flip_late, flip_far_late, gate_late = after((flip_both, flip_far, gate_b), three_far)
     flip_mate, flip_far_mate = swap(flip_late, "tensor", 1), swap(flip_far_late, "tensor", 1)
     gate_got_b = swap(gate_late, "seq", 1)
@@ -1053,9 +1060,8 @@
     one_parts = (
         grad_one, swap(grad_one, "tensor", 1), one_far_rows, swap(one_far_rows, "tensor", 1)
     )
-    *one_parts, front_other, context_got, gate_got_b, lifted_got_a = meeting(
-        *one_parts, swap(after(front_both, grad_one), "tensor", 1), context_got,
-        gate_got_b, lifted_got_a,
+    *one_parts, front_other, context_got, lifted_got_a = meeting(
+        *one_parts, swap(after(front_both, grad_one), "tensor", 1), context_got, lifted_got_a
     )
     context_low = (
         context_parts[2].astype(F32) + context_got[context_parts[2].shape[0] :].astype(F32)
@@ -1063,25 +1069,26 @@
     context_far = swap(context_low, "tensor", 2)
     back_far = swap(after(back_rows, one_parts[3]), "tensor", 2)
     lifted_got_b = swap(after(lifted_b, grad_one), "seq", 1)
-    query_grad, to_prev, kept, to_next, time_key_grad, time_value_grad = attend_back(
+    query_grad, to_prev, kept, to_next, time_grads = attend_back(
         spans, queries, (behind, both, ahead), time_keys, time_values, label_row, label_column,
         w_out, attended, log_totals, one_parts,
     )
-    to_prev, to_next, back_far, lifted_got_b, down_got, context_far = meeting(
-        to_prev, to_next, back_far, lifted_got_b, down_got, context_far
+    to_prev, to_next, back_far, gate_got_b, lifted_got_b, down_got, context_far = meeting(
+        to_prev, to_next, back_far, gate_got_b, lifted_got_b, down_got, context_far
     )
     from_next, from_prev = shift(to_prev, "seq", -1), shift(to_next, "seq", 1)
     down_keep, down_got = halve(added(down_keep, down_got).astype(BF16), 2)
     flip_near = (flip_both, flip_mate, flip_far, flip_far_mate)
-    first_keep, first_got = traded(
-        meet_cols(rows, level_side, flip_near, after((gate_a, gate_got_a, lifted_a, lifted_got_a), to_prev))
-    )
-    second_keep, second_got = traded(
+    both_keep, both_got = traded(
         meet_cols(
-            rows, level_side, flip_near, (gate_b, gate_got_b, lifted_b, lifted_got_b)
+            rows, level_side, flip_near,
+            after(
+                (gate_a, gate_got_a, lifted_a, lifted_got_a, gate_b, gate_got_b, lifted_b,
+                 lifted_got_b),
+                to_prev,
+            ),
         )
     )
-    down_away, down_own, down_low = down_parts(after(hidden_a, to_prev), hidden_b, w_down)
     back_both = jnp.stack([back_rows, back_far])
     back_other = swap(back_both, "tensor", 1)
     context_own = (
@@ -1089,11 +1096,10 @@
         + context_got[: context_far.shape[0]].astype(F32)
         + context_far.astype(F32)
     )
-    time_both = jnp.concatenate([time_key_grad, time_value_grad], 0)
     keep_a, send_a, keep_b, send_b = bundle_grads(
         count, places, (front_both, front_other), (back_both, back_other), one_parts, attended,
         row_context,
-        context_own.astype(BF16), time_both,
+        context_own.astype(BF16), time_grads,
     )
     from_next, from_prev, down_got, send_a, send_b = meeting(
         from_next, from_prev, down_got, send_a, send_b
@@ -1107,45 +1113,43 @@
     last_sum = (
         last_low.astype(F32) + last_got[local_rows:].astype(F32)
     ).astype(BF16)
-    last_sum, first_got, second_got = meeting(last_sum, first_got, second_got)
-    first_keep, first_got = halve(added(first_keep, first_got).astype(BF16), 2)
-    second_keep, second_got = halve(added(second_keep, second_got).astype(BF16), 2)
-    last_far = swap(last_sum, "tensor", 2)
+    last_far, both_got = meeting(swap(last_sum, "tensor", 2), both_got)
+    both_keep, both_got = halve(added(both_keep, both_got).astype(BF16), 2)
     frame_grad = last_own + last_got[:local_rows].astype(F32) + last_far.astype(F32)
 
-    def to_frames(rows, weight):
-        return jnp.einsum("fn,df->nd", rows, weight, preferred_element_type=F32)
-
-    time_key_grad, time_value_grad = after((time_key_grad, time_value_grad), from_next)
-    time_grad = to_frames(time_key_grad.astype(BF16), w_key) + to_frames(
-        time_value_grad.astype(BF16), w_value
-    )
-    own_scaled = (frames.astype(F32) - means_one) * inverse_one
+    time_late, means_late, inverse_late, vectors_late = after(
+        (time_grads, means_one, inverse_one, norm_vectors), last_far
+    )
+    time_grad = sum(
+        jnp.einsum("of,df->od", time_late[i : i + 1].astype(BF16), w, preferred_element_type=F32)
+        for i, w in enumerate((w_key, w_value))
+    )
+    own_scaled = (frames.astype(F32) - means_late) * inverse_late
     scaled_grad = frame_grad * gain_attn[None]
     sums = jnp.concatenate(
         [
             jnp.sum(scaled_grad, -1),
             jnp.sum(scaled_grad * own_scaled, -1),
             time_grad[0],
-            norm_vectors.reshape(-1),
+            vectors_late.reshape(-1),
         ]
     )[None]
     sums = sums + swap(sums, "tensor", 1)
     sums = sums + swap(sums, "tensor", 2)
     sums, got_a, raw_got = meeting(sums, got_a, raw_got)
     got_b = swap(after(send_b, got_a), "seq", 1)
-    time_both = time_both + got_a[0, rows, :, None].astype(F32)
+    time_both = time_grads.reshape(1, -1) + got_a[0, rows : rows + 1].astype(F32)
     left_keep, left_got = halve(added(keep_a, got_a[:, :rows]).astype(BF16), 1)
     plain = sums[0, :local_rows, None] / model_width
     cross = sums[0, local_rows : 2 * local_rows, None] / model_width
     vectors = own_cols(sums[0, 2 * local_rows :].reshape(5, model_width))
     attend_full = ordered(*[after(one_parts, from_next)[i] for i in (0, 2, 1, 3)], 0)
-    d_frames = own_cols(attend_full).astype(F32) + inverse_one * (
+    d_frames = own_cols(attend_full).astype(F32) + inverse_late * (
         scaled_grad - plain - own_scaled * cross
     )
     d_gain_attn = jnp.sum(frame_grad * own_scaled, 0) + vectors[0] * own_cols(scaled_time)[0]
     d_bias_attn = jnp.sum(frame_grad, 0) + vectors[0]
-    down_away, down_low = after((down_away, down_low), last_far)
+    down_away, down_own, down_low = down_parts(after(hidden_a, last_far), hidden_b, w_down)
     branch_got, _, branch_far = scatter_near(down_away, down_low)
     block_rows = (
         residual_two + down_own + branch_got[:share].astype(F32) + branch_far.astype(F32)
@@ -1163,15 +1167,16 @@
 
     normed_pair = (one_own_half, normed_got)
     grad_down = halve_end(down_keep, down_got, 3)
-    first, second = halve_end(first_keep, first_got, 3), halve_end(second_keep, second_got, 3)
-    units = first.shape[1] // 2
-    grad_gate_w = jnp.concatenate([first[:, :units], second[:, :units]], 1)
-    grad_up_w = jnp.concatenate([first[:, units:], second[:, units:]], 1)
+    gate_up = halve_end(both_keep, both_got, 3)
+    units = gate_up.shape[1] // 4
+    gate_a, up_a, gate_b, up_b = (gate_up[:, i * units : (i + 1) * units] for i in range(4))
+    grad_gate_w = jnp.concatenate([gate_a, gate_b], 1)
+    grad_up_w = jnp.concatenate([up_a, up_b], 1)
     raw_pair = (raw, raw_got)
     own_time_rows = lax.dynamic_index_in_dim(
         time_column.reshape(count // 2, 2, -1), column, 1, False
     ).reshape(-1, 1)
-    outer = own_time_rows * jnp.concatenate([jnp.zeros((head_cols, 1), F32), time_both], 0).T
+    outer = own_time_rows * jnp.concatenate([jnp.zeros((1, head_cols), F32), time_both], 1)
     blocks = sum(
         jnp.einsum("dn,fn->df", r, c, preferred_element_type=F32)
         for r, c in zip(normed_pair, raw_pair)
@@ -1182,16 +1187,17 @@
     heads_got, got_b = meeting(heads_got, got_b)
     heads_next = added(heads_keep, heads_got).astype(BF16)
     heads_sum = halve_all(heads_next, 2)
+    last_next = added(*halve(added(keep_b, got_b).astype(BF16), 1))
     small = jnp.stack(
         [d_gain_attn, d_bias_attn, vectors[3], vectors[4], vectors[1], vectors[2]]
     ).reshape(6, devices, -1).transpose(1, 0, 2)
-    small = after(small, heads_next)
+    small = after(small, last_next)
     bit = 0
     while small.shape[0] > 1:
         small = added(*halve(small, bit))
         bit += 1
     small = small[0]
-    left, right = halve_end(left_keep, left_got, 2), halve_end(keep_b, got_b, 1)
+    left, right = halve_end(left_keep, left_got, 2), halve_all(last_next, 2)
     part, rows = head_cols // count, model_width // count
     grad_c_query = left[:, :head_cols]
     grad_c_key, grad_c_value = left[: rows // 2, head_cols:], left[rows // 2 :, head_cols:]

time: 532 us -> 596 us (1.12)
  waiting for transfers between devices: 198 us -> 267 us
    ppermute x71 -> x69, waiting for transfers between devices: 180 us -> 247 us  [swap(): lax.ppermute(value, axis, [(i, i ^ by) for i in range(lax.axis_size(axis))])]
    pallas_call x2 -> x1, Pallas kernels: 15.4 us -> 13.1 us  [meet_cols(): pl.pallas_call(functools.partial(meet_cols_body, size), in_specs=[pl.Bloc...]
    ppermute x71 -> x69, starting transfers between devices: 65.6 us -> 65 us  [swap(): lax.ppermute(value, axis, [(i, i ^ by) for i in range(lax.axis_size(axis))])]
  transfers between devices with their start and end apart: 75 -> 73, of which waited for: 31 -> 26; matrix products, arithmetic and copies ran while one was open for 13% -> 12% of each run, Pallas kernels for 31% -> 27%
where the time goes in v3:
time: 596 us; the launch traced here: 584 us
  waiting for transfers between devices  267 us (45%)
  Pallas kernels  159 us (27%)
  starting transfers between devices  75.5 us (13%)
  other arithmetic  41.6 us (7%)
  local copies, waits for them, and re-layouts  34.3 us (6%)
    ppermute x69, waiting for transfers between devices, swap(): lax.ppermute(value, axis, [(i, i ^ by) for i in range(lax.axis_size(axis))])  247 us
    ppermute x69, starting transfers between devices, swap(): lax.ppermute(value, axis, [(i, i ^ by) for i in range(lax.axis_size(axis))])  65 us
    pallas_call x2, Pallas kernels, ffn(): pl.pallas_call(functools.partial(ffn_second_body if half else ffn_first_b...  29.5 us
    pallas_call x1, Pallas kernels, cross_backward(): pl.pallas_call(cross_backward_body, grid=(1,), out_shape=[jax.ShapeDtypeS...  21 us
    ppermute x4, waiting for transfers between devices, shift(): return lax.ppermute(value, axis, pairs)  19.9 us
    pallas_call x1, Pallas kernels, attend_back(): pl.pallas_call(backward_body, in_specs=[pl.BlockSpec(memory_space=pltpu.S...  17.9 us
    pallas_call x1, Pallas kernels, cross_forward(): pl.pallas_call(functools.partial(cross_forward_body, width // devices), g...  16.8 us
    pallas_call x1, Pallas kernels, meet_cols(): pl.pallas_call(functools.partial(meet_cols_body, size), in_specs=[pl.Bloc...  13.1 us
  transfers between devices with their start and end apart: 73, of which 26 were waited for; matrix products, arithmetic and copies ran while one was open for 12% of the time, Pallas kernels for 27%

profile of v3, /device:TPU:0, one launch (start us, length us, event | category | flops | bytes accessed | tf_op | source)
XLA Modules:
  0.0 583.8 jit_solution(18114772314585923402)
XLA Ops:
  1.2 2.6 collective-permute-start.1
  11.5 2.2 collective-permute-done.1.x2
  14.8 1.7 collective-permute-start.6
  22.1 48.3 %collective-permute-done.4.g2 = f32[6,384]{1,0:T(8,128)S(1)} collective-permute-done((f32[6,384]{1,0:T(8,128)S(1)}, f32[6,384]{1,0:T(8,128)S(1)}, u32[]{:S(2)}, u32[]{:S(2)}) %collective-permute-start.4) | collective-permute-done | bytes 9248 | tf_op jit(solution)/shard_map/ppermute | solution.py:27
  72.3 9.6 %front.1 = (bf16[384,512]{1,0:T(8,128)(2,1)}, bf16[2,384,512]{2,1,0:T(8,128)(2,1)}, bf16[128,1536]{1,0:T(8,128)(2,1)}, bf16[512,1536]{1,0:T(8,128)(2,1)}, bf16[7...) custom-call(s32[2]{0:T(128)} %rev.4.place, ...), custom_call_target="tpu_custom_call" | custom-call | flops 1 | bytes 1 | tf_op jit(solution)/shard_map/front/pallas_call | solution.py:885
  81.9 2.5 collective-permute-start.7
  88.4 10.4 %attend_near.1 = (f32[6,512]{1,0:T(8,128)}, f32[6,512]{1,0:T(8,128)}, f32[384,512]{1,0:T(8,128)}) custom-call(s32[5]{0:T(128)} %pad_add_fusion.2.span, bf16[384,512]{1,0:T(8,128)(2,1)} %get-tuple-element.188.q, bf16[2,384,512]{2,1,0:T(8,128)(2,1)} %get-tuple-element.191.kv.kv1, f32[384,1]{1,0:T(8,128)} %get-tuple-element.194.tk, ...), custom_call_target="tpu_custom_call" | custom-call | flops 1 | bytes 1 | tf_op jit(solution)/shard_map/attend_near/pallas_call | solution.py:304
  98.8 19.9 %collective-permute-done.7.kv0 = bf16[2,384,512]{2,1,0:T(8,128)(2,1)S(1)} collective-permute-done((bf16[2,384,512]{2,1,0:T(8,128)(2,1)}, bf16[2,384,512]{2,1,0:T(8,128)(2,1)S(1)}, u32[]{:S(2)}, u32[]{:S(2)}) %collective-permute-start.7) | collective-permute-done | bytes 786464 | tf_op jit(solution)/shard_map/ppermute | solution.py:33
  121.3 8.8 %attend_far.1 = (bf16[384,512]{1,0:T(8,128)(2,1)}, f32[6,512]{1,0:T(8,128)}, bf16[256,1536]{1,0:T(8,128)(2,1)}, f32[128,1536]{1,0:T(8,128)}, bf16[128,1536]{1,0:T(8,128)(2,1)}) custom-call(s32[5]{0:T(128)} %pad_add_fusion.2.span, bf16[384,512]{1,0:T(8,128)(2,1)} %get-tuple-element.188.q, bf16[2,384,512]{2,1,0:T(8,128)(2,1)} %copy-done.19, ...), custom_call_target="tpu_custom_call" | custom-call | flops 1 | bytes 1 | tf_op jit(solution)/shard_map/attend_far/pallas_call | solution.py:322
  130.2 2.5 collective-permute-done.16.got
  134.8 5.9 %collective-permute-start.19 = (bf16[768,512]{1,0:T(8,128)(2,1)}, bf16[768,512]{1,0:T(8,128)(2,1)S(1)}, u32[]{:S(2)}, u32[]{:S(2)}) collective-permute-start(bf16[768,512]{1,0:T(8,128)(2,1)} %get-tuple-element.224), channel_id=1, source_target_pairs={{0,1},{1,0},{2,3},{3,2},{4,5},{5,4},{6,7},{7,6},{8,9},{9,8},{10,11... | collective-permute-start | bytes 2359304 | tf_op jit(solution)/shard_map/ppermute | solution.py:27
  140.7 4.6 collective-permute-done.17.far
  145.9 1.7 collective-permute-done.18
  148.5 16.8 %cross.1 = (bf16[128,3072]{1,0:T(8,128)(2,1)}, bf16[128,1536]{1,0:T(8,128)(2,1)}, f32[128,1536]{1,0:T(8,128)}, f32[128,1536]{1,0:T(8,128)}, bf16[128,1536]{1,0:T...) custom-call(s32[2]{0:T(128)} %copy-done.70, bf16[128,1536]{1,0:T(8,128)(2,1)} %get-tuple-element.187.rows, ...), custom_call_target="tpu_custom_call" | custom-call | flops 1 | bytes 1 | tf_op jit(solution)/shard_map/cross/pallas_call | solution.py:526
  167.4 9.4 %collective-permute-done.22.n2 = bf16[128,1536]{1,0:T(8,128)(2,1)S(1)} collective-permute-done((bf16[128,1536]{1,0:T(8,128)(2,1)}, bf16[128,1536]{1,0:T(8,128)(2,1)S(1)}, u32[]{:S(2)}, u32[]{:S(2)}) %collective-permute-start.22) | collective-permute-done | bytes 393248 | tf_op jit(solution)/shard_map/ppermute | solution.py:27
  177.2 1.7 collective-permute-done.23.n3
  180.5 5.9 %collective-permute-start.26 = (bf16[768,128]{1,0:T(8,128)(2,1)}, bf16[768,128]{1,0:T(8,128)(2,1)}, u32[]{:S(2)}, u32[]{:S(2)}) collective-permute-start(bf16[768,128]{1,0:T(8,128)(2,1)} %get-tuple-element.238), channel_id=1, source_target_pairs={{0,1},{1,0},{2,3},{3,2},{4,5},{5,4},{6,7},{7,6},{8,9},{9,8},{10,11... | collective-permute-start | bytes 589832 | tf_op jit(solution)/shard_map/ppermute | solution.py:27
  188.9 14.7 %ffn.2 = (bf16[512,768]{1,0:T(8,128)(2,1)}, bf16[384,512]{1,0:T(8,128)(2,1)}, bf16[384,512]{1,0:T(8,128)(2,1)}, bf16[512,768]{1,0:T(8,128)(2,1)}, bf16[512,768]{...) custom-call(s32[2]{0:T(128)} %copy-done.70, ...), custom_call_target="tpu_custom_call" | custom-call | flops 1 | bytes 1 | tf_op jit(solution)/shard_map/ffn/pallas_call | solution.py:615
  205.2 14.8 %ffn.3 = (bf16[512,768]{1,0:T(8,128)(2,1)}, bf16[384,512]{1,0:T(8,128)(2,1)}, bf16[384,512]{1,0:T(8,128)(2,1)}, bf16[512,768]{1,0:T(8,128)(2,1)}, bf16[512,768]{...) custom-call(s32[2]{0:T(128)} %copy-done.70, ...), custom_call_target="tpu_custom_call" | custom-call | flops 1 | bytes 1 | tf_op jit(solution)/shard_map/ffn/pallas_call | solution.py:615
  220.2 2.5 collective-permute-done.30.got
  224.0 1.6 collective-permute-start.31
  225.6 2.0 collective-permute-start.32
  227.6 7.6 %collective-permute-done.31.far = bf16[128,1536]{1,0:T(8,128)(2,1)S(1)} collective-permute-done((bf16[128,1536]{1,0:T(8,128)(2,1)S(1)}, bf16[128,1536]{1,0:T(8,128)(2,1)S(1)}, u32[]{:S(2)}, u32[]{:S(2)}) %collective-permute-start.31) | collective-permute-done | bytes 393248 | tf_op jit(solution)/shard_map/ppermute | solution.py:27
  237.3 21.0 %cross_back.1 = (bf16[128,3072]{1,0:T(8,128)(2,1)}, bf16[256,1536]{1,0:T(8,128)(2,1)}, f32[4,1536]{1,0:T(4,128)}, bf16[128,1536]{1,0:T(8,128)(2,1)}) custom-call(f32[128,1536]{1,0:T(8,128)} %get-tuple-element.240.own, bf16[256,1536]{1,0:T(8,128)(2,1)} %copy-done.21, bf16[128,1536]{1,0:T(8,128)(2,1)} %copy-done.53, ...), custom_call_target="tpu_custom_call" | custom-call | flops 1 | bytes 1 | tf_op jit(solution)/shard_map/cross_back/pallas_call | solution.py:680
  258.5 2.1 collective-permute-start.41
  263.8 6.9 %meet_rows.1 = (bf16[384,1536]{1,0:T(8,128)(2,1)}, bf16[384,1536]{1,0:T(8,128)(2,1)}) custom-call(s32[1]{0:T(128)} %bitcast.12.side, bf16[384,512]{1,0:T(8,128)(2,1)} %get-tuple-element.261.own_a, bf16[384,512]{1,0:T(8,128)(2,1)} %copy-done.46, bf16[384,512]{1,0:T(8,128)(2,1)} %get-tuple-element.263.own_b, bf16[384,512]{1,0:T(8,128)(2,1)} %collective-permute-done.33.pair_b, ...), custom_call_target="tpu_custom_call" | custom-call | flops 1 | bytes 1 | tf_op jit(solution)/shard_map/meet_rows/pallas_call | solution.py:705
  272.0 7.0 %collective-permute-done.41.refs_3_ = bf16[512,768]{1,0:T(8,128)(2,1)} collective-permute-done((bf16[512,768]{1,0:T(8,128)(2,1)}, bf16[512,768]{1,0:T(8,128)(2,1)}, u32[]{:S(2)}, u32[]{:S(2)}) %collective-permute-start.41) | collective-permute-done | bytes 786464 | tf_op jit(solution)/shard_map/ppermute | solution.py:27
  279.0 2.0 collective-permute-start.45
  281.3 1.8 collective-permute-start.44
  283.1 1.6 collective-permute-start.42
  286.3 17.9 %attend_back.1 = (f32[384,512]{1,0:T(8,128)}, bf16[2,384,512]{2,1,0:T(8,128)(2,1)}, f32[2,384,512]{2,1,0:T(8,128)}, bf16[2,384,512]{2,1,0:T(8,128)(2,1)}, f32[2,384]{1,0:T(2,128)}) custom-call(s32[5]{0:T(128)} %pad_add_fusion.2.span, bf16[384,512]{1,0:T(8,128)(2,1)} %get-tuple-element.188.q, bf16[2,384,512]{2,1,0:T(8,128)(2,1)} %copy-done.19, ...), custom_call_target="tpu_custom_call" | custom-call | flops 1 | bytes 1 | tf_op jit(solution)/shard_map/attend_back/pallas_call | solution.py:339
  304.2 12.8 %collective-permute-done.44.refs_7_ = bf16[512,768]{1,0:T(8,128)(2,1)} collective-permute-done((bf16[512,768]{1,0:T(8,128)(2,1)}, bf16[512,768]{1,0:T(8,128)(2,1)}, u32[]{:S(2)}, u32[]{:S(2)}) %collective-permute-start.44) | collective-permute-done | bytes 786464 | tf_op jit(solution)/shard_map/ppermute | solution.py:27
  320.7 5.4 collective-permute-start.48
  326.1 13.1 %meet_cols.1 = (bf16[384,3072]{1,0:T(8,128)(2,1)}, bf16[384,3072]{1,0:T(8,128)(2,1)}) custom-call(s32[1]{0:T(128)} %bitcast.12.side, bf16[2,768,128]{2,1,0:T(8,128)(2,1)} %copy-done.27, bf16[2,768,128]{2,1,0:T(8,128)(2,1)} %collective-permute-done.34.p1, bf16[2,768,128]{2,1,0:T(8,128)(2,1)} %copy-done.41, bf16[2,768,128]{2,1,0:T(8,128)(2,1)} %collective-permute-done.35.p3, ...), custom_call_target="tpu_custom_call" | custom-call | flops 1 | bytes 1 | tf_op jit(solution)/shard_map/meet_cols/pallas_call | solution.py:729
  339.2 1.9 add_convert_fusion.2
  342.4 1.8 add_convert_fusion.8.kv
  344.2 10.7 %bundle.1 = (bf16[4,192,768]{2,1,0:T(8,128)(2,1)}, bf16[4,208,768]{2,1,0:T(8,128)(2,1)}, bf16[4,192,768]{2,1,0:T(8,128)(2,1)}, bf16[4,192,768]{2,1,0:T(8,128)(2,1)}) custom-call(s32[2]{0:T(128)} %copy-done.70, bf16[2,128,3072]{2,1,0:T(8,128)(2,1)} %copy-done.4, bf16[2,128,3072]{2,1,0:T(8,128)(2,1)} %collective-permute-done.39.f13, ...), custom_call_target="tpu_custom_call" | custom-call | flops 1 | bytes 1 | tf_op jit(solution)/shard_map/bundle/pallas_call | solution.py:817
  354.9 48.1 %collective-permute-done.49 = bf16[1,192,1536]{2,1,0:T(8,128)(2,1)} collective-permute-done((bf16[1,192,1536]{2,1,0:T(8,128)(2,1)}, bf16[1,192,1536]{2,1,0:T(8,128)(2,1)}, u32[]{:S(2)}, u32[]{:S(2)}) %collective-permute-start.49) | collective-permute-done | bytes 589856 | tf_op jit(solution)/shard_map/ppermute | solution.py:27
  403.9 7.5 %tail.1 = (bf16[1152,512]{1,0:T(8,128)(2,1)}, bf16[1024,384]{1,0:T(8,128)(2,1)}, f32[512,384]{1,0:T(8,128)}, bf16[512,384]{1,0:T(8,128)(2,1)}) custom-call(s32[1]{0:T(128)} %bitcast.1.place, f32[384,512]{1,0:T(8,128)} %get-tuple-element.277.dq, f32[2,384,512]{2,1,0:T(8,128)} %get-tuple-element.278.kept, bf16[2,384,512]{2,1,0:T(8,128)(2,1)} %copy-done.33, ...), custom_call_target="tpu_custom_call" | custom-call | flops 1 | bytes 1 | tf_op jit(solution)/shard_map/tail/pallas_call | solution.py:392
  413.6 4.3 collective-permute-start.60
  419.6 1.6 collective-permute-start.52
  421.2 2.2 add_bitcast_fusion.1
  423.4 7.5 %collective-permute-done.52 = bf16[512,384]{1,0:T(8,128)(2,1)S(1)} collective-permute-done((bf16[512,384]{1,0:T(8,128)(2,1)S(1)}, bf16[512,384]{1,0:T(8,128)(2,1)S(1)}, u32[]{:S(2)}, u32[]{:S(2)}) %collective-permute-start.52) | collective-permute-done | bytes 393248 | tf_op jit(solution)/shard_map/ppermute | solution.py:27
  431.8 6.5 %down.1 = (bf16[256,1536]{1,0:T(8,128)(2,1)}, f32[128,1536]{1,0:T(8,128)}, bf16[128,1536]{1,0:T(8,128)(2,1)}) custom-call(bf16[512,768]{1,0:T(8,128)(2,1)} %get-tuple-element.318.first, bf16[512,768]{1,0:T(8,128)(2,1)} %get-tuple-element.319.second, bf16[1536,1536]{1,0:T(8,128)(2,1)} %down_w.5), custom_call_target="tpu_custom_call" | custom-call | flops 1 | bytes 1 | tf_op jit(solution)/shard_map/down/pallas_call | solution.py:753
  438.8 1.8 multiply_reduce_fusion
  441.2 2.6 fusion
  443.9 1.6 collective-permute-start.59
  446.6 3.4 collective-permute-start.72
  450.0 22.3 %collective-permute-done.61 = bf16[1152,512]{1,0:T(8,128)(2,1)} collective-permute-done((bf16[1152,512]{1,0:T(8,128)(2,1)}, bf16[1152,512]{1,0:T(8,128)(2,1)}, u32[]{:S(2)}, u32[]{:S(2)}) %collective-permute-start.61) | collective-permute-done | bytes 1179680 | tf_op jit(solution)/shard_map/ppermute | solution.py:27
  473.6 1.7 add_convert_fusion
  475.3 2.6 fusion.30
  489.6 2.0 collective-permute-start.62
  491.6 1.8 collective-permute-start.63
  494.1 2.6 multiply_add_fusion
  496.6 15.9 %collective-permute-done.70 = bf16[2,192,768]{2,1,0:T(8,128)(2,1)} collective-permute-done((bf16[2,192,768]{2,1,0:T(8,128)(2,1)}, bf16[2,192,768]{2,1,0:T(8,128)(2,1)}, u32[]{:S(2)}, u32[]{:S(2)}) %collective-permute-start.70) | collective-permute-done | bytes 589856 | tf_op jit(solution)/shard_map/ppermute | solution.py:27
  515.7 14.4 %collective-permute-done.71 = bf16[1,192,768]{2,1,0:T(8,128)(2,1)S(1)} collective-permute-done((bf16[1,192,768]{2,1,0:T(8,128)(2,1)S(1)}, bf16[1,192,768]{2,1,0:T(8,128)(2,1)S(1)}, u32[]{:S(2)}, u32[]{:S(2)}) %collective-permute-start.71) | collective-permute-done | bytes 294944 | tf_op jit(solution)/shard_map/ppermute | solution.py:27
  533.6 1.6 add_bitcast_fusion
  535.3 1.7 pad_maximum_fusion.2
  541.8 21.0 %collective-permute-done.64 = bf16[2,192,768]{2,1,0:T(8,128)(2,1)S(1)} collective-permute-done((bf16[2,192,768]{2,1,0:T(8,128)(2,1)S(1)}, bf16[2,192,768]{2,1,0:T(8,128)(2,1)S(1)}, u32[]{:S(2)}, u32[]{:S(2)}) %collective-permute-start.64) | collective-permute-done | bytes 589856 | tf_op jit(solution)/shard_map/ppermute | solution.py:27
  564.0 2.7 collective-permute-done.65
  567.8 3.3 collective-permute-done.66
  571.2 3.0 collective-permute-start.69
  574.1 4.6 collective-permute-done.67
  579.3 3.3 collective-permute-done.69
  (365 shorter events, 86.7 us)
Async XLA Ops:
  0.7 70.9 %collective-permute-start = (bf16[512,384]{1,0:T(8,128)(2,1)}, bf16[512,384]{1,0:T(8,128)(2,1)S(1)}, u32[]{:S(2)}, u32[]{:S(2)}) collective-permute-start(bf16[512,384]{1,0:T(8,128)(2,1)} %x0.1), channel_id=1, source_target_pairs={{0,8},{8,0},{16,24},{24,16},{1,9},{9,1},{17,25},{25,17},{2,10},{10... | collective-permute-start | bytes 1179656 | tf_op jit(solution)/shard_map/ppermute | solution.py:27
  1.2 12.5 %collective-permute-start.1 = (bf16[512,384]{1,0:T(8,128)(2,1)}, bf16[512,384]{1,0:T(8,128)(2,1)S(1)}, u32[]{:S(2)}, u32[]{:S(2)}) collective-permute-start(bf16[512,384]{1,0:T(8,128)(2,1)} %x0.1), channel_id=1, source_target_pairs={{0,16},{8,24},{16,0},{24,8},{1,17},{9,25},{17,1},{25,9},{2,18},{10... | collective-permute-start | bytes 1179656 | tf_op jit(solution)/shard_map/ppermute | solution.py:27
  7.9 11.9 %collective-permute-start.3 = (f32[6,384]{1,0:T(8,128)S(1)}, f32[6,384]{1,0:T(8,128)S(1)}, u32[]{:S(2)}, u32[]{:S(2)}) collective-permute-start(f32[6,384]{1,0:T(8,128)S(1)} %stack.98.g0), channel_id=1, source_target_pairs={{0,8},{8,0},{16,24},{24,16},{1,9},{9,1},{17,25},{25,17},{2,10},{10... | collective-permute-start | bytes 27656 | tf_op jit(solution)/shard_map/ppermute | solution.py:27
  14.8 67.1 %collective-permute-start.6 = (bf16[512,384]{1,0:T(8,128)(2,1)}, bf16[512,384]{1,0:T(8,128)(2,1)S(1)}, u32[]{:S(2)}, u32[]{:S(2)}) collective-permute-start(bf16[512,384]{1,0:T(8,128)(2,1)} %param.43), channel_id=1, source_target_pairs={{0,1},{1,0},{2,3},{3,2},{4,5},{5,4},{6,7},{7,6},{8,9},{9,8},{10,11... | collective-permute-start | bytes 1179656 | tf_op jit(solution)/shard_map/ppermute | solution.py:27
  16.5 102.2 %collective-permute-start.9 = (bf16[1536,384]{1,0:T(8,128)(2,1)}, bf16[1536,384]{1,0:T(8,128)(2,1)}, u32[]{:S(2)}, u32[]{:S(2)}) collective-permute-start(bf16[1536,384]{1,0:T(8,128)(2,1)} %q0.3), channel_id=1, source_target_pairs={{0,16},{8,24},{16,0},{24,8},{1,17},{9,25},{17,1},{25,9},{2,18},{10... | collective-permute-start | bytes 3538952 | tf_op jit(solution)/shard_map/ppermute | solution.py:27
  18.0 100.6 %collective-permute-start.10 = (bf16[384,1536]{1,0:T(8,128)(2,1)}, bf16[384,1536]{1,0:T(8,128)(2,1)}, u32[]{:S(2)}, u32[]{:S(2)}) collective-permute-start(bf16[384,1536]{1,0:T(8,128)(2,1)} %o0.3), channel_id=1, source_target_pairs={{0,16},{8,24},{16,0},{24,8},{1,17},{9,25},{17,1},{25,9},{2,18},{10... | collective-permute-start | bytes 3538952 | tf_op jit(solution)/shard_map/ppermute | solution.py:27
  19.9 50.5 %collective-permute-start.4 = (f32[6,384]{1,0:T(8,128)S(1)}, f32[6,384]{1,0:T(8,128)S(1)}, u32[]{:S(2)}, u32[]{:S(2)}) collective-permute-start(f32[6,384]{1,0:T(8,128)S(1)} %stack.98.g0), channel_id=1, source_target_pairs={{0,16},{8,24},{16,0},{24,8},{1,17},{9,25},{17,1},{25,9},{2,18},{10... | collective-permute-start | bytes 27656 | tf_op jit(solution)/shard_map/ppermute | solution.py:27
  81.9 36.8 %collective-permute-start.7 = (bf16[2,384,512]{2,1,0:T(8,128)(2,1)}, bf16[2,384,512]{2,1,0:T(8,128)(2,1)S(1)}, u32[]{:S(2)}, u32[]{:S(2)}) collective-permute-start(bf16[2,384,512]{2,1,0:T(8,128)(2,1)} %get-tuple-element.191.kv.kv1), channel_id=1, source_target_pairs={{0,1},{1,2},{2,3},{3,4},{4,5},{5,6},{6,7},{8,9},{9,10},{10,11},{11... | collective-permute-start | bytes 2359304 | tf_op jit(solution)/shard_map/ppermute | solution.py:33
  84.5 34.2 %collective-permute-start.8 = (bf16[2,384,512]{2,1,0:T(8,128)(2,1)}, bf16[2,384,512]{2,1,0:T(8,128)(2,1)}, u32[]{:S(2)}, u32[]{:S(2)}) collective-permute-start(bf16[2,384,512]{2,1,0:T(8,128)(2,1)} %get-tuple-element.191.kv.kv1), channel_id=1, source_target_pairs={{1,0},{2,1},{3,2},{4,3},{5,4},{6,5},{7,6},{9,8},{10,9},{11,10},{12... | collective-permute-start | bytes 2359304 | tf_op jit(solution)/shard_map/ppermute | solution.py:33
  118.7 11.4 %collective-permute-start.12 = (bf16[1536,384]{1,0:T(8,128)(2,1)S(1)}, bf16[1536,384]{1,0:T(8,128)(2,1)}, u32[]{:S(2)}, u32[]{:S(2)}) collective-permute-start(bf16[1536,384]{1,0:T(8,128)(2,1)S(1)} %copy-done.6), channel_id=1, source_target_pairs={{0,8},{8,0},{16,24},{24,16},{1,9},{9,1},{17,25},{25,17},{2,10},{10... | collective-permute-start | bytes 3538952 | tf_op jit(solution)/shard_map/ppermute | solution.py:27
  118.8 11.3 %collective-permute-start.13 = (bf16[1536,384]{1,0:T(8,128)(2,1)}, bf16[1536,384]{1,0:T(8,128)(2,1)}, u32[]{:S(2)}, u32[]{:S(2)}) collective-permute-start(bf16[1536,384]{1,0:T(8,128)(2,1)} %collective-permute-done.9.q2), channel_id=1, source_target_pairs={{0,8},{8,0},{16,24},{24,16},{1,9},{9,1},{17,25},{25,17},{2,10},{10... | collective-permute-start | bytes 3538952 | tf_op jit(solution)/shard_map/ppermute | solution.py:27
  119.3 10.8 %collective-permute-start.14 = (bf16[384,1536]{1,0:T(8,128)(2,1)S(1)}, bf16[384,1536]{1,0:T(8,128)(2,1)}, u32[]{:S(2)}, u32[]{:S(2)}) collective-permute-start(bf16[384,1536]{1,0:T(8,128)(2,1)S(1)} %copy-done.7), channel_id=1, source_target_pairs={{0,8},{8,0},{16,24},{24,16},{1,9},{9,1},{17,25},{25,17},{2,10},{10... | collective-permute-start | bytes 3538952 | tf_op jit(solution)/shard_map/ppermute | solution.py:27
  119.4 10.8 %collective-permute-start.15 = (bf16[384,1536]{1,0:T(8,128)(2,1)}, bf16[384,1536]{1,0:T(8,128)(2,1)}, u32[]{:S(2)}, u32[]{:S(2)}) collective-permute-start(bf16[384,1536]{1,0:T(8,128)(2,1)} %collective-permute-done.10.o2), channel_id=1, source_target_pairs={{0,8},{8,0},{16,24},{24,16},{1,9},{9,1},{17,25},{25,17},{2,10},{10... | collective-permute-start | bytes 3538952 | tf_op jit(solution)/shard_map/ppermute | solution.py:27
  119.8 10.3 %collective-permute-start.11 = (bf16[256,384]{1,0:T(8,128)(2,1)S(1)}, bf16[256,384]{1,0:T(8,128)(2,1)S(1)}, u32[]{:S(2)}, u32[]{:S(2)}) collective-permute-start(bf16[256,384]{1,0:T(8,128)(2,1)S(1)} %copy-done.22), channel_id=1, source_target_pairs={{0,16},{8,24},{16,0},{24,8},{1,17},{9,25},{17,1},{25,9},{2,18},{10... | collective-permute-start | bytes 589832 | tf_op jit(solution)/shard_map/ppermute | solution.py:27
  134.1 11.2 %collective-permute-start.17 = (bf16[128,1536]{1,0:T(8,128)(2,1)S(1)}, bf16[128,1536]{1,0:T(8,128)(2,1)S(1)}, u32[]{:S(2)}, u32[]{:S(2)}) collective-permute-start(bf16[128,1536]{1,0:T(8,128)(2,1)S(1)} %add_convert_fusion.7), channel_id=1, source_target_pairs={{0,16},{8,24},{16,0},{24,8},{1,17},{9,25},{17,1},{25,9},{2,18},{10... | collective-permute-start | bytes 1179656 | tf_op jit(solution)/shard_map/ppermute | solution.py:27
  134.8 30.5 %collective-permute-start.19 = (bf16[768,512]{1,0:T(8,128)(2,1)}, bf16[768,512]{1,0:T(8,128)(2,1)S(1)}, u32[]{:S(2)}, u32[]{:S(2)}) collective-permute-start(bf16[768,512]{1,0:T(8,128)(2,1)} %get-tuple-element.224), channel_id=1, source_target_pairs={{0,1},{1,0},{2,3},{3,2},{4,5},{5,4},{6,7},{7,6},{8,9},{9,8},{10,11... | collective-permute-start | bytes 2359304 | tf_op jit(solution)/shard_map/ppermute | solution.py:27
  145.3 20.0 %collective-permute-start.20 = (bf16[2,512,384]{2,1,0:T(8,128)(2,1)S(1)}, bf16[2,512,384]{2,1,0:T(8,128)(2,1)S(1)}, u32[]{:S(2)}, u32[]{:S(2)}) collective-permute-start(bf16[2,512,384]{2,1,0:T(8,128)(2,1)S(1)} %pad_maximum_fusion.4.g0), channel_id=1, source_target_pairs={{0,16},{8,24},{16,0},{24,8},{1,17},{9,25},{17,1},{25,9},{2,18},{10... | collective-permute-start | bytes 2359304 | tf_op jit(solution)/shard_map/ppermute | solution.py:27
  165.3 11.4 %collective-permute-start.22 = (bf16[128,1536]{1,0:T(8,128)(2,1)}, bf16[128,1536]{1,0:T(8,128)(2,1)S(1)}, u32[]{:S(2)}, u32[]{:S(2)}) collective-permute-start(bf16[128,1536]{1,0:T(8,128)(2,1)} %get-tuple-element.227.n0), channel_id=1, source_target_pairs={{0,16},{8,24},{16,0},{24,8},{1,17},{9,25},{17,1},{25,9},{2,18},{10... | collective-permute-start | bytes 1179656 | tf_op jit(solution)/shard_map/ppermute | solution.py:27
  166.9 19.5 %collective-permute-start.24 = (bf16[2,512,384]{2,1,0:T(8,128)(2,1)S(1)}, bf16[2,512,384]{2,1,0:T(8,128)(2,1)S(1)}, u32[]{:S(2)}, u32[]{:S(2)}) collective-permute-start(bf16[2,512,384]{2,1,0:T(8,128)(2,1)S(1)} %pad_maximum_fusion.4.g0), channel_id=1, source_target_pairs={{0,8},{8,0},{16,24},{24,16},{1,9},{9,1},{17,25},{25,17},{2,10},{10... | collective-permute-start | bytes 2359304 | tf_op jit(solution)/shard_map/ppermute | solution.py:27
  166.9 20.2 %collective-permute-start.25 = (bf16[2,512,384]{2,1,0:T(8,128)(2,1)S(1)}, bf16[2,512,384]{2,1,0:T(8,128)(2,1)S(1)}, u32[]{:S(2)}, u32[]{:S(2)}) collective-permute-start(bf16[2,512,384]{2,1,0:T(8,128)(2,1)S(1)} %collective-permute-done.20.g2), channel_id=1, source_target_pairs={{0,8},{8,0},{16,24},{24,16},{1,9},{9,1},{17,25},{25,17},{2,10},{10... | collective-permute-start | bytes 2359304 | tf_op jit(solution)/shard_map/ppermute | solution.py:27
  176.7 9.6 %collective-permute-start.21 = (bf16[128,1536]{1,0:T(8,128)(2,1)}, bf16[128,1536]{1,0:T(8,128)(2,1)S(1)}, u32[]{:S(2)}, u32[]{:S(2)}) collective-permute-start(bf16[128,1536]{1,0:T(8,128)(2,1)} %get-tuple-element.227.n0), channel_id=1, source_target_pairs={{0,8},{8,0},{16,24},{24,16},{1,9},{9,1},{17,25},{25,17},{2,10},{10... | collective-permute-start | bytes 1179656 | tf_op jit(solution)/shard_map/ppermute | solution.py:27
  179.0 41.1 %collective-permute-start.28 = (bf16[128,3072]{1,0:T(8,128)(2,1)}, bf16[128,3072]{1,0:T(8,128)(2,1)}, u32[]{:S(2)}, u32[]{:S(2)}) collective-permute-start(bf16[128,3072]{1,0:T(8,128)(2,1)} %get-tuple-element.246), channel_id=1, source_target_pairs={{0,16},{8,24},{16,0},{24,8},{1,17},{9,25},{17,1},{25,9},{2,18},{10... | collective-permute-start | bytes 2359304 | tf_op jit(solution)/shard_map/ppermute | solution.py:27
  180.5 23.1 %collective-permute-start.26 = (bf16[768,128]{1,0:T(8,128)(2,1)}, bf16[768,128]{1,0:T(8,128)(2,1)}, u32[]{:S(2)}, u32[]{:S(2)}) collective-permute-start(bf16[768,128]{1,0:T(8,128)(2,1)} %get-tuple-element.238), channel_id=1, source_target_pairs={{0,1},{1,0},{2,3},{3,2},{4,5},{5,4},{6,7},{7,6},{8,9},{9,8},{10,11... | collective-permute-start | bytes 589832 | tf_op jit(solution)/shard_map/ppermute | solution.py:27
  204.7 15.4 %collective-permute-start.27 = (bf16[2,768,128]{2,1,0:T(8,128)(2,1)S(1)}, bf16[2,768,128]{2,1,0:T(8,128)(2,1)S(1)}, u32[]{:S(2)}, u32[]{:S(2)}) collective-permute-start(bf16[2,768,128]{2,1,0:T(8,128)(2,1)S(1)} %pad_maximum_fusion.6.p0), channel_id=1, source_target_pairs={{0,16},{8,24},{16,0},{24,8},{1,17},{9,25},{17,1},{25,9},{2,18},{10... | collective-permute-start | bytes 1179656 | tf_op jit(solution)/shard_map/ppermute | solution.py:27
  205.2 14.8 %collective-permute-start.29 = (bf16[384,512]{1,0:T(8,128)(2,1)}, bf16[384,512]{1,0:T(8,128)(2,1)S(1)}, u32[]{:S(2)}, u32[]{:S(2)}) collective-permute-start(bf16[384,512]{1,0:T(8,128)(2,1)} %get-tuple-element.247), channel_id=1, source_target_pairs={{0,1},{1,0},{2,3},{3,2},{4,5},{5,4},{6,7},{7,6},{8,9},{9,8},{10,11... | collective-permute-start | bytes 1179656 | tf_op jit(solution)/shard_map/ppermute | solution.py:27
  224.0 11.2 %collective-permute-start.31 = (bf16[128,1536]{1,0:T(8,128)(2,1)S(1)}, bf16[128,1536]{1,0:T(8,128)(2,1)S(1)}, u32[]{:S(2)}, u32[]{:S(2)}) collective-permute-start(bf16[128,1536]{1,0:T(8,128)(2,1)S(1)} %add_convert_fusion.6), channel_id=1, source_target_pairs={{0,16},{8,24},{16,0},{24,8},{1,17},{9,25},{17,1},{25,9},{2,18},{10... | collective-permute-start | bytes 1179656 | tf_op jit(solution)/shard_map/ppermute | solution.py:27
  225.6 32.8 %collective-permute-start.32 = (bf16[512,768]{1,0:T(8,128)(2,1)}, bf16[512,768]{1,0:T(8,128)(2,1)}, u32[]{:S(2)}, u32[]{:S(2)}) collective-permute-start(bf16[512,768]{1,0:T(8,128)(2,1)} %get-tuple-element.308.refs_0_), channel_id=1, source_target_pairs={{0,1},{1,0},{2,3},{3,2},{4,5},{5,4},{6,7},{7,6},{8,9},{9,8},{10,11... | collective-permute-start | bytes 2359304 | tf_op jit(solution)/shard_map/ppermute | solution.py:27
  227.6 30.7 %collective-permute-start.33 = (bf16[384,512]{1,0:T(8,128)(2,1)}, bf16[384,512]{1,0:T(8,128)(2,1)}, u32[]{:S(2)}, u32[]{:S(2)}) collective-permute-start(bf16[384,512]{1,0:T(8,128)(2,1)} %get-tuple-element.255), channel_id=1, source_target_pairs={{0,1},{1,0},{2,3},{3,2},{4,5},{5,4},{6,7},{7,6},{8,9},{9,8},{10,11... | collective-permute-start | bytes 1179656 | tf_op jit(solution)/shard_map/ppermute | solution.py:27
  235.2 23.1 %collective-permute-start.34 = (bf16[2,768,128]{2,1,0:T(8,128)(2,1)S(1)}, bf16[2,768,128]{2,1,0:T(8,128)(2,1)}, u32[]{:S(2)}, u32[]{:S(2)}) collective-permute-start(bf16[2,768,128]{2,1,0:T(8,128)(2,1)S(1)} %pad_maximum_fusion.6.p0), channel_id=1, source_target_pairs={{0,8},{8,0},{16,24},{24,16},{1,9},{9,1},{17,25},{25,17},{2,10},{10... | collective-permute-start | bytes 1179656 | tf_op jit(solution)/shard_map/ppermute | solution.py:27
  235.2 23.1 %collective-permute-start.35 = (bf16[2,768,128]{2,1,0:T(8,128)(2,1)S(1)}, bf16[2,768,128]{2,1,0:T(8,128)(2,1)}, u32[]{:S(2)}, u32[]{:S(2)}) collective-permute-start(bf16[2,768,128]{2,1,0:T(8,128)(2,1)S(1)} %collective-permute-done.27.p2), channel_id=1, source_target_pairs={{0,8},{8,0},{16,24},{24,16},{1,9},{9,1},{17,25},{25,17},{2,10},{10... | collective-permute-start | bytes 1179656 | tf_op jit(solution)/shard_map/ppermute | solution.py:27
  258.4 24.7 %collective-permute-start.39 = (bf16[2,128,3072]{2,1,0:T(8,128)(2,1)S(1)}, bf16[2,128,3072]{2,1,0:T(8,128)(2,1)}, u32[]{:S(2)}, u32[]{:S(2)}) collective-permute-start(bf16[2,128,3072]{2,1,0:T(8,128)(2,1)S(1)} %pad_maximum_fusion.f02), channel_id=1, source_target_pairs={{0,8},{8,0},{16,24},{24,16},{1,9},{9,1},{17,25},{25,17},{2,10},{10... | collective-permute-start | bytes 4718600 | tf_op jit(solution)/shard_map/ppermute | solution.py:27
  258.5 20.5 %collective-permute-start.41 = (bf16[512,768]{1,0:T(8,128)(2,1)}, bf16[512,768]{1,0:T(8,128)(2,1)}, u32[]{:S(2)}, u32[]{:S(2)}) collective-permute-start(bf16[512,768]{1,0:T(8,128)(2,1)} %get-tuple-element.310.refs_2_), channel_id=1, source_target_pairs={{0,1},{1,0},{2,3},{3,2},{4,5},{5,4},{6,7},{7,6},{8,9},{9,8},{10,11... | collective-permute-start | bytes 2359304 | tf_op jit(solution)/shard_map/ppermute | solution.py:27
  260.6 11.4 %collective-permute-start.37 = (bf16[128,1536]{1,0:T(8,128)(2,1)}, bf16[128,1536]{1,0:T(8,128)(2,1)S(1)}, u32[]{:S(2)}, u32[]{:S(2)}) collective-permute-start(bf16[128,1536]{1,0:T(8,128)(2,1)} %get-tuple-element.324.g0.a0), channel_id=1, source_target_pairs={{0,16},{8,24},{16,0},{24,8},{1,17},{9,25},{17,1},{25,9},{2,18},{10... | collective-permute-start | bytes 1179656 | tf_op jit(solution)/shard_map/ppermute | solution.py:27
  263.2 17.8 %collective-permute-start.40 = (bf16[512,384]{1,0:T(8,128)(2,1)S(1)}, bf16[512,384]{1,0:T(8,128)(2,1)}, u32[]{:S(2)}, u32[]{:S(2)}) collective-permute-start(bf16[512,384]{1,0:T(8,128)(2,1)S(1)} %pad_maximum_fusion.7), channel_id=1, source_target_pairs={{0,8},{8,0},{16,24},{24,16},{1,9},{9,1},{17,25},{25,17},{2,10},{10... | collective-permute-start | bytes 1179656 | tf_op jit(solution)/shard_map/ppermute | solution.py:27
  263.3 18.0 %collective-permute-start.36 = (bf16[128,1536]{1,0:T(8,128)(2,1)S(1)}, bf16[128,1536]{1,0:T(8,128)(2,1)S(1)}, u32[]{:S(2)}, u32[]{:S(2)}) collective-permute-start(bf16[128,1536]{1,0:T(8,128)(2,1)S(1)} %copy-done.9), channel_id=1, source_target_pairs={{0,8},{8,0},{16,24},{24,16},{1,9},{9,1},{17,25},{25,17},{2,10},{10... | collective-permute-start | bytes 1179656 | tf_op jit(solution)/shard_map/ppermute | solution.py:27
  272.0 11.1 %collective-permute-start.38 = (bf16[128,1536]{1,0:T(8,128)(2,1)S(1)}, bf16[128,1536]{1,0:T(8,128)(2,1)S(1)}, u32[]{:S(2)}, u32[]{:S(2)}) collective-permute-start(bf16[128,1536]{1,0:T(8,128)(2,1)S(1)} %collective-permute-done.37.g2.a2), channel_id=1, source_target_pairs={{0,8},{8,0},{16,24},{24,16},{1,9},{9,1},{17,25},{25,17},{2,10},{10... | collective-permute-start | bytes 1179656 | tf_op jit(solution)/shard_map/ppermute | solution.py:27
  279.0 38.0 %collective-permute-start.45 = (bf16[2,192,1536]{2,1,0:T(8,128)(2,1)}, bf16[2,192,1536]{2,1,0:T(8,128)(2,1)}, u32[]{:S(2)}, u32[]{:S(2)}) collective-permute-start(bf16[2,192,1536]{2,1,0:T(8,128)(2,1)} %bitcast.141), channel_id=1, source_target_pairs={{0,2},{1,3},{2,0},{3,1},{4,6},{5,7},{6,4},{7,5},{8,10},{9,11},{10,... | collective-permute-start | bytes 3538952 | tf_op jit(solution)/shard_map/ppermute | solution.py:27
  281.0 23.2 %collective-permute-start.43 = (bf16[512,768]{1,0:T(8,128)(2,1)}, bf16[512,768]{1,0:T(8,128)(2,1)}, u32[]{:S(2)}, u32[]{:S(2)}) collective-permute-start(bf16[512,768]{1,0:T(8,128)(2,1)} %get-tuple-element.312.refs_4_), channel_id=1, source_target_pairs={{0,1},{1,0},{2,3},{3,2},{4,5},{5,4},{6,7},{7,6},{8,9},{9,8},{10,11... | collective-permute-start | bytes 2359304 | tf_op jit(solution)/shard_map/ppermute | solution.py:27
  281.3 35.7 %collective-permute-start.44 = (bf16[512,768]{1,0:T(8,128)(2,1)}, bf16[512,768]{1,0:T(8,128)(2,1)}, u32[]{:S(2)}, u32[]{:S(2)}) collective-permute-start(bf16[512,768]{1,0:T(8,128)(2,1)} %get-tuple-element.314.refs_6_), channel_id=1, source_target_pairs={{0,1},{1,0},{2,3},{3,2},{4,5},{5,4},{6,7},{7,6},{8,9},{9,8},{10,11... | collective-permute-start | bytes 2359304 | tf_op jit(solution)/shard_map/ppermute | solution.py:27
  283.1 34.0 %collective-permute-start.42 = (bf16[128,3072]{1,0:T(8,128)(2,1)}, bf16[128,3072]{1,0:T(8,128)(2,1)S(1)}, u32[]{:S(2)}, u32[]{:S(2)}) collective-permute-start(bf16[128,3072]{1,0:T(8,128)(2,1)} %get-tuple-element.282), channel_id=1, source_target_pairs={{0,16},{8,24},{16,0},{24,8},{1,17},{9,25},{17,1},{25,9},{2,18},{10... | collective-permute-start | bytes 2359304 | tf_op jit(solution)/shard_map/ppermute | solution.py:27
  285.7 31.3 %collective-permute-start.46 = (bf16[256,384]{1,0:T(8,128)(2,1)S(1)}, bf16[256,384]{1,0:T(8,128)(2,1)S(1)}, u32[]{:S(2)}, u32[]{:S(2)}) collective-permute-start(bf16[256,384]{1,0:T(8,128)(2,1)S(1)} %add_convert_fusion.9), channel_id=1, source_target_pairs={{0,16},{8,24},{16,0},{24,8},{1,17},{9,25},{17,1},{25,9},{2,18},{10... | collective-permute-start | bytes 589832 | tf_op jit(solution)/shard_map/ppermute | solution.py:27
  319.3 25.0 %collective-permute-start.50 = (bf16[2,128,3072]{2,1,0:T(8,128)(2,1)S(1)}, bf16[2,128,3072]{2,1,0:T(8,128)(2,1)}, u32[]{:S(2)}, u32[]{:S(2)}) collective-permute-start(bf16[2,128,3072]{2,1,0:T(8,128)(2,1)S(1)} %pad_maximum_fusion.1.b02), channel_id=1, source_target_pairs={{0,8},{8,0},{16,24},{24,16},{1,9},{9,1},{17,25},{25,17},{2,10},{10... | collective-permute-start | bytes 4718600 | tf_op jit(solution)/shard_map/ppermute | solution.py:27
  319.4 83.6 %collective-permute-start.47 = (bf16[2,384,512]{2,1,0:T(8,128)(2,1)}, bf16[2,384,512]{2,1,0:T(8,128)(2,1)S(1)}, u32[]{:S(2)}, u32[]{:S(2)}) collective-permute-start(bf16[2,384,512]{2,1,0:T(8,128)(2,1)} %get-tuple-element.288), channel_id=1, source_target_pairs={{1,0},{2,1},{3,2},{4,3},{5,4},{6,5},{7,6},{9,8},{10,9},{11,10},{12... | collective-permute-start | bytes 2359304 | tf_op jit(solution)/shard_map/ppermute | solution.py:33
  320.7 82.4 %collective-permute-start.48 = (bf16[2,384,512]{2,1,0:T(8,128)(2,1)}, bf16[2,384,512]{2,1,0:T(8,128)(2,1)}, u32[]{:S(2)}, u32[]{:S(2)}) collective-permute-start(bf16[2,384,512]{2,1,0:T(8,128)(2,1)} %get-tuple-element.289), channel_id=1, source_target_pairs={{0,1},{1,2},{2,3},{3,4},{4,5},{5,6},{6,7},{8,9},{9,10},{10,11},{11... | collective-permute-start | bytes 2359304 | tf_op jit(solution)/shard_map/ppermute | solution.py:33
  339.2 84.2 %collective-permute-start.53 = (bf16[2,192,3072]{2,1,0:T(8,128)(2,1)}, bf16[2,192,3072]{2,1,0:T(8,128)(2,1)}, u32[]{:S(2)}, u32[]{:S(2)}) collective-permute-start(bf16[2,192,3072]{2,1,0:T(8,128)(2,1)} %bitcast.140), channel_id=1, source_target_pairs={{0,2},{1,3},{2,0},{3,1},{4,6},{5,7},{6,4},{7,5},{8,10},{9,11},{10,... | collective-permute-start | bytes 7077896 | tf_op jit(solution)/shard_map/ppermute | solution.py:27
  342.0 61.0 %collective-permute-start.49 = (bf16[1,192,1536]{2,1,0:T(8,128)(2,1)}, bf16[1,192,1536]{2,1,0:T(8,128)(2,1)}, u32[]{:S(2)}, u32[]{:S(2)}) collective-permute-start(bf16[1,192,1536]{2,1,0:T(8,128)(2,1)} %constant_dynamic-slice_fusion.21), channel_id=1, source_target_pairs={{0,4},{1,5},{2,6},{3,7},{4,0},{5,1},{6,2},{7,3},{8,12},{9,13},{10,... | collective-permute-start | bytes 1769480 | tf_op jit(solution)/shard_map/ppermute | solution.py:27
  411.4 8.0 %collective-permute-start.51 = (bf16[1024,384]{1,0:T(8,128)(2,1)}, bf16[1024,384]{1,0:T(8,128)(2,1)S(1)}, u32[]{:S(2)}, u32[]{:S(2)}) collective-permute-start(bf16[1024,384]{1,0:T(8,128)(2,1)} %get-tuple-element.301), channel_id=1, source_target_pairs={{0,8},{8,0},{16,24},{24,16},{1,9},{9,1},{17,25},{25,17},{2,10},{10... | collective-permute-start | bytes 2359304 | tf_op jit(solution)/shard_map/ppermute | solution.py:27
  413.6 58.6 %collective-permute-start.60 = (bf16[4,208,768]{2,1,0:T(8,128)(2,1)}, bf16[4,208,768]{2,1,0:T(8,128)(2,1)}, u32[]{:S(2)}, u32[]{:S(2)}) collective-permute-start(bf16[4,208,768]{2,1,0:T(8,128)(2,1)} %get-tuple-element.336), channel_id=1, source_target_pairs={{0,1},{1,0},{2,3},{3,2},{4,5},{5,4},{6,7},{7,6},{8,9},{9,8},{10,11... | collective-permute-start | bytes 3833864 | tf_op jit(solution)/shard_map/ppermute | solution.py:27
  417.9 54.3 %collective-permute-start.61 = (bf16[1152,512]{1,0:T(8,128)(2,1)}, bf16[1152,512]{1,0:T(8,128)(2,1)}, u32[]{:S(2)}, u32[]{:S(2)}) collective-permute-start(bf16[1152,512]{1,0:T(8,128)(2,1)} %get-tuple-element.337), channel_id=1, source_target_pairs={{0,1},{1,0},{2,3},{3,2},{4,5},{5,4},{6,7},{7,6},{8,9},{9,8},{10,11... | collective-permute-start | bytes 3538952 | tf_op jit(solution)/shard_map/ppermute | solution.py:27
  419.6 11.3 %collective-permute-start.52 = (bf16[512,384]{1,0:T(8,128)(2,1)S(1)}, bf16[512,384]{1,0:T(8,128)(2,1)S(1)}, u32[]{:S(2)}, u32[]{:S(2)}) collective-permute-start(bf16[512,384]{1,0:T(8,128)(2,1)S(1)} %add_convert_fusion.5), channel_id=1, source_target_pairs={{0,16},{8,24},{16,0},{24,8},{1,17},{9,25},{17,1},{25,9},{2,18},{10... | collective-permute-start | bytes 1179656 | tf_op jit(solution)/shard_map/ppermute | solution.py:27
  438.4 75.7 %collective-permute-start.54 = (bf16[256,1536]{1,0:T(8,128)(2,1)}, bf16[256,1536]{1,0:T(8,128)(2,1)}, u32[]{:S(2)}, u32[]{:S(2)}) collective-permute-start(bf16[256,1536]{1,0:T(8,128)(2,1)} %get-tuple-element.321), channel_id=1, source_target_pairs={{0,8},{8,0},{16,24},{24,16},{1,9},{9,1},{17,25},{25,17},{2,10},{10... | collective-permute-start | bytes 2359304 | tf_op jit(solution)/shard_map/ppermute | solution.py:27
  443.9 6.1 %collective-permute-start.59 = (f32[1,8704]{1,0:T(1,128)S(1)}, f32[1,8704]{1,0:T(1,128)S(1)}, u32[]{:S(2)}, u32[]{:S(2)}) collective-permute-start(f32[1,8704]{1,0:T(1,128)S(1)} %reshape_add_fusion), channel_id=1, source_target_pairs={{0,16},{8,24},{16,0},{24,8},{1,17},{9,25},{17,1},{25,9},{2,18},{10... | collective-permute-start | bytes 104456 | tf_op jit(solution)/shard_map/ppermute | solution.py:27
  446.6 87.0 %collective-permute-start.72 = (bf16[1,192,3072]{2,1,0:T(8,128)(2,1)}, bf16[1,192,3072]{2,1,0:T(8,128)(2,1)}, u32[]{:S(2)}, u32[]{:S(2)}) collective-permute-start(bf16[1,192,3072]{2,1,0:T(8,128)(2,1)} %constant_dynamic-slice_fusion), channel_id=1, source_target_pairs={{0,4},{1,5},{2,6},{3,7},{4,0},{5,1},{6,2},{7,3},{8,12},{9,13},{10,... | collective-permute-start | bytes 3538952 | tf_op jit(solution)/shard_map/ppermute | solution.py:27
  481.2 31.3 %collective-permute-start.70 = (bf16[2,192,768]{2,1,0:T(8,128)(2,1)}, bf16[2,192,768]{2,1,0:T(8,128)(2,1)}, u32[]{:S(2)}, u32[]{:S(2)}) collective-permute-start(bf16[2,192,768]{2,1,0:T(8,128)(2,1)} %dynamic-slice_bitcast_fusion.1), channel_id=1, source_target_pairs={{0,2},{1,3},{2,0},{3,1},{4,6},{5,7},{6,4},{7,5},{8,10},{9,11},{10,... | collective-permute-start | bytes 1769480 | tf_op jit(solution)/shard_map/ppermute | solution.py:27
  489.6 48.0 %collective-permute-start.62 = (bf16[2,192,1152]{2,1,0:T(8,128)(2,1)}, bf16[2,192,1152]{2,1,0:T(8,128)(2,1)S(1)}, u32[]{:S(2)}, u32[]{:S(2)}) collective-permute-start(bf16[2,192,1152]{2,1,0:T(8,128)(2,1)} %dynamic-slice_bitcast_fusion), channel_id=1, source_target_pairs={{0,2},{1,3},{2,0},{3,1},{4,6},{5,7},{6,4},{7,5},{8,10},{9,11},{10,... | collective-permute-start | bytes 2654216 | tf_op jit(solution)/shard_map/ppermute | solution.py:27
  491.6 46.0 %collective-permute-start.63 = (bf16[4,192,768]{2,1,0:T(8,128)(2,1)}, bf16[4,192,768]{2,1,0:T(8,128)(2,1)S(1)}, u32[]{:S(2)}, u32[]{:S(2)}) collective-permute-start(bf16[4,192,768]{2,1,0:T(8,128)(2,1)} %get-tuple-element.347), channel_id=1, source_target_pairs={{0,1},{1,0},{2,3},{3,2},{4,5},{5,4},{6,7},{7,6},{8,9},{9,8},{10,11... | collective-permute-start | bytes 3538952 | tf_op jit(solution)/shard_map/ppermute | solution.py:27
  514.0 16.2 %collective-permute-start.71 = (bf16[1,192,768]{2,1,0:T(8,128)(2,1)S(1)}, bf16[1,192,768]{2,1,0:T(8,128)(2,1)S(1)}, u32[]{:S(2)}, u32[]{:S(2)}) collective-permute-start(bf16[1,192,768]{2,1,0:T(8,128)(2,1)S(1)} %constant_dynamic-slice_fusion.1), channel_id=1, source_target_pairs={{0,4},{1,5},{2,6},{3,7},{4,0},{5,1},{6,2},{7,3},{8,12},{9,13},{10,... | collective-permute-start | bytes 884744 | tf_op jit(solution)/shard_map/ppermute | solution.py:27
  515.2 16.5 %collective-permute-start.55 = (bf16[128,1536]{1,0:T(8,128)(2,1)S(1)}, bf16[128,1536]{1,0:T(8,128)(2,1)S(1)}, u32[]{:S(2)}, u32[]{:S(2)}) collective-permute-start(bf16[128,1536]{1,0:T(8,128)(2,1)S(1)} %add_convert_fusion.4), channel_id=1, source_target_pairs={{0,16},{8,24},{16,0},{24,8},{1,17},{9,25},{17,1},{25,9},{2,18},{10... | collective-permute-start | bytes 1179656 | tf_op jit(solution)/shard_map/ppermute | solution.py:27
  532.9 6.4 %collective-permute-start.56 = (bf16[128,768]{1,0:T(8,128)(2,1)S(1)}, bf16[128,768]{1,0:T(8,128)(2,1)S(1)}, u32[]{:S(2)}, u32[]{:S(2)}) collective-permute-start(bf16[128,768]{1,0:T(8,128)(2,1)S(1)} %pad_maximum_fusion.12), channel_id=1, source_target_pairs={{0,16},{8,24},{16,0},{24,8},{1,17},{9,25},{17,1},{25,9},{2,18},{10... | collective-permute-start | bytes 589832 | tf_op jit(solution)/shard_map/ppermute | solution.py:27
  538.0 24.8 %collective-permute-start.64 = (bf16[2,192,768]{2,1,0:T(8,128)(2,1)S(1)}, bf16[2,192,768]{2,1,0:T(8,128)(2,1)S(1)}, u32[]{:S(2)}, u32[]{:S(2)}) collective-permute-start(bf16[2,192,768]{2,1,0:T(8,128)(2,1)S(1)} %dynamic-slice_bitcast_fusion.2), channel_id=1, source_target_pairs={{0,2},{1,3},{2,0},{3,1},{4,6},{5,7},{6,4},{7,5},{8,10},{9,11},{10,... | collective-permute-start | bytes 1769480 | tf_op jit(solution)/shard_map/ppermute | solution.py:27
  539.5 24.4 %collective-permute-start.68 = (bf16[1,192,1152]{2,1,0:T(8,128)(2,1)S(1)}, bf16[1,192,1152]{2,1,0:T(8,128)(2,1)S(1)}, u32[]{:S(2)}, u32[]{:S(2)}) collective-permute-start(bf16[1,192,1152]{2,1,0:T(8,128)(2,1)S(1)} %constant_dynamic-slice_fusion.3), channel_id=1, source_target_pairs={{0,4},{1,5},{2,6},{3,7},{4,0},{5,1},{6,2},{7,3},{8,12},{9,13},{10,... | collective-permute-start | bytes 1327112 | tf_op jit(solution)/shard_map/ppermute | solution.py:27
  566.8 4.3 collective-permute-start.66
  571.1 7.7 %collective-permute-start.67 = (f32[1,6,48]{2,0,1:T(1,128)S(1)}, f32[1,6,48]{2,0,1:T(1,128)S(1)}, u32[]{:S(2)}, u32[]{:S(2)}) collective-permute-start(f32[1,6,48]{2,0,1:T(1,128)S(1)} %constant_dynamic-slice_fusion.4), channel_id=1, source_target_pairs={{0,4},{1,5},{2,6},{3,7},{4,0},{5,1},{6,2},{7,3},{8,12},{9,13},{10,... | collective-permute-start | bytes 3464 | tf_op jit(solution)/shard_map/ppermute | solution.py:27
  571.2 11.4 %collective-permute-start.69 = (bf16[1,192,768]{2,1,0:T(8,128)(2,1)S(1)}, bf16[1,192,768]{2,1,0:T(8,128)(2,1)S(1)}, u32[]{:S(2)}, u32[]{:S(2)}) collective-permute-start(bf16[1,192,768]{2,1,0:T(8,128)(2,1)S(1)} %constant_dynamic-slice_fusion.2), channel_id=1, source_target_pairs={{0,4},{1,5},{2,6},{3,7},{4,0},{5,1},{6,2},{7,3},{8,12},{9,13},{10,... | collective-permute-start | bytes 884744 | tf_op jit(solution)/shard_map/ppermute | solution.py:27
  (82 other events, 996.8 us)

commit v4 on v3

--- a/solution.py
+++ b/solution.py
@@ -350,7 +350,8 @@
     )(span, q, *kvs, tk, tv, qlab, klab, w_out, out, lse, *grads)
 
 
-def tail_body(place, dq, kept, ahead, behind, cosine, sine, wq, wk, wv, raw, away, own, low, flipped):
+def tail_body(place, dq, kept, ahead, behind, cosine, sine, wq, wk, wv, times,
+              raw, away, own, low, flipped):
     part, size = dq.shape
     half = HEAD_SIZE // 2
 
@@ -369,8 +370,10 @@
 
     returned(dq[...], 0, 1.0 / math.sqrt(HEAD_SIZE))
     returned(whole(0), part, 1.0)
-    raw[2 * part :, :] = whole(1).astype(BF16)
-    flipped[...] = raw[...].T
+    raw[2 * part : 3 * part, :] = whole(1).astype(BF16)
+    raw[3 * part :, :] = jnp.zeros((16, size), BF16)
+    raw[3 * part : 3 * part + 2, :part] = times[...].astype(BF16)
+    flipped[...] = raw[: 3 * part, :].T
 
     def sent(r):
         at = relative(place[0], r, part)
@@ -385,19 +388,19 @@
     own[...] = sent(0)
 
 
-def tail(place, dq, kept, ahead, behind, tables, wq, wk, wv):
+def tail(place, dq, kept, ahead, behind, tables, wq, wk, wv, times):
     part, size = dq.shape
     low = lambda *dims: jax.ShapeDtypeStruct(dims, BF16)
     vmem = pl.BlockSpec(memory_space=pltpu.VMEM)
     return pl.pallas_call(
         tail_body,
-        in_specs=[pl.BlockSpec(memory_space=pltpu.SMEM)] + [vmem] * 9,
+        in_specs=[pl.BlockSpec(memory_space=pltpu.SMEM)] + [vmem] * 10,
         out_specs=[vmem] * 4,
-        out_shape=[low(3 * part, size), low(2 * size, part), jax.ShapeDtypeStruct((size, part), F32),
+        out_shape=[low(3 * part + 16, size), low(2 * size, part), jax.ShapeDtypeStruct((size, part), F32),
                    low(size, part)],
         scratch_shapes=[pltpu.VMEM((size, 3 * part), BF16)],
         name="tail", cost_estimate=FREE,
-    )(place, dq, kept, ahead, behind, *tables, wq, wk, wv)
+    )(place, dq, kept, ahead, behind, *tables, wq, wk, wv, times)
 
 
 def rotary_tables(frame_positions):
@@ -759,7 +762,7 @@
 
 
 def bundle_body(devices, place, f02, f13, b02, b13, a0, a1, a2, a3, attended,
-                context, kv, times, keep_a, send_a, keep_b, send_b):
+                context, kv, keep_a, send_a, keep_b, send_b):
     width = a0.shape[1]
     part, share = width // 4, a0.shape[0]
 
@@ -793,9 +796,6 @@
                 out[0][d // 2, at, cols] = odd
                 out[1][d // 2, at, cols] = even
 
-    send_a[:, rows:, :] = jnp.zeros((devices // 2, send_a.shape[1] - rows, half), BF16)
-    for at in (0, 1):
-        send_a[0, rows : rows + 1, at * part : (at + 1) * part] = times[at : at + 1, :].astype(BF16)
     put(dot_tn(full(fronts), own(backs)), 0, 0, (keep_a, send_a))
     count = context.shape[0]
     put(dot_tn(context[...], kv[:count, :]), 0, part, (keep_a, send_a))
@@ -811,19 +811,16 @@
     put(grads[:, half:], 3 * small, 0, (keep_b, send_b))
 
 
-def bundle_grads(devices, place, fronts, backs, ones, attended, context, kv, times):
+def bundle_grads(devices, place, fronts, backs, ones, attended, context, kv):
     width = ones[0].shape[1]
     vmem = pl.BlockSpec(memory_space=pltpu.VMEM)
     return pl.pallas_call(
         functools.partial(bundle_body, devices),
-        in_specs=[pl.BlockSpec(memory_space=pltpu.SMEM)] + [vmem] * 12,
+        in_specs=[pl.BlockSpec(memory_space=pltpu.SMEM)] + [vmem] * 11,
         out_specs=[vmem] * 4,
-        out_shape=[
-            jax.ShapeDtypeStruct((devices // 2, width // devices + more, width // 2), BF16)
-            for more in (0, 16, 0, 0)
-        ],
+        out_shape=[jax.ShapeDtypeStruct((devices // 2, width // devices, width // 2), BF16)] * 4,
         name="bundle", cost_estimate=FREE,
-    )(place, *fronts, *backs, *ones, attended, context, kv, times)
+    )(place, *fronts, *backs, *ones, attended, context, kv)
 
 
 def front_body(width_block, place, x0, x1, x2, x3, g0, g1, g2, g3, cosine, sine, wq, wk, wv,
@@ -973,8 +970,8 @@
     both, out_pair = meeting(both, swap(after(out_grad, frame_parts_near[2]), "seq", 1))
     grad_both = jnp.stack([out_grad, out_pair])
     behind, ahead = shift(both, "seq", 1), shift(both, "seq", -1)
-    query_far = swap(after(c_query, frame_parts_near[3]), "tensor", 2)
-    out_far = swap(after(c_out, frame_parts_near[3]), "tensor", 2)
+    query_late, out_late = after((c_query, c_out), (frame_parts_near[2], norm_parts[2]))
+    query_far, out_far = swap(query_late, "tensor", 2), swap(out_late, "tensor", 2)
     state = attend_near(spans, queries, both, time_keys, time_values, label_row, label_column)
     behind, ahead, query_far, out_far, *state = meeting(
         behind, ahead, query_far, out_far, *state
@@ -1056,12 +1053,14 @@
     )
     context_parts = quarters(kv_grad, 1)
     context_got = swap(jnp.concatenate([context_parts[1], context_parts[3]], 0), "tensor", 1)
-    one_far_rows, down_keep = meeting(swap(grad_one, "tensor", 2), down_keep)
+    one_far_rows, down_keep, lifted_got_a = meeting(
+        swap(grad_one, "tensor", 2), down_keep, lifted_got_a
+    )
     one_parts = (
         grad_one, swap(grad_one, "tensor", 1), one_far_rows, swap(one_far_rows, "tensor", 1)
     )
-    *one_parts, front_other, context_got, lifted_got_a = meeting(
-        *one_parts, swap(after(front_both, grad_one), "tensor", 1), context_got, lifted_got_a
+    *one_parts, front_other, context_got = meeting(
+        *one_parts, swap(after(front_both, grad_one), "tensor", 1), context_got
     )
     context_low = (
         context_parts[2].astype(F32) + context_got[context_parts[2].shape[0] :].astype(F32)
@@ -1079,14 +1078,10 @@
     from_next, from_prev = shift(to_prev, "seq", -1), shift(to_next, "seq", 1)
     down_keep, down_got = halve(added(down_keep, down_got).astype(BF16), 2)
     flip_near = (flip_both, flip_mate, flip_far, flip_far_mate)
-    both_keep, both_got = traded(
+    first_keep, first_got = traded(
         meet_cols(
             rows, level_side, flip_near,
-            after(
-                (gate_a, gate_got_a, lifted_a, lifted_got_a, gate_b, gate_got_b, lifted_b,
-                 lifted_got_b),
-                to_prev,
-            ),
+            after((gate_a, gate_got_a, lifted_a, lifted_got_a), to_prev),
         )
     )
     back_both = jnp.stack([back_rows, back_far])
@@ -1099,22 +1094,30 @@
     keep_a, send_a, keep_b, send_b = bundle_grads(
         count, places, (front_both, front_other), (back_both, back_other), one_parts, attended,
         row_context,
-        context_own.astype(BF16), time_grads,
+        context_own.astype(BF16),
     )
     from_next, from_prev, down_got, send_a, send_b = meeting(
         from_next, from_prev, down_got, send_a, send_b
     )
     got_a = swap(send_a, "seq", 1)
     raw, last_away, last_own, last_low = tail(
-        places[1:], query_grad, kept, from_next, from_prev, tables, w_query, w_key, w_value
+        places[1:], query_grad, kept, from_next, from_prev, tables, w_query, w_key, w_value,
+        time_grads,
     )
     last_got = swap(last_away, "tensor", 1)
     raw_got = swap(raw, "seq", 1)
     last_sum = (
         last_low.astype(F32) + last_got[local_rows:].astype(F32)
     ).astype(BF16)
-    last_far, both_got = meeting(swap(last_sum, "tensor", 2), both_got)
-    both_keep, both_got = halve(added(both_keep, both_got).astype(BF16), 2)
+    second_keep, second_got = traded(
+        meet_cols(
+            rows, level_side, flip_near,
+            after((gate_b, gate_got_b, lifted_b, lifted_got_b), last_away),
+        )
+    )
+    last_sum, first_got = meeting(last_sum, first_got)
+    first_keep, first_got = halve(added(first_keep, first_got).astype(BF16), 2)
+    last_far, raw_got = meeting(swap(last_sum, "tensor", 2), raw_got)
     frame_grad = last_own + last_got[:local_rows].astype(F32) + last_far.astype(F32)
 
     time_late, means_late, inverse_late, vectors_late = after(
@@ -1136,10 +1139,8 @@
     )[None]
     sums = sums + swap(sums, "tensor", 1)
     sums = sums + swap(sums, "tensor", 2)
-    sums, got_a, raw_got = meeting(sums, got_a, raw_got)
-    got_b = swap(after(send_b, got_a), "seq", 1)
-    time_both = time_grads.reshape(1, -1) + got_a[0, rows : rows + 1].astype(F32)
-    left_keep, left_got = halve(added(keep_a, got_a[:, :rows]).astype(BF16), 1)
+    sums, first_got, second_got = meeting(sums, first_got, second_got)
+    second_keep, second_got = halve(added(second_keep, second_got).astype(BF16), 2)
     plain = sums[0, :local_rows, None] / model_width
     cross = sums[0, local_rows : 2 * local_rows, None] / model_width
     vectors = own_cols(sums[0, 2 * local_rows :].reshape(5, model_width))
@@ -1167,12 +1168,9 @@
 
     normed_pair = (one_own_half, normed_got)
     grad_down = halve_end(down_keep, down_got, 3)
-    gate_up = halve_end(both_keep, both_got, 3)
-    units = gate_up.shape[1] // 4
-    gate_a, up_a, gate_b, up_b = (gate_up[:, i * units : (i + 1) * units] for i in range(4))
-    grad_gate_w = jnp.concatenate([gate_a, gate_b], 1)
-    grad_up_w = jnp.concatenate([up_a, up_b], 1)
-    raw_pair = (raw, raw_got)
+    raw_pair = (raw[: 3 * head_cols], raw_got[: 3 * head_cols])
+    time_got = raw_got[3 * head_cols : 3 * head_cols + 2, :head_cols].astype(F32)
+    time_both = (time_grads + time_got).reshape(1, 2 * head_cols)
     own_time_rows = lax.dynamic_index_in_dim(
         time_column.reshape(count // 2, 2, -1), column, 1, False
     ).reshape(-1, 1)
@@ -1184,19 +1182,27 @@
     heads_keep, heads_got = halve(
         (blocks + outer).astype(BF16).reshape(count // 2, rows, 3 * head_cols), 1
     )
-    heads_got, got_b = meeting(heads_got, got_b)
+    heads_got, got_a = meeting(heads_got, got_a)
     heads_next = added(heads_keep, heads_got).astype(BF16)
+    got_b = swap(after(send_b, got_a), "seq", 1)
+    left_keep, left_got = halve(added(keep_a, got_a).astype(BF16), 1)
     heads_sum = halve_all(heads_next, 2)
+    got_b, second_got = meeting(got_b, second_got)
     last_next = added(*halve(added(keep_b, got_b).astype(BF16), 1))
+    first, second = halve_end(first_keep, first_got, 3), halve_end(second_keep, second_got, 3)
+    units = first.shape[1] // 2
+    grad_gate_w = jnp.concatenate([first[:, :units], second[:, :units]], 1)
+    grad_up_w = jnp.concatenate([first[:, units:], second[:, units:]], 1)
     small = jnp.stack(
         [d_gain_attn, d_bias_attn, vectors[3], vectors[4], vectors[1], vectors[2]]
     ).reshape(6, devices, -1).transpose(1, 0, 2)
-    small = after(small, last_next)
-    bit = 0
-    while small.shape[0] > 1:
+    small = small.reshape(count // 2, 2, 6, -1).transpose(1, 0, 2, 3).reshape(count, 6, -1)
+    small = after(small, heads_next)
+    bit = 1
+    while small.shape[0] > 2:
         small = added(*halve(small, bit))
         bit += 1
-    small = small[0]
+    small = added(*halve(small, 0))[0]
     left, right = halve_end(left_keep, left_got, 2), halve_all(last_next, 2)
     part, rows = head_cols // count, model_width // count
     grad_c_query = left[:, :head_cols]

time: 596 us -> 508 us (0.85)
  waiting for transfers between devices: 267 us -> 183 us
  starting transfers between devices: 75.5 us -> 85.1 us
  local copies, waits for them, and re-layouts: 34.3 us -> 27.2 us
    ppermute x69 -> x71, waiting for transfers between devices: 247 us -> 162 us  [swap(): lax.ppermute(value, axis, [(i, i ^ by) for i in range(lax.axis_size(axis))])]
    ppermute x69 -> x71, starting transfers between devices: 65 us -> 74.8 us  [swap(): lax.ppermute(value, axis, [(i, i ^ by) for i in range(lax.axis_size(axis))])]
    pallas_call x1 -> x2, Pallas kernels: 13.1 us -> 15.4 us  [meet_cols(): pl.pallas_call(functools.partial(meet_cols_body, size), in_specs=[pl.Bloc...]
  transfers between devices with their start and end apart: 73 -> 75, of which waited for: 26 -> 24; matrix products, arithmetic and copies ran while one was open for 12% -> 12% of each run, Pallas kernels for 27% -> 32%
where the time goes in v4:
time: 508 us; the launch traced here: 501 us
  waiting for transfers between devices  183 us (36%)
  Pallas kernels  158 us (31%)
  starting transfers between devices  85.1 us (17%)
  other arithmetic  40.8 us (8%)
  local copies, waits for them, and re-layouts  27.2 us (5%)
    ppermute x71, waiting for transfers between devices, swap(): lax.ppermute(value, axis, [(i, i ^ by) for i in range(lax.axis_size(axis))])  162 us
    ppermute x71, starting transfers between devices, swap(): lax.ppermute(value, axis, [(i, i ^ by) for i in range(lax.axis_size(axis))])  74.8 us
    pallas_call x2, Pallas kernels, ffn(): pl.pallas_call(functools.partial(ffn_second_body if half else ffn_first_b...  29.7 us
    pallas_call x1, Pallas kernels, cross_backward(): pl.pallas_call(cross_backward_body, grid=(1,), out_shape=[jax.ShapeDtypeS...  21 us
    ppermute x4, waiting for transfers between devices, shift(): return lax.ppermute(value, axis, pairs)  20.2 us
    pallas_call x1, Pallas kernels, cross_forward(): pl.pallas_call(functools.partial(cross_forward_body, width // devices), g...  16.7 us
    pallas_call x1, Pallas kernels, attend_back(): pl.pallas_call(backward_body, in_specs=[pl.BlockSpec(memory_space=pltpu.S...  16.3 us
    pallas_call x2, Pallas kernels, meet_cols(): pl.pallas_call(functools.partial(meet_cols_body, size), in_specs=[pl.Bloc...  15.4 us
  transfers between devices with their start and end apart: 75, of which 24 were waited for; matrix products, arithmetic and copies ran while one was open for 12% of the time, Pallas kernels for 32%

profile of v4, /device:TPU:0, one launch (start us, length us, event | category | flops | bytes accessed | tf_op | source)
XLA Modules:
  0.0 500.6 jit_solution(11675371706994448277)
XLA Ops:
  1.2 2.6 collective-permute-start.1
  14.0 1.8 collective-permute-start.6
  21.1 9.6 %front.1 = (bf16[384,512]{1,0:T(8,128)(2,1)}, bf16[2,384,512]{2,1,0:T(8,128)(2,1)}, bf16[128,1536]{1,0:T(8,128)(2,1)}, bf16[512,1536]{1,0:T(8,128)(2,1)}, bf16[7...) custom-call(s32[2]{0:T(128)} %rev.4.place, ...), custom_call_target="tpu_custom_call" | custom-call | flops 1 | bytes 1 | tf_op jit(solution)/shard_map/front/pallas_call | solution.py:882
  30.7 2.3 collective-permute-start.7
  36.9 10.4 %attend_near.1 = (f32[6,512]{1,0:T(8,128)}, f32[6,512]{1,0:T(8,128)}, f32[384,512]{1,0:T(8,128)}) custom-call(s32[5]{0:T(128)} %pad_add_fusion.2.span, bf16[384,512]{1,0:T(8,128)(2,1)} %get-tuple-element.194.q, bf16[2,384,512]{2,1,0:T(8,128)(2,1)} %get-tuple-element.197.kv.kv1, f32[384,1]{1,0:T(8,128)} %get-tuple-element.200.tk, ...), custom_call_target="tpu_custom_call" | custom-call | flops 1 | bytes 1 | tf_op jit(solution)/shard_map/attend_near/pallas_call | solution.py:304
  47.3 20.2 %collective-permute-done.7.kv0 = bf16[2,384,512]{2,1,0:T(8,128)(2,1)S(1)} collective-permute-done((bf16[2,384,512]{2,1,0:T(8,128)(2,1)}, bf16[2,384,512]{2,1,0:T(8,128)(2,1)S(1)}, u32[]{:S(2)}, u32[]{:S(2)}) %collective-permute-start.7) | collective-permute-done | bytes 786464 | tf_op jit(solution)/shard_map/ppermute | solution.py:33
  67.5 1.9 collective-permute-done.10.o2
  72.0 7.0 %attend_far.1 = (bf16[384,512]{1,0:T(8,128)(2,1)}, f32[6,512]{1,0:T(8,128)}, bf16[256,1536]{1,0:T(8,128)(2,1)}, f32[128,1536]{1,0:T(8,128)}, bf16[128,1536]{1,0:T(8,128)(2,1)}) custom-call(s32[5]{0:T(128)} %pad_add_fusion.2.span, bf16[384,512]{1,0:T(8,128)(2,1)} %get-tuple-element.194.q, bf16[2,384,512]{2,1,0:T(8,128)(2,1)} %copy-done.20, ...), custom_call_target="tpu_custom_call" | custom-call | flops 1 | bytes 1 | tf_op jit(solution)/shard_map/attend_far/pallas_call | solution.py:322
  79.2 2.5 collective-permute-done.16.got
  83.8 4.0 collective-permute-start.19
  87.8 6.5 %collective-permute-done.17.far = bf16[128,1536]{1,0:T(8,128)(2,1)S(1)} collective-permute-done((bf16[128,1536]{1,0:T(8,128)(2,1)S(1)}, bf16[128,1536]{1,0:T(8,128)(2,1)S(1)}, u32[]{:S(2)}, u32[]{:S(2)}) %collective-permute-start.17) | collective-permute-done | bytes 393248 | tf_op jit(solution)/shard_map/ppermute | solution.py:27
  94.9 1.7 collective-permute-done.18
  97.4 16.7 %cross.1 = (bf16[128,3072]{1,0:T(8,128)(2,1)}, bf16[128,1536]{1,0:T(8,128)(2,1)}, f32[128,1536]{1,0:T(8,128)}, f32[128,1536]{1,0:T(8,128)}, bf16[128,1536]{1,0:T...) custom-call(s32[2]{0:T(128)} %copy-done.68, bf16[128,1536]{1,0:T(8,128)(2,1)} %get-tuple-element.193.rows, ...), custom_call_target="tpu_custom_call" | custom-call | flops 1 | bytes 1 | tf_op jit(solution)/shard_map/cross/pallas_call | solution.py:529
  117.0 9.3 %collective-permute-done.22.n2 = bf16[128,1536]{1,0:T(8,128)(2,1)S(1)} collective-permute-done((bf16[128,1536]{1,0:T(8,128)(2,1)}, bf16[128,1536]{1,0:T(8,128)(2,1)S(1)}, u32[]{:S(2)}, u32[]{:S(2)}) %collective-permute-start.22) | collective-permute-done | bytes 393248 | tf_op jit(solution)/shard_map/ppermute | solution.py:27
  126.9 1.7 collective-permute-done.23.n3
  130.1 4.2 collective-permute-start.26
  136.9 14.7 %ffn.2 = (bf16[512,768]{1,0:T(8,128)(2,1)}, bf16[384,512]{1,0:T(8,128)(2,1)}, bf16[384,512]{1,0:T(8,128)(2,1)}, bf16[512,768]{1,0:T(8,128)(2,1)}, bf16[512,768]{...) custom-call(s32[2]{0:T(128)} %copy-done.68, ...), custom_call_target="tpu_custom_call" | custom-call | flops 1 | bytes 1 | tf_op jit(solution)/shard_map/ffn/pallas_call | solution.py:618
  153.0 15.0 %ffn.3 = (bf16[512,768]{1,0:T(8,128)(2,1)}, bf16[384,512]{1,0:T(8,128)(2,1)}, bf16[384,512]{1,0:T(8,128)(2,1)}, bf16[512,768]{1,0:T(8,128)(2,1)}, bf16[512,768]{...) custom-call(s32[2]{0:T(128)} %copy-done.68, ...), custom_call_target="tpu_custom_call" | custom-call | flops 1 | bytes 1 | tf_op jit(solution)/shard_map/ffn/pallas_call | solution.py:618
  168.2 2.5 collective-permute-done.30.got
  172.0 1.8 collective-permute-start.31
  173.8 2.0 collective-permute-start.32
  175.8 7.4 %collective-permute-done.31.far = bf16[128,1536]{1,0:T(8,128)(2,1)S(1)} collective-permute-done((bf16[128,1536]{1,0:T(8,128)(2,1)S(1)}, bf16[128,1536]{1,0:T(8,128)(2,1)S(1)}, u32[]{:S(2)}, u32[]{:S(2)}) %collective-permute-start.31) | collective-permute-done | bytes 393248 | tf_op jit(solution)/shard_map/ppermute | solution.py:27
  185.3 21.0 %cross_back.1 = (bf16[128,3072]{1,0:T(8,128)(2,1)}, bf16[256,1536]{1,0:T(8,128)(2,1)}, f32[4,1536]{1,0:T(4,128)}, bf16[128,1536]{1,0:T(8,128)(2,1)}) custom-call(f32[128,1536]{1,0:T(8,128)} %get-tuple-element.246.own, bf16[256,1536]{1,0:T(8,128)(2,1)} %copy-done.21, bf16[128,1536]{1,0:T(8,128)(2,1)} %copy-done.54, ...), custom_call_target="tpu_custom_call" | custom-call | flops 1 | bytes 1 | tf_op jit(solution)/shard_map/cross_back/pallas_call | solution.py:683
  206.5 2.0 collective-permute-start.38
  208.5 1.7 collective-permute-start.37
  212.7 6.7 %meet_rows.1 = (bf16[384,1536]{1,0:T(8,128)(2,1)}, bf16[384,1536]{1,0:T(8,128)(2,1)}) custom-call(s32[1]{0:T(128)} %bitcast.12.side, bf16[384,512]{1,0:T(8,128)(2,1)} %get-tuple-element.267.own_a, bf16[384,512]{1,0:T(8,128)(2,1)} %copy-done.46, bf16[384,512]{1,0:T(8,128)(2,1)} %get-tuple-element.269.own_b, bf16[384,512]{1,0:T(8,128)(2,1)} %collective-permute-done.33.pair_b, ...), custom_call_target="tpu_custom_call" | custom-call | flops 1 | bytes 1 | tf_op jit(solution)/shard_map/meet_rows/pallas_call | solution.py:708
  219.3 7.6 %collective-permute-done.38.refs_3_ = bf16[512,768]{1,0:T(8,128)(2,1)S(1)} collective-permute-done((bf16[512,768]{1,0:T(8,128)(2,1)}, bf16[512,768]{1,0:T(8,128)(2,1)S(1)}, u32[]{:S(2)}, u32[]{:S(2)}) %collective-permute-start.38) | collective-permute-done | bytes 786464 | tf_op jit(solution)/shard_map/ppermute | solution.py:27
  227.8 5.7 %collective-permute-start.45 = (bf16[2,192,1536]{2,1,0:T(8,128)(2,1)}, bf16[2,192,1536]{2,1,0:T(8,128)(2,1)}, u32[]{:S(2)}, u32[]{:S(2)}) collective-permute-start(bf16[2,192,1536]{2,1,0:T(8,128)(2,1)} %bitcast.144), channel_id=1, source_target_pairs={{0,2},{1,3},{2,0},{3,1},{4,6},{5,7},{6,4},{7,5},{8,10},{9,11},{10,... | collective-permute-start | bytes 3538952 | tf_op jit(solution)/shard_map/ppermute | solution.py:27
  233.8 1.8 collective-permute-start.44
  238.8 16.3 %attend_back.1 = (f32[384,512]{1,0:T(8,128)}, bf16[2,384,512]{2,1,0:T(8,128)(2,1)}, f32[2,384,512]{2,1,0:T(8,128)}, bf16[2,384,512]{2,1,0:T(8,128)(2,1)}, f32[2,384]{1,0:T(2,128)}) custom-call(s32[5]{0:T(128)} %pad_add_fusion.2.span, bf16[384,512]{1,0:T(8,128)(2,1)} %get-tuple-element.194.q, bf16[2,384,512]{2,1,0:T(8,128)(2,1)} %copy-done.20, ...), custom_call_target="tpu_custom_call" | custom-call | flops 1 | bytes 1 | tf_op jit(solution)/shard_map/attend_back/pallas_call | solution.py:339
  255.1 15.3 %collective-permute-done.44.refs_3_ = bf16[512,768]{1,0:T(8,128)(2,1)} collective-permute-done((bf16[512,768]{1,0:T(8,128)(2,1)}, bf16[512,768]{1,0:T(8,128)(2,1)}, u32[]{:S(2)}, u32[]{:S(2)}) %collective-permute-start.44) | collective-permute-done | bytes 786464 | tf_op jit(solution)/shard_map/ppermute | solution.py:27
  274.0 5.5 %collective-permute-start.48 = (bf16[2,384,512]{2,1,0:T(8,128)(2,1)}, bf16[2,384,512]{2,1,0:T(8,128)(2,1)}, u32[]{:S(2)}, u32[]{:S(2)}) collective-permute-start(bf16[2,384,512]{2,1,0:T(8,128)(2,1)} %get-tuple-element.295), channel_id=1, source_target_pairs={{0,1},{1,2},{2,3},{3,4},{4,5},{5,6},{6,7},{8,9},{9,10},{10,11},{11... | collective-permute-start | bytes 2359304 | tf_op jit(solution)/shard_map/ppermute | solution.py:33
  279.4 1.9 add_convert_fusion.2
  282.2 1.7 collective-permute-start.49
  284.7 7.6 %meet_cols.2 = (bf16[384,1536]{1,0:T(8,128)(2,1)}, bf16[384,1536]{1,0:T(8,128)(2,1)}) custom-call(s32[1]{0:T(128)} %bitcast.12.side, bf16[2,768,128]{2,1,0:T(8,128)(2,1)} %copy-done.9, bf16[2,768,128]{2,1,0:T(8,128)(2,1)} %collective-permute-done.34.p1, bf16[2,768,128]{2,1,0:T(8,128)(2,1)} %copy-done.27, bf16[2,768,128]{2,1,0:T(8,128)(2,1)} %collective-permute-done.35.p3, ...), custom_call_target="tpu_custom_call" | custom-call | flops 1 | bytes 1 | tf_op jit(solution)/shard_map/meet_cols/pallas_call | solution.py:732
  293.4 1.8 add_convert_fusion.8.kv
  295.2 10.7 %bundle.1 = (bf16[4,192,768]{2,1,0:T(8,128)(2,1)}, bf16[4,192,768]{2,1,0:T(8,128)(2,1)}, bf16[4,192,768]{2,1,0:T(8,128)(2,1)}, bf16[4,192,768]{2,1,0:T(8,128)(2,1)}) custom-call(s32[2]{0:T(128)} %copy-done.68, bf16[2,128,3072]{2,1,0:T(8,128)(2,1)} %copy-done.4, bf16[2,128,3072]{2,1,0:T(8,128)(2,1)} %collective-permute-done.40.f13, ...), custom_call_target="tpu_custom_call" | custom-call | flops 1 | bytes 1 | tf_op jit(solution)/shard_map/bundle/pallas_call | solution.py:817
  305.9 15.2 %collective-permute-done.49 = bf16[1,192,1536]{2,1,0:T(8,128)(2,1)} collective-permute-done((bf16[1,192,1536]{2,1,0:T(8,128)(2,1)}, bf16[1,192,1536]{2,1,0:T(8,128)(2,1)}, u32[]{:S(2)}, u32[]{:S(2)}) %collective-permute-start.49) | collective-permute-done | bytes 589856 | tf_op jit(solution)/shard_map/ppermute | solution.py:27
  321.1 7.7 %tail.1 = (bf16[1168,512]{1,0:T(8,128)(2,1)}, bf16[1024,384]{1,0:T(8,128)(2,1)}, f32[512,384]{1,0:T(8,128)}, bf16[512,384]{1,0:T(8,128)(2,1)}) custom-call(s32[1]{0:T(128)} %bitcast.1.place, f32[384,512]{1,0:T(8,128)} %get-tuple-element.283.dq, f32[2,384,512]{2,1,0:T(8,128)} %get-tuple-element.284.kept, bf16[2,384,512]{2,1,0:T(8,128)(2,1)} %collective-permute-done.47.ahead, ...), custom_call_target="tpu_custom_call" | custom-call | flops 1 | bytes 1 | tf_op jit(solution)/shard_map/tail/pallas_call | solution.py:395
  328.9 7.9 %meet_cols.3 = (bf16[384,1536]{1,0:T(8,128)(2,1)}, bf16[384,1536]{1,0:T(8,128)(2,1)}) custom-call(s32[1]{0:T(128)} %bitcast.12.side, bf16[2,768,128]{2,1,0:T(8,128)(2,1)} %copy-done.9, bf16[2,768,128]{2,1,0:T(8,128)(2,1)} %collective-permute-done.34.p1, bf16[2,768,128]{2,1,0:T(8,128)(2,1)} %copy-done.27, bf16[2,768,128]{2,1,0:T(8,128)(2,1)} %collective-permute-done.35.p3, ...), custom_call_target="tpu_custom_call" | custom-call | flops 1 | bytes 1 | tf_op jit(solution)/shard_map/meet_cols/pallas_call | solution.py:732
  336.8 3.0 collective-permute-start.62
  341.0 2.3 add_bitcast_fusion
  346.1 1.6 fusion.3
  348.5 3.4 collective-permute-start.61
  352.0 3.5 collective-permute-done.53
  355.5 2.8 collective-permute-done.54
  359.3 6.5 %down.1 = (bf16[256,1536]{1,0:T(8,128)(2,1)}, f32[128,1536]{1,0:T(8,128)}, bf16[128,1536]{1,0:T(8,128)(2,1)}) custom-call(bf16[512,768]{1,0:T(8,128)(2,1)} %get-tuple-element.320.first, bf16[512,768]{1,0:T(8,128)(2,1)} %get-tuple-element.321.second, bf16[1536,1536]{1,0:T(8,128)(2,1)} %down_w.5), custom_call_target="tpu_custom_call" | custom-call | flops 1 | bytes 1 | tf_op jit(solution)/shard_map/down/pallas_call | solution.py:756
  366.8 2.4 multiply_reduce_fusion
  370.5 2.6 fusion.7
  381.1 1.9 fusion.2
  383.1 3.5 collective-permute-start.70
  392.9 19.5 %collective-permute-done.63 = bf16[2,192,1152]{2,1,0:T(8,128)(2,1)} collective-permute-done((bf16[2,192,1152]{2,1,0:T(8,128)(2,1)}, bf16[2,192,1152]{2,1,0:T(8,128)(2,1)}, u32[]{:S(2)}, u32[]{:S(2)}) %collective-permute-start.63) | collective-permute-done | bytes 884768 | tf_op jit(solution)/shard_map/ppermute | solution.py:27
  414.0 4.7 collective-permute-start.68
  418.6 2.0 collective-permute-start.69
  420.8 1.7 add_convert_fusion
  422.5 14.1 %collective-permute-done.66 = f32[2,6,48]{2,0,1:T(2,128)S(1)} collective-permute-done((f32[2,6,48]{2,0,1:T(2,128)S(1)}, f32[2,6,48]{2,0,1:T(2,128)S(1)}, u32[]{:S(2)}, u32[]{:S(2)}) %collective-permute-start.66) | collective-permute-done | bytes 2336 | tf_op jit(solution)/shard_map/ppermute | solution.py:27
  436.5 2.0 collective-permute-start.67
  438.6 6.0 %collective-permute-done.67 = f32[1,6,48]{2,0,1:T(1,128)S(1)} collective-permute-done((f32[1,6,48]{2,0,1:T(1,128)S(1)}, f32[1,6,48]{2,0,1:T(1,128)S(1)}, u32[]{:S(2)}, u32[]{:S(2)}) %collective-permute-start.67) | collective-permute-done | bytes 1184 | tf_op jit(solution)/shard_map/ppermute | solution.py:27
  449.3 3.1 collective-permute-done.57
  452.6 4.3 collective-permute-done.73
  458.7 10.8 %collective-permute-done.74 = bf16[1,192,768]{2,1,0:T(8,128)(2,1)S(1)} collective-permute-done((bf16[1,192,768]{2,1,0:T(8,128)(2,1)S(1)}, bf16[1,192,768]{2,1,0:T(8,128)(2,1)S(1)}, u32[]{:S(2)}, u32[]{:S(2)}) %collective-permute-start.74) | collective-permute-done | bytes 294944 | tf_op jit(solution)/shard_map/ppermute | solution.py:27
  471.8 13.4 %collective-permute-done.71 = bf16[2,192,768]{2,1,0:T(8,128)(2,1)S(1)} collective-permute-done((bf16[2,192,768]{2,1,0:T(8,128)(2,1)S(1)}, bf16[2,192,768]{2,1,0:T(8,128)(2,1)S(1)}, u32[]{:S(2)}, u32[]{:S(2)}) %collective-permute-start.71) | collective-permute-done | bytes 589856 | tf_op jit(solution)/shard_map/ppermute | solution.py:27
  486.4 1.7 pad_maximum_fusion.2
  488.2 11.0 %collective-permute-done.72 = bf16[1,192,768]{2,1,0:T(8,128)(2,1)S(1)} collective-permute-done((bf16[1,192,768]{2,1,0:T(8,128)(2,1)S(1)}, bf16[1,192,768]{2,1,0:T(8,128)(2,1)S(1)}, u32[]{:S(2)}, u32[]{:S(2)}) %collective-permute-start.72) | collective-permute-done | bytes 294944 | tf_op jit(solution)/shard_map/ppermute | solution.py:27
  (381 shorter events, 86.5 us)
Async XLA Ops:
  0.7 19.5 %collective-permute-start = (bf16[512,384]{1,0:T(8,128)(2,1)}, bf16[512,384]{1,0:T(8,128)(2,1)S(1)}, u32[]{:S(2)}, u32[]{:S(2)}) collective-permute-start(bf16[512,384]{1,0:T(8,128)(2,1)} %x0.1), channel_id=1, source_target_pairs={{0,8},{8,0},{16,24},{24,16},{1,9},{9,1},{17,25},{25,17},{2,10},{10... | collective-permute-start | bytes 1179656 | tf_op jit(solution)/shard_map/ppermute | solution.py:27
  1.2 12.8 %collective-permute-start.1 = (bf16[512,384]{1,0:T(8,128)(2,1)}, bf16[512,384]{1,0:T(8,128)(2,1)S(1)}, u32[]{:S(2)}, u32[]{:S(2)}) collective-permute-start(bf16[512,384]{1,0:T(8,128)(2,1)} %x0.1), channel_id=1, source_target_pairs={{0,16},{8,24},{16,0},{24,8},{1,17},{9,25},{17,1},{25,9},{2,18},{10... | collective-permute-start | bytes 1179656 | tf_op jit(solution)/shard_map/ppermute | solution.py:27
  7.9 9.4 %collective-permute-start.3 = (f32[6,384]{1,0:T(8,128)S(1)}, f32[6,384]{1,0:T(8,128)S(1)}, u32[]{:S(2)}, u32[]{:S(2)}) collective-permute-start(f32[6,384]{1,0:T(8,128)S(1)} %stack.98.g0), channel_id=1, source_target_pairs={{0,8},{8,0},{16,24},{24,16},{1,9},{9,1},{17,25},{25,17},{2,10},{10... | collective-permute-start | bytes 27656 | tf_op jit(solution)/shard_map/ppermute | solution.py:27
  14.0 16.7 %collective-permute-start.6 = (bf16[512,384]{1,0:T(8,128)(2,1)}, bf16[512,384]{1,0:T(8,128)(2,1)S(1)}, u32[]{:S(2)}, u32[]{:S(2)}) collective-permute-start(bf16[512,384]{1,0:T(8,128)(2,1)} %param.43), channel_id=1, source_target_pairs={{0,1},{1,0},{2,3},{3,2},{4,5},{5,4},{6,7},{7,6},{8,9},{9,8},{10,11... | collective-permute-start | bytes 1179656 | tf_op jit(solution)/shard_map/ppermute | solution.py:27
  15.8 51.7 %collective-permute-start.9 = (bf16[1536,384]{1,0:T(8,128)(2,1)}, bf16[1536,384]{1,0:T(8,128)(2,1)}, u32[]{:S(2)}, u32[]{:S(2)}) collective-permute-start(bf16[1536,384]{1,0:T(8,128)(2,1)} %q0.3), channel_id=1, source_target_pairs={{0,16},{8,24},{16,0},{24,8},{1,17},{9,25},{17,1},{25,9},{2,18},{10... | collective-permute-start | bytes 3538952 | tf_op jit(solution)/shard_map/ppermute | solution.py:27
  17.3 52.1 %collective-permute-start.10 = (bf16[384,1536]{1,0:T(8,128)(2,1)}, bf16[384,1536]{1,0:T(8,128)(2,1)}, u32[]{:S(2)}, u32[]{:S(2)}) collective-permute-start(bf16[384,1536]{1,0:T(8,128)(2,1)} %o0.3), channel_id=1, source_target_pairs={{0,16},{8,24},{16,0},{24,8},{1,17},{9,25},{17,1},{25,9},{2,18},{10... | collective-permute-start | bytes 3538952 | tf_op jit(solution)/shard_map/ppermute | solution.py:27
  30.7 36.8 %collective-permute-start.7 = (bf16[2,384,512]{2,1,0:T(8,128)(2,1)}, bf16[2,384,512]{2,1,0:T(8,128)(2,1)S(1)}, u32[]{:S(2)}, u32[]{:S(2)}) collective-permute-start(bf16[2,384,512]{2,1,0:T(8,128)(2,1)} %get-tuple-element.197.kv.kv1), channel_id=1, source_target_pairs={{0,1},{1,2},{2,3},{3,4},{4,5},{5,6},{6,7},{8,9},{9,10},{10,11},{11... | collective-permute-start | bytes 2359304 | tf_op jit(solution)/shard_map/ppermute | solution.py:33
  33.0 34.6 %collective-permute-start.8 = (bf16[2,384,512]{2,1,0:T(8,128)(2,1)}, bf16[2,384,512]{2,1,0:T(8,128)(2,1)}, u32[]{:S(2)}, u32[]{:S(2)}) collective-permute-start(bf16[2,384,512]{2,1,0:T(8,128)(2,1)} %get-tuple-element.197.kv.kv1), channel_id=1, source_target_pairs={{1,0},{2,1},{3,2},{4,3},{5,4},{6,5},{7,6},{9,8},{10,9},{11,10},{12... | collective-permute-start | bytes 2359304 | tf_op jit(solution)/shard_map/ppermute | solution.py:33
  69.5 9.6 %collective-permute-start.12 = (bf16[1536,384]{1,0:T(8,128)(2,1)S(1)}, bf16[1536,384]{1,0:T(8,128)(2,1)}, u32[]{:S(2)}, u32[]{:S(2)}) collective-permute-start(bf16[1536,384]{1,0:T(8,128)(2,1)S(1)} %copy-done.6), channel_id=1, source_target_pairs={{0,8},{8,0},{16,24},{24,16},{1,9},{9,1},{17,25},{25,17},{2,10},{10... | collective-permute-start | bytes 3538952 | tf_op jit(solution)/shard_map/ppermute | solution.py:27
  69.5 9.6 %collective-permute-start.13 = (bf16[1536,384]{1,0:T(8,128)(2,1)}, bf16[1536,384]{1,0:T(8,128)(2,1)}, u32[]{:S(2)}, u32[]{:S(2)}) collective-permute-start(bf16[1536,384]{1,0:T(8,128)(2,1)} %collective-permute-done.9.q2), channel_id=1, source_target_pairs={{0,8},{8,0},{16,24},{24,16},{1,9},{9,1},{17,25},{25,17},{2,10},{10... | collective-permute-start | bytes 3538952 | tf_op jit(solution)/shard_map/ppermute | solution.py:27
  70.0 9.1 %collective-permute-start.14 = (bf16[384,1536]{1,0:T(8,128)(2,1)S(1)}, bf16[384,1536]{1,0:T(8,128)(2,1)}, u32[]{:S(2)}, u32[]{:S(2)}) collective-permute-start(bf16[384,1536]{1,0:T(8,128)(2,1)S(1)} %copy-done.7), channel_id=1, source_target_pairs={{0,8},{8,0},{16,24},{24,16},{1,9},{9,1},{17,25},{25,17},{2,10},{10... | collective-permute-start | bytes 3538952 | tf_op jit(solution)/shard_map/ppermute | solution.py:27
  70.0 9.1 %collective-permute-start.15 = (bf16[384,1536]{1,0:T(8,128)(2,1)}, bf16[384,1536]{1,0:T(8,128)(2,1)}, u32[]{:S(2)}, u32[]{:S(2)}) collective-permute-start(bf16[384,1536]{1,0:T(8,128)(2,1)} %collective-permute-done.10.o2), channel_id=1, source_target_pairs={{0,8},{8,0},{16,24},{24,16},{1,9},{9,1},{17,25},{25,17},{2,10},{10... | collective-permute-start | bytes 3538952 | tf_op jit(solution)/shard_map/ppermute | solution.py:27
  70.5 8.6 %collective-permute-start.11 = (bf16[256,384]{1,0:T(8,128)(2,1)S(1)}, bf16[256,384]{1,0:T(8,128)(2,1)S(1)}, u32[]{:S(2)}, u32[]{:S(2)}) collective-permute-start(bf16[256,384]{1,0:T(8,128)(2,1)S(1)} %copy-done.22), channel_id=1, source_target_pairs={{0,16},{8,24},{16,0},{24,8},{1,17},{9,25},{17,1},{25,9},{2,18},{10... | collective-permute-start | bytes 589832 | tf_op jit(solution)/shard_map/ppermute | solution.py:27
  83.1 11.2 %collective-permute-start.17 = (bf16[128,1536]{1,0:T(8,128)(2,1)S(1)}, bf16[128,1536]{1,0:T(8,128)(2,1)S(1)}, u32[]{:S(2)}, u32[]{:S(2)}) collective-permute-start(bf16[128,1536]{1,0:T(8,128)(2,1)S(1)} %add_convert_fusion.7), channel_id=1, source_target_pairs={{0,16},{8,24},{16,0},{24,8},{1,17},{9,25},{17,1},{25,9},{2,18},{10... | collective-permute-start | bytes 1179656 | tf_op jit(solution)/shard_map/ppermute | solution.py:27
  83.8 30.4 %collective-permute-start.19 = (bf16[768,512]{1,0:T(8,128)(2,1)}, bf16[768,512]{1,0:T(8,128)(2,1)S(1)}, u32[]{:S(2)}, u32[]{:S(2)}) collective-permute-start(bf16[768,512]{1,0:T(8,128)(2,1)} %get-tuple-element.230), channel_id=1, source_target_pairs={{0,1},{1,0},{2,3},{3,2},{4,5},{5,4},{6,7},{7,6},{8,9},{9,8},{10,11... | collective-permute-start | bytes 2359304 | tf_op jit(solution)/shard_map/ppermute | solution.py:27
  94.3 19.8 %collective-permute-start.20 = (bf16[2,512,384]{2,1,0:T(8,128)(2,1)S(1)}, bf16[2,512,384]{2,1,0:T(8,128)(2,1)S(1)}, u32[]{:S(2)}, u32[]{:S(2)}) collective-permute-start(bf16[2,512,384]{2,1,0:T(8,128)(2,1)S(1)} %pad_maximum_fusion.4.g0), channel_id=1, source_target_pairs={{0,16},{8,24},{16,0},{24,8},{1,17},{9,25},{17,1},{25,9},{2,18},{10... | collective-permute-start | bytes 2359304 | tf_op jit(solution)/shard_map/ppermute | solution.py:27
  115.0 11.3 %collective-permute-start.22 = (bf16[128,1536]{1,0:T(8,128)(2,1)}, bf16[128,1536]{1,0:T(8,128)(2,1)S(1)}, u32[]{:S(2)}, u32[]{:S(2)}) collective-permute-start(bf16[128,1536]{1,0:T(8,128)(2,1)} %get-tuple-element.233.n0), channel_id=1, source_target_pairs={{0,16},{8,24},{16,0},{24,8},{1,17},{9,25},{17,1},{25,9},{2,18},{10... | collective-permute-start | bytes 1179656 | tf_op jit(solution)/shard_map/ppermute | solution.py:27
  116.5 17.8 %collective-permute-start.24 = (bf16[2,512,384]{2,1,0:T(8,128)(2,1)S(1)}, bf16[2,512,384]{2,1,0:T(8,128)(2,1)S(1)}, u32[]{:S(2)}, u32[]{:S(2)}) collective-permute-start(bf16[2,512,384]{2,1,0:T(8,128)(2,1)S(1)} %pad_maximum_fusion.4.g0), channel_id=1, source_target_pairs={{0,8},{8,0},{16,24},{24,16},{1,9},{9,1},{17,25},{25,17},{2,10},{10... | collective-permute-start | bytes 2359304 | tf_op jit(solution)/shard_map/ppermute | solution.py:27
  116.5 18.6 %collective-permute-start.25 = (bf16[2,512,384]{2,1,0:T(8,128)(2,1)S(1)}, bf16[2,512,384]{2,1,0:T(8,128)(2,1)S(1)}, u32[]{:S(2)}, u32[]{:S(2)}) collective-permute-start(bf16[2,512,384]{2,1,0:T(8,128)(2,1)S(1)} %collective-permute-done.20.g2), channel_id=1, source_target_pairs={{0,8},{8,0},{16,24},{24,16},{1,9},{9,1},{17,25},{25,17},{2,10},{10... | collective-permute-start | bytes 2359304 | tf_op jit(solution)/shard_map/ppermute | solution.py:27
  126.4 8.0 %collective-permute-start.21 = (bf16[128,1536]{1,0:T(8,128)(2,1)}, bf16[128,1536]{1,0:T(8,128)(2,1)S(1)}, u32[]{:S(2)}, u32[]{:S(2)}) collective-permute-start(bf16[128,1536]{1,0:T(8,128)(2,1)} %get-tuple-element.233.n0), channel_id=1, source_target_pairs={{0,8},{8,0},{16,24},{24,16},{1,9},{9,1},{17,25},{25,17},{2,10},{10... | collective-permute-start | bytes 1179656 | tf_op jit(solution)/shard_map/ppermute | solution.py:27
  128.6 39.5 %collective-permute-start.28 = (bf16[128,3072]{1,0:T(8,128)(2,1)}, bf16[128,3072]{1,0:T(8,128)(2,1)}, u32[]{:S(2)}, u32[]{:S(2)}) collective-permute-start(bf16[128,3072]{1,0:T(8,128)(2,1)} %get-tuple-element.252), channel_id=1, source_target_pairs={{0,16},{8,24},{16,0},{24,8},{1,17},{9,25},{17,1},{25,9},{2,18},{10... | collective-permute-start | bytes 2359304 | tf_op jit(solution)/shard_map/ppermute | solution.py:27
  130.1 21.4 %collective-permute-start.26 = (bf16[768,128]{1,0:T(8,128)(2,1)}, bf16[768,128]{1,0:T(8,128)(2,1)}, u32[]{:S(2)}, u32[]{:S(2)}) collective-permute-start(bf16[768,128]{1,0:T(8,128)(2,1)} %get-tuple-element.244), channel_id=1, source_target_pairs={{0,1},{1,0},{2,3},{3,2},{4,5},{5,4},{6,7},{7,6},{8,9},{9,8},{10,11... | collective-permute-start | bytes 589832 | tf_op jit(solution)/shard_map/ppermute | solution.py:27
  152.7 15.4 %collective-permute-start.27 = (bf16[2,768,128]{2,1,0:T(8,128)(2,1)S(1)}, bf16[2,768,128]{2,1,0:T(8,128)(2,1)S(1)}, u32[]{:S(2)}, u32[]{:S(2)}) collective-permute-start(bf16[2,768,128]{2,1,0:T(8,128)(2,1)S(1)} %pad_maximum_fusion.6.p0), channel_id=1, source_target_pairs={{0,16},{8,24},{16,0},{24,8},{1,17},{9,25},{17,1},{25,9},{2,18},{10... | collective-permute-start | bytes 1179656 | tf_op jit(solution)/shard_map/ppermute | solution.py:27
  153.0 15.0 %collective-permute-start.29 = (bf16[384,512]{1,0:T(8,128)(2,1)}, bf16[384,512]{1,0:T(8,128)(2,1)S(1)}, u32[]{:S(2)}, u32[]{:S(2)}) collective-permute-start(bf16[384,512]{1,0:T(8,128)(2,1)} %get-tuple-element.253), channel_id=1, source_target_pairs={{0,1},{1,0},{2,3},{3,2},{4,5},{5,4},{6,7},{7,6},{8,9},{9,8},{10,11... | collective-permute-start | bytes 1179656 | tf_op jit(solution)/shard_map/ppermute | solution.py:27
  172.0 11.2 %collective-permute-start.31 = (bf16[128,1536]{1,0:T(8,128)(2,1)S(1)}, bf16[128,1536]{1,0:T(8,128)(2,1)S(1)}, u32[]{:S(2)}, u32[]{:S(2)}) collective-permute-start(bf16[128,1536]{1,0:T(8,128)(2,1)S(1)} %add_convert_fusion.6), channel_id=1, source_target_pairs={{0,16},{8,24},{16,0},{24,8},{1,17},{9,25},{17,1},{25,9},{2,18},{10... | collective-permute-start | bytes 1179656 | tf_op jit(solution)/shard_map/ppermute | solution.py:27
  173.8 32.5 %collective-permute-start.32 = (bf16[512,768]{1,0:T(8,128)(2,1)S(1)}, bf16[512,768]{1,0:T(8,128)(2,1)}, u32[]{:S(2)}, u32[]{:S(2)}) collective-permute-start(bf16[512,768]{1,0:T(8,128)(2,1)S(1)} %copy-done.36), channel_id=1, source_target_pairs={{0,1},{1,0},{2,3},{3,2},{4,5},{5,4},{6,7},{7,6},{8,9},{9,8},{10,11... | collective-permute-start | bytes 2359304 | tf_op jit(solution)/shard_map/ppermute | solution.py:27
  175.8 30.5 %collective-permute-start.33 = (bf16[384,512]{1,0:T(8,128)(2,1)}, bf16[384,512]{1,0:T(8,128)(2,1)}, u32[]{:S(2)}, u32[]{:S(2)}) collective-permute-start(bf16[384,512]{1,0:T(8,128)(2,1)} %get-tuple-element.261), channel_id=1, source_target_pairs={{0,1},{1,0},{2,3},{3,2},{4,5},{5,4},{6,7},{7,6},{8,9},{9,8},{10,11... | collective-permute-start | bytes 1179656 | tf_op jit(solution)/shard_map/ppermute | solution.py:27
  183.2 23.1 %collective-permute-start.34 = (bf16[2,768,128]{2,1,0:T(8,128)(2,1)S(1)}, bf16[2,768,128]{2,1,0:T(8,128)(2,1)}, u32[]{:S(2)}, u32[]{:S(2)}) collective-permute-start(bf16[2,768,128]{2,1,0:T(8,128)(2,1)S(1)} %pad_maximum_fusion.6.p0), channel_id=1, source_target_pairs={{0,8},{8,0},{16,24},{24,16},{1,9},{9,1},{17,25},{25,17},{2,10},{10... | collective-permute-start | bytes 1179656 | tf_op jit(solution)/shard_map/ppermute | solution.py:27
  183.2 23.1 %collective-permute-start.35 = (bf16[2,768,128]{2,1,0:T(8,128)(2,1)S(1)}, bf16[2,768,128]{2,1,0:T(8,128)(2,1)}, u32[]{:S(2)}, u32[]{:S(2)}) collective-permute-start(bf16[2,768,128]{2,1,0:T(8,128)(2,1)S(1)} %collective-permute-done.27.p2), channel_id=1, source_target_pairs={{0,8},{8,0},{16,24},{24,16},{1,9},{9,1},{17,25},{25,17},{2,10},{10... | collective-permute-start | bytes 1179656 | tf_op jit(solution)/shard_map/ppermute | solution.py:27
  206.4 29.2 %collective-permute-start.40 = (bf16[2,128,3072]{2,1,0:T(8,128)(2,1)S(1)}, bf16[2,128,3072]{2,1,0:T(8,128)(2,1)}, u32[]{:S(2)}, u32[]{:S(2)}) collective-permute-start(bf16[2,128,3072]{2,1,0:T(8,128)(2,1)S(1)} %pad_maximum_fusion.f02), channel_id=1, source_target_pairs={{0,8},{8,0},{16,24},{24,16},{1,9},{9,1},{17,25},{25,17},{2,10},{10... | collective-permute-start | bytes 4718600 | tf_op jit(solution)/shard_map/ppermute | solution.py:27
  206.5 20.4 %collective-permute-start.38 = (bf16[512,768]{1,0:T(8,128)(2,1)}, bf16[512,768]{1,0:T(8,128)(2,1)S(1)}, u32[]{:S(2)}, u32[]{:S(2)}) collective-permute-start(bf16[512,768]{1,0:T(8,128)(2,1)} %get-tuple-element.314.refs_2_), channel_id=1, source_target_pairs={{0,1},{1,0},{2,3},{3,2},{4,5},{5,4},{6,7},{7,6},{8,9},{9,8},{10,11... | collective-permute-start | bytes 2359304 | tf_op jit(solution)/shard_map/ppermute | solution.py:27
  208.5 18.3 %collective-permute-start.37 = (bf16[128,1536]{1,0:T(8,128)(2,1)}, bf16[128,1536]{1,0:T(8,128)(2,1)S(1)}, u32[]{:S(2)}, u32[]{:S(2)}) collective-permute-start(bf16[128,1536]{1,0:T(8,128)(2,1)} %get-tuple-element.326.g0.a0), channel_id=1, source_target_pairs={{0,16},{8,24},{16,0},{24,8},{1,17},{9,25},{17,1},{25,9},{2,18},{10... | collective-permute-start | bytes 1179656 | tf_op jit(solution)/shard_map/ppermute | solution.py:27
  212.2 21.4 %collective-permute-start.41 = (bf16[512,384]{1,0:T(8,128)(2,1)}, bf16[512,384]{1,0:T(8,128)(2,1)}, u32[]{:S(2)}, u32[]{:S(2)}) collective-permute-start(bf16[512,384]{1,0:T(8,128)(2,1)} %pad_maximum_fusion.7), channel_id=1, source_target_pairs={{0,8},{8,0},{16,24},{24,16},{1,9},{9,1},{17,25},{25,17},{2,10},{10... | collective-permute-start | bytes 1179656 | tf_op jit(solution)/shard_map/ppermute | solution.py:27
  212.2 21.6 %collective-permute-start.36 = (bf16[128,1536]{1,0:T(8,128)(2,1)S(1)}, bf16[128,1536]{1,0:T(8,128)(2,1)S(1)}, u32[]{:S(2)}, u32[]{:S(2)}) collective-permute-start(bf16[128,1536]{1,0:T(8,128)(2,1)S(1)} %copy-done.10), channel_id=1, source_target_pairs={{0,8},{8,0},{16,24},{24,16},{1,9},{9,1},{17,25},{25,17},{2,10},{10... | collective-permute-start | bytes 1179656 | tf_op jit(solution)/shard_map/ppermute | solution.py:27
  227.8 7.8 %collective-permute-start.39 = (bf16[128,1536]{1,0:T(8,128)(2,1)S(1)}, bf16[128,1536]{1,0:T(8,128)(2,1)S(1)}, u32[]{:S(2)}, u32[]{:S(2)}) collective-permute-start(bf16[128,1536]{1,0:T(8,128)(2,1)S(1)} %collective-permute-done.37.g2.a2), channel_id=1, source_target_pairs={{0,8},{8,0},{16,24},{24,16},{1,9},{9,1},{17,25},{25,17},{2,10},{10... | collective-permute-start | bytes 1179656 | tf_op jit(solution)/shard_map/ppermute | solution.py:27
  227.8 42.6 %collective-permute-start.45 = (bf16[2,192,1536]{2,1,0:T(8,128)(2,1)}, bf16[2,192,1536]{2,1,0:T(8,128)(2,1)}, u32[]{:S(2)}, u32[]{:S(2)}) collective-permute-start(bf16[2,192,1536]{2,1,0:T(8,128)(2,1)} %bitcast.144), channel_id=1, source_target_pairs={{0,2},{1,3},{2,0},{3,1},{4,6},{5,7},{6,4},{7,5},{8,10},{9,11},{10,... | collective-permute-start | bytes 3538952 | tf_op jit(solution)/shard_map/ppermute | solution.py:27
  233.5 21.6 %collective-permute-start.43 = (bf16[512,768]{1,0:T(8,128)(2,1)}, bf16[512,768]{1,0:T(8,128)(2,1)}, u32[]{:S(2)}, u32[]{:S(2)}) collective-permute-start(bf16[512,768]{1,0:T(8,128)(2,1)} %get-tuple-element.342.refs_0_), channel_id=1, source_target_pairs={{0,1},{1,0},{2,3},{3,2},{4,5},{5,4},{6,7},{7,6},{8,9},{9,8},{10,11... | collective-permute-start | bytes 2359304 | tf_op jit(solution)/shard_map/ppermute | solution.py:27
  233.8 36.6 %collective-permute-start.44 = (bf16[512,768]{1,0:T(8,128)(2,1)}, bf16[512,768]{1,0:T(8,128)(2,1)}, u32[]{:S(2)}, u32[]{:S(2)}) collective-permute-start(bf16[512,768]{1,0:T(8,128)(2,1)} %get-tuple-element.344.refs_2_), channel_id=1, source_target_pairs={{0,1},{1,0},{2,3},{3,2},{4,5},{5,4},{6,7},{7,6},{8,9},{9,8},{10,11... | collective-permute-start | bytes 2359304 | tf_op jit(solution)/shard_map/ppermute | solution.py:27
  235.6 34.8 %collective-permute-start.42 = (bf16[128,3072]{1,0:T(8,128)(2,1)}, bf16[128,3072]{1,0:T(8,128)(2,1)S(1)}, u32[]{:S(2)}, u32[]{:S(2)}) collective-permute-start(bf16[128,3072]{1,0:T(8,128)(2,1)} %get-tuple-element.288), channel_id=1, source_target_pairs={{0,16},{8,24},{16,0},{24,8},{1,17},{9,25},{17,1},{25,9},{2,18},{10... | collective-permute-start | bytes 2359304 | tf_op jit(solution)/shard_map/ppermute | solution.py:27
  238.2 32.2 %collective-permute-start.46 = (bf16[256,384]{1,0:T(8,128)(2,1)S(1)}, bf16[256,384]{1,0:T(8,128)(2,1)S(1)}, u32[]{:S(2)}, u32[]{:S(2)}) collective-permute-start(bf16[256,384]{1,0:T(8,128)(2,1)S(1)} %add_convert_fusion.9), channel_id=1, source_target_pairs={{0,16},{8,24},{16,0},{24,8},{1,17},{9,25},{17,1},{25,9},{2,18},{10... | collective-permute-start | bytes 589832 | tf_op jit(solution)/shard_map/ppermute | solution.py:27
  272.6 22.6 %collective-permute-start.50 = (bf16[2,128,3072]{2,1,0:T(8,128)(2,1)S(1)}, bf16[2,128,3072]{2,1,0:T(8,128)(2,1)}, u32[]{:S(2)}, u32[]{:S(2)}) collective-permute-start(bf16[2,128,3072]{2,1,0:T(8,128)(2,1)S(1)} %pad_maximum_fusion.1.b02), channel_id=1, source_target_pairs={{0,8},{8,0},{16,24},{24,16},{1,9},{9,1},{17,25},{25,17},{2,10},{10... | collective-permute-start | bytes 4718600 | tf_op jit(solution)/shard_map/ppermute | solution.py:27
  272.7 48.4 %collective-permute-start.47 = (bf16[2,384,512]{2,1,0:T(8,128)(2,1)}, bf16[2,384,512]{2,1,0:T(8,128)(2,1)}, u32[]{:S(2)}, u32[]{:S(2)}) collective-permute-start(bf16[2,384,512]{2,1,0:T(8,128)(2,1)} %get-tuple-element.294), channel_id=1, source_target_pairs={{1,0},{2,1},{3,2},{4,3},{5,4},{6,5},{7,6},{9,8},{10,9},{11,10},{12... | collective-permute-start | bytes 2359304 | tf_op jit(solution)/shard_map/ppermute | solution.py:33
  274.0 47.1 %collective-permute-start.48 = (bf16[2,384,512]{2,1,0:T(8,128)(2,1)}, bf16[2,384,512]{2,1,0:T(8,128)(2,1)}, u32[]{:S(2)}, u32[]{:S(2)}) collective-permute-start(bf16[2,384,512]{2,1,0:T(8,128)(2,1)} %get-tuple-element.295), channel_id=1, source_target_pairs={{0,1},{1,2},{2,3},{3,4},{4,5},{5,6},{6,7},{8,9},{9,10},{10,11},{11... | collective-permute-start | bytes 2359304 | tf_op jit(solution)/shard_map/ppermute | solution.py:33
  282.2 38.9 %collective-permute-start.49 = (bf16[1,192,1536]{2,1,0:T(8,128)(2,1)}, bf16[1,192,1536]{2,1,0:T(8,128)(2,1)}, u32[]{:S(2)}, u32[]{:S(2)}) collective-permute-start(bf16[1,192,1536]{2,1,0:T(8,128)(2,1)} %constant_dynamic-slice_fusion.22), channel_id=1, source_target_pairs={{0,4},{1,5},{2,6},{3,7},{4,0},{5,1},{6,2},{7,3},{8,12},{9,13},{10,... | collective-permute-start | bytes 1769480 | tf_op jit(solution)/shard_map/ppermute | solution.py:27
  292.3 52.2 %collective-permute-start.52 = (bf16[2,192,1536]{2,1,0:T(8,128)(2,1)}, bf16[2,192,1536]{2,1,0:T(8,128)(2,1)}, u32[]{:S(2)}, u32[]{:S(2)}) collective-permute-start(bf16[2,192,1536]{2,1,0:T(8,128)(2,1)} %bitcast.143), channel_id=1, source_target_pairs={{0,2},{1,3},{2,0},{3,1},{4,6},{5,7},{6,4},{7,5},{8,10},{9,11},{10,... | collective-permute-start | bytes 3538952 | tf_op jit(solution)/shard_map/ppermute | solution.py:27
  328.8 14.5 %collective-permute-start.51 = (bf16[1024,384]{1,0:T(8,128)(2,1)}, bf16[1024,384]{1,0:T(8,128)(2,1)}, u32[]{:S(2)}, u32[]{:S(2)}) collective-permute-start(bf16[1024,384]{1,0:T(8,128)(2,1)} %get-tuple-element.307), channel_id=1, source_target_pairs={{0,8},{8,0},{16,24},{24,16},{1,9},{9,1},{17,25},{25,17},{2,10},{10... | collective-permute-start | bytes 2359304 | tf_op jit(solution)/shard_map/ppermute | solution.py:27
  328.9 29.5 %collective-permute-start.54 = (bf16[1168,512]{1,0:T(8,128)(2,1)}, bf16[1168,512]{1,0:T(8,128)(2,1)}, u32[]{:S(2)}, u32[]{:S(2)}) collective-permute-start(bf16[1168,512]{1,0:T(8,128)(2,1)} %get-tuple-element.318), channel_id=1, source_target_pairs={{0,1},{1,0},{2,3},{3,2},{4,5},{5,4},{6,7},{7,6},{8,9},{9,8},{10,11... | collective-permute-start | bytes 3588104 | tf_op jit(solution)/shard_map/ppermute | solution.py:27
  336.8 43.1 %collective-permute-start.62 = (bf16[2,192,1536]{2,1,0:T(8,128)(2,1)}, bf16[2,192,1536]{2,1,0:T(8,128)(2,1)}, u32[]{:S(2)}, u32[]{:S(2)}) collective-permute-start(bf16[2,192,1536]{2,1,0:T(8,128)(2,1)} %bitcast.142), channel_id=1, source_target_pairs={{0,2},{1,3},{2,0},{3,1},{4,6},{5,7},{6,4},{7,5},{8,10},{9,11},{10,... | collective-permute-start | bytes 3538952 | tf_op jit(solution)/shard_map/ppermute | solution.py:27
  339.8 53.0 %collective-permute-start.64 = (bf16[4,192,768]{2,1,0:T(8,128)(2,1)}, bf16[4,192,768]{2,1,0:T(8,128)(2,1)}, u32[]{:S(2)}, u32[]{:S(2)}) collective-permute-start(bf16[4,192,768]{2,1,0:T(8,128)(2,1)} %get-tuple-element.353), channel_id=1, source_target_pairs={{0,1},{1,0},{2,3},{3,2},{4,5},{5,4},{6,7},{7,6},{8,9},{9,8},{10,11... | collective-permute-start | bytes 3538952 | tf_op jit(solution)/shard_map/ppermute | solution.py:27
  344.5 11.0 %collective-permute-start.53 = (bf16[512,384]{1,0:T(8,128)(2,1)S(1)}, bf16[512,384]{1,0:T(8,128)(2,1)S(1)}, u32[]{:S(2)}, u32[]{:S(2)}) collective-permute-start(bf16[512,384]{1,0:T(8,128)(2,1)S(1)} %add_convert_fusion.5), channel_id=1, source_target_pairs={{0,16},{8,24},{16,0},{24,8},{1,17},{9,25},{17,1},{25,9},{2,18},{10... | collective-permute-start | bytes 1179656 | tf_op jit(solution)/shard_map/ppermute | solution.py:27
  348.5 31.3 %collective-permute-start.61 = (bf16[1,192,1536]{2,1,0:T(8,128)(2,1)}, bf16[1,192,1536]{2,1,0:T(8,128)(2,1)}, u32[]{:S(2)}, u32[]{:S(2)}) collective-permute-start(bf16[1,192,1536]{2,1,0:T(8,128)(2,1)} %constant_dynamic-slice_fusion.12), channel_id=1, source_target_pairs={{0,4},{1,5},{2,6},{3,7},{4,0},{5,1},{6,2},{7,3},{8,12},{9,13},{10,... | collective-permute-start | bytes 1769480 | tf_op jit(solution)/shard_map/ppermute | solution.py:27
  365.8 24.4 %collective-permute-start.55 = (bf16[256,1536]{1,0:T(8,128)(2,1)}, bf16[256,1536]{1,0:T(8,128)(2,1)}, u32[]{:S(2)}, u32[]{:S(2)}) collective-permute-start(bf16[256,1536]{1,0:T(8,128)(2,1)} %get-tuple-element.323), channel_id=1, source_target_pairs={{0,8},{8,0},{16,24},{24,16},{1,9},{9,1},{17,25},{25,17},{2,10},{10... | collective-permute-start | bytes 2359304 | tf_op jit(solution)/shard_map/ppermute | solution.py:27
  378.6 33.8 %collective-permute-start.63 = (bf16[2,192,1152]{2,1,0:T(8,128)(2,1)}, bf16[2,192,1152]{2,1,0:T(8,128)(2,1)}, u32[]{:S(2)}, u32[]{:S(2)}) collective-permute-start(bf16[2,192,1152]{2,1,0:T(8,128)(2,1)} %dynamic-slice_bitcast_fusion), channel_id=1, source_target_pairs={{0,2},{1,3},{2,0},{3,1},{4,6},{5,7},{6,4},{7,5},{8,10},{9,11},{10,... | collective-permute-start | bytes 2654216 | tf_op jit(solution)/shard_map/ppermute | solution.py:27
  383.1 88.0 %collective-permute-start.70 = (bf16[1,192,1536]{2,1,0:T(8,128)(2,1)S(1)}, bf16[1,192,1536]{2,1,0:T(8,128)(2,1)S(1)}, u32[]{:S(2)}, u32[]{:S(2)}) collective-permute-start(bf16[1,192,1536]{2,1,0:T(8,128)(2,1)S(1)} %constant_dynamic-slice_fusion.2), channel_id=1, source_target_pairs={{0,4},{1,5},{2,6},{3,7},{4,0},{5,1},{6,2},{7,3},{8,12},{9,13},{10,... | collective-permute-start | bytes 1769480 | tf_op jit(solution)/shard_map/ppermute | solution.py:27
  391.3 54.1 %collective-permute-start.56 = (bf16[128,1536]{1,0:T(8,128)(2,1)S(1)}, bf16[128,1536]{1,0:T(8,128)(2,1)S(1)}, u32[]{:S(2)}, u32[]{:S(2)}) collective-permute-start(bf16[128,1536]{1,0:T(8,128)(2,1)S(1)} %add_convert_fusion.4), channel_id=1, source_target_pairs={{0,16},{8,24},{16,0},{24,8},{1,17},{9,25},{17,1},{25,9},{2,18},{10... | collective-permute-start | bytes 1179656 | tf_op jit(solution)/shard_map/ppermute | solution.py:27
  413.8 6.8 %collective-permute-start.65 = (f32[4,6,48]{2,0,1:T(4,128)S(1)}, f32[4,6,48]{2,0,1:T(4,128)S(1)}, u32[]{:S(2)}, u32[]{:S(2)}) collective-permute-start(f32[4,6,48]{2,0,1:T(4,128)S(1)} %bitcast.136), channel_id=1, source_target_pairs={{0,2},{1,3},{2,0},{3,1},{4,6},{5,7},{6,4},{7,5},{8,10},{9,11},{10,... | collective-permute-start | bytes 13832 | tf_op jit(solution)/shard_map/ppermute | solution.py:27
  414.0 34.3 %collective-permute-start.68 = (bf16[1,192,1152]{2,1,0:T(8,128)(2,1)S(1)}, bf16[1,192,1152]{2,1,0:T(8,128)(2,1)S(1)}, u32[]{:S(2)}, u32[]{:S(2)}) collective-permute-start(bf16[1,192,1152]{2,1,0:T(8,128)(2,1)S(1)} %constant_dynamic-slice_fusion.3), channel_id=1, source_target_pairs={{0,4},{1,5},{2,6},{3,7},{4,0},{5,1},{6,2},{7,3},{8,12},{9,13},{10,... | collective-permute-start | bytes 1327112 | tf_op jit(solution)/shard_map/ppermute | solution.py:27
  418.6 52.4 %collective-permute-start.69 = (bf16[4,192,768]{2,1,0:T(8,128)(2,1)S(1)}, bf16[4,192,768]{2,1,0:T(8,128)(2,1)S(1)}, u32[]{:S(2)}, u32[]{:S(2)}) collective-permute-start(bf16[4,192,768]{2,1,0:T(8,128)(2,1)S(1)} %copy-done.74), channel_id=1, source_target_pairs={{0,1},{1,0},{2,3},{3,2},{4,5},{5,4},{6,7},{7,6},{8,9},{9,8},{10,11... | collective-permute-start | bytes 3538952 | tf_op jit(solution)/shard_map/ppermute | solution.py:27
  420.6 15.9 %collective-permute-start.66 = (f32[2,6,48]{2,0,1:T(2,128)S(1)}, f32[2,6,48]{2,0,1:T(2,128)S(1)}, u32[]{:S(2)}, u32[]{:S(2)}) collective-permute-start(f32[2,6,48]{2,0,1:T(2,128)S(1)} %bitcast.139), channel_id=1, source_target_pairs={{0,4},{1,5},{2,6},{3,7},{4,0},{5,1},{6,2},{7,3},{8,12},{9,13},{10,... | collective-permute-start | bytes 6920 | tf_op jit(solution)/shard_map/ppermute | solution.py:27
  436.5 8.0 %collective-permute-start.67 = (f32[1,6,48]{2,0,1:T(1,128)S(1)}, f32[1,6,48]{2,0,1:T(1,128)S(1)}, u32[]{:S(2)}, u32[]{:S(2)}) collective-permute-start(f32[1,6,48]{2,0,1:T(1,128)S(1)} %constant_dynamic-slice_fusion.4), channel_id=1, source_target_pairs={{0,1},{1,0},{2,3},{3,2},{4,5},{5,4},{6,7},{7,6},{8,9},{9,8},{10,11... | collective-permute-start | bytes 3464 | tf_op jit(solution)/shard_map/ppermute | solution.py:27
  444.6 12.3 %collective-permute-start.73 = (bf16[2,192,768]{2,1,0:T(8,128)(2,1)S(1)}, bf16[2,192,768]{2,1,0:T(8,128)(2,1)S(1)}, u32[]{:S(2)}, u32[]{:S(2)}) collective-permute-start(bf16[2,192,768]{2,1,0:T(8,128)(2,1)S(1)} %dynamic-slice_bitcast_fusion.1), channel_id=1, source_target_pairs={{0,2},{1,3},{2,0},{3,1},{4,6},{5,7},{6,4},{7,5},{8,10},{9,11},{10,... | collective-permute-start | bytes 1769480 | tf_op jit(solution)/shard_map/ppermute | solution.py:27
  457.1 12.4 %collective-permute-start.74 = (bf16[1,192,768]{2,1,0:T(8,128)(2,1)S(1)}, bf16[1,192,768]{2,1,0:T(8,128)(2,1)S(1)}, u32[]{:S(2)}, u32[]{:S(2)}) collective-permute-start(bf16[1,192,768]{2,1,0:T(8,128)(2,1)S(1)} %constant_dynamic-slice_fusion), channel_id=1, source_target_pairs={{0,4},{1,5},{2,6},{3,7},{4,0},{5,1},{6,2},{7,3},{8,12},{9,13},{10,... | collective-permute-start | bytes 884744 | tf_op jit(solution)/shard_map/ppermute | solution.py:27
  471.4 13.8 %collective-permute-start.71 = (bf16[2,192,768]{2,1,0:T(8,128)(2,1)S(1)}, bf16[2,192,768]{2,1,0:T(8,128)(2,1)S(1)}, u32[]{:S(2)}, u32[]{:S(2)}) collective-permute-start(bf16[2,192,768]{2,1,0:T(8,128)(2,1)S(1)} %dynamic-slice_bitcast_fusion.2), channel_id=1, source_target_pairs={{0,2},{1,3},{2,0},{3,1},{4,6},{5,7},{6,4},{7,5},{8,10},{9,11},{10,... | collective-permute-start | bytes 1769480 | tf_op jit(solution)/shard_map/ppermute | solution.py:27
  485.4 13.7 %collective-permute-start.72 = (bf16[1,192,768]{2,1,0:T(8,128)(2,1)S(1)}, bf16[1,192,768]{2,1,0:T(8,128)(2,1)S(1)}, u32[]{:S(2)}, u32[]{:S(2)}) collective-permute-start(bf16[1,192,768]{2,1,0:T(8,128)(2,1)S(1)} %constant_dynamic-slice_fusion.1), channel_id=1, source_target_pairs={{0,4},{1,5},{2,6},{3,7},{4,0},{5,1},{6,2},{7,3},{8,12},{9,13},{10,... | collective-permute-start | bytes 884744 | tf_op jit(solution)/shard_map/ppermute | solution.py:27
  (87 other events, 809.7 us)

commit v5 on v4

--- a/solution.py
+++ b/solution.py
@@ -1053,14 +1053,12 @@
     )
     context_parts = quarters(kv_grad, 1)
     context_got = swap(jnp.concatenate([context_parts[1], context_parts[3]], 0), "tensor", 1)
-    one_far_rows, down_keep, lifted_got_a = meeting(
-        swap(grad_one, "tensor", 2), down_keep, lifted_got_a
-    )
+    one_far_rows, down_keep = meeting(swap(grad_one, "tensor", 2), down_keep)
     one_parts = (
         grad_one, swap(grad_one, "tensor", 1), one_far_rows, swap(one_far_rows, "tensor", 1)
     )
-    *one_parts, front_other, context_got = meeting(
-        *one_parts, swap(after(front_both, grad_one), "tensor", 1), context_got
+    *one_parts, front_other, context_got, lifted_got_a = meeting(
+        *one_parts, swap(after(front_both, grad_one), "tensor", 1), context_got, lifted_got_a
     )
     context_low = (
         context_parts[2].astype(F32) + context_got[context_parts[2].shape[0] :].astype(F32)
@@ -1072,8 +1070,8 @@
         spans, queries, (behind, both, ahead), time_keys, time_values, label_row, label_column,
         w_out, attended, log_totals, one_parts,
     )
-    to_prev, to_next, back_far, gate_got_b, lifted_got_b, down_got, context_far = meeting(
-        to_prev, to_next, back_far, gate_got_b, lifted_got_b, down_got, context_far
+    to_prev, to_next, back_far, gate_got_b, down_got, context_far = meeting(
+        to_prev, to_next, back_far, gate_got_b, down_got, context_far
     )
     from_next, from_prev = shift(to_prev, "seq", -1), shift(to_next, "seq", 1)
     down_keep, down_got = halve(added(down_keep, down_got).astype(BF16), 2)
@@ -1096,9 +1094,7 @@
         row_context,
         context_own.astype(BF16),
     )
-    from_next, from_prev, down_got, send_a, send_b = meeting(
-        from_next, from_prev, down_got, send_a, send_b
-    )
+    from_next, from_prev, send_a, send_b = meeting(from_next, from_prev, send_a, send_b)
     got_a = swap(send_a, "seq", 1)
     raw, last_away, last_own, last_low = tail(
         places[1:], query_grad, kept, from_next, from_prev, tables, w_query, w_key, w_value,
@@ -1115,7 +1111,7 @@
             after((gate_b, gate_got_b, lifted_b, lifted_got_b), last_away),
         )
     )
-    last_sum, first_got = meeting(last_sum, first_got)
+    last_sum, first_got, down_got = meeting(last_sum, first_got, down_got)
     first_keep, first_got = halve(added(first_keep, first_got).astype(BF16), 2)
     last_far, raw_got = meeting(swap(last_sum, "tensor", 2), raw_got)
     frame_grad = last_own + last_got[:local_rows].astype(F32) + last_far.astype(F32)
@@ -1179,16 +1175,17 @@
         jnp.einsum("dn,fn->df", r, c, preferred_element_type=F32)
         for r, c in zip(normed_pair, raw_pair)
     )
-    heads_keep, heads_got = halve(
-        (blocks + outer).astype(BF16).reshape(count // 2, rows, 3 * head_cols), 1
-    )
-    heads_got, got_a = meeting(heads_got, got_a)
+    blocks, got_a = meeting(
+        (blocks + outer).astype(BF16).reshape(count // 2, rows, 3 * head_cols), got_a
+    )
+    heads_keep, heads_got = halve(blocks, 1)
+    left_keep, left_got = halve(added(keep_a, got_a).astype(BF16), 1)
+    got_b = swap(after(send_b, from_next), "seq", 1)
+    heads_got, got_b = meeting(heads_got, got_b)
     heads_next = added(heads_keep, heads_got).astype(BF16)
-    got_b = swap(after(send_b, got_a), "seq", 1)
-    left_keep, left_got = halve(added(keep_a, got_a).astype(BF16), 1)
     heads_sum = halve_all(heads_next, 2)
-    got_b, second_got = meeting(got_b, second_got)
     last_next = added(*halve(added(keep_b, got_b).astype(BF16), 1))
+    last_next, second_got = meeting(last_next, second_got)
     first, second = halve_end(first_keep, first_got, 3), halve_end(second_keep, second_got, 3)
     units = first.shape[1] // 2
     grad_gate_w = jnp.concatenate([first[:, :units], second[:, :units]], 1)
@@ -1196,13 +1193,12 @@
     small = jnp.stack(
         [d_gain_attn, d_bias_attn, vectors[3], vectors[4], vectors[1], vectors[2]]
     ).reshape(6, devices, -1).transpose(1, 0, 2)
-    small = small.reshape(count // 2, 2, 6, -1).transpose(1, 0, 2, 3).reshape(count, 6, -1)
+    small = small.reshape(count // 4, 2, 2, 6, -1).swapaxes(1, 2).reshape(count, 6, -1)
     small = after(small, heads_next)
-    bit = 1
-    while small.shape[0] > 2:
+    bits = [1, 0] + list(range(2, count.bit_length() - 1))
+    for bit in bits:
         small = added(*halve(small, bit))
-        bit += 1
-    small = added(*halve(small, 0))[0]
+    small = small[0]
     left, right = halve_end(left_keep, left_got, 2), halve_all(last_next, 2)
     part, rows = head_cols // count, model_width // count
     grad_c_query = left[:, :head_cols]

time: 508 us -> 513 us (level)
  starting transfers between devices: 85.1 us -> 73.7 us
  local copies, waits for them, and re-layouts: 27.2 us -> 34.4 us
    ppermute x4, waiting for transfers between devices: 20.2 us -> 42.7 us  [shift(): return lax.ppermute(value, axis, pairs)]
    ppermute x71, waiting for transfers between devices: 162 us -> 142 us  [swap(): lax.ppermute(value, axis, [(i, i ^ by) for i in range(lax.axis_size(axis))])]
    ppermute x71, starting transfers between devices: 74.8 us -> 63.4 us  [swap(): lax.ppermute(value, axis, [(i, i ^ by) for i in range(lax.axis_size(axis))])]
  transfers between devices with their start and end apart: 75 -> 75, of which waited for: 24 -> 26; matrix products, arithmetic and copies ran while one was open for 12% -> 14% of each run, Pallas kernels for 32% -> 32%
where the time goes in v5:
time: 513 us; the launch traced here: 505 us
  waiting for transfers between devices  184 us (36%)
  Pallas kernels  161 us (31%)
  starting transfers between devices  73.7 us (14%)
  other arithmetic  43.8 us (9%)
  local copies, waits for them, and re-layouts  34.4 us (7%)
    ppermute x71, waiting for transfers between devices, swap(): lax.ppermute(value, axis, [(i, i ^ by) for i in range(lax.axis_size(axis))])  142 us
    ppermute x71, starting transfers between devices, swap(): lax.ppermute(value, axis, [(i, i ^ by) for i in range(lax.axis_size(axis))])  63.4 us
    ppermute x4, waiting for transfers between devices, shift(): return lax.ppermute(value, axis, pairs)  42.7 us
    pallas_call x2, Pallas kernels, ffn(): pl.pallas_call(functools.partial(ffn_second_body if half else ffn_first_b...  29.7 us
    pallas_call x1, Pallas kernels, cross_backward(): pl.pallas_call(cross_backward_body, grid=(1,), out_shape=[jax.ShapeDtypeS...  21 us
    pallas_call x1, Pallas kernels, attend_back(): pl.pallas_call(backward_body, in_specs=[pl.BlockSpec(memory_space=pltpu.S...  17.8 us
    pallas_call x1, Pallas kernels, cross_forward(): pl.pallas_call(functools.partial(cross_forward_body, width // devices), g...  16.6 us
    pallas_call x2, Pallas kernels, meet_cols(): pl.pallas_call(functools.partial(meet_cols_body, size), in_specs=[pl.Bloc...  15.4 us
  transfers between devices with their start and end apart: 75, of which 26 were waited for; matrix products, arithmetic and copies ran while one was open for 14% of the time, Pallas kernels for 32%

profile of v5, /device:TPU:0, one launch (start us, length us, event | category | flops | bytes accessed | tf_op | source)
XLA Modules:
  0.0 504.6 jit_solution(7110166946156907489)
XLA Ops:
  1.2 2.6 collective-permute-start.1
  14.0 1.8 collective-permute-start.6
  21.1 9.6 %front.1 = (bf16[384,512]{1,0:T(8,128)(2,1)}, bf16[2,384,512]{2,1,0:T(8,128)(2,1)}, bf16[128,1536]{1,0:T(8,128)(2,1)}, bf16[512,1536]{1,0:T(8,128)(2,1)}, bf16[7...) custom-call(s32[2]{0:T(128)} %rev.4.place, ...), custom_call_target="tpu_custom_call" | custom-call | flops 1 | bytes 1 | tf_op jit(solution)/shard_map/front/pallas_call | solution.py:882
  30.7 2.3 collective-permute-start.7
  37.0 10.4 %attend_near.1 = (f32[6,512]{1,0:T(8,128)}, f32[6,512]{1,0:T(8,128)}, f32[384,512]{1,0:T(8,128)}) custom-call(s32[5]{0:T(128)} %pad_add_fusion.2.span, bf16[384,512]{1,0:T(8,128)(2,1)} %get-tuple-element.195.q, bf16[2,384,512]{2,1,0:T(8,128)(2,1)} %get-tuple-element.198.kv.kv1, f32[384,1]{1,0:T(8,128)} %get-tuple-element.201.tk, ...), custom_call_target="tpu_custom_call" | custom-call | flops 1 | bytes 1 | tf_op jit(solution)/shard_map/attend_near/pallas_call | solution.py:304
  47.3 20.2 %collective-permute-done.7.kv0 = bf16[2,384,512]{2,1,0:T(8,128)(2,1)S(1)} collective-permute-done((bf16[2,384,512]{2,1,0:T(8,128)(2,1)}, bf16[2,384,512]{2,1,0:T(8,128)(2,1)S(1)}, u32[]{:S(2)}, u32[]{:S(2)}) %collective-permute-start.7) | collective-permute-done | bytes 786464 | tf_op jit(solution)/shard_map/ppermute | solution.py:33
  67.5 1.9 collective-permute-done.10.o2
  72.0 8.7 %attend_far.1 = (bf16[384,512]{1,0:T(8,128)(2,1)}, f32[6,512]{1,0:T(8,128)}, bf16[256,1536]{1,0:T(8,128)(2,1)}, f32[128,1536]{1,0:T(8,128)}, bf16[128,1536]{1,0:T(8,128)(2,1)}) custom-call(s32[5]{0:T(128)} %pad_add_fusion.2.span, bf16[384,512]{1,0:T(8,128)(2,1)} %get-tuple-element.195.q, bf16[2,384,512]{2,1,0:T(8,128)(2,1)} %copy-done.20, ...), custom_call_target="tpu_custom_call" | custom-call | flops 1 | bytes 1 | tf_op jit(solution)/shard_map/attend_far/pallas_call | solution.py:322
  80.9 2.5 collective-permute-done.16.got
  85.4 2.4 collective-permute-start.19
  87.8 8.2 %collective-permute-done.17.far = bf16[128,1536]{1,0:T(8,128)(2,1)S(1)} collective-permute-done((bf16[128,1536]{1,0:T(8,128)(2,1)S(1)}, bf16[128,1536]{1,0:T(8,128)(2,1)S(1)}, u32[]{:S(2)}, u32[]{:S(2)}) %collective-permute-start.17) | collective-permute-done | bytes 393248 | tf_op jit(solution)/shard_map/ppermute | solution.py:27
  96.6 1.7 collective-permute-done.18
  99.1 16.6 %cross.1 = (bf16[128,3072]{1,0:T(8,128)(2,1)}, bf16[128,1536]{1,0:T(8,128)(2,1)}, f32[128,1536]{1,0:T(8,128)}, f32[128,1536]{1,0:T(8,128)}, bf16[128,1536]{1,0:T...) custom-call(s32[2]{0:T(128)} %copy-done.78, bf16[128,1536]{1,0:T(8,128)(2,1)} %get-tuple-element.194.rows, ...), custom_call_target="tpu_custom_call" | custom-call | flops 1 | bytes 1 | tf_op jit(solution)/shard_map/cross/pallas_call | solution.py:529
  118.6 9.3 %collective-permute-done.22.n2 = bf16[128,1536]{1,0:T(8,128)(2,1)S(1)} collective-permute-done((bf16[128,1536]{1,0:T(8,128)(2,1)}, bf16[128,1536]{1,0:T(8,128)(2,1)S(1)}, u32[]{:S(2)}, u32[]{:S(2)}) %collective-permute-start.22) | collective-permute-done | bytes 393248 | tf_op jit(solution)/shard_map/ppermute | solution.py:27
  128.5 1.7 collective-permute-done.23.n3
  131.7 2.5 collective-permute-start.26
  136.8 14.7 %ffn.2 = (bf16[512,768]{1,0:T(8,128)(2,1)}, bf16[384,512]{1,0:T(8,128)(2,1)}, bf16[384,512]{1,0:T(8,128)(2,1)}, bf16[512,768]{1,0:T(8,128)(2,1)}, bf16[512,768]{...) custom-call(s32[2]{0:T(128)} %copy-done.78, ...), custom_call_target="tpu_custom_call" | custom-call | flops 1 | bytes 1 | tf_op jit(solution)/shard_map/ffn/pallas_call | solution.py:618
  152.9 15.0 %ffn.3 = (bf16[512,768]{1,0:T(8,128)(2,1)}, bf16[384,512]{1,0:T(8,128)(2,1)}, bf16[384,512]{1,0:T(8,128)(2,1)}, bf16[512,768]{1,0:T(8,128)(2,1)}, bf16[512,768]{...) custom-call(s32[2]{0:T(128)} %copy-done.78, ...), custom_call_target="tpu_custom_call" | custom-call | flops 1 | bytes 1 | tf_op jit(solution)/shard_map/ffn/pallas_call | solution.py:618
  168.1 2.5 collective-permute-done.30.got
  171.9 1.8 collective-permute-start.31
  173.7 2.0 collective-permute-start.32
  175.8 7.4 %collective-permute-done.31.far = bf16[128,1536]{1,0:T(8,128)(2,1)S(1)} collective-permute-done((bf16[128,1536]{1,0:T(8,128)(2,1)S(1)}, bf16[128,1536]{1,0:T(8,128)(2,1)S(1)}, u32[]{:S(2)}, u32[]{:S(2)}) %collective-permute-start.31) | collective-permute-done | bytes 393248 | tf_op jit(solution)/shard_map/ppermute | solution.py:27
  185.2 21.0 %cross_back.1 = (bf16[128,3072]{1,0:T(8,128)(2,1)}, bf16[256,1536]{1,0:T(8,128)(2,1)}, f32[4,1536]{1,0:T(4,128)}, bf16[128,1536]{1,0:T(8,128)(2,1)}) custom-call(f32[128,1536]{1,0:T(8,128)} %get-tuple-element.247.own, bf16[256,1536]{1,0:T(8,128)(2,1)} %copy-done.21, bf16[128,1536]{1,0:T(8,128)(2,1)} %copy-done.55, ...), custom_call_target="tpu_custom_call" | custom-call | flops 1 | bytes 1 | tf_op jit(solution)/shard_map/cross_back/pallas_call | solution.py:683
  206.4 2.0 collective-permute-start.41
  208.5 1.7 collective-permute-start.37
  211.9 6.7 %meet_rows.1 = (bf16[384,1536]{1,0:T(8,128)(2,1)}, bf16[384,1536]{1,0:T(8,128)(2,1)}) custom-call(s32[1]{0:T(128)} %bitcast.12.side, bf16[384,512]{1,0:T(8,128)(2,1)} %get-tuple-element.268.own_a, bf16[384,512]{1,0:T(8,128)(2,1)} %copy-done.47, bf16[384,512]{1,0:T(8,128)(2,1)} %get-tuple-element.270.own_b, bf16[384,512]{1,0:T(8,128)(2,1)} %collective-permute-done.33.pair_b, ...), custom_call_target="tpu_custom_call" | custom-call | flops 1 | bytes 1 | tf_op jit(solution)/shard_map/meet_rows/pallas_call | solution.py:708
  219.9 7.0 %collective-permute-done.41.refs_3_ = bf16[512,768]{1,0:T(8,128)(2,1)} collective-permute-done((bf16[512,768]{1,0:T(8,128)(2,1)}, bf16[512,768]{1,0:T(8,128)(2,1)}, u32[]{:S(2)}, u32[]{:S(2)}) %collective-permute-start.41) | collective-permute-done | bytes 786464 | tf_op jit(solution)/shard_map/ppermute | solution.py:27
  226.9 2.2 collective-permute-start.44
  229.5 1.6 collective-permute-start.42
  232.7 17.8 %attend_back.1 = (f32[384,512]{1,0:T(8,128)}, bf16[2,384,512]{2,1,0:T(8,128)(2,1)}, f32[2,384,512]{2,1,0:T(8,128)}, bf16[2,384,512]{2,1,0:T(8,128)(2,1)}, f32[2,384]{1,0:T(2,128)}) custom-call(s32[5]{0:T(128)} %pad_add_fusion.2.span, bf16[384,512]{1,0:T(8,128)(2,1)} %get-tuple-element.195.q, bf16[2,384,512]{2,1,0:T(8,128)(2,1)} %copy-done.20, ...), custom_call_target="tpu_custom_call" | custom-call | flops 1 | bytes 1 | tf_op jit(solution)/shard_map/attend_back/pallas_call | solution.py:339
  250.5 4.7 collective-permute-done.44
  261.4 5.5 %collective-permute-start.47 = (bf16[2,384,512]{2,1,0:T(8,128)(2,1)}, bf16[2,384,512]{2,1,0:T(8,128)(2,1)}, u32[]{:S(2)}, u32[]{:S(2)}) collective-permute-start(bf16[2,384,512]{2,1,0:T(8,128)(2,1)} %get-tuple-element.294), channel_id=1, source_target_pairs={{0,1},{1,2},{2,3},{3,4},{4,5},{5,6},{6,7},{8,9},{9,10},{10,11},{11... | collective-permute-start | bytes 2359304 | tf_op jit(solution)/shard_map/ppermute | solution.py:33
  266.8 7.6 %meet_cols.2 = (bf16[384,1536]{1,0:T(8,128)(2,1)}, bf16[384,1536]{1,0:T(8,128)(2,1)}) custom-call(s32[1]{0:T(128)} %bitcast.12.side, bf16[2,768,128]{2,1,0:T(8,128)(2,1)} %copy-done.9, bf16[2,768,128]{2,1,0:T(8,128)(2,1)} %collective-permute-done.34.p1, bf16[2,768,128]{2,1,0:T(8,128)(2,1)} %copy-done.27, bf16[2,768,128]{2,1,0:T(8,128)(2,1)} %collective-permute-done.35.p3, ...), custom_call_target="tpu_custom_call" | custom-call | flops 1 | bytes 1 | tf_op jit(solution)/shard_map/meet_cols/pallas_call | solution.py:732
  274.4 1.9 add_convert_fusion.2
  276.3 1.8 add_convert_fusion.8.kv
  278.1 10.8 %bundle.1 = (bf16[4,192,768]{2,1,0:T(8,128)(2,1)}, bf16[4,192,768]{2,1,0:T(8,128)(2,1)}, bf16[4,192,768]{2,1,0:T(8,128)(2,1)}, bf16[4,192,768]{2,1,0:T(8,128)(2,1)}) custom-call(s32[2]{0:T(128)} %copy-done.78, bf16[2,128,3072]{2,1,0:T(8,128)(2,1)} %copy-done.4, bf16[2,128,3072]{2,1,0:T(8,128)(2,1)} %collective-permute-done.39.f13, ...), custom_call_target="tpu_custom_call" | custom-call | flops 1 | bytes 1 | tf_op jit(solution)/shard_map/bundle/pallas_call | solution.py:817
  288.9 6.8 %collective-permute-done.46.ahead = bf16[2,384,512]{2,1,0:T(8,128)(2,1)} collective-permute-done((bf16[2,384,512]{2,1,0:T(8,128)(2,1)}, bf16[2,384,512]{2,1,0:T(8,128)(2,1)}, u32[]{:S(2)}, u32[]{:S(2)}) %collective-permute-start.46) | collective-permute-done | bytes 786464 | tf_op jit(solution)/shard_map/ppermute | solution.py:33
  295.7 15.6 %collective-permute-done.47.behind = bf16[2,384,512]{2,1,0:T(8,128)(2,1)} collective-permute-done((bf16[2,384,512]{2,1,0:T(8,128)(2,1)}, bf16[2,384,512]{2,1,0:T(8,128)(2,1)}, u32[]{:S(2)}, u32[]{:S(2)}) %collective-permute-start.47) | collective-permute-done | bytes 786464 | tf_op jit(solution)/shard_map/ppermute | solution.py:33
  311.3 7.7 %tail.1 = (bf16[1168,512]{1,0:T(8,128)(2,1)}, bf16[1024,384]{1,0:T(8,128)(2,1)}, f32[512,384]{1,0:T(8,128)}, bf16[512,384]{1,0:T(8,128)(2,1)}) custom-call(s32[1]{0:T(128)} %bitcast.1.place, f32[384,512]{1,0:T(8,128)} %get-tuple-element.284.dq, f32[2,384,512]{2,1,0:T(8,128)} %get-tuple-element.285.kept, bf16[2,384,512]{2,1,0:T(8,128)(2,1)} %collective-permute-done.46.ahead, ...), custom_call_target="tpu_custom_call" | custom-call | flops 1 | bytes 1 | tf_op jit(solution)/shard_map/tail/pallas_call | solution.py:395
  319.9 7.2 %collective-permute-start.51 = (bf16[1,192,1536]{2,1,0:T(8,128)(2,1)}, bf16[1,192,1536]{2,1,0:T(8,128)(2,1)}, u32[]{:S(2)}, u32[]{:S(2)}) collective-permute-start(bf16[1,192,1536]{2,1,0:T(8,128)(2,1)} %constant_dynamic-slice_fusion.22), channel_id=1, source_target_pairs={{0,4},{1,5},{2,6},{3,7},{4,0},{5,1},{6,2},{7,3},{8,12},{9,13},{10,... | collective-permute-start | bytes 1769480 | tf_op jit(solution)/shard_map/ppermute | solution.py:27
  327.7 7.8 %meet_cols.3 = (bf16[384,1536]{1,0:T(8,128)(2,1)}, bf16[384,1536]{1,0:T(8,128)(2,1)}) custom-call(s32[1]{0:T(128)} %bitcast.12.side, bf16[2,768,128]{2,1,0:T(8,128)(2,1)} %copy-done.9, bf16[2,768,128]{2,1,0:T(8,128)(2,1)} %collective-permute-done.34.p1, bf16[2,768,128]{2,1,0:T(8,128)(2,1)} %copy-done.27, bf16[2,768,128]{2,1,0:T(8,128)(2,1)} %collective-permute-done.35.p3, ...), custom_call_target="tpu_custom_call" | custom-call | flops 1 | bytes 1 | tf_op jit(solution)/shard_map/meet_cols/pallas_call | solution.py:732
  338.3 1.9 collective-permute-start.63
  341.3 12.9 %collective-permute-done.51 = bf16[1,192,1536]{2,1,0:T(8,128)(2,1)} collective-permute-done((bf16[1,192,1536]{2,1,0:T(8,128)(2,1)}, bf16[1,192,1536]{2,1,0:T(8,128)(2,1)}, u32[]{:S(2)}, u32[]{:S(2)}) %collective-permute-start.51) | collective-permute-done | bytes 589856 | tf_op jit(solution)/shard_map/ppermute | solution.py:27
  358.6 2.3 add_bitcast_fusion
  360.9 4.3 collective-permute-done.52
  366.2 6.5 %down.1 = (bf16[256,1536]{1,0:T(8,128)(2,1)}, f32[128,1536]{1,0:T(8,128)}, bf16[128,1536]{1,0:T(8,128)(2,1)}) custom-call(bf16[512,768]{1,0:T(8,128)(2,1)} %get-tuple-element.319.first, bf16[512,768]{1,0:T(8,128)(2,1)} %get-tuple-element.320.second, bf16[1536,1536]{1,0:T(8,128)(2,1)} %down_w.5), custom_call_target="tpu_custom_call" | custom-call | flops 1 | bytes 1 | tf_op jit(solution)/shard_map/down/pallas_call | solution.py:756
  373.8 2.2 multiply_reduce_fusion
  376.8 2.6 fusion.6
  382.0 1.6 add_convert_fusion
  384.6 1.6 collective-permute-start.59
  387.1 1.6 collective-permute-done.59
  388.6 3.4 collective-permute-start.64
  402.1 1.9 fusion.2
  408.6 28.8 %collective-permute-done.73 = bf16[2,192,768]{2,1,0:T(8,128)(2,1)} collective-permute-done((bf16[2,192,768]{2,1,0:T(8,128)(2,1)}, bf16[2,192,768]{2,1,0:T(8,128)(2,1)}, u32[]{:S(2)}, u32[]{:S(2)}) %collective-permute-start.73) | collective-permute-done | bytes 589856 | tf_op jit(solution)/shard_map/ppermute | solution.py:27
  440.3 1.6 collective-permute-start.55
  443.4 2.5 collective-permute-start.66
  445.9 1.6 add_convert_fusion.1
  447.5 6.7 %collective-permute-done.74 = bf16[1,192,768]{2,1,0:T(8,128)(2,1)S(1)} collective-permute-done((bf16[1,192,768]{2,1,0:T(8,128)(2,1)S(1)}, bf16[1,192,768]{2,1,0:T(8,128)(2,1)S(1)}, u32[]{:S(2)}, u32[]{:S(2)}) %collective-permute-start.74) | collective-permute-done | bytes 294944 | tf_op jit(solution)/shard_map/ppermute | solution.py:27
  456.4 1.7 collective-permute-done.67
  460.9 17.2 %collective-permute-done.68 = f32[1,6,48]{2,0,1:T(1,128)S(1)} collective-permute-done((f32[1,6,48]{2,0,1:T(1,128)S(1)}, f32[1,6,48]{2,0,1:T(1,128)S(1)}, u32[]{:S(2)}, u32[]{:S(2)}) %collective-permute-start.68) | collective-permute-done | bytes 1184 | tf_op jit(solution)/shard_map/ppermute | solution.py:27
  480.0 1.6 collective-permute-start.56
  482.6 4.2 collective-permute-done.56
  487.5 1.7 pad_maximum_fusion.2
  490.2 12.9 %collective-permute-done.72 = bf16[1,192,768]{2,1,0:T(8,128)(2,1)S(1)} collective-permute-done((bf16[1,192,768]{2,1,0:T(8,128)(2,1)S(1)}, bf16[1,192,768]{2,1,0:T(8,128)(2,1)S(1)}, u32[]{:S(2)}, u32[]{:S(2)}) %collective-permute-start.72) | collective-permute-done | bytes 294944 | tf_op jit(solution)/shard_map/ppermute | solution.py:27
  (395 shorter events, 95.1 us)
Async XLA Ops:
  0.7 19.5 %collective-permute-start = (bf16[512,384]{1,0:T(8,128)(2,1)}, bf16[512,384]{1,0:T(8,128)(2,1)S(1)}, u32[]{:S(2)}, u32[]{:S(2)}) collective-permute-start(bf16[512,384]{1,0:T(8,128)(2,1)} %x0.1), channel_id=1, source_target_pairs={{0,8},{8,0},{16,24},{24,16},{1,9},{9,1},{17,25},{25,17},{2,10},{10... | collective-permute-start | bytes 1179656 | tf_op jit(solution)/shard_map/ppermute | solution.py:27
  1.2 12.8 %collective-permute-start.1 = (bf16[512,384]{1,0:T(8,128)(2,1)}, bf16[512,384]{1,0:T(8,128)(2,1)S(1)}, u32[]{:S(2)}, u32[]{:S(2)}) collective-permute-start(bf16[512,384]{1,0:T(8,128)(2,1)} %x0.1), channel_id=1, source_target_pairs={{0,16},{8,24},{16,0},{24,8},{1,17},{9,25},{17,1},{25,9},{2,18},{10... | collective-permute-start | bytes 1179656 | tf_op jit(solution)/shard_map/ppermute | solution.py:27
  7.9 9.4 %collective-permute-start.3 = (f32[6,384]{1,0:T(8,128)S(1)}, f32[6,384]{1,0:T(8,128)S(1)}, u32[]{:S(2)}, u32[]{:S(2)}) collective-permute-start(f32[6,384]{1,0:T(8,128)S(1)} %stack.98.g0), channel_id=1, source_target_pairs={{0,8},{8,0},{16,24},{24,16},{1,9},{9,1},{17,25},{25,17},{2,10},{10... | collective-permute-start | bytes 27656 | tf_op jit(solution)/shard_map/ppermute | solution.py:27
  14.0 16.7 %collective-permute-start.6 = (bf16[512,384]{1,0:T(8,128)(2,1)}, bf16[512,384]{1,0:T(8,128)(2,1)S(1)}, u32[]{:S(2)}, u32[]{:S(2)}) collective-permute-start(bf16[512,384]{1,0:T(8,128)(2,1)} %param.43), channel_id=1, source_target_pairs={{0,1},{1,0},{2,3},{3,2},{4,5},{5,4},{6,7},{7,6},{8,9},{9,8},{10,11... | collective-permute-start | bytes 1179656 | tf_op jit(solution)/shard_map/ppermute | solution.py:27
  15.8 51.7 %collective-permute-start.9 = (bf16[1536,384]{1,0:T(8,128)(2,1)}, bf16[1536,384]{1,0:T(8,128)(2,1)}, u32[]{:S(2)}, u32[]{:S(2)}) collective-permute-start(bf16[1536,384]{1,0:T(8,128)(2,1)} %q0.3), channel_id=1, source_target_pairs={{0,16},{8,24},{16,0},{24,8},{1,17},{9,25},{17,1},{25,9},{2,18},{10... | collective-permute-start | bytes 3538952 | tf_op jit(solution)/shard_map/ppermute | solution.py:27
  17.3 52.1 %collective-permute-start.10 = (bf16[384,1536]{1,0:T(8,128)(2,1)}, bf16[384,1536]{1,0:T(8,128)(2,1)}, u32[]{:S(2)}, u32[]{:S(2)}) collective-permute-start(bf16[384,1536]{1,0:T(8,128)(2,1)} %o0.3), channel_id=1, source_target_pairs={{0,16},{8,24},{16,0},{24,8},{1,17},{9,25},{17,1},{25,9},{2,18},{10... | collective-permute-start | bytes 3538952 | tf_op jit(solution)/shard_map/ppermute | solution.py:27
  30.7 36.8 %collective-permute-start.7 = (bf16[2,384,512]{2,1,0:T(8,128)(2,1)}, bf16[2,384,512]{2,1,0:T(8,128)(2,1)S(1)}, u32[]{:S(2)}, u32[]{:S(2)}) collective-permute-start(bf16[2,384,512]{2,1,0:T(8,128)(2,1)} %get-tuple-element.198.kv.kv1), channel_id=1, source_target_pairs={{0,1},{1,2},{2,3},{3,4},{4,5},{5,6},{6,7},{8,9},{9,10},{10,11},{11... | collective-permute-start | bytes 2359304 | tf_op jit(solution)/shard_map/ppermute | solution.py:33
  33.0 34.6 %collective-permute-start.8 = (bf16[2,384,512]{2,1,0:T(8,128)(2,1)}, bf16[2,384,512]{2,1,0:T(8,128)(2,1)}, u32[]{:S(2)}, u32[]{:S(2)}) collective-permute-start(bf16[2,384,512]{2,1,0:T(8,128)(2,1)} %get-tuple-element.198.kv.kv1), channel_id=1, source_target_pairs={{1,0},{2,1},{3,2},{4,3},{5,4},{6,5},{7,6},{9,8},{10,9},{11,10},{12... | collective-permute-start | bytes 2359304 | tf_op jit(solution)/shard_map/ppermute | solution.py:33
  69.5 11.3 %collective-permute-start.12 = (bf16[1536,384]{1,0:T(8,128)(2,1)S(1)}, bf16[1536,384]{1,0:T(8,128)(2,1)}, u32[]{:S(2)}, u32[]{:S(2)}) collective-permute-start(bf16[1536,384]{1,0:T(8,128)(2,1)S(1)} %copy-done.6), channel_id=1, source_target_pairs={{0,8},{8,0},{16,24},{24,16},{1,9},{9,1},{17,25},{25,17},{2,10},{10... | collective-permute-start | bytes 3538952 | tf_op jit(solution)/shard_map/ppermute | solution.py:27
  69.5 11.3 %collective-permute-start.13 = (bf16[1536,384]{1,0:T(8,128)(2,1)}, bf16[1536,384]{1,0:T(8,128)(2,1)}, u32[]{:S(2)}, u32[]{:S(2)}) collective-permute-start(bf16[1536,384]{1,0:T(8,128)(2,1)} %collective-permute-done.9.q2), channel_id=1, source_target_pairs={{0,8},{8,0},{16,24},{24,16},{1,9},{9,1},{17,25},{25,17},{2,10},{10... | collective-permute-start | bytes 3538952 | tf_op jit(solution)/shard_map/ppermute | solution.py:27
  70.0 10.8 %collective-permute-start.14 = (bf16[384,1536]{1,0:T(8,128)(2,1)S(1)}, bf16[384,1536]{1,0:T(8,128)(2,1)}, u32[]{:S(2)}, u32[]{:S(2)}) collective-permute-start(bf16[384,1536]{1,0:T(8,128)(2,1)S(1)} %copy-done.7), channel_id=1, source_target_pairs={{0,8},{8,0},{16,24},{24,16},{1,9},{9,1},{17,25},{25,17},{2,10},{10... | collective-permute-start | bytes 3538952 | tf_op jit(solution)/shard_map/ppermute | solution.py:27
  70.0 10.8 %collective-permute-start.15 = (bf16[384,1536]{1,0:T(8,128)(2,1)}, bf16[384,1536]{1,0:T(8,128)(2,1)}, u32[]{:S(2)}, u32[]{:S(2)}) collective-permute-start(bf16[384,1536]{1,0:T(8,128)(2,1)} %collective-permute-done.10.o2), channel_id=1, source_target_pairs={{0,8},{8,0},{16,24},{24,16},{1,9},{9,1},{17,25},{25,17},{2,10},{10... | collective-permute-start | bytes 3538952 | tf_op jit(solution)/shard_map/ppermute | solution.py:27
  70.5 10.2 %collective-permute-start.11 = (bf16[256,384]{1,0:T(8,128)(2,1)S(1)}, bf16[256,384]{1,0:T(8,128)(2,1)S(1)}, u32[]{:S(2)}, u32[]{:S(2)}) collective-permute-start(bf16[256,384]{1,0:T(8,128)(2,1)S(1)} %copy-done.22), channel_id=1, source_target_pairs={{0,16},{8,24},{16,0},{24,8},{1,17},{9,25},{17,1},{25,9},{2,18},{10... | collective-permute-start | bytes 589832 | tf_op jit(solution)/shard_map/ppermute | solution.py:27
  84.7 11.2 %collective-permute-start.17 = (bf16[128,1536]{1,0:T(8,128)(2,1)S(1)}, bf16[128,1536]{1,0:T(8,128)(2,1)S(1)}, u32[]{:S(2)}, u32[]{:S(2)}) collective-permute-start(bf16[128,1536]{1,0:T(8,128)(2,1)S(1)} %add_convert_fusion.7), channel_id=1, source_target_pairs={{0,16},{8,24},{16,0},{24,8},{1,17},{9,25},{17,1},{25,9},{2,18},{10... | collective-permute-start | bytes 1179656 | tf_op jit(solution)/shard_map/ppermute | solution.py:27
  85.4 30.3 %collective-permute-start.19 = (bf16[768,512]{1,0:T(8,128)(2,1)}, bf16[768,512]{1,0:T(8,128)(2,1)S(1)}, u32[]{:S(2)}, u32[]{:S(2)}) collective-permute-start(bf16[768,512]{1,0:T(8,128)(2,1)} %get-tuple-element.231), channel_id=1, source_target_pairs={{0,1},{1,0},{2,3},{3,2},{4,5},{5,4},{6,7},{7,6},{8,9},{9,8},{10,11... | collective-permute-start | bytes 2359304 | tf_op jit(solution)/shard_map/ppermute | solution.py:27
  95.9 19.8 %collective-permute-start.20 = (bf16[2,512,384]{2,1,0:T(8,128)(2,1)S(1)}, bf16[2,512,384]{2,1,0:T(8,128)(2,1)S(1)}, u32[]{:S(2)}, u32[]{:S(2)}) collective-permute-start(bf16[2,512,384]{2,1,0:T(8,128)(2,1)S(1)} %pad_maximum_fusion.4.g0), channel_id=1, source_target_pairs={{0,16},{8,24},{16,0},{24,8},{1,17},{9,25},{17,1},{25,9},{2,18},{10... | collective-permute-start | bytes 2359304 | tf_op jit(solution)/shard_map/ppermute | solution.py:27
  116.6 11.4 %collective-permute-start.22 = (bf16[128,1536]{1,0:T(8,128)(2,1)}, bf16[128,1536]{1,0:T(8,128)(2,1)S(1)}, u32[]{:S(2)}, u32[]{:S(2)}) collective-permute-start(bf16[128,1536]{1,0:T(8,128)(2,1)} %get-tuple-element.234.n0), channel_id=1, source_target_pairs={{0,16},{8,24},{16,0},{24,8},{1,17},{9,25},{17,1},{25,9},{2,18},{10... | collective-permute-start | bytes 1179656 | tf_op jit(solution)/shard_map/ppermute | solution.py:27
  118.1 16.2 %collective-permute-start.24 = (bf16[2,512,384]{2,1,0:T(8,128)(2,1)S(1)}, bf16[2,512,384]{2,1,0:T(8,128)(2,1)S(1)}, u32[]{:S(2)}, u32[]{:S(2)}) collective-permute-start(bf16[2,512,384]{2,1,0:T(8,128)(2,1)S(1)} %pad_maximum_fusion.4.g0), channel_id=1, source_target_pairs={{0,8},{8,0},{16,24},{24,16},{1,9},{9,1},{17,25},{25,17},{2,10},{10... | collective-permute-start | bytes 2359304 | tf_op jit(solution)/shard_map/ppermute | solution.py:27
  118.1 16.9 %collective-permute-start.25 = (bf16[2,512,384]{2,1,0:T(8,128)(2,1)S(1)}, bf16[2,512,384]{2,1,0:T(8,128)(2,1)S(1)}, u32[]{:S(2)}, u32[]{:S(2)}) collective-permute-start(bf16[2,512,384]{2,1,0:T(8,128)(2,1)S(1)} %collective-permute-done.20.g2), channel_id=1, source_target_pairs={{0,8},{8,0},{16,24},{24,16},{1,9},{9,1},{17,25},{25,17},{2,10},{10... | collective-permute-start | bytes 2359304 | tf_op jit(solution)/shard_map/ppermute | solution.py:27
  128.0 6.3 %collective-permute-start.21 = (bf16[128,1536]{1,0:T(8,128)(2,1)}, bf16[128,1536]{1,0:T(8,128)(2,1)S(1)}, u32[]{:S(2)}, u32[]{:S(2)}) collective-permute-start(bf16[128,1536]{1,0:T(8,128)(2,1)} %get-tuple-element.234.n0), channel_id=1, source_target_pairs={{0,8},{8,0},{16,24},{24,16},{1,9},{9,1},{17,25},{25,17},{2,10},{10... | collective-permute-start | bytes 1179656 | tf_op jit(solution)/shard_map/ppermute | solution.py:27
  130.2 37.8 %collective-permute-start.28 = (bf16[128,3072]{1,0:T(8,128)(2,1)}, bf16[128,3072]{1,0:T(8,128)(2,1)}, u32[]{:S(2)}, u32[]{:S(2)}) collective-permute-start(bf16[128,3072]{1,0:T(8,128)(2,1)} %get-tuple-element.253), channel_id=1, source_target_pairs={{0,16},{8,24},{16,0},{24,8},{1,17},{9,25},{17,1},{25,9},{2,18},{10... | collective-permute-start | bytes 2359304 | tf_op jit(solution)/shard_map/ppermute | solution.py:27
  131.7 19.8 %collective-permute-start.26 = (bf16[768,128]{1,0:T(8,128)(2,1)}, bf16[768,128]{1,0:T(8,128)(2,1)}, u32[]{:S(2)}, u32[]{:S(2)}) collective-permute-start(bf16[768,128]{1,0:T(8,128)(2,1)} %get-tuple-element.245), channel_id=1, source_target_pairs={{0,1},{1,0},{2,3},{3,2},{4,5},{5,4},{6,7},{7,6},{8,9},{9,8},{10,11... | collective-permute-start | bytes 589832 | tf_op jit(solution)/shard_map/ppermute | solution.py:27
  152.6 15.4 %collective-permute-start.27 = (bf16[2,768,128]{2,1,0:T(8,128)(2,1)S(1)}, bf16[2,768,128]{2,1,0:T(8,128)(2,1)S(1)}, u32[]{:S(2)}, u32[]{:S(2)}) collective-permute-start(bf16[2,768,128]{2,1,0:T(8,128)(2,1)S(1)} %pad_maximum_fusion.6.p0), channel_id=1, source_target_pairs={{0,16},{8,24},{16,0},{24,8},{1,17},{9,25},{17,1},{25,9},{2,18},{10... | collective-permute-start | bytes 1179656 | tf_op jit(solution)/shard_map/ppermute | solution.py:27
  152.9 15.0 %collective-permute-start.29 = (bf16[384,512]{1,0:T(8,128)(2,1)}, bf16[384,512]{1,0:T(8,128)(2,1)S(1)}, u32[]{:S(2)}, u32[]{:S(2)}) collective-permute-start(bf16[384,512]{1,0:T(8,128)(2,1)} %get-tuple-element.254), channel_id=1, source_target_pairs={{0,1},{1,0},{2,3},{3,2},{4,5},{5,4},{6,7},{7,6},{8,9},{9,8},{10,11... | collective-permute-start | bytes 1179656 | tf_op jit(solution)/shard_map/ppermute | solution.py:27
  171.9 11.2 %collective-permute-start.31 = (bf16[128,1536]{1,0:T(8,128)(2,1)S(1)}, bf16[128,1536]{1,0:T(8,128)(2,1)S(1)}, u32[]{:S(2)}, u32[]{:S(2)}) collective-permute-start(bf16[128,1536]{1,0:T(8,128)(2,1)S(1)} %add_convert_fusion.6), channel_id=1, source_target_pairs={{0,16},{8,24},{16,0},{24,8},{1,17},{9,25},{17,1},{25,9},{2,18},{10... | collective-permute-start | bytes 1179656 | tf_op jit(solution)/shard_map/ppermute | solution.py:27
  173.7 32.5 %collective-permute-start.32 = (bf16[512,768]{1,0:T(8,128)(2,1)S(1)}, bf16[512,768]{1,0:T(8,128)(2,1)}, u32[]{:S(2)}, u32[]{:S(2)}) collective-permute-start(bf16[512,768]{1,0:T(8,128)(2,1)S(1)} %copy-done.38), channel_id=1, source_target_pairs={{0,1},{1,0},{2,3},{3,2},{4,5},{5,4},{6,7},{7,6},{8,9},{9,8},{10,11... | collective-permute-start | bytes 2359304 | tf_op jit(solution)/shard_map/ppermute | solution.py:27
  175.7 30.5 %collective-permute-start.33 = (bf16[384,512]{1,0:T(8,128)(2,1)}, bf16[384,512]{1,0:T(8,128)(2,1)}, u32[]{:S(2)}, u32[]{:S(2)}) collective-permute-start(bf16[384,512]{1,0:T(8,128)(2,1)} %get-tuple-element.262), channel_id=1, source_target_pairs={{0,1},{1,0},{2,3},{3,2},{4,5},{5,4},{6,7},{7,6},{8,9},{9,8},{10,11... | collective-permute-start | bytes 1179656 | tf_op jit(solution)/shard_map/ppermute | solution.py:27
  183.1 23.1 %collective-permute-start.34 = (bf16[2,768,128]{2,1,0:T(8,128)(2,1)S(1)}, bf16[2,768,128]{2,1,0:T(8,128)(2,1)}, u32[]{:S(2)}, u32[]{:S(2)}) collective-permute-start(bf16[2,768,128]{2,1,0:T(8,128)(2,1)S(1)} %pad_maximum_fusion.6.p0), channel_id=1, source_target_pairs={{0,8},{8,0},{16,24},{24,16},{1,9},{9,1},{17,25},{25,17},{2,10},{10... | collective-permute-start | bytes 1179656 | tf_op jit(solution)/shard_map/ppermute | solution.py:27
  183.1 23.1 %collective-permute-start.35 = (bf16[2,768,128]{2,1,0:T(8,128)(2,1)S(1)}, bf16[2,768,128]{2,1,0:T(8,128)(2,1)}, u32[]{:S(2)}, u32[]{:S(2)}) collective-permute-start(bf16[2,768,128]{2,1,0:T(8,128)(2,1)S(1)} %collective-permute-done.27.p2), channel_id=1, source_target_pairs={{0,8},{8,0},{16,24},{24,16},{1,9},{9,1},{17,25},{25,17},{2,10},{10... | collective-permute-start | bytes 1179656 | tf_op jit(solution)/shard_map/ppermute | solution.py:27
  206.3 23.2 %collective-permute-start.39 = (bf16[2,128,3072]{2,1,0:T(8,128)(2,1)S(1)}, bf16[2,128,3072]{2,1,0:T(8,128)(2,1)}, u32[]{:S(2)}, u32[]{:S(2)}) collective-permute-start(bf16[2,128,3072]{2,1,0:T(8,128)(2,1)S(1)} %pad_maximum_fusion.f02), channel_id=1, source_target_pairs={{0,8},{8,0},{16,24},{24,16},{1,9},{9,1},{17,25},{25,17},{2,10},{10... | collective-permute-start | bytes 4718600 | tf_op jit(solution)/shard_map/ppermute | solution.py:27
  206.4 20.5 %collective-permute-start.41 = (bf16[512,768]{1,0:T(8,128)(2,1)}, bf16[512,768]{1,0:T(8,128)(2,1)}, u32[]{:S(2)}, u32[]{:S(2)}) collective-permute-start(bf16[512,768]{1,0:T(8,128)(2,1)} %get-tuple-element.311.refs_2_), channel_id=1, source_target_pairs={{0,1},{1,0},{2,3},{3,2},{4,5},{5,4},{6,7},{7,6},{8,9},{9,8},{10,11... | collective-permute-start | bytes 2359304 | tf_op jit(solution)/shard_map/ppermute | solution.py:27
  208.5 11.4 %collective-permute-start.37 = (bf16[128,1536]{1,0:T(8,128)(2,1)}, bf16[128,1536]{1,0:T(8,128)(2,1)S(1)}, u32[]{:S(2)}, u32[]{:S(2)}) collective-permute-start(bf16[128,1536]{1,0:T(8,128)(2,1)} %get-tuple-element.325.g0.a0), channel_id=1, source_target_pairs={{0,16},{8,24},{16,0},{24,8},{1,17},{9,25},{17,1},{25,9},{2,18},{10... | collective-permute-start | bytes 1179656 | tf_op jit(solution)/shard_map/ppermute | solution.py:27
  211.3 17.8 %collective-permute-start.40 = (bf16[512,384]{1,0:T(8,128)(2,1)S(1)}, bf16[512,384]{1,0:T(8,128)(2,1)}, u32[]{:S(2)}, u32[]{:S(2)}) collective-permute-start(bf16[512,384]{1,0:T(8,128)(2,1)S(1)} %pad_maximum_fusion.7), channel_id=1, source_target_pairs={{0,8},{8,0},{16,24},{24,16},{1,9},{9,1},{17,25},{25,17},{2,10},{10... | collective-permute-start | bytes 1179656 | tf_op jit(solution)/shard_map/ppermute | solution.py:27
  211.4 18.0 %collective-permute-start.36 = (bf16[128,1536]{1,0:T(8,128)(2,1)S(1)}, bf16[128,1536]{1,0:T(8,128)(2,1)S(1)}, u32[]{:S(2)}, u32[]{:S(2)}) collective-permute-start(bf16[128,1536]{1,0:T(8,128)(2,1)S(1)} %copy-done.10), channel_id=1, source_target_pairs={{0,8},{8,0},{16,24},{24,16},{1,9},{9,1},{17,25},{25,17},{2,10},{10... | collective-permute-start | bytes 1179656 | tf_op jit(solution)/shard_map/ppermute | solution.py:27
  219.9 9.6 %collective-permute-start.38 = (bf16[128,1536]{1,0:T(8,128)(2,1)S(1)}, bf16[128,1536]{1,0:T(8,128)(2,1)S(1)}, u32[]{:S(2)}, u32[]{:S(2)}) collective-permute-start(bf16[128,1536]{1,0:T(8,128)(2,1)S(1)} %collective-permute-done.37.g2.a2), channel_id=1, source_target_pairs={{0,8},{8,0},{16,24},{24,16},{1,9},{9,1},{17,25},{25,17},{2,10},{10... | collective-permute-start | bytes 1179656 | tf_op jit(solution)/shard_map/ppermute | solution.py:27
  226.9 28.3 %collective-permute-start.44 = (bf16[2,192,1536]{2,1,0:T(8,128)(2,1)}, bf16[2,192,1536]{2,1,0:T(8,128)(2,1)}, u32[]{:S(2)}, u32[]{:S(2)}) collective-permute-start(bf16[2,192,1536]{2,1,0:T(8,128)(2,1)} %bitcast.143), channel_id=1, source_target_pairs={{0,2},{1,3},{2,0},{3,1},{4,6},{5,7},{6,4},{7,5},{8,10},{9,11},{10,... | collective-permute-start | bytes 3538952 | tf_op jit(solution)/shard_map/ppermute | solution.py:27
  229.2 21.4 %collective-permute-start.43 = (bf16[512,768]{1,0:T(8,128)(2,1)}, bf16[512,768]{1,0:T(8,128)(2,1)}, u32[]{:S(2)}, u32[]{:S(2)}) collective-permute-start(bf16[512,768]{1,0:T(8,128)(2,1)} %get-tuple-element.342.refs_0_), channel_id=1, source_target_pairs={{0,1},{1,0},{2,3},{3,2},{4,5},{5,4},{6,7},{7,6},{8,9},{9,8},{10,11... | collective-permute-start | bytes 2359304 | tf_op jit(solution)/shard_map/ppermute | solution.py:27
  229.5 25.8 %collective-permute-start.42 = (bf16[128,3072]{1,0:T(8,128)(2,1)}, bf16[128,3072]{1,0:T(8,128)(2,1)S(1)}, u32[]{:S(2)}, u32[]{:S(2)}) collective-permute-start(bf16[128,3072]{1,0:T(8,128)(2,1)} %get-tuple-element.289), channel_id=1, source_target_pairs={{0,16},{8,24},{16,0},{24,8},{1,17},{9,25},{17,1},{25,9},{2,18},{10... | collective-permute-start | bytes 2359304 | tf_op jit(solution)/shard_map/ppermute | solution.py:27
  232.1 23.2 %collective-permute-start.45 = (bf16[256,384]{1,0:T(8,128)(2,1)S(1)}, bf16[256,384]{1,0:T(8,128)(2,1)S(1)}, u32[]{:S(2)}, u32[]{:S(2)}) collective-permute-start(bf16[256,384]{1,0:T(8,128)(2,1)S(1)} %add_convert_fusion.9), channel_id=1, source_target_pairs={{0,16},{8,24},{16,0},{24,8},{1,17},{9,25},{17,1},{25,9},{2,18},{10... | collective-permute-start | bytes 589832 | tf_op jit(solution)/shard_map/ppermute | solution.py:27
  257.7 20.4 %collective-permute-start.48 = (bf16[2,128,3072]{2,1,0:T(8,128)(2,1)S(1)}, bf16[2,128,3072]{2,1,0:T(8,128)(2,1)}, u32[]{:S(2)}, u32[]{:S(2)}) collective-permute-start(bf16[2,128,3072]{2,1,0:T(8,128)(2,1)S(1)} %pad_maximum_fusion.1.b02), channel_id=1, source_target_pairs={{0,8},{8,0},{16,24},{24,16},{1,9},{9,1},{17,25},{25,17},{2,10},{10... | collective-permute-start | bytes 4718600 | tf_op jit(solution)/shard_map/ppermute | solution.py:27
  258.8 68.9 %collective-permute-start.61 = (bf16[512,768]{1,0:T(8,128)(2,1)}, bf16[512,768]{1,0:T(8,128)(2,1)}, u32[]{:S(2)}, u32[]{:S(2)}) collective-permute-start(bf16[512,768]{1,0:T(8,128)(2,1)} %get-tuple-element.344.refs_2_), channel_id=1, source_target_pairs={{0,1},{1,0},{2,3},{3,2},{4,5},{5,4},{6,7},{7,6},{8,9},{9,8},{10,11... | collective-permute-start | bytes 2359304 | tf_op jit(solution)/shard_map/ppermute | solution.py:27
  260.1 35.6 %collective-permute-start.46 = (bf16[2,384,512]{2,1,0:T(8,128)(2,1)}, bf16[2,384,512]{2,1,0:T(8,128)(2,1)}, u32[]{:S(2)}, u32[]{:S(2)}) collective-permute-start(bf16[2,384,512]{2,1,0:T(8,128)(2,1)} %get-tuple-element.293), channel_id=1, source_target_pairs={{1,0},{2,1},{3,2},{4,3},{5,4},{6,5},{7,6},{9,8},{10,9},{11,10},{12... | collective-permute-start | bytes 2359304 | tf_op jit(solution)/shard_map/ppermute | solution.py:33
  261.4 50.0 %collective-permute-start.47 = (bf16[2,384,512]{2,1,0:T(8,128)(2,1)}, bf16[2,384,512]{2,1,0:T(8,128)(2,1)}, u32[]{:S(2)}, u32[]{:S(2)}) collective-permute-start(bf16[2,384,512]{2,1,0:T(8,128)(2,1)} %get-tuple-element.294), channel_id=1, source_target_pairs={{0,1},{1,2},{2,3},{3,4},{4,5},{5,6},{6,7},{8,9},{9,10},{10,11},{11... | collective-permute-start | bytes 2359304 | tf_op jit(solution)/shard_map/ppermute | solution.py:33
  274.4 80.2 %collective-permute-start.50 = (bf16[2,192,1536]{2,1,0:T(8,128)(2,1)}, bf16[2,192,1536]{2,1,0:T(8,128)(2,1)}, u32[]{:S(2)}, u32[]{:S(2)}) collective-permute-start(bf16[2,192,1536]{2,1,0:T(8,128)(2,1)} %bitcast.142), channel_id=1, source_target_pairs={{0,2},{1,3},{2,0},{3,1},{4,6},{5,7},{6,4},{7,5},{8,10},{9,11},{10,... | collective-permute-start | bytes 3538952 | tf_op jit(solution)/shard_map/ppermute | solution.py:27
  319.1 19.2 %collective-permute-start.49 = (bf16[1024,384]{1,0:T(8,128)(2,1)}, bf16[1024,384]{1,0:T(8,128)(2,1)}, u32[]{:S(2)}, u32[]{:S(2)}) collective-permute-start(bf16[1024,384]{1,0:T(8,128)(2,1)} %get-tuple-element.304), channel_id=1, source_target_pairs={{0,8},{8,0},{16,24},{24,16},{1,9},{9,1},{17,25},{25,17},{2,10},{10... | collective-permute-start | bytes 2359304 | tf_op jit(solution)/shard_map/ppermute | solution.py:27
  319.9 34.3 %collective-permute-start.51 = (bf16[1,192,1536]{2,1,0:T(8,128)(2,1)}, bf16[1,192,1536]{2,1,0:T(8,128)(2,1)}, u32[]{:S(2)}, u32[]{:S(2)}) collective-permute-start(bf16[1,192,1536]{2,1,0:T(8,128)(2,1)} %constant_dynamic-slice_fusion.22), channel_id=1, source_target_pairs={{0,4},{1,5},{2,6},{3,7},{4,0},{5,1},{6,2},{7,3},{8,12},{9,13},{10,... | collective-permute-start | bytes 1769480 | tf_op jit(solution)/shard_map/ppermute | solution.py:27
  327.2 38.1 %collective-permute-start.53 = (bf16[1168,512]{1,0:T(8,128)(2,1)}, bf16[1168,512]{1,0:T(8,128)(2,1)}, u32[]{:S(2)}, u32[]{:S(2)}) collective-permute-start(bf16[1168,512]{1,0:T(8,128)(2,1)} %get-tuple-element.317), channel_id=1, source_target_pairs={{0,1},{1,0},{2,3},{3,2},{4,5},{5,4},{6,7},{7,6},{8,9},{9,8},{10,11... | collective-permute-start | bytes 3588104 | tf_op jit(solution)/shard_map/ppermute | solution.py:27
  335.5 56.6 %collective-permute-start.62 = (bf16[2,192,1536]{2,1,0:T(8,128)(2,1)}, bf16[2,192,1536]{2,1,0:T(8,128)(2,1)}, u32[]{:S(2)}, u32[]{:S(2)}) collective-permute-start(bf16[2,192,1536]{2,1,0:T(8,128)(2,1)} %bitcast.141), channel_id=1, source_target_pairs={{0,2},{1,3},{2,0},{3,1},{4,6},{5,7},{6,4},{7,5},{8,10},{9,11},{10,... | collective-permute-start | bytes 3538952 | tf_op jit(solution)/shard_map/ppermute | solution.py:27
  338.3 43.7 %collective-permute-start.63 = (bf16[4,192,768]{2,1,0:T(8,128)(2,1)}, bf16[4,192,768]{2,1,0:T(8,128)(2,1)}, u32[]{:S(2)}, u32[]{:S(2)}) collective-permute-start(bf16[4,192,768]{2,1,0:T(8,128)(2,1)} %get-tuple-element.353), channel_id=1, source_target_pairs={{0,1},{1,0},{2,3},{3,2},{4,5},{5,4},{6,7},{7,6},{8,9},{9,8},{10,11... | collective-permute-start | bytes 3538952 | tf_op jit(solution)/shard_map/ppermute | solution.py:27
  354.2 87.7 %collective-permute-start.65 = (bf16[4,192,768]{2,1,0:T(8,128)(2,1)}, bf16[4,192,768]{2,1,0:T(8,128)(2,1)}, u32[]{:S(2)}, u32[]{:S(2)}) collective-permute-start(bf16[4,192,768]{2,1,0:T(8,128)(2,1)} %get-tuple-element.356), channel_id=1, source_target_pairs={{0,1},{1,0},{2,3},{3,2},{4,5},{5,4},{6,7},{7,6},{8,9},{9,8},{10,11... | collective-permute-start | bytes 3538952 | tf_op jit(solution)/shard_map/ppermute | solution.py:27
  354.7 10.6 %collective-permute-start.52 = (bf16[512,384]{1,0:T(8,128)(2,1)S(1)}, bf16[512,384]{1,0:T(8,128)(2,1)S(1)}, u32[]{:S(2)}, u32[]{:S(2)}) collective-permute-start(bf16[512,384]{1,0:T(8,128)(2,1)S(1)} %add_convert_fusion.5), channel_id=1, source_target_pairs={{0,16},{8,24},{16,0},{24,8},{1,17},{9,25},{17,1},{25,9},{2,18},{10... | collective-permute-start | bytes 1179656 | tf_op jit(solution)/shard_map/ppermute | solution.py:27
  365.3 27.9 %collective-permute-start.60 = (bf16[1,192,1536]{2,1,0:T(8,128)(2,1)}, bf16[1,192,1536]{2,1,0:T(8,128)(2,1)}, u32[]{:S(2)}, u32[]{:S(2)}) collective-permute-start(bf16[1,192,1536]{2,1,0:T(8,128)(2,1)} %constant_dynamic-slice_fusion.12), channel_id=1, source_target_pairs={{0,4},{1,5},{2,6},{3,7},{4,0},{5,1},{6,2},{7,3},{8,12},{9,13},{10,... | collective-permute-start | bytes 1769480 | tf_op jit(solution)/shard_map/ppermute | solution.py:27
  372.8 66.5 %collective-permute-start.54 = (bf16[256,1536]{1,0:T(8,128)(2,1)}, bf16[256,1536]{1,0:T(8,128)(2,1)}, u32[]{:S(2)}, u32[]{:S(2)}) collective-permute-start(bf16[256,1536]{1,0:T(8,128)(2,1)} %get-tuple-element.322), channel_id=1, source_target_pairs={{0,8},{8,0},{16,24},{24,16},{1,9},{9,1},{17,25},{25,17},{2,10},{10... | collective-permute-start | bytes 2359304 | tf_op jit(solution)/shard_map/ppermute | solution.py:27
  388.6 53.3 %collective-permute-start.64 = (bf16[2,192,1152]{2,1,0:T(8,128)(2,1)}, bf16[2,192,1152]{2,1,0:T(8,128)(2,1)}, u32[]{:S(2)}, u32[]{:S(2)}) collective-permute-start(bf16[2,192,1152]{2,1,0:T(8,128)(2,1)} %dynamic-slice_bitcast_fusion), channel_id=1, source_target_pairs={{0,2},{1,3},{2,0},{3,1},{4,6},{5,7},{6,4},{7,5},{8,10},{9,11},{10,... | collective-permute-start | bytes 2654216 | tf_op jit(solution)/shard_map/ppermute | solution.py:27
  392.1 45.3 %collective-permute-start.73 = (bf16[2,192,768]{2,1,0:T(8,128)(2,1)}, bf16[2,192,768]{2,1,0:T(8,128)(2,1)}, u32[]{:S(2)}, u32[]{:S(2)}) collective-permute-start(bf16[2,192,768]{2,1,0:T(8,128)(2,1)} %dynamic-slice_bitcast_fusion.1), channel_id=1, source_target_pairs={{0,2},{1,3},{2,0},{3,1},{4,6},{5,7},{6,4},{7,5},{8,10},{9,11},{10,... | collective-permute-start | bytes 1769480 | tf_op jit(solution)/shard_map/ppermute | solution.py:27
  404.2 82.9 %collective-permute-start.71 = (bf16[1,192,1536]{2,1,0:T(8,128)(2,1)S(1)}, bf16[1,192,1536]{2,1,0:T(8,128)(2,1)S(1)}, u32[]{:S(2)}, u32[]{:S(2)}) collective-permute-start(bf16[1,192,1536]{2,1,0:T(8,128)(2,1)S(1)} %constant_dynamic-slice_fusion.2), channel_id=1, source_target_pairs={{0,4},{1,5},{2,6},{3,7},{4,0},{5,1},{6,2},{7,3},{8,12},{9,13},{10,... | collective-permute-start | bytes 1769480 | tf_op jit(solution)/shard_map/ppermute | solution.py:27
  438.6 15.6 %collective-permute-start.74 = (bf16[1,192,768]{2,1,0:T(8,128)(2,1)S(1)}, bf16[1,192,768]{2,1,0:T(8,128)(2,1)S(1)}, u32[]{:S(2)}, u32[]{:S(2)}) collective-permute-start(bf16[1,192,768]{2,1,0:T(8,128)(2,1)S(1)} %constant_dynamic-slice_fusion), channel_id=1, source_target_pairs={{0,4},{1,5},{2,6},{3,7},{4,0},{5,1},{6,2},{7,3},{8,12},{9,13},{10,... | collective-permute-start | bytes 884744 | tf_op jit(solution)/shard_map/ppermute | solution.py:27
  440.3 38.3 %collective-permute-start.55 = (bf16[128,1536]{1,0:T(8,128)(2,1)S(1)}, bf16[128,1536]{1,0:T(8,128)(2,1)S(1)}, u32[]{:S(2)}, u32[]{:S(2)}) collective-permute-start(bf16[128,1536]{1,0:T(8,128)(2,1)S(1)} %add_convert_fusion.4), channel_id=1, source_target_pairs={{0,16},{8,24},{16,0},{24,8},{1,17},{9,25},{17,1},{25,9},{2,18},{10... | collective-permute-start | bytes 1179656 | tf_op jit(solution)/shard_map/ppermute | solution.py:27
  443.4 11.0 %collective-permute-start.66 = (f32[4,6,48]{2,0,1:T(4,128)S(1)}, f32[4,6,48]{2,0,1:T(4,128)S(1)}, u32[]{:S(2)}, u32[]{:S(2)}) collective-permute-start(f32[4,6,48]{2,0,1:T(4,128)S(1)} %bitcast.135), channel_id=1, source_target_pairs={{0,2},{1,3},{2,0},{3,1},{4,6},{5,7},{6,4},{7,5},{8,10},{9,11},{10,... | collective-permute-start | bytes 13832 | tf_op jit(solution)/shard_map/ppermute | solution.py:27
  456.4 25.2 %collective-permute-start.69 = (bf16[1,192,1152]{2,1,0:T(8,128)(2,1)S(1)}, bf16[1,192,1152]{2,1,0:T(8,128)(2,1)S(1)}, u32[]{:S(2)}, u32[]{:S(2)}) collective-permute-start(bf16[1,192,1152]{2,1,0:T(8,128)(2,1)S(1)} %constant_dynamic-slice_fusion.3), channel_id=1, source_target_pairs={{0,4},{1,5},{2,6},{3,7},{4,0},{5,1},{6,2},{7,3},{8,12},{9,13},{10,... | collective-permute-start | bytes 1327112 | tf_op jit(solution)/shard_map/ppermute | solution.py:27
  458.1 20.0 %collective-permute-start.68 = (f32[1,6,48]{2,0,1:T(1,128)S(1)}, f32[1,6,48]{2,0,1:T(1,128)S(1)}, u32[]{:S(2)}, u32[]{:S(2)}) collective-permute-start(f32[1,6,48]{2,0,1:T(1,128)S(1)} %constant_dynamic-slice_fusion.4), channel_id=1, source_target_pairs={{0,4},{1,5},{2,6},{3,7},{4,0},{5,1},{6,2},{7,3},{8,12},{9,13},{10,... | collective-permute-start | bytes 3464 | tf_op jit(solution)/shard_map/ppermute | solution.py:27
  459.5 27.5 %collective-permute-start.70 = (bf16[2,192,768]{2,1,0:T(8,128)(2,1)S(1)}, bf16[2,192,768]{2,1,0:T(8,128)(2,1)S(1)}, u32[]{:S(2)}, u32[]{:S(2)}) collective-permute-start(bf16[2,192,768]{2,1,0:T(8,128)(2,1)S(1)} %dynamic-slice_bitcast_fusion.2), channel_id=1, source_target_pairs={{0,2},{1,3},{2,0},{3,1},{4,6},{5,7},{6,4},{7,5},{8,10},{9,11},{10,... | collective-permute-start | bytes 1769480 | tf_op jit(solution)/shard_map/ppermute | solution.py:27
  480.0 6.8 %collective-permute-start.56 = (bf16[128,768]{1,0:T(8,128)(2,1)S(1)}, bf16[128,768]{1,0:T(8,128)(2,1)S(1)}, u32[]{:S(2)}, u32[]{:S(2)}) collective-permute-start(bf16[128,768]{1,0:T(8,128)(2,1)S(1)} %pad_maximum_fusion.12), channel_id=1, source_target_pairs={{0,16},{8,24},{16,0},{24,8},{1,17},{9,25},{17,1},{25,9},{2,18},{10... | collective-permute-start | bytes 589832 | tf_op jit(solution)/shard_map/ppermute | solution.py:27
  487.2 16.0 %collective-permute-start.72 = (bf16[1,192,768]{2,1,0:T(8,128)(2,1)S(1)}, bf16[1,192,768]{2,1,0:T(8,128)(2,1)S(1)}, u32[]{:S(2)}, u32[]{:S(2)}) collective-permute-start(bf16[1,192,768]{2,1,0:T(8,128)(2,1)S(1)} %constant_dynamic-slice_fusion.1), channel_id=1, source_target_pairs={{0,4},{1,5},{2,6},{3,7},{4,0},{5,1},{6,2},{7,3},{8,12},{9,13},{10,... | collective-permute-start | bytes 884744 | tf_op jit(solution)/shard_map/ppermute | solution.py:27
  (94 other events, 727.6 us)
